TPU v7x, 256 devices: a whole 4x4x8 slice. The times are simulated.
256 devices in a mesh: tm: 64 (over y_hi, x, z), rows: 4 (over y_lo, core).
Axes of the slice: x: 4, y: 4 (y_hi: 2, y_lo: 2; y = y_hi * 2 + y_lo), z: 8, core: 2. Of those that a mesh axis runs over, the one named last changes fastest.
Arguments:
- frames: bfloat16 [64, 32, 32, 640], P('tm', 'rows'), may hold values from -24 to 24
- conv_weight: bfloat16 [3, 3, 640, 640], replicated, may hold values from -0.078125 to 0.078125
- conv_bias: float32 [640], replicated, may hold values from -1.5 to 1.5
- ref_features: bfloat16 [1024, 640], P('tm'), may hold values from -6 to 6
- w_query: bfloat16 [640, 640], replicated, may hold values from -0.25 to 0.25
- w_key: bfloat16 [640, 640], replicated, may hold values from -0.25 to 0.25
- w_value: bfloat16 [640, 640], replicated, may hold values from -0.25 to 0.25
- w_out: bfloat16 [640, 640], replicated, may hold values from -0.25 to 0.25
- out_bias: float32 [640], replicated, may hold values from -1.5 to 1.5
Outputs:
- hidden: bfloat16 [64, 32, 32, 640], P('tm', 'rows')
- attended: bfloat16 [64, 32, 32, 640], P('tm', 'rows')
All inputs are finite; a program needn't handle non-finite values.
Results may differ from a plain program's by a relative error of at most 0.025.
Values may be sent and summed in bfloat16 or wider, within the bound.
A program may use at most 128 MiB of HBM per device.

v0:
```python
import jax
import jax.numpy as jnp
from jax import lax
from jax.sharding import PartitionSpec as P

HD = 80


key_block = 1024


def extended(value, sides, width):
    for axis, dim in sides:
        size, length = (lax.axis_size(axis), value.shape[dim])
        up = [(i, (i + 1) % size) for i in range(size - 1)]
        down = [(j, i) for i, j in up]
        last = lax.slice_in_dim(value, length - width, length, axis=dim)
        initial = lax.slice_in_dim(value, 0, width, axis=dim)
        before = lax.ppermute(last, axis, up)
        after = lax.ppermute(initial, axis, down)
        value = jnp.concatenate([before, value, after], axis=dim)
    return value


def attend_update(carry, query_heads, keys, values, heads):
    top, total, summed = carry
    count, band = (query_heads.shape[0], query_heads.shape[1])
    length = keys.shape[1]
    summed = summed.reshape(count, band, heads, HD)
    width = min(key_block, length)
    key_part = keys.reshape(keys.shape[0], width, heads, HD)
    value_part = values.reshape(values.shape[0], width, heads, HD)
    scores = jnp.einsum(
        "fqhd,khd->fhqk", query_heads, key_part[0], preferred_element_type=jnp.float32
    )
    scores = scores * HD ** (-0.5)
    new_top = jnp.maximum(top, jnp.max(scores, axis=3))
    factor = jnp.exp(top - new_top)
    weights = jnp.exp(scores - new_top[..., None])
    total = total * factor + jnp.sum(weights, axis=3)
    product = jnp.einsum(
        "fhqk,khd->fqhd",
        weights.astype(jnp.bfloat16),
        value_part[0],
        preferred_element_type=jnp.float32,
    )
    summed = summed * jnp.transpose(factor, (0, 2, 1))[..., None] + product
    return (new_top, total, summed.reshape(count, band, heads * HD))


def project_pair(source, w_key, w_value, count, channels):
    key = (
        jnp.dot(source, w_key, preferred_element_type=jnp.float32)
        .astype(jnp.bfloat16)
        .reshape(count, -1, channels)
    )
    value = (
        jnp.dot(source, w_value, preferred_element_type=jnp.float32)
        .astype(jnp.bfloat16)
        .reshape(count, -1, channels)
    )
    return (key, value)


def shards(frames, conv_weight, conv_bias, ref_features, w_query, w_key, w_value, w_out, out_bias):
    count, band_rows, width, channels = frames.shape
    heads = channels // HD
    band = band_rows * width
    activated = jax.nn.silu(frames.astype(jnp.float32)).astype(jnp.bfloat16)
    padded = extended(activated, (("rows", 1),), 1)
    padded = jnp.pad(padded, ((0, 0), (0, 0), (1, 1), (0, 0)))
    convolved = jnp.zeros((count * band, channels), jnp.float32)
    for row_tap in range(3):
        for col_tap in range(3):
            window = padded[:, row_tap : row_tap + band_rows, col_tap : col_tap + width].reshape(
                count * band, channels
            )
            convolved = convolved + jnp.dot(
                window, conv_weight[row_tap, col_tap], preferred_element_type=jnp.float32
            )
    hidden = (
        frames.reshape(count * band, channels).astype(jnp.float32) + convolved + conv_bias
    ).astype(jnp.bfloat16)
    query = jnp.dot(hidden, w_query, preferred_element_type=jnp.float32).astype(jnp.bfloat16)
    query_heads = query.reshape(count, band, heads, HD)
    start_state = (
        jnp.full((count, heads, band), -1e30, jnp.float32),
        jnp.zeros((count, heads, band), jnp.float32),
        jnp.zeros((count, band, channels), jnp.float32),
    )
    key, value = project_pair(hidden, w_key, w_value, count, channels)
    all_keys, all_values = (
        lax.all_gather(key, "rows", axis=1, tiled=True),
        lax.all_gather(value, "rows", axis=1, tiled=True),
    )
    state = attend_update(start_state, query_heads, all_keys, all_values, heads)
    ref_key = jnp.dot(ref_features, w_key, preferred_element_type=jnp.float32).astype(jnp.bfloat16)
    ref_value = jnp.dot(ref_features, w_value, preferred_element_type=jnp.float32).astype(
        jnp.bfloat16
    )
    every_key, every_value = (
        lax.all_gather(ref_key, "tm", axis=0, tiled=True),
        lax.all_gather(ref_value, "tm", axis=0, tiled=True),
    )
    state = attend_update(state, query_heads, every_key[None], every_value[None], heads)
    top, total, summed = state
    mixed = summed.reshape(count, band, heads, HD) / jnp.transpose(total, (0, 2, 1))[..., None]
    mixed = mixed.reshape(count * band, channels).astype(jnp.bfloat16)
    attended = (jnp.dot(mixed, w_out, preferred_element_type=jnp.float32) + out_bias).astype(
        jnp.bfloat16
    )
    return (
        hidden.reshape(count, band_rows, width, channels),
        attended.reshape(count, band_rows, width, channels),
    )


def solution(mesh):
    return jax.shard_map(
        shards,
        mesh=mesh,
        in_specs=(P("tm", "rows", None, None), P(), P(), P("tm", None), P(), P(), P(), P(), P()),
        out_specs=(P("tm", "rows", None, None), P("tm", "rows", None, None)),
        check_vma=False,
    )
```

profile of v0, /device:TPU:1, one launch (start us, length us, event | category | flops | bytes accessed | tf_op | source)
XLA Modules:
  0.0 326.9 jit_solution(8142130882859470929)
XLA Ops:
  7.2 0.0 copy-start
  7.2 0.0 all-gather.11.cloned.1.call-start
  7.2 0.0 copy-start.3
  7.2 1.3 multiply_convert_fusion
  8.6 4.9 %collective-permute-start = (bf16[1,1,32,640]{3,2,1,0:T(8,128)(2,1)S(1)}, bf16[1,1,32,640]{3,2,1,0:T(8,128)(2,1)S(1)}, u32[]{:S(2)}, u32[]{:S(2)}) collective-permute-start(bf16[1,1,32,640]{3,2,1,0:T(8,128)(2,1)S(1)} %get-tuple-element.10), channel_id=1, source_target_pairs={{0,1},{1,2},{2,3},{4,5},{5,6},{6,7},{8,9},{9,10},{10,11},{12,13},{... | collective-permute-start | bytes 122888 | tf_op jit(solution)/shard_map/ppermute | solution.py:19
  13.4 1.9 collective-permute-start.1
  15.4 3.4 %collective-permute-done.1 = bf16[1,1,32,640]{3,2,1,0:T(8,128)(2,1)S(1)} collective-permute-done((bf16[1,1,32,640]{3,2,1,0:T(8,128)(2,1)S(1)}, bf16[1,1,32,640]{3,2,1,0:T(8,128)(2,1)S(1)}, u32[]{:S(2)}, u32[]{:S(2)}) %collective-permute-start.1) | collective-permute-done | bytes 40992 | tf_op jit(solution)/shard_map/ppermute | solution.py:20
  18.8 0.2 fusion.67
  18.9 0.2 fusion.78
  19.1 1.6 fusion.52
  20.8 0.5 fusion.43
  21.2 0.1 pad_maximum_fusion
  21.3 0.5 convolution_add_fusion.7
  21.8 0.5 convolution_add_fusion.6
  22.3 0.5 convolution_add_fusion.5
  22.8 0.5 convolution_add_fusion.4
  23.2 0.5 convolution_add_fusion.3
  23.7 0.5 convolution_add_fusion.2
  24.2 0.5 fusion.35
  24.7 0.0 copy-start.4
  24.7 1.2 convolution_convert_fusion.2
  25.9 0.0 all-gather.11.cloned.1.call-update
  25.9 0.0 all-gather.13.cloned.1.call-start
  25.9 1.2 convolution_convert_fusion
  27.1 0.0 all-gather.13.cloned.1.call-update
  27.2 0.0 all-gather.7.cloned.1.call-start
  27.2 0.8 convolution_convert_fusion.4
  28.0 0.0 all-gather.7.cloned.1.call-update
  28.1 0.2 all-gather.9.cloned.1.call-start
  28.3 0.8 convolution_convert_fusion.3
  29.1 0.0 all-gather.9.cloned.1.call-update
  29.2 0.5 convolution_convert_fusion.1
  29.6 0.2 copy.20
  29.8 24.0 %all-gather.11.cloned.1.call-done = bf16[1024,640]{1,0:T(8,128)(2,1)} async-done(((bf16[256,640]{1,0:T(8,128)(2,1)}), bf16[1024,640]{1,0:T(8,128)(2,1)}) %all-gather.11.cloned.1.call-update) | async-done | bytes 1310736 | tf_op jit(solution)/shard_map/all_gather | solution.py:93
  53.8 1.6 copy.19
  55.4 4.5 %bitcast_reduce_fusion.1 = (f32[8,256]{1,0:T(8,128)S(1)}, f32[8,1024,256]{2,1,0:T(8,128)}) fusion(bf16[1024,8,80]{0,2,1:T(8,128)(2,1)S(1)} %bitcast.200, bf16[256,8,80]{0,2,1:T(8,128)(2,1)S(1)} %bitcast.201), kind=kOutput, calls=%fused_computation.4 | convolution fusion | flops 339736576 | bytes 10035200 | tf_op jit(solution)/shard_map/fqhd,khd->fhqk/dot_general | solution.py:33
  60.0 22.4 %all-gather.13.cloned.1.call-done = bf16[1024,640]{1,0:T(8,128)(2,1)} async-done(((bf16[256,640]{1,0:T(8,128)(2,1)}), bf16[1024,640]{1,0:T(8,128)(2,1)}) %all-gather.13.cloned.1.call-update) | async-done | bytes 1310736 | tf_op jit(solution)/shard_map/all_gather | solution.py:94
  82.4 1.6 copy.21
  84.0 113.8 %all-gather.7.cloned.1.call-done = bf16[1024,640]{1,0:T(8,128)(2,1)} async-done(((bf16[16,640]{1,0:T(8,128)(2,1)}), bf16[1024,640]{1,0:T(8,128)(2,1)}) %all-gather.7.cloned.1.call-update) | async-done | bytes 1310736 | tf_op jit(solution)/shard_map/all_gather | solution.py:102
  197.8 1.6 copy.23
  199.4 2.4 bitcast_reduce_fusion
  201.9 1.1 copy-done.1
  203.0 2.7 fusion.2
  205.8 1.6 fusion.31
  207.3 105.2 %all-gather.9.cloned.1.call-done = bf16[1024,640]{1,0:T(8,128)(2,1)} async-done(((bf16[16,640]{1,0:T(8,128)(2,1)}), bf16[1024,640]{1,0:T(8,128)(2,1)}) %all-gather.9.cloned.1.call-update) | async-done | bytes 1310736 | tf_op jit(solution)/shard_map/all_gather | solution.py:103
  312.5 1.6 copy.24
  314.2 5.0 %fusion.40 = bf16[1,256,8,80]{1,3,2,0:T(8,128)(2,1)S(1)} fusion(f32[1,256,8,80]{1,3,2,0:T(8,128)S(1)} %fusion.31, bf16[1024,8,80]{0,2,1:T(8,128)(2,1)S(1)} %bitcast.206, f32[8,1024,256]{2,1,0:T(8,128)} %copy-done.2, f32[8,256]{1,0:T(8,128)S(1)} %get-tuple-element.15, f32[256,8]{0,1:T(8,128)S(1)} %get-tuple-element.12), kind=kOutput, calls=%fused_computation.45 | convolution fusion | flops 342327296 | bytes 10698752 | tf_op jit(solution)/shard_map/fhqk,khd->fqhd/dot_general | solution.py:41
  319.2 1.2 fusion.34
  (26 shorter events, 0.1 us)
Async XLA Ops:
  7.2 17.5 %copy-start = (bf16[640,640]{1,0:T(8,128)(2,1)S(1)}, bf16[640,640]{1,0:T(8,128)(2,1)}, u32[]{:S(2)}) copy-start(bf16[640,640]{1,0:T(8,128)(2,1)} %param.14) | copy-start | bytes 2457604
  7.2 46.6 %all-gather.11.cloned.1.call-start = ((), (), s32[]{:S(2)}) async-start(), calls=%async_computation.2 | async-start | bytes 1638400 | tf_op jit(solution)/shard_map/all_gather | solution.py:93
  7.2 13.5 %copy-start.3 = (bf16[3,3,640,640]{3,2,1,0:T(8,128)(2,1)S(1)}, bf16[3,3,640,640]{3,2,1,0:T(8,128)(2,1)}, u32[]{:S(2)}) copy-start(bf16[3,3,640,640]{3,2,1,0:T(8,128)(2,1)} %param.10) | copy-start | bytes 22118404
  8.6 6.8 %collective-permute-start = (bf16[1,1,32,640]{3,2,1,0:T(8,128)(2,1)S(1)}, bf16[1,1,32,640]{3,2,1,0:T(8,128)(2,1)S(1)}, u32[]{:S(2)}, u32[]{:S(2)}) collective-permute-start(bf16[1,1,32,640]{3,2,1,0:T(8,128)(2,1)S(1)} %get-tuple-element.10), channel_id=1, source_target_pairs={{0,1},{1,2},{2,3},{4,5},{5,6},{6,7},{8,9},{9,10},{10,11},{12,13},{... | collective-permute-start | bytes 122888 | tf_op jit(solution)/shard_map/ppermute | solution.py:19
  13.4 5.3 %collective-permute-start.1 = (bf16[1,1,32,640]{3,2,1,0:T(8,128)(2,1)S(1)}, bf16[1,1,32,640]{3,2,1,0:T(8,128)(2,1)S(1)}, u32[]{:S(2)}, u32[]{:S(2)}) collective-permute-start(bf16[1,1,32,640]{3,2,1,0:T(8,128)(2,1)S(1)} %get-tuple-element.11), channel_id=1, source_target_pairs={{1,0},{2,1},{3,2},{5,4},{6,5},{7,6},{9,8},{10,9},{11,10},{13,12},{... | collective-permute-start | bytes 122888 | tf_op jit(solution)/shard_map/ppermute | solution.py:20
  21.3 2.9 copy-start.7
  21.3 2.9 copy-start.10
  22.2 3.7 %copy-start.5 = (bf16[640,640]{1,0:T(8,128)(2,1)S(1)}, bf16[640,640]{1,0:T(8,128)(2,1)}, u32[]{:S(2)}) copy-start(bf16[640,640]{1,0:T(8,128)(2,1)} %param.15) | copy-start | bytes 2457604
  22.7 4.5 %copy-start.9 = (bf16[16,640]{1,0:T(8,128)(2,1)S(1)}, bf16[16,640]{1,0:T(8,128)(2,1)}, u32[]{:S(2)}) copy-start(bf16[16,640]{1,0:T(8,128)(2,1)} %param.12) | copy-start | bytes 61444
  22.7 6.4 %copy-start.8 = (bf16[640,640]{1,0:T(8,128)(2,1)S(1)}, bf16[640,640]{1,0:T(8,128)(2,1)}, u32[]{:S(2)}) copy-start(bf16[640,640]{1,0:T(8,128)(2,1)} %param.13) | copy-start | bytes 2457604
  24.7 35.3 %copy-start.4 = (bf16[256,640]{1,0:T(8,128)(2,1)}, bf16[256,640]{1,0:T(8,128)(2,1)S(1)}, u32[]{:S(2)}) copy-start(bf16[256,640]{1,0:T(8,128)(2,1)S(1)} %fusion.35) | copy-start | bytes 983044
  25.9 56.5 %all-gather.13.cloned.1.call-start = ((), (), s32[]{:S(2)}) async-start(), calls=%async_computation.3 | async-start | bytes 1638400 | tf_op jit(solution)/shard_map/all_gather | solution.py:94
  27.2 170.7 %all-gather.7.cloned.1.call-start = ((), (), s32[]{:S(2)}) async-start(), calls=%async_computation | async-start | bytes 1331200 | tf_op jit(solution)/shard_map/all_gather | solution.py:102
  28.1 284.5 %all-gather.9.cloned.1.call-start = ((), (), s32[]{:S(2)}) async-start(), calls=%async_computation.1 | async-start | bytes 1331200 | tf_op jit(solution)/shard_map/all_gather | solution.py:103
  29.8 54.2 %copy-start.6 = (bf16[256,640]{0,1:T(8,128)(2,1)}, bf16[256,640]{0,1:T(8,128)(2,1)S(1)}, u32[]{:S(2)}) copy-start(bf16[256,640]{0,1:T(8,128)(2,1)S(1)} %copy.20) | copy-start | bytes 983044
  199.4 3.6 %copy-start.1 = (f32[8,1024,256]{2,1,0:T(8,128)S(1)}, f32[8,1024,256]{2,1,0:T(8,128)}, u32[]{:S(2)}) copy-start(f32[8,1024,256]{2,1,0:T(8,128)} %get-tuple-element.20) | copy-start | bytes 25165828
  201.9 3.9 %copy-start.2 = (f32[8,1024,256]{2,1,0:T(8,128)}, f32[8,1024,256]{2,1,0:T(8,128)S(1)}, u32[]{:S(2)}) copy-start(f32[8,1024,256]{2,1,0:T(8,128)S(1)} %get-tuple-element.18) | copy-start | bytes 25165828
  207.3 111.8 %copy-start.12 = (f32[640]{0:T(1024)S(1)}, f32[640]{0:T(1024)}, u32[]{:S(2)}) copy-start(f32[640]{0:T(1024)} %param.17) | copy-start | bytes 7684
  314.1 5.0 %copy-start.11 = (bf16[640,640]{1,0:T(8,128)(2,1)S(1)}, bf16[640,640]{1,0:T(8,128)(2,1)}, u32[]{:S(2)}) copy-start(bf16[640,640]{1,0:T(8,128)(2,1)} %param.16) | copy-start | bytes 2457604
Sparse Core Ops, SparseCore 0:
  26.0 27.7 all-gather.10
  56.2 26.1 all-gather.12
  86.0 111.7 all-gather.6
  201.3 111.2 all-gather.8
where the time goes:
time: 330 us; the launch traced here: 327 us
  waiting for transfers between devices  269 us (82%)
  matrix products  24.5 us (7%)
  between operations  14.1 us (4%)
  local copies, waits for them, and re-layouts  7.96 us (2%)
  starting transfers between devices  7.12 us (2%)
  other arithmetic  4.31 us (1%)
    all_gather x1, waiting for transfers between devices, shards(): lax.all_gather(ref_key, 'tm', axis=0, tiled=True)  114 us
    all_gather x1, waiting for transfers between devices, shards(): lax.all_gather(ref_value, 'tm', axis=0, tiled=True)  105 us
    all_gather x1, waiting for transfers between devices, shards(): lax.all_gather(key, 'rows', axis=1, tiled=True)  24 us
    all_gather x1, waiting for transfers between devices, shards(): lax.all_gather(value, 'rows', axis=1, tiled=True)  22.4 us
    dot_general x2, matrix products, attend_update(): jnp.einsum('fqhd,khd->fhqk', query_heads, key_part[0], preferred_element_...  6.97 us
  transfers between devices with their start and end apart: 6, of which 5 were waited for; matrix products, arithmetic and copies ran while one was open for 6% of the time, Pallas kernels for 0%

commit v1 on v0

v1 whole, which is shorter than its diff:
```python
import jax
import jax.numpy as jnp
import numpy as np
from jax import lax
from jax.sharding import Mesh
from jax.sharding import PartitionSpec as P

HD = 80

TM_PARTS = ("y_hi", "x", "z")
ROW_PARTS = ("y_lo", "core")


def distinct(values):
    return len(set(values))


def fine_mesh(mesh):
    devices = np.asarray(mesh.devices)
    tm, rows = devices.shape
    try:
        column = devices[:, 0]
        nx = distinct(d.coords[0] for d in column)
        nz = distinct(d.coords[2] for d in column)
        cores = distinct(d.core_on_chip for d in devices[0])
    except (AttributeError, IndexError, TypeError):
        nx, nz, cores = tm, 1, rows
    if tm % (nx * nz) or rows % cores:
        nx, nz, cores = tm, 1, rows
    shape = (tm // (nx * nz), nx, nz, rows // cores, cores)
    return Mesh(devices.reshape(shape), TM_PARTS + ROW_PARTS)


def gather_in_steps(value, axes, dim):
    for axis in reversed(axes):
        value = lax.all_gather(value, axis, axis=dim, tiled=True)
    return value


def extended(value, axes, dim, width):
    size = 1
    for axis in axes:
        size *= lax.axis_size(axis)
    length = value.shape[dim]
    up = [(i, i + 1) for i in range(size - 1)]
    down = [(j, i) for i, j in up]
    last = lax.slice_in_dim(value, length - width, length, axis=dim)
    initial = lax.slice_in_dim(value, 0, width, axis=dim)
    before = lax.ppermute(last, axes, up)
    after = lax.ppermute(initial, axes, down)
    return jnp.concatenate([before, value, after], axis=dim)


def attend(query, keys, values, heads):
    tokens = query.shape[0]
    length = keys.shape[0]
    query_heads = query.reshape(tokens, heads, HD)
    key_heads = keys.reshape(length, heads, HD)
    value_heads = values.reshape(length, heads, HD)
    scores = jnp.einsum(
        "qhd,khd->hqk", query_heads, key_heads, preferred_element_type=jnp.float32
    )
    scores = scores * HD ** (-0.5)
    top = jnp.max(scores, axis=2, keepdims=True)
    weights = jnp.exp(scores - top)
    total = jnp.sum(weights, axis=2)
    summed = jnp.einsum(
        "hqk,khd->qhd",
        weights.astype(jnp.bfloat16),
        value_heads,
        preferred_element_type=jnp.float32,
    )
    mixed = summed / jnp.transpose(total)[..., None]
    return mixed.reshape(tokens, heads * HD).astype(jnp.bfloat16)


def shards(frames, conv_weight, conv_bias, ref_features, w_query, w_key, w_value, w_out, out_bias):
    count, band_rows, width, channels = frames.shape
    heads = channels // HD
    band = band_rows * width
    w_pair = jnp.concatenate([w_key, w_value], axis=1)
    ref_pair = jnp.dot(ref_features, w_pair, preferred_element_type=jnp.float32).astype(
        jnp.bfloat16
    )
    every_pair = gather_in_steps(ref_pair, TM_PARTS, 0)
    activated = jax.nn.silu(frames.astype(jnp.float32)).astype(jnp.bfloat16)
    padded = extended(activated, ROW_PARTS, 1, 1)
    padded = jnp.pad(padded, ((0, 0), (0, 0), (1, 1), (0, 0)))
    convolved = jnp.zeros((count * band, channels), jnp.float32)
    for row_tap in range(3):
        for col_tap in range(3):
            window = padded[:, row_tap : row_tap + band_rows, col_tap : col_tap + width].reshape(
                count * band, channels
            )
            convolved = convolved + jnp.dot(
                window, conv_weight[row_tap, col_tap], preferred_element_type=jnp.float32
            )
    hidden = (
        frames.reshape(count * band, channels).astype(jnp.float32) + convolved + conv_bias
    ).astype(jnp.bfloat16)
    whole = gather_in_steps(hidden, ROW_PARTS, 0)
    query = jnp.dot(hidden, w_query, preferred_element_type=jnp.float32).astype(jnp.bfloat16)
    pair = jnp.dot(whole, w_pair, preferred_element_type=jnp.float32).astype(jnp.bfloat16)
    keys = jnp.concatenate([pair[:, :channels], every_pair[:, :channels]], axis=0)
    values = jnp.concatenate([pair[:, channels:], every_pair[:, channels:]], axis=0)
    mixed = attend(query, keys, values, heads)
    attended = (jnp.dot(mixed, w_out, preferred_element_type=jnp.float32) + out_bias).astype(
        jnp.bfloat16
    )
    return (
        hidden.reshape(count, band_rows, width, channels),
        attended.reshape(count, band_rows, width, channels),
    )


def solution(mesh):
    fine = fine_mesh(mesh)
    blocks = P(TM_PARTS, ROW_PARTS, None, None)
    return jax.shard_map(
        shards,
        mesh=fine,
        in_specs=(blocks, P(), P(), P(TM_PARTS, None), P(), P(), P(), P(), P()),
        out_specs=(blocks, blocks),
        check_vma=False,
    )
```

time: 330 us -> 194 us (0.59)
  waiting for transfers between devices: 269 us -> 92.9 us
  blocking collectives: 0 us -> 30.6 us
  local copies, waits for them, and re-layouts: 7.96 us -> 16.8 us
  other arithmetic: 4.31 us -> 10.9 us
    all_gather x4 -> x3, waiting for transfers between devices: 265 us -> 92.8 us  [gather_in_steps(): value = lax.all_gather(value, axis, axis=dim, tiled=True)]
    all_gather x0 -> x2, blocking collectives: none -> 30.6 us  [gather_in_steps(): value = lax.all_gather(value, axis, axis=dim, tiled=True)]
    all_gather x4 -> x0, local copies, waits for them, and re-layouts: 6.41 us -> none  [the longest x1 1.6 us: shards(): lax.all_gather(value, 'rows', axis=1, tiled=True)]
    concatenate x2 -> x3, other arithmetic: 0.22 us -> 6.33 us  [the longest x1 6.12 us: shards(): jnp.concatenate([pair[:, channels:], every_pair[:, channels:]], axis=0)]
    concatenate x0 -> x3, local copies, waits for them, and re-layouts: none -> 5.84 us  [the longest x1 2.99 us: shards(): jnp.concatenate([pair[:, :channels], every_pair[:, :channels]], axis=0)]
    unnamed x26 -> x27, local copies, waits for them, and re-layouts: 1.16 us -> 5.99 us
    slice x0 -> x2, local copies, waits for them, and re-layouts: none -> 3.85 us  [the longest x1 2.09 us: shards(): every_pair[:, :channels]]
    ppermute x2, waiting for transfers between devices: 3.38 us -> 0.01 us  [the longest x1 0.01 us: extended(): before = lax.ppermute(last, axes, up)]
  transfers between devices with their start and end apart: 6 -> 5, of which waited for: 5 -> 3; matrix products, arithmetic and copies ran while one was open for 6% -> 7% of each run, Pallas kernels for 0% -> 0%
where the time goes in v1:
time: 194 us
  waiting for transfers between devices  92.9 us (48%)
  blocking collectives  30.6 us (16%)
  matrix products  22 us (11%)
  local copies, waits for them, and re-layouts  16.8 us (9%)
  between operations  14.1 us (7%)
  other arithmetic  10.9 us (6%)
  starting transfers between devices  6.82 us (4%)
    all_gather x3, waiting for transfers between devices, gather_in_steps(): value = lax.all_gather(value, axis, axis=dim, tiled=True)  92.8 us
    all_gather x2, blocking collectives, gather_in_steps(): value = lax.all_gather(value, axis, axis=dim, tiled=True)  30.6 us
    dot_general x1, matrix products, attend(): jnp.einsum('hqk,khd->qhd', weights.astype(jnp.bfloat16), value_heads, pre...  7.57 us
    concatenate x1, other arithmetic, shards(): jnp.concatenate([pair[:, channels:], every_pair[:, channels:]], axis=0)  6.12 us
    unnamed x27, local copies, waits for them, and re-layouts  5.99 us
    dot_general x9, matrix products, shards(): jnp.dot(window, conv_weight[row_tap, col_tap], preferred_element_type=jnp...  5.46 us
    ppermute x1, starting transfers between devices, extended(): before = lax.ppermute(last, axes, up)  4.59 us
  transfers between devices with their start and end apart: 5, of which 3 were waited for; matrix products, arithmetic and copies ran while one was open for 7% of the time, Pallas kernels for 0%

profile of v1, /device:TPU:1, one launch (start us, length us, event | category | flops | bytes accessed | tf_op | source)
XLA Modules:
  0.0 194.0 jit_solution(3866425185488509936)
XLA Ops:
  7.2 0.0 copy-start
  7.2 0.0 all-gather.6.cloned.1.call-start
  7.2 1.3 multiply_convert_fusion
  8.5 4.6 %collective-permute-start = (bf16[1,1,32,640]{3,2,1,0:T(8,128)(2,1)S(1)}, bf16[1,1,32,640]{3,2,1,0:T(8,128)(2,1)S(1)}, u32[]{:S(2)}, u32[]{:S(2)}) collective-permute-start(bf16[1,1,32,640]{3,2,1,0:T(8,128)(2,1)S(1)} %get-tuple-element.14), channel_id=1, source_target_pairs={{0,1},{1,2},{2,3},{4,5},{5,6},{6,7},{8,9},{9,10},{10,11},{12,13},{... | collective-permute-start | bytes 122888 | tf_op jit(solution)/shard_map/ppermute | solution.py:49
  13.1 1.9 collective-permute-start.1
  15.1 1.2 constant_dynamic-update-slice_fusion.1
  16.3 0.1 constant_dynamic-update-slice_fusion
  16.4 0.3 fusion.6
  16.8 24.6 %all_gather.17 = bf16[128,1280]{1,0:T(8,128)(2,1)} all-gather(bf16[16,1280]{1,0:T(8,128)(2,1)S(1)} %fusion.6), channel_id=1, replica_groups=mesh['y_hi'=2,'x'=4,'z'=8,'y_lo'=2,'core'=2] {'z'}, dimensions={0}, use_global_device_ids=true | all-gather | bytes 368640 | tf_op jit(solution)/shard_map/all_gather | solution.py:36
  41.3 0.0 all-gather.6.cloned.1.call-update
  41.4 0.0 all-gather.4.cloned.1.call-start
  41.5 0.2 fusion.46
  41.6 0.2 fusion.50
  41.8 1.8 fusion.31
  43.6 0.1 pad_maximum_fusion.2
  43.7 1.1 copy-done.3
  44.8 0.5 convolution_add_fusion.7
  45.2 0.5 fusion.22
  45.7 0.5 convolution_add_fusion.6
  46.2 0.5 convolution_add_fusion.5
  46.7 0.5 convolution_add_fusion.4
  47.1 0.5 convolution_add_fusion.3
  47.6 0.5 convolution_add_fusion.2
  48.1 0.0 copy-done.7
  48.1 0.5 fusion.14
  48.6 0.0 copy-start.6
  48.6 6.0 %all_gather.15 = bf16[512,640]{1,0:T(8,128)(2,1)} all-gather(bf16[256,640]{1,0:T(8,128)(2,1)S(1)} %fusion.14), channel_id=1, replica_groups=mesh['y_hi'=2,'x'=4,'z'=8,'y_lo'=2,'core'=2] {'core'}, dimensions={0}, use_global_device_ids=true | all-gather | bytes 983040 | tf_op jit(solution)/shard_map/all_gather | solution.py:36
  54.6 0.0 all-gather.4.cloned.1.call-update
  54.6 0.2 all-gather.8.cloned.1.call-start
  54.9 18.1 %all-gather.6.cloned.1.call-done = bf16[512,1280]{1,0:T(8,128)(2,1)} async-done(((bf16[128,1280]{1,0:T(8,128)(2,1)}), bf16[512,1280]{1,0:T(8,128)(2,1)}) %all-gather.6.cloned.1.call-update) | async-done | bytes 1310736 | tf_op jit(solution)/shard_map/all_gather | solution.py:36
  72.9 0.0 all-gather.8.cloned.1.call-update
  73.0 0.5 convolution_convert_fusion.2
  73.4 0.9 copy.15
  74.3 31.6 %all-gather.4.cloned.1.call-done = bf16[1024,640]{1,0:T(8,128)(2,1)} async-done(((bf16[512,640]{1,0:T(8,128)(2,1)}), bf16[1024,640]{1,0:T(8,128)(2,1)}) %all-gather.4.cloned.1.call-update) | async-done | bytes 1310736 | tf_op jit(solution)/shard_map/all_gather | solution.py:36
  105.9 3.5 %convolution_convert_fusion = bf16[1024,1280]{1,0:T(8,128)(2,1)S(1)} fusion(bf16[1024,640]{1,0:T(8,128)(2,1)} %all-gather.4.cloned.1.call-done, bf16[640,1280]{1,0:T(8,128)(2,1)S(1)} %constant_dynamic-update-slice_fusion), kind=kOutput, calls=%fused_computation.7 | convolution fusion | flops 1679032320 | bytes 5570560 | tf_op jit(solution)/shard_map/dot_general | solution.py:103
  109.4 1.8 fusion.48
  111.2 43.2 %all-gather.8.cloned.1.call-done = bf16[1024,1280]{1,0:T(8,128)(2,1)} async-done(((bf16[512,1280]{1,0:T(8,128)(2,1)}), bf16[1024,1280]{1,0:T(8,128)(2,1)}) %all-gather.8.cloned.1.call-update) | async-done | bytes 2621456 | tf_op jit(solution)/shard_map/all_gather | solution.py:36
  154.4 2.1 %fusion.49 = (bf16[1024,640]{1,0:T(8,128)(2,1)S(1)}, bf16[1024,640]{1,0:T(8,128)(2,1)S(1)}) fusion(bf16[1024,1280]{1,0:T(8,128)(2,1)} %all-gather.8.cloned.1.call-done), kind=kLoop, calls=%fused_computation.64 | loop fusion | bytes 5242880 | tf_op jit(solution)/shard_map/slice | solution.py:104
  156.5 0.0 copy-done.4
  156.5 0.4 copy-done.5
  156.9 6.1 %pad_maximum_fusion = (bf16[2048,640]{1,0:T(8,128)(2,1)S(1)}, bf16[2048,640]{1,0:T(8,128)(2,1)}) fusion(bf16[1024,640]{1,0:T(8,128)(2,1)S(1)} %get-tuple-element.5, bf16[1024,640]{1,0:T(8,128)(2,1)S(1)} %copy-done.5, bf16[1024,640]{1,0:T(8,128)(2,1)S(1)} %get-tuple-element.4, bf16[1024,640]{1,0:T(8,128)(2,1)S(1)} %copy-done.4), kind=kLoop, calls=%fused_computation.8 | loop fusion | flops 10485760 | bytes 10485760 | tf_op jit(solution)/shard_map/concatenate | solution.py:105
  163.0 2.7 %copy.14 = bf16[2048,640]{0,1:T(8,128)(2,1)} copy(bf16[2048,640]{1,0:T(8,128)(2,1)S(1)} %get-tuple-element.18) | data formatting | bytes 5242880 | tf_op jit(solution)/shard_map/concatenate | solution.py:105
  165.7 3.0 %copy.16 = bf16[2048,640]{0,1:T(8,128)(2,1)S(1)} copy(bf16[2048,640]{1,0:T(8,128)(2,1)} %get-tuple-element.19) | data formatting | bytes 5242880 | tf_op jit(solution)/shard_map/concatenate | solution.py:104
  168.7 3.5 %multiply_reduce_fusion = (f32[8,256]{1,0:T(8,128)S(1)}, f32[8,256,2048]{2,1,0:T(8,128)S(1)}) fusion(bf16[256,8,80]{0,2,1:T(8,128)(2,1)} %bitcast.77, bf16[2048,8,80]{0,2,1:T(8,128)(2,1)S(1)} %bitcast.73), kind=kOutput, calls=%fused_computation.1 | convolution fusion | flops 679475200 | bytes 19734528 | tf_op jit(solution)/shard_map/qhd,khd->hqk/dot_general | solution.py:60
  172.2 3.3 %fusion = f32[8,256]{1,0:T(8,128)S(1)} fusion(f32[8,256,2048]{2,1,0:T(8,128)S(1)} %get-tuple-element.17, f32[8,256]{1,0:T(8,128)S(1)} %get-tuple-element.16), kind=kLoop, calls=%fused_computation.2 | loop fusion | flops 12580864 | bytes 16793600 | tf_op jit(solution)/shard_map/reduce_sum | solution.py:66
  175.5 3.2 %copy-done.1 = f32[8,256,2048]{2,1,0:T(8,128)} copy-done((f32[8,256,2048]{2,1,0:T(8,128)}, f32[8,256,2048]{2,1,0:T(8,128)S(1)}, u32[]{:S(2)}) %copy-start.1) | copy-done | bytes 16777240
  178.7 7.6 %fusion.19 = bf16[256,8,80]{0,2,1:T(8,128)(2,1)S(1)} fusion(bf16[2048,8,80]{0,2,1:T(8,128)(2,1)S(1)} %bitcast.74, f32[8,256,2048]{2,1,0:T(8,128)} %copy-done.1, f32[8,256]{1,0:T(8,128)S(1)} %get-tuple-element.16, f32[256,8]{0,1:T(8,128)S(1)} %bitcast.88), kind=kOutput, calls=%fused_computation.31 | convolution fusion | flops 683999232 | bytes 19742720 | tf_op jit(solution)/shard_map/hqk,khd->qhd/dot_general | solution.py:67
  186.3 1.2 fusion.13
  (22 shorter events, 0.1 us)
Async XLA Ops:
  7.2 65.8 %copy-start = (bf16[640,640]{1,0:T(8,128)(2,1)S(1)}, bf16[640,640]{1,0:T(8,128)(2,1)}, u32[]{:S(2)}) copy-start(bf16[640,640]{1,0:T(8,128)(2,1)} %param.13) | copy-start | bytes 2457604
  7.2 9.3 %copy-start.9 = (bf16[16,640]{1,0:T(8,128)(2,1)S(1)}, bf16[16,640]{1,0:T(8,128)(2,1)}, u32[]{:S(2)}) copy-start(bf16[16,640]{1,0:T(8,128)(2,1)} %param.12) | copy-start | bytes 61444
  7.2 65.7 %all-gather.6.cloned.1.call-start = ((), (), s32[]{:S(2)}) async-start(), calls=%async_computation.1 | async-start | bytes 1638400 | tf_op jit(solution)/shard_map/all_gather | solution.py:36
  7.2 9.1 %copy-start.8 = (bf16[640,640]{1,0:T(8,128)(2,1)S(1)}, bf16[640,640]{1,0:T(8,128)(2,1)}, u32[]{:S(2)}) copy-start(bf16[640,640]{1,0:T(8,128)(2,1)} %param.15) | copy-start | bytes 2457604
  8.5 32.9 %collective-permute-start = (bf16[1,1,32,640]{3,2,1,0:T(8,128)(2,1)S(1)}, bf16[1,1,32,640]{3,2,1,0:T(8,128)(2,1)S(1)}, u32[]{:S(2)}, u32[]{:S(2)}) collective-permute-start(bf16[1,1,32,640]{3,2,1,0:T(8,128)(2,1)S(1)} %get-tuple-element.14), channel_id=1, source_target_pairs={{0,1},{1,2},{2,3},{4,5},{5,6},{6,7},{8,9},{9,10},{10,11},{12,13},{... | collective-permute-start | bytes 122888 | tf_op jit(solution)/shard_map/ppermute | solution.py:49
  13.1 28.3 %collective-permute-start.1 = (bf16[1,1,32,640]{3,2,1,0:T(8,128)(2,1)S(1)}, bf16[1,1,32,640]{3,2,1,0:T(8,128)(2,1)S(1)}, u32[]{:S(2)}, u32[]{:S(2)}) collective-permute-start(bf16[1,1,32,640]{3,2,1,0:T(8,128)(2,1)S(1)} %get-tuple-element.15), channel_id=1, source_target_pairs={{1,0},{2,1},{3,2},{5,4},{6,5},{7,6},{9,8},{10,9},{11,10},{13,12},{... | collective-permute-start | bytes 122888 | tf_op jit(solution)/shard_map/ppermute | solution.py:50
  41.4 64.5 %all-gather.4.cloned.1.call-start = ((), (), s32[]{:S(2)}) async-start(), calls=%async_computation | async-start | bytes 1966080 | tf_op jit(solution)/shard_map/all_gather | solution.py:36
  41.4 3.3 %copy-start.3 = (bf16[3,3,640,640]{3,2,1,0:T(8,128)(2,1)S(1)}, bf16[3,3,640,640]{3,2,1,0:T(8,128)(2,1)}, u32[]{:S(2)}) copy-start(bf16[3,3,640,640]{3,2,1,0:T(8,128)(2,1)} %param.10) | copy-start | bytes 22118404
  47.1 1.0 copy-start.7
  47.1 1.0 copy-start.10
  48.6 60.9 %copy-start.6 = (bf16[256,640]{1,0:T(8,128)(2,1)}, bf16[256,640]{1,0:T(8,128)(2,1)S(1)}, u32[]{:S(2)}) copy-start(bf16[256,640]{1,0:T(8,128)(2,1)S(1)} %fusion.14) | copy-start | bytes 983044
  54.6 99.7 %all-gather.8.cloned.1.call-start = ((), (), s32[]{:S(2)}) async-start(), calls=%async_computation.2 | async-start | bytes 3932160 | tf_op jit(solution)/shard_map/all_gather | solution.py:36
  154.4 2.1 %copy-start.4 = (bf16[1024,640]{1,0:T(8,128)(2,1)S(1)}, bf16[1024,640]{1,0:T(8,128)(2,1)}, u32[]{:S(2)}) copy-start(bf16[1024,640]{1,0:T(8,128)(2,1)} %get-tuple-element.2) | copy-start | bytes 3932164
  154.4 2.5 %copy-start.5 = (bf16[1024,640]{1,0:T(8,128)(2,1)S(1)}, bf16[1024,640]{1,0:T(8,128)(2,1)}, u32[]{:S(2)}) copy-start(bf16[1024,640]{1,0:T(8,128)(2,1)} %get-tuple-element.3) | copy-start | bytes 3932164
  172.2 6.5 %copy-start.1 = (f32[8,256,2048]{2,1,0:T(8,128)}, f32[8,256,2048]{2,1,0:T(8,128)S(1)}, u32[]{:S(2)}) copy-start(f32[8,256,2048]{2,1,0:T(8,128)S(1)} %get-tuple-element.17) | copy-start | bytes 50331652
  172.2 6.5 %copy-start.2 = (bf16[2048,640]{0,1:T(8,128)(2,1)S(1)}, bf16[2048,640]{0,1:T(8,128)(2,1)}, u32[]{:S(2)}) copy-start(bf16[2048,640]{0,1:T(8,128)(2,1)} %copy.14) | copy-start | bytes 7864324
  178.7 7.6 %copy-start.11 = (bf16[640,640]{1,0:T(8,128)(2,1)S(1)}, bf16[640,640]{1,0:T(8,128)(2,1)}, u32[]{:S(2)}) copy-start(bf16[640,640]{1,0:T(8,128)(2,1)} %param.16) | copy-start | bytes 2457604
  178.7 7.6 %copy-start.12 = (f32[640]{0:T(1024)S(1)}, f32[640]{0:T(1024)}, u32[]{:S(2)}) copy-start(f32[640]{0:T(1024)} %param.17) | copy-start | bytes 7684
Sparse Core Ops, SparseCore 0:
  41.5 31.3 all-gather.5
  74.7 31.1 all-gather.3
  107.7 46.6 all-gather.7

commit v2 on v1

v2 whole, which is shorter than its diff:
```python
import functools

import jax
import jax.numpy as jnp
from jax import lax
from jax.experimental import pallas as pl
from jax.experimental.pallas import tpu as pltpu
from jax.sharding import PartitionSpec as P

HD = 80


MESH = pl.DeviceIdType.MESH


def gather_kernel(axis, other, size, x_ref, out_ref, local_sem, send_sem, recv_sem):
    me = lax.axis_index(axis)
    there = lax.axis_index(other)

    def device(peer):
        return {axis: peer, other: there}

    barrier = pltpu.get_barrier_semaphore()

    def greet(step, carry):
        peer = lax.rem(me + step, size)
        pl.semaphore_signal(barrier, inc=1, device_id=device(peer), device_id_type=MESH)
        return carry

    lax.fori_loop(1, size, greet, 0)
    pl.semaphore_wait(barrier, size - 1)

    def remote(step):
        return pltpu.make_async_remote_copy(
            src_ref=x_ref,
            dst_ref=out_ref.at[me],
            send_sem=send_sem.at[step],
            recv_sem=recv_sem.at[step],
            device_id=device(lax.rem(me + step, size)),
            device_id_type=MESH,
        )

    def launch(step, carry):
        remote(step).start()
        return carry

    lax.fori_loop(1, size, launch, 0)
    local = pltpu.make_async_copy(x_ref, out_ref.at[me], local_sem)
    local.start()
    local.wait()

    def finish(step, carry):
        remote(step).wait()
        return carry

    lax.fori_loop(1, size, finish, 0)


def gather_all(value, axis, other, collective):
    size = lax.axis_size(axis)
    return pl.pallas_call(
        functools.partial(gather_kernel, axis, other, size),
        out_shape=jax.ShapeDtypeStruct((size,) + value.shape, value.dtype),
        in_specs=[pl.BlockSpec(memory_space=pl.ANY)],
        out_specs=pl.BlockSpec(memory_space=pl.ANY),
        scratch_shapes=[
            pltpu.SemaphoreType.DMA,
            pltpu.SemaphoreType.DMA((size,)),
            pltpu.SemaphoreType.DMA((size,)),
        ],
        compiler_params=pltpu.CompilerParams(collective_id=collective, has_side_effects=True),
    )(value)


def extended(value, axis, dim, width):
    size = lax.axis_size(axis)
    length = value.shape[dim]
    up = [(i, i + 1) for i in range(size - 1)]
    down = [(j, i) for i, j in up]
    last = lax.slice_in_dim(value, length - width, length, axis=dim)
    initial = lax.slice_in_dim(value, 0, width, axis=dim)
    before = lax.ppermute(last, axis, up)
    after = lax.ppermute(initial, axis, down)
    return jnp.concatenate([before, value, after], axis=dim)


def attend(query, keys, values, heads):
    tokens = query.shape[0]
    length = keys.shape[0]
    query_heads = query.reshape(tokens, heads, HD)
    key_heads = keys.reshape(length, heads, HD)
    value_heads = values.reshape(length, heads, HD)
    scores = jnp.einsum(
        "qhd,khd->hqk", query_heads, key_heads, preferred_element_type=jnp.float32
    )
    scores = scores * HD ** (-0.5)
    top = jnp.max(scores, axis=2, keepdims=True)
    weights = jnp.exp(scores - top)
    total = jnp.sum(weights, axis=2)
    summed = jnp.einsum(
        "hqk,khd->qhd",
        weights.astype(jnp.bfloat16),
        value_heads,
        preferred_element_type=jnp.float32,
    )
    mixed = summed / jnp.transpose(total)[..., None]
    return mixed.reshape(tokens, heads * HD).astype(jnp.bfloat16)


def shards(frames, conv_weight, conv_bias, ref_features, w_query, w_key, w_value, w_out, out_bias):
    count, band_rows, width, channels = frames.shape
    heads = channels // HD
    band = band_rows * width
    w_pair = jnp.concatenate([w_key, w_value], axis=1)
    every_feature = gather_all(ref_features, "tm", "rows", 0)
    every_feature = every_feature.reshape(-1, channels)
    every_pair = jnp.dot(every_feature, w_pair, preferred_element_type=jnp.float32).astype(
        jnp.bfloat16
    )
    activated = jax.nn.silu(frames.astype(jnp.float32)).astype(jnp.bfloat16)
    padded = extended(activated, "rows", 1, 1)
    padded = jnp.pad(padded, ((0, 0), (0, 0), (1, 1), (0, 0)))
    convolved = jnp.zeros((count * band, channels), jnp.float32)
    for row_tap in range(3):
        for col_tap in range(3):
            window = padded[:, row_tap : row_tap + band_rows, col_tap : col_tap + width].reshape(
                count * band, channels
            )
            convolved = convolved + jnp.dot(
                window, conv_weight[row_tap, col_tap], preferred_element_type=jnp.float32
            )
    hidden = (
        frames.reshape(count * band, channels).astype(jnp.float32) + convolved + conv_bias
    ).astype(jnp.bfloat16)
    whole = gather_all(hidden, "rows", "tm", 1).reshape(-1, channels)
    query = jnp.dot(hidden, w_query, preferred_element_type=jnp.float32).astype(jnp.bfloat16)
    pair = jnp.dot(whole, w_pair, preferred_element_type=jnp.float32).astype(jnp.bfloat16)
    keys = jnp.concatenate([pair[:, :channels], every_pair[:, :channels]], axis=0)
    values = jnp.concatenate([pair[:, channels:], every_pair[:, channels:]], axis=0)
    mixed = attend(query, keys, values, heads)
    attended = (jnp.dot(mixed, w_out, preferred_element_type=jnp.float32) + out_bias).astype(
        jnp.bfloat16
    )
    return (
        hidden.reshape(count, band_rows, width, channels),
        attended.reshape(count, band_rows, width, channels),
    )


def solution(mesh):
    blocks = P("tm", "rows", None, None)
    return jax.shard_map(
        shards,
        mesh=mesh,
        in_specs=(blocks, P(), P(), P("tm", None), P(), P(), P(), P(), P()),
        out_specs=(blocks, blocks),
        check_vma=False,
    )
```

time: 194 us -> 118 us (0.61)
  waiting for transfers between devices: 92.9 us -> 0.01 us
  Pallas kernels: 0 us -> 59.4 us
  blocking collectives: 30.6 us -> 0 us
  between operations: 14.1 us -> 1 us
  matrix products: 22 us -> 24.3 us
    all_gather x3 -> x0, waiting for transfers between devices: 92.8 us -> none  [gather_in_steps(): value = lax.all_gather(value, axis, axis=dim, tiled=True)]
    pallas_call x0 -> x2, Pallas kernels: none -> 59.4 us  [gather_all(): pl.pallas_call(functools.partial(gather_kernel, axis, other, size), out_s...]
    all_gather x2 -> x0, blocking collectives: 30.6 us -> none  [gather_in_steps(): value = lax.all_gather(value, axis, axis=dim, tiled=True)]
    unnamed x27 -> x33, local copies, waits for them, and re-layouts: 5.99 us -> 6.23 us
  transfers between devices with their start and end apart: 5 -> 2, of which waited for: 3 -> 0; matrix products, arithmetic and copies ran while one was open for 7% -> 3% of each run, Pallas kernels for 0% -> 36%
where the time goes in v2:
time: 118 us; the launch traced here: 117 us
  Pallas kernels  59.4 us (50%)
  matrix products  24.3 us (21%)
  local copies, waits for them, and re-layouts  15.3 us (13%)
  other arithmetic  10.9 us (9%)
  starting transfers between devices  6.52 us (6%)
    pallas_call x2, Pallas kernels, gather_all(): pl.pallas_call(functools.partial(gather_kernel, axis, other, size), out_s...  59.4 us
    dot_general x1, matrix products, attend(): jnp.einsum('hqk,khd->qhd', weights.astype(jnp.bfloat16), value_heads, pre...  7.57 us
    unnamed x33, local copies, waits for them, and re-layouts  6.23 us
    concatenate x1, other arithmetic, shards(): jnp.concatenate([pair[:, channels:], every_pair[:, channels:]], axis=0)  6.12 us
    dot_general x9, matrix products, shards(): jnp.dot(window, conv_weight[row_tap, col_tap], preferred_element_type=jnp...  4.9 us
    ppermute x1, starting transfers between devices, extended(): before = lax.ppermute(last, axis, up)  4.59 us
    dot_general x1, matrix products, shards(): jnp.dot(whole, w_pair, preferred_element_type=jnp.float32)  3.52 us
    dot_general x1, matrix products, attend(): jnp.einsum('qhd,khd->hqk', query_heads, key_heads, preferred_element_type...  3.46 us
  transfers between devices with their start and end apart: 2, of which 0 were waited for; matrix products, arithmetic and copies ran while one was open for 3% of the time, Pallas kernels for 36%

profile of v2, /device:TPU:1, one launch (start us, length us, event | category | flops | bytes accessed | tf_op | source)
XLA Modules:
  0.0 117.4 jit_solution(1597413401284723876)
XLA Ops:
  0.6 0.0 copy-start
  0.6 0.0 copy-start.7
  0.7 0.0 copy-start.8
  0.7 1.3 %multiply_convert_fusion = bf16[1,8,32,640]{3,2,1,0:T(8,128)(2,1)S(1)} fusion(bf16[1,8,32,640]{3,2,1,0:T(8,128)(2,1)} %param.9), kind=kLoop, calls=%fused_computation.52 | loop fusion | flops 983040 | bytes 655360 | tf_op jit(solution)/shard_map/convert_element_type | solution.py:120
  2.0 4.6 %collective-permute-start = (bf16[1,1,32,640]{3,2,1,0:T(8,128)(2,1)S(1)}, bf16[1,1,32,640]{3,2,1,0:T(8,128)(2,1)S(1)}, u32[]{:S(2)}, u32[]{:S(2)}) collective-permute-start(bf16[1,1,32,640]{3,2,1,0:T(8,128)(2,1)S(1)} %get-tuple-element.14), channel_id=1, source_target_pairs={{0,1},{1,2},{2,3},{4,5},{5,6},{6,7},{8,9},{9,10},{10,11},{12,13},{... | collective-permute-start | bytes 122888 | tf_op jit(solution)/shard_map/ppermute | solution.py:82
  6.6 1.9 %collective-permute-start.1 = (bf16[1,1,32,640]{3,2,1,0:T(8,128)(2,1)S(1)}, bf16[1,1,32,640]{3,2,1,0:T(8,128)(2,1)S(1)}, u32[]{:S(2)}, u32[]{:S(2)}) collective-permute-start(bf16[1,1,32,640]{3,2,1,0:T(8,128)(2,1)S(1)} %get-tuple-element.15), channel_id=1, source_target_pairs={{1,0},{2,1},{3,2},{5,4},{6,5},{7,6},{9,8},{10,9},{11,10},{13,12},{... | collective-permute-start | bytes 122888 | tf_op jit(solution)/shard_map/ppermute | solution.py:83
  8.5 42.5 %shard_map.105 = bf16[64,16,640]{2,1,0:T(8,128)(2,1)} custom-call(bf16[16,640]{1,0:T(8,128)(2,1)} %x_ref.1), custom_call_target="tpu_custom_call" | custom-call | tf_op jit(solution)/shard_map/pallas_call | solution.py:61
  51.0 0.0 copy-done.7
  51.1 0.1 constant_dynamic-update-slice_fusion.1
  51.1 0.1 constant_dynamic-update-slice_fusion
  51.3 0.0 slice-start
  51.3 1.4 %copy-done.6 = bf16[64,16,640]{2,1,0:T(8,128)(2,1)S(1)} copy-done((bf16[64,16,640]{2,1,0:T(8,128)(2,1)S(1)}, bf16[64,16,640]{2,1,0:T(8,128)(2,1)}, u32[]{:S(2)}) %copy-start.6) | copy-done | bytes 1310744
  52.7 2.2 %fusion.6 = bf16[1024,1280]{1,0:T(8,128)(2,1)S(1)} fusion(bf16[1024,640]{1,0:T(8,128)(2,1)S(1)} %bitcast.86, bf16[640,1280]{1,0:T(8,128)(2,1)S(1)} %constant_dynamic-update-slice_fusion), kind=kOutput, calls=%fused_computation.9 | convolution fusion | flops 1679032320 | bytes 5570560 | tf_op jit(solution)/shard_map/dot_general | solution.py:117
  55.0 0.0 copy-done.9
  55.0 1.7 %fusion.49 = (bf16[1024,640]{1,0:T(8,128)(2,1)}, bf16[1024,640]{1,0:T(8,128)(2,1)}) fusion(bf16[1024,1280]{1,0:T(8,128)(2,1)S(1)} %fusion.6), kind=kLoop, calls=%fused_computation.64 | loop fusion | bytes 5242880 | tf_op jit(solution)/shard_map/slice | solution.py:138
  56.7 0.0 collective-permute-done
  56.7 0.0 collective-permute-done.1
  56.7 0.2 fusion.46
  56.8 0.2 fusion.50
  57.1 0.5 fusion.31
  57.5 0.5 fusion.22
  58.0 0.1 pad_maximum_fusion.2
  58.1 0.5 convolution_add_fusion.7
  58.5 0.5 convolution_add_fusion.6
  59.0 0.5 convolution_add_fusion.5
  59.5 0.5 convolution_add_fusion.4
  60.0 0.0 copy-start.5
  60.0 0.0 copy-start.11
  60.0 0.5 convolution_add_fusion.3
  60.4 0.5 convolution_add_fusion.2
  60.9 0.0 copy-done.5
  60.9 1.2 %fusion.14.x_ref = bf16[256,640]{1,0:T(8,128)(2,1)} fusion(f32[256,640]{1,0:T(8,128)S(1)} %fusion.22, f32[256,640]{1,0:T(8,128)S(1)} %convolution_add_fusion.2, bf16[256,640]{1,0:T(8,128)(2,1)S(1)} %bitcast.83, bf16[3,3,640,640]{3,2,1,0:T(8,128)(2,1)S(1)} %bitcast.78, f32[640]{0:T(1024)S(1)} %copy-done.11, bf16[256,640]{1,0:T(8,128)(2,1)S(1)} %bitcast.82), kind=kOutput, calls=%fused_computation.27 | convolution fusion | flops 210698240 | bytes 3117056 | tf_op jit(solution)/shard_map/dot_general | solution.py:129
  62.1 16.9 %shard_map.104 = bf16[4,256,640]{2,1,0:T(8,128)(2,1)} custom-call(bf16[256,640]{1,0:T(8,128)(2,1)} %fusion.14.x_ref), custom_call_target="tpu_custom_call" | custom-call | tf_op jit(solution)/shard_map/pallas_call | solution.py:61
  79.0 0.0 copy-done
  79.0 1.4 %convolution_convert_fusion.2 = bf16[256,640]{1,0:T(8,128)(2,1)S(1)} fusion(bf16[256,640]{1,0:T(8,128)(2,1)} %fusion.14.x_ref, bf16[640,640]{1,0:T(8,128)(2,1)S(1)} %copy-done), kind=kOutput, calls=%fused_computation.28 | convolution fusion | flops 209879040 | bytes 1474560 | tf_op jit(solution)/shard_map/dot_general | solution.py:136
  80.5 0.9 copy.15
  81.4 3.5 %convolution_convert_fusion.1 = bf16[1024,1280]{1,0:T(8,128)(2,1)S(1)} fusion(bf16[1024,640]{1,0:T(8,128)(2,1)} %bitcast.85, bf16[640,1280]{1,0:T(8,128)(2,1)S(1)} %copy-done.10), kind=kOutput, calls=%fused_computation.8 | convolution fusion | flops 1679032320 | bytes 5570560 | tf_op jit(solution)/shard_map/dot_general | solution.py:137
  84.9 0.2 fusion.48
  85.2 1.1 copy-done.3
  86.2 0.4 copy-done.4
  86.6 6.1 %pad_maximum_fusion = (bf16[2048,640]{1,0:T(8,128)(2,1)S(1)}, bf16[2048,640]{1,0:T(8,128)(2,1)}) fusion(bf16[1024,640]{1,0:T(8,128)(2,1)S(1)} %copy-done.4, bf16[1024,640]{1,0:T(8,128)(2,1)S(1)} %get-tuple-element.3, bf16[1024,640]{1,0:T(8,128)(2,1)S(1)} %copy-done.3, bf16[1024,640]{1,0:T(8,128)(2,1)S(1)} %get-tuple-element.2), kind=kLoop, calls=%fused_computation.10 | loop fusion | flops 10485760 | bytes 10485760 | tf_op jit(solution)/shard_map/concatenate | solution.py:139
  92.7 2.7 %copy.14 = bf16[2048,640]{0,1:T(8,128)(2,1)} copy(bf16[2048,640]{1,0:T(8,128)(2,1)S(1)} %get-tuple-element.18) | data formatting | bytes 5242880 | tf_op jit(solution)/shard_map/concatenate | solution.py:139
  95.5 3.2 %copy.16 = bf16[2048,640]{0,1:T(8,128)(2,1)S(1)} copy(bf16[2048,640]{1,0:T(8,128)(2,1)} %get-tuple-element.19) | data formatting | bytes 5242880 | tf_op jit(solution)/shard_map/concatenate | solution.py:138
  98.6 3.5 %multiply_reduce_fusion = (f32[8,256]{1,0:T(8,128)S(1)}, f32[8,256,2048]{2,1,0:T(8,128)S(1)}) fusion(bf16[256,8,80]{0,2,1:T(8,128)(2,1)} %bitcast.81, bf16[2048,8,80]{0,2,1:T(8,128)(2,1)S(1)} %bitcast.75), kind=kOutput, calls=%fused_computation.1 | convolution fusion | flops 679475200 | bytes 19734528 | tf_op jit(solution)/shard_map/qhd,khd->hqk/dot_general | solution.py:93
  102.1 3.3 %fusion = f32[8,256]{1,0:T(8,128)S(1)} fusion(f32[8,256,2048]{2,1,0:T(8,128)S(1)} %get-tuple-element.17, f32[8,256]{1,0:T(8,128)S(1)} %get-tuple-element.16), kind=kLoop, calls=%fused_computation.2 | loop fusion | flops 12580864 | bytes 16793600 | tf_op jit(solution)/shard_map/reduce_sum | solution.py:99
  105.4 3.2 %copy-done.1 = f32[8,256,2048]{2,1,0:T(8,128)} copy-done((f32[8,256,2048]{2,1,0:T(8,128)}, f32[8,256,2048]{2,1,0:T(8,128)S(1)}, u32[]{:S(2)}) %copy-start.1) | copy-done | bytes 16777240
  108.6 7.6 %fusion.19 = bf16[256,8,80]{0,2,1:T(8,128)(2,1)S(1)} fusion(bf16[2048,8,80]{0,2,1:T(8,128)(2,1)S(1)} %bitcast.76, f32[8,256,2048]{2,1,0:T(8,128)} %copy-done.1, f32[8,256]{1,0:T(8,128)S(1)} %get-tuple-element.16, f32[256,8]{0,1:T(8,128)S(1)} %bitcast.94), kind=kOutput, calls=%fused_computation.31 | convolution fusion | flops 683999232 | bytes 19742720 | tf_op jit(solution)/shard_map/hqk,khd->qhd/dot_general | solution.py:100
  116.2 1.2 %fusion.13 = bf16[256,640]{1,0:T(8,128)(2,1)} fusion(bf16[256,640]{0,1:T(8,128)(2,1)S(1)} %bitcast.93, bf16[640,640]{1,0:T(8,128)(2,1)S(1)} %copy-done.12, f32[640]{0:T(1024)S(1)} %copy-done.13), kind=kOutput, calls=%fused_computation.26 | convolution fusion | flops 210042880 | bytes 1477120 | tf_op jit(solution)/shard_map/dot_general | solution.py:141
  (20 shorter events, 0.0 us)
Async XLA Ops:
  0.6 78.4 %copy-start = (bf16[640,640]{1,0:T(8,128)(2,1)S(1)}, bf16[640,640]{1,0:T(8,128)(2,1)}, u32[]{:S(2)}) copy-start(bf16[640,640]{1,0:T(8,128)(2,1)} %param.13) | copy-start | bytes 2457604
  0.6 50.4 %copy-start.7 = (bf16[640,640]{1,0:T(8,128)(2,1)S(1)}, bf16[640,640]{1,0:T(8,128)(2,1)}, u32[]{:S(2)}) copy-start(bf16[640,640]{1,0:T(8,128)(2,1)} %param.14) | copy-start | bytes 2457604
  0.7 50.5 %copy-start.8 = (bf16[640,640]{1,0:T(8,128)(2,1)S(1)}, bf16[640,640]{1,0:T(8,128)(2,1)}, u32[]{:S(2)}) copy-start(bf16[640,640]{1,0:T(8,128)(2,1)} %param.15) | copy-start | bytes 2457604
  2.0 54.7 %collective-permute-start = (bf16[1,1,32,640]{3,2,1,0:T(8,128)(2,1)S(1)}, bf16[1,1,32,640]{3,2,1,0:T(8,128)(2,1)S(1)}, u32[]{:S(2)}, u32[]{:S(2)}) collective-permute-start(bf16[1,1,32,640]{3,2,1,0:T(8,128)(2,1)S(1)} %get-tuple-element.14), channel_id=1, source_target_pairs={{0,1},{1,2},{2,3},{4,5},{5,6},{6,7},{8,9},{9,10},{10,11},{12,13},{... | collective-permute-start | bytes 122888 | tf_op jit(solution)/shard_map/ppermute | solution.py:82
  6.6 50.1 %collective-permute-start.1 = (bf16[1,1,32,640]{3,2,1,0:T(8,128)(2,1)S(1)}, bf16[1,1,32,640]{3,2,1,0:T(8,128)(2,1)S(1)}, u32[]{:S(2)}, u32[]{:S(2)}) collective-permute-start(bf16[1,1,32,640]{3,2,1,0:T(8,128)(2,1)S(1)} %get-tuple-element.15), channel_id=1, source_target_pairs={{1,0},{2,1},{3,2},{5,4},{6,5},{7,6},{9,8},{10,9},{11,10},{13,12},{... | collective-permute-start | bytes 122888 | tf_op jit(solution)/shard_map/ppermute | solution.py:83
  51.0 1.7 %copy-start.6 = (bf16[64,16,640]{2,1,0:T(8,128)(2,1)S(1)}, bf16[64,16,640]{2,1,0:T(8,128)(2,1)}, u32[]{:S(2)}) copy-start(bf16[64,16,640]{2,1,0:T(8,128)(2,1)} %shard_map.105) | copy-start | bytes 3932164
  51.3 3.7 %copy-start.9 = (bf16[640,1280]{1,0:T(8,128)(2,1)}, bf16[640,1280]{1,0:T(8,128)(2,1)S(1)}, u32[]{:S(2)}) copy-start(bf16[640,1280]{1,0:T(8,128)(2,1)S(1)} %constant_dynamic-update-slice_fusion) | copy-start | bytes 4915204
  51.3 5.8 %slice-start = ((s8[7372800]{0:T(1024)(128)(4,1)}), s8[4194304]{0:T(1024)(128)(4,1)S(1)}, s32[]{:S(2)}) async-start(s8[7372800]{0:T(1024)(128)(4,1)} %bitcast.77), calls=%async_computation | async-start | bytes 8388608
  52.7 4.3 %slice-start.1 = ((s8[7372800]{0:T(1024)(128)(4,1)}), s8[3178496]{0:T(1024)(128)(4,1)S(1)}, s32[]{:S(2)}) async-start(s8[7372800]{0:T(1024)(128)(4,1)} %bitcast.77), calls=%async_computation.1 | async-start | bytes 6356992
  60.0 1.0 copy-start.5
  60.0 1.0 copy-start.11
  62.1 19.3 %copy-start.10 = (bf16[640,1280]{1,0:T(8,128)(2,1)S(1)}, bf16[640,1280]{1,0:T(8,128)(2,1)}, u32[]{:S(2)}) copy-start(bf16[640,1280]{1,0:T(8,128)(2,1)} %copy-done.9) | copy-start | bytes 4915204
  84.9 1.3 %copy-start.3 = (bf16[1024,640]{1,0:T(8,128)(2,1)S(1)}, bf16[1024,640]{1,0:T(8,128)(2,1)}, u32[]{:S(2)}) copy-start(bf16[1024,640]{1,0:T(8,128)(2,1)} %get-tuple-element.4) | copy-start | bytes 3932164
  84.9 1.7 %copy-start.4 = (bf16[1024,640]{1,0:T(8,128)(2,1)S(1)}, bf16[1024,640]{1,0:T(8,128)(2,1)}, u32[]{:S(2)}) copy-start(bf16[1024,640]{1,0:T(8,128)(2,1)} %get-tuple-element.5) | copy-start | bytes 3932164
  102.1 6.5 %copy-start.1 = (f32[8,256,2048]{2,1,0:T(8,128)}, f32[8,256,2048]{2,1,0:T(8,128)S(1)}, u32[]{:S(2)}) copy-start(f32[8,256,2048]{2,1,0:T(8,128)S(1)} %get-tuple-element.17) | copy-start | bytes 50331652
  102.1 6.5 %copy-start.2 = (bf16[2048,640]{0,1:T(8,128)(2,1)S(1)}, bf16[2048,640]{0,1:T(8,128)(2,1)}, u32[]{:S(2)}) copy-start(bf16[2048,640]{0,1:T(8,128)(2,1)} %copy.14) | copy-start | bytes 7864324
  108.6 7.6 %copy-start.12 = (bf16[640,640]{1,0:T(8,128)(2,1)S(1)}, bf16[640,640]{1,0:T(8,128)(2,1)}, u32[]{:S(2)}) copy-start(bf16[640,640]{1,0:T(8,128)(2,1)} %param.16) | copy-start | bytes 2457604
  108.6 7.6 %copy-start.13 = (f32[640]{0:T(1024)S(1)}, f32[640]{0:T(1024)}, u32[]{:S(2)}) copy-start(f32[640]{0:T(1024)} %param.17) | copy-start | bytes 7684

commit v3 on v1

v3 whole, which is shorter than its diff:
```python
import jax
import jax.numpy as jnp
from jax import lax
from jax.sharding import PartitionSpec as P

HD = 80


def extended(value, axis, dim, width):
    size = lax.axis_size(axis)
    length = value.shape[dim]
    up = [(i, i + 1) for i in range(size - 1)]
    down = [(j, i) for i, j in up]
    last = lax.slice_in_dim(value, length - width, length, axis=dim)
    initial = lax.slice_in_dim(value, 0, width, axis=dim)
    before = lax.ppermute(last, axis, up)
    after = lax.ppermute(initial, axis, down)
    return jnp.concatenate([before, value, after], axis=dim)


def attend_block(state, query_heads, keys, values, heads):
    top, total, summed = state
    length = keys.shape[0]
    key_heads = keys.reshape(length, heads, HD)
    value_heads = values.reshape(length, heads, HD)
    scores = jnp.einsum(
        "qhd,khd->hqk", query_heads, key_heads, preferred_element_type=jnp.float32
    )
    scores = scores * HD ** (-0.5)
    block_top = jnp.max(scores, axis=2)
    new_top = block_top if top is None else jnp.maximum(top, block_top)
    weights = jnp.exp(scores - new_top[..., None])
    block_total = jnp.sum(weights, axis=2)
    product = jnp.einsum(
        "hqk,khd->hqd",
        weights.astype(jnp.bfloat16),
        value_heads,
        preferred_element_type=jnp.float32,
    )
    if top is None:
        return (new_top, block_total, product)
    factor = jnp.exp(top - new_top)
    return (new_top, total * factor + block_total, summed * factor[..., None] + product)


def doubling_gather(value, axis):
    size = lax.axis_size(axis)
    step = 1
    while step < size:
        pairs = [(j, j ^ step) for j in range(size)]
        value = jnp.concatenate([value, lax.ppermute(value, axis, pairs)], axis=0)
        step *= 2
    return value


def shards(frames, conv_weight, conv_bias, ref_features, w_query, w_key, w_value, w_out, out_bias):
    count, band_rows, width, channels = frames.shape
    heads = channels // HD
    band = band_rows * width
    w_pair = jnp.concatenate([w_key, w_value], axis=1)
    every_feature = doubling_gather(ref_features, "tm")
    activated = jax.nn.silu(frames.astype(jnp.float32)).astype(jnp.bfloat16)
    padded = extended(activated, "rows", 1, 1)
    padded = jnp.pad(padded, ((0, 0), (0, 0), (1, 1), (0, 0)))
    convolved = jnp.zeros((count * band, channels), jnp.float32)
    for row_tap in range(3):
        for col_tap in range(3):
            window = padded[:, row_tap : row_tap + band_rows, col_tap : col_tap + width].reshape(
                count * band, channels
            )
            convolved = convolved + jnp.dot(
                window, conv_weight[row_tap, col_tap], preferred_element_type=jnp.float32
            )
    hidden = (
        frames.reshape(count * band, channels).astype(jnp.float32) + convolved + conv_bias
    ).astype(jnp.bfloat16)
    rows = lax.axis_size("rows")
    others = jnp.concatenate(
        [
            lax.ppermute(hidden, "rows", [(j, (j + shift) % rows) for j in range(rows)])
            for shift in range(1, rows)
        ],
        axis=0,
    )
    query = jnp.dot(hidden, w_query, preferred_element_type=jnp.float32).astype(jnp.bfloat16)
    query_heads = query.reshape(band, heads, HD)
    state = (None, None, None)
    for source in (hidden, others, every_feature):
        pair = jnp.dot(source, w_pair, preferred_element_type=jnp.float32).astype(jnp.bfloat16)
        state = attend_block(state, query_heads, pair[:, :channels], pair[:, channels:], heads)
    top, total, summed = state
    mixed = summed / total[..., None]
    mixed = jnp.transpose(mixed, (1, 0, 2)).reshape(band, channels).astype(jnp.bfloat16)
    attended = (jnp.dot(mixed, w_out, preferred_element_type=jnp.float32) + out_bias).astype(
        jnp.bfloat16
    )
    return (
        hidden.reshape(count, band_rows, width, channels),
        attended.reshape(count, band_rows, width, channels),
    )


def solution(mesh):
    blocks = P("tm", "rows", None, None)
    return jax.shard_map(
        shards,
        mesh=mesh,
        in_specs=(blocks, P(), P(), P("tm", None), P(), P(), P(), P(), P()),
        out_specs=(blocks, blocks),
        check_vma=False,
    )
```

time: 194 us -> 105 us (0.54)
  the two profiles are of different devices: /device:TPU:1 before, /device:TPU:56 now
where the time goes in v3:
time: 105 us
  matrix products  30.9 us (29%)
  local copies, waits for them, and re-layouts  23.9 us (23%)
  starting transfers between devices  21.3 us (20%)
  waiting for transfers between devices  20.2 us (19%)
  other arithmetic  7.71 us (7%)
  between operations  1.1 us (1%)
    ppermute x6, waiting for transfers between devices, doubling_gather(): value = jnp.concatenate([value, lax.ppermute(value, axis, pairs)], axis=0)  20.2 us
    ppermute x6, starting transfers between devices, doubling_gather(): value = jnp.concatenate([value, lax.ppermute(value, axis, pairs)], axis=0)  13.9 us
    dot_general x3, matrix products, attend_block(): jnp.einsum('qhd,khd->hqk', query_heads, key_heads, preferred_element_type...  11.2 us
    slice x4, local copies, waits for them, and re-layouts, shards(): pair[:, :channels]  7.92 us
    dot_general x3, matrix products, attend_block(): jnp.einsum('hqk,khd->hqd', weights.astype(jnp.bfloat16), value_heads, pre...  7.41 us
    slice x5, local copies, waits for them, and re-layouts, shards(): pair[:, channels:]  6.88 us
    reduce_sum x3, other arithmetic, attend_block(): block_total = jnp.sum(weights, axis=2)  6.15 us
    dot_general x3, matrix products, shards(): jnp.dot(source, w_pair, preferred_element_type=jnp.float32)  5.75 us
  transfers between devices with their start and end apart: 11, of which 5 were waited for; matrix products, arithmetic and copies ran while one was open for 28% of the time, Pallas kernels for 0%

profile of v3, /device:TPU:56, one launch (start us, length us, event | category | flops | bytes accessed | tf_op | source)
XLA Modules:
  0.0 105.0 jit_solution(8527488075095914194)
XLA Ops:
  0.7 1.3 %multiply_convert_fusion = bf16[1,8,32,640]{3,2,1,0:T(8,128)(2,1)S(1)} fusion(bf16[1,8,32,640]{3,2,1,0:T(8,128)(2,1)} %param.9), kind=kLoop, calls=%fused_computation.74 | loop fusion | flops 983040 | bytes 655360 | tf_op jit(solution)/shard_map/convert_element_type | solution.py:62
  2.0 1.9 %collective-permute-start = (bf16[1,1,32,640]{3,2,1,0:T(8,128)(2,1)S(1)}, bf16[1,1,32,640]{3,2,1,0:T(8,128)(2,1)S(1)}, u32[]{:S(2)}, u32[]{:S(2)}) collective-permute-start(bf16[1,1,32,640]{3,2,1,0:T(8,128)(2,1)S(1)} %get-tuple-element.23), channel_id=1, source_target_pairs={{0,1},{1,2},{2,3},{4,5},{5,6},{6,7},{8,9},{9,10},{10,11},{12,13},{... | collective-permute-start | bytes 122888 | tf_op jit(solution)/shard_map/ppermute | solution.py:16
  3.9 3.6 %collective-permute-start.1 = (bf16[1,1,32,640]{3,2,1,0:T(8,128)(2,1)S(1)}, bf16[1,1,32,640]{3,2,1,0:T(8,128)(2,1)S(1)}, u32[]{:S(2)}, u32[]{:S(2)}) collective-permute-start(bf16[1,1,32,640]{3,2,1,0:T(8,128)(2,1)S(1)} %get-tuple-element.24), channel_id=1, source_target_pairs={{1,0},{2,1},{3,2},{5,4},{6,5},{7,6},{9,8},{10,9},{11,10},{13,12},{... | collective-permute-start | bytes 122888 | tf_op jit(solution)/shard_map/ppermute | solution.py:17
  7.8 1.4 %constant_dynamic-update-slice_fusion.1 = bf16[640,1280]{1,0:T(8,128)(2,1)S(1)} fusion(bf16[640,640]{1,0:T(8,128)(2,1)} %param.14), kind=kLoop, calls=%fused_computation.85 | loop fusion | bytes 1638400
  9.3 0.6 constant_dynamic-update-slice_fusion.12
  9.9 1.7 %collective-permute-done.5 = bf16[16,640]{1,0:T(8,128)(2,1)S(1)} collective-permute-done((bf16[16,640]{1,0:T(8,128)(2,1)}, bf16[16,640]{1,0:T(8,128)(2,1)S(1)}, u32[]{:S(2)}, u32[]{:S(2)}) %collective-permute-start.5) | collective-permute-done | bytes 20512 | tf_op jit(solution)/shard_map/ppermute | solution.py:51
  11.6 3.3 %collective-permute-start.6 = (bf16[32,640]{1,0:T(8,128)(2,1)S(1)}, bf16[32,640]{1,0:T(8,128)(2,1)S(1)}, u32[]{:S(2)}, u32[]{:S(2)}) collective-permute-start(bf16[32,640]{1,0:T(8,128)(2,1)S(1)} %pad_maximum_fusion.4), channel_id=1, source_target_pairs={{0,8},{4,12},{8,0},{12,4},{16,24},{20,28},{24,16},{28,20},{32,40},... | collective-permute-start | bytes 122888 | tf_op jit(solution)/shard_map/ppermute | solution.py:51
  14.9 0.6 constant_dynamic-update-slice_fusion.11
  19.3 0.5 convolution_add_fusion.2
  19.8 0.5 fusion.30
  20.4 1.7 %collective-permute-start.4 = (bf16[256,640]{1,0:T(8,128)(2,1)S(1)}, bf16[256,640]{1,0:T(8,128)(2,1)}, u32[]{:S(2)}, u32[]{:S(2)}) collective-permute-start(bf16[256,640]{1,0:T(8,128)(2,1)S(1)} %fusion.30), channel_id=1, source_target_pairs={{0,3},{1,0},{2,1},{3,2},{4,7},{5,4},{6,5},{7,6},{8,11},{9,8},{10,9... | collective-permute-start | bytes 983048 | tf_op jit(solution)/shard_map/ppermute | solution.py:80
  22.1 1.2 %convolution_convert_fusion.3 = bf16[256,640]{1,0:T(8,128)(2,1)} fusion(bf16[256,640]{1,0:T(8,128)(2,1)S(1)} %fusion.30, bf16[640,640]{1,0:T(8,128)(2,1)S(1)} %copy-done), kind=kOutput, calls=%fused_computation.45 | convolution fusion | flops 209879040 | bytes 1474560 | tf_op jit(solution)/shard_map/dot_general | solution.py:85
  23.3 1.1 %copy.21 = bf16[256,640]{0,1:T(8,128)(2,1)S(1)} copy(bf16[256,640]{1,0:T(8,128)(2,1)} %convolution_convert_fusion.3) | data formatting | bytes 655360 | tf_op jit(solution)/shard_map/convert_element_type | solution.py:85
  24.4 0.7 convolution_convert_fusion.2
  25.1 0.9 fusion.77
  26.0 1.9 %copy.22 = bf16[256,640]{0,1:T(8,128)(2,1)} copy(bf16[256,640]{1,0:T(8,128)(2,1)} %get-tuple-element.12) | data formatting | bytes 655360 | tf_op jit(solution)/shard_map/slice | solution.py:90
  27.9 1.5 %multiply_reduce_fusion.2 = (f32[8,256]{1,0:T(8,128)S(1)}, f32[8,256,256]{1,2,0:T(8,128)S(1)}) fusion(bf16[256,8,80]{0,2,1:T(8,128)(2,1)S(1)} %bitcast.130, bf16[256,8,80]{0,2,1:T(8,128)(2,1)} %bitcast.147), kind=kOutput, calls=%fused_computation.18 | convolution fusion | flops 84932608 | bytes 2760704 | tf_op jit(solution)/shard_map/qhd,khd->hqk/dot_general | solution.py:26
  29.4 4.6 %collective-permute-start.7 = (bf16[64,640]{1,0:T(8,128)(2,1)S(1)}, bf16[64,640]{1,0:T(8,128)(2,1)S(1)}, u32[]{:S(2)}, u32[]{:S(2)}) collective-permute-start(bf16[64,640]{1,0:T(8,128)(2,1)S(1)} %pad_maximum_fusion.3), channel_id=1, source_target_pairs={{0,16},{4,20},{8,24},{12,28},{16,0},{20,4},{24,8},{28,12},{32,48},... | collective-permute-start | bytes 245768 | tf_op jit(solution)/shard_map/ppermute | solution.py:51
  34.4 1.9 %copy.23 = bf16[256,640]{0,1:T(8,128)(2,1)} copy(bf16[256,640]{1,0:T(8,128)(2,1)} %get-tuple-element.11) | data formatting | bytes 655360 | tf_op jit(solution)/shard_map/slice | solution.py:90
  36.2 3.2 %collective-permute-done.7 = bf16[64,640]{1,0:T(8,128)(2,1)S(1)} collective-permute-done((bf16[64,640]{1,0:T(8,128)(2,1)S(1)}, bf16[64,640]{1,0:T(8,128)(2,1)S(1)}, u32[]{:S(2)}, u32[]{:S(2)}) %collective-permute-start.7) | collective-permute-done | bytes 81952 | tf_op jit(solution)/shard_map/ppermute | solution.py:51
  39.5 1.6 %collective-permute-start.8 = (bf16[128,640]{1,0:T(8,128)(2,1)S(1)}, bf16[128,640]{1,0:T(8,128)(2,1)S(1)}, u32[]{:S(2)}, u32[]{:S(2)}) collective-permute-start(bf16[128,640]{1,0:T(8,128)(2,1)S(1)} %pad_maximum_fusion.2), channel_id=1, source_target_pairs={{0,32},{4,36},{8,40},{12,44},{16,48},{20,52},{24,56},{28,60},{32,0... | collective-permute-start | bytes 491528 | tf_op jit(solution)/shard_map/ppermute | solution.py:51
  41.0 0.7 constant_dynamic-update-slice_fusion.10
  41.7 0.7 constant_dynamic-update-slice_fusion.9
  42.4 3.2 %collective-permute-done.8 = bf16[128,640]{1,0:T(8,128)(2,1)S(1)} collective-permute-done((bf16[128,640]{1,0:T(8,128)(2,1)S(1)}, bf16[128,640]{1,0:T(8,128)(2,1)S(1)}, u32[]{:S(2)}, u32[]{:S(2)}) %collective-permute-start.8) | collective-permute-done | bytes 163872 | tf_op jit(solution)/shard_map/ppermute | solution.py:51
  45.6 0.8 constant_dynamic-update-slice_fusion.8
  46.4 3.0 %collective-permute-start.9 = (bf16[256,640]{1,0:T(8,128)(2,1)}, bf16[256,640]{1,0:T(8,128)(2,1)S(1)}, u32[]{:S(2)}, u32[]{:S(2)}) collective-permute-start(bf16[256,640]{1,0:T(8,128)(2,1)} %get-tuple-element.27), channel_id=1, source_target_pairs={{0,64},{4,68},{8,72},{12,76},{16,80},{20,84},{24,88},{28,92},{32,9... | collective-permute-start | bytes 983048 | tf_op jit(solution)/shard_map/ppermute | solution.py:51
  49.4 2.9 %convolution_convert_fusion.1 = bf16[768,1280]{1,0:T(8,128)(2,1)S(1)} fusion(bf16[640,1280]{1,0:T(8,128)(2,1)S(1)} %constant_dynamic-update-slice_fusion, bf16[256,640]{1,0:T(8,128)(2,1)} %collective-permute-done.4, bf16[256,640]{1,0:T(8,128)(2,1)} %collective-permute-done.3, bf16[256,640]{1,0:T(8,128)(2,1)} %collective-permute-done.2), kind=kOutput, calls=%fused_computation.12 | convolution fusion | flops 1262223360 | bytes 4587520 | tf_op jit(solution)/shard_map/dot_general | solution.py:89
  52.3 4.5 %collective-permute-done.9 = bf16[256,640]{1,0:T(8,128)(2,1)S(1)} collective-permute-done((bf16[256,640]{1,0:T(8,128)(2,1)}, bf16[256,640]{1,0:T(8,128)(2,1)S(1)}, u32[]{:S(2)}, u32[]{:S(2)}) %collective-permute-start.9) | collective-permute-done | bytes 327712 | tf_op jit(solution)/shard_map/ppermute | solution.py:51
  56.8 0.9 constant_dynamic-update-slice_fusion.7
  57.7 1.2 %collective-permute-start.10 = (bf16[512,640]{1,0:T(8,128)(2,1)}, bf16[512,640]{1,0:T(8,128)(2,1)}, u32[]{:S(2)}, u32[]{:S(2)}) collective-permute-start(bf16[512,640]{1,0:T(8,128)(2,1)} %get-tuple-element.19), channel_id=1, source_target_pairs={{0,128},{4,132},{8,136},{12,140},{16,144},{20,148},{24,152},{28,15... | collective-permute-start | bytes 1966088 | tf_op jit(solution)/shard_map/ppermute | solution.py:51
  58.9 1.1 %fusion.76 = (bf16[768,640]{1,0:T(8,128)(2,1)S(1)}, bf16[768,640]{1,0:T(8,128)(2,1)}) fusion(bf16[768,1280]{1,0:T(8,128)(2,1)S(1)} %convolution_convert_fusion.1), kind=kLoop, calls=%fused_computation.120 | loop fusion | bytes 3932160 | tf_op jit(solution)/shard_map/slice | solution.py:90
  60.1 1.6 %copy.25 = bf16[768,640]{0,1:T(8,128)(2,1)S(1)} copy(bf16[768,640]{1,0:T(8,128)(2,1)} %get-tuple-element.10) | data formatting | bytes 1966080 | tf_op jit(solution)/shard_map/slice | solution.py:90
  61.6 1.4 %copy.26 = bf16[768,640]{0,1:T(8,128)(2,1)} copy(bf16[768,640]{1,0:T(8,128)(2,1)S(1)} %get-tuple-element.9) | data formatting | bytes 1966080 | tf_op jit(solution)/shard_map/slice | solution.py:90
  63.0 3.7 %multiply_reduce_fusion.1 = (f32[8,256]{1,0:T(8,128)S(1)}, f32[8,256,768]{2,1,0:T(8,128)}) fusion(bf16[256,8,80]{0,2,1:T(8,128)(2,1)S(1)} %bitcast.131, bf16[768,8,80]{0,2,1:T(8,128)(2,1)S(1)} %bitcast.136), kind=kOutput, calls=%fused_computation.5 | convolution fusion | flops 254801920 | bytes 7610368 | tf_op jit(solution)/shard_map/qhd,khd->hqk/dot_general | solution.py:26
  66.7 7.6 %collective-permute-done.10 = bf16[512,640]{1,0:T(8,128)(2,1)} collective-permute-done((bf16[512,640]{1,0:T(8,128)(2,1)}, bf16[512,640]{1,0:T(8,128)(2,1)}, u32[]{:S(2)}, u32[]{:S(2)}) %collective-permute-start.10) | collective-permute-done | bytes 655392 | tf_op jit(solution)/shard_map/ppermute | solution.py:51
  74.3 1.2 %constant_dynamic-update-slice_fusion.13 = bf16[1024,640]{1,0:T(8,128)(2,1)S(1)} fusion(bf16[1024,640]{1,0:T(8,128)(2,1)S(1)} %copy-done.14, bf16[512,640]{1,0:T(8,128)(2,1)} %collective-permute-done.10), kind=kLoop, calls=%fused_computation.97 | loop fusion | bytes 1310720 | tf_op jit(solution)/shard_map/concatenate | solution.py:51
  75.5 2.2 %convolution_convert_fusion = bf16[1024,1280]{1,0:T(8,128)(2,1)S(1)} fusion(bf16[1024,640]{1,0:T(8,128)(2,1)S(1)} %constant_dynamic-update-slice_fusion.13, bf16[640,1280]{1,0:T(8,128)(2,1)S(1)} %copy-done.6), kind=kOutput, calls=%fused_computation.11 | convolution fusion | flops 1679032320 | bytes 5570560 | tf_op jit(solution)/shard_map/dot_general | solution.py:89
  77.7 1.8 %fusion.75 = (bf16[1024,640]{1,0:T(8,128)(2,1)}, bf16[1024,640]{1,0:T(8,128)(2,1)}) fusion(bf16[1024,1280]{1,0:T(8,128)(2,1)S(1)} %convolution_convert_fusion), kind=kLoop, calls=%fused_computation.119 | loop fusion | bytes 5242880 | tf_op jit(solution)/shard_map/slice | solution.py:90
  79.5 2.7 %copy.27 = bf16[1024,640]{0,1:T(8,128)(2,1)} copy(bf16[1024,640]{1,0:T(8,128)(2,1)} %get-tuple-element.7) | data formatting | bytes 2621440 | tf_op jit(solution)/shard_map/slice | solution.py:90
  82.2 6.0 %multiply_reduce_fusion = (f32[8,256]{1,0:T(8,128)S(1)}, f32[8,256,1024]{2,1,0:T(8,128)}) fusion(bf16[256,8,80]{0,2,1:T(8,128)(2,1)S(1)} %bitcast.132, bf16[1024,8,80]{0,2,1:T(8,128)(2,1)} %bitcast.134), kind=kOutput, calls=%fused_computation.1 | convolution fusion | flops 339736576 | bytes 10035200 | tf_op jit(solution)/shard_map/qhd,khd->hqk/dot_general | solution.py:26
  88.3 1.4 %fusion.2 = f32[8,256]{1,0:T(8,128)S(1)} fusion(f32[8,256,768]{2,1,0:T(8,128)S(1)} %bitcast.128, f32[8,256]{1,0:T(8,128)S(1)} %get-tuple-element.6), kind=kLoop, calls=%fused_computation.6 | loop fusion | flops 4716544 | bytes 6307840 | tf_op jit(solution)/shard_map/reduce_sum | solution.py:33
  89.7 2.3 %fusion.25 = f32[256,8,80]{0,2,1:T(8,128)} fusion(bf16[768,8,80]{0,2,1:T(8,128)(2,1)S(1)} %bitcast.135, f32[8,256,768]{2,1,0:T(8,128)S(1)} %bitcast.128, f32[8,256]{1,0:T(8,128)S(1)} %get-tuple-element.6), kind=kOutput, calls=%fused_computation.41 | convolution fusion | flops 256376832 | bytes 7938048 | tf_op jit(solution)/shard_map/hqk,khd->hqd/dot_general | solution.py:34
  92.1 1.6 %copy.28 = bf16[1024,640]{0,1:T(8,128)(2,1)S(1)} copy(bf16[1024,640]{1,0:T(8,128)(2,1)} %get-tuple-element.8) | data formatting | bytes 2621440 | tf_op jit(solution)/shard_map/slice | solution.py:90
  93.7 4.4 %fusion = f32[8,256]{1,0:T(8,128)S(1)} fusion(f32[8,256,1024]{2,1,0:T(8,128)} %get-tuple-element.41, f32[8,256]{1,0:T(8,128)S(1)} %get-tuple-element.5), kind=kLoop, calls=%fused_computation.2 | loop fusion | flops 6289408 | bytes 8404992 | tf_op jit(solution)/shard_map/reduce_sum | solution.py:33
  98.1 4.6 %fusion.14 = f32[256,8,80]{0,2,1:T(8,128)S(1)} fusion(bf16[1024,8,80]{0,2,1:T(8,128)(2,1)S(1)} %bitcast.133, f32[8,256,1024]{2,1,0:T(8,128)} %get-tuple-element.41, f32[8,256]{1,0:T(8,128)S(1)} %get-tuple-element.5), kind=kOutput, calls=%fused_computation.23 | convolution fusion | flops 341835776 | bytes 10362880 | tf_op jit(solution)/shard_map/hqk,khd->hqd/dot_general | solution.py:34
  102.7 0.5 fusion.29
  103.2 0.6 copy-done.15
  103.8 1.2 %fusion.28 = bf16[256,640]{1,0:T(8,128)(2,1)} fusion(bf16[256,640]{0,1:T(8,128)(2,1)S(1)} %bitcast.150, bf16[640,640]{1,0:T(8,128)(2,1)S(1)} %copy-done.15, f32[640]{0:T(1024)S(1)} %copy-done.16), kind=kOutput, calls=%fused_computation.42 | convolution fusion | flops 210042880 | bytes 1477120 | tf_op jit(solution)/shard_map/dot_general | solution.py:94
  (65 shorter events, 4.7 us)
Async XLA Ops:
  0.6 21.5 %copy-start = (bf16[640,640]{1,0:T(8,128)(2,1)S(1)}, bf16[640,640]{1,0:T(8,128)(2,1)}, u32[]{:S(2)}) copy-start(bf16[640,640]{1,0:T(8,128)(2,1)} %param.13) | copy-start | bytes 2457604
  0.6 8.6 %copy-start.11 = (bf16[16,640]{1,0:T(8,128)(2,1)S(1)}, bf16[16,640]{1,0:T(8,128)(2,1)}, u32[]{:S(2)}) copy-start(bf16[16,640]{1,0:T(8,128)(2,1)} %param.12) | copy-start | bytes 61444
  0.7 8.5 %copy-start.9 = (bf16[640,640]{1,0:T(8,128)(2,1)S(1)}, bf16[640,640]{1,0:T(8,128)(2,1)}, u32[]{:S(2)}) copy-start(bf16[640,640]{1,0:T(8,128)(2,1)} %param.15) | copy-start | bytes 2457604
  2.0 13.6 %collective-permute-start = (bf16[1,1,32,640]{3,2,1,0:T(8,128)(2,1)S(1)}, bf16[1,1,32,640]{3,2,1,0:T(8,128)(2,1)S(1)}, u32[]{:S(2)}, u32[]{:S(2)}) collective-permute-start(bf16[1,1,32,640]{3,2,1,0:T(8,128)(2,1)S(1)} %get-tuple-element.23), channel_id=1, source_target_pairs={{0,1},{1,2},{2,3},{4,5},{5,6},{6,7},{8,9},{9,10},{10,11},{12,13},{... | collective-permute-start | bytes 122888 | tf_op jit(solution)/shard_map/ppermute | solution.py:16
  3.9 11.6 %collective-permute-start.1 = (bf16[1,1,32,640]{3,2,1,0:T(8,128)(2,1)S(1)}, bf16[1,1,32,640]{3,2,1,0:T(8,128)(2,1)S(1)}, u32[]{:S(2)}, u32[]{:S(2)}) collective-permute-start(bf16[1,1,32,640]{3,2,1,0:T(8,128)(2,1)S(1)} %get-tuple-element.24), channel_id=1, source_target_pairs={{1,0},{2,1},{3,2},{5,4},{6,5},{7,6},{9,8},{10,9},{11,10},{13,12},{... | collective-permute-start | bytes 122888 | tf_op jit(solution)/shard_map/ppermute | solution.py:17
  7.6 4.1 %collective-permute-start.5 = (bf16[16,640]{1,0:T(8,128)(2,1)}, bf16[16,640]{1,0:T(8,128)(2,1)S(1)}, u32[]{:S(2)}, u32[]{:S(2)}) collective-permute-start(bf16[16,640]{1,0:T(8,128)(2,1)} %param.12), channel_id=1, source_target_pairs={{0,4},{4,0},{8,12},{12,8},{16,20},{20,16},{24,28},{28,24},{32,36},... | collective-permute-start | bytes 61448 | tf_op jit(solution)/shard_map/ppermute | solution.py:51
  7.8 8.2 %copy-start.3 = (bf16[3,3,640,640]{3,2,1,0:T(8,128)(2,1)S(1)}, bf16[3,3,640,640]{3,2,1,0:T(8,128)(2,1)}, u32[]{:S(2)}) copy-start(bf16[3,3,640,640]{3,2,1,0:T(8,128)(2,1)} %param.10) | copy-start | bytes 22118404
  9.3 40.1 %copy-start.5 = (bf16[640,1280]{1,0:T(8,128)(2,1)}, bf16[640,1280]{1,0:T(8,128)(2,1)S(1)}, u32[]{:S(2)}) copy-start(bf16[640,1280]{1,0:T(8,128)(2,1)S(1)} %constant_dynamic-update-slice_fusion) | copy-start | bytes 4915204
  11.6 17.7 %collective-permute-start.6 = (bf16[32,640]{1,0:T(8,128)(2,1)S(1)}, bf16[32,640]{1,0:T(8,128)(2,1)S(1)}, u32[]{:S(2)}, u32[]{:S(2)}) collective-permute-start(bf16[32,640]{1,0:T(8,128)(2,1)S(1)} %pad_maximum_fusion.4), channel_id=1, source_target_pairs={{0,8},{4,12},{8,0},{12,4},{16,24},{20,28},{24,16},{28,20},{32,40},... | collective-permute-start | bytes 122888 | tf_op jit(solution)/shard_map/ppermute | solution.py:51
  18.8 1.0 copy-start.8
  18.8 1.0 copy-start.13
  20.2 4.9 %copy-start.7 = (bf16[256,640]{1,0:T(8,128)(2,1)}, bf16[256,640]{1,0:T(8,128)(2,1)S(1)}, u32[]{:S(2)}) copy-start(bf16[256,640]{1,0:T(8,128)(2,1)S(1)} %fusion.30) | copy-start | bytes 983044
  20.2 29.2 %collective-permute-start.2 = (bf16[256,640]{1,0:T(8,128)(2,1)S(1)}, bf16[256,640]{1,0:T(8,128)(2,1)}, u32[]{:S(2)}, u32[]{:S(2)}) collective-permute-start(bf16[256,640]{1,0:T(8,128)(2,1)S(1)} %fusion.30), channel_id=1, source_target_pairs={{0,1},{1,2},{2,3},{3,0},{4,5},{5,6},{6,7},{7,4},{8,9},{9,10},{10,1... | collective-permute-start | bytes 983048 | tf_op jit(solution)/shard_map/ppermute | solution.py:80
  20.3 29.1 %collective-permute-start.3 = (bf16[256,640]{1,0:T(8,128)(2,1)S(1)}, bf16[256,640]{1,0:T(8,128)(2,1)}, u32[]{:S(2)}, u32[]{:S(2)}) collective-permute-start(bf16[256,640]{1,0:T(8,128)(2,1)S(1)} %fusion.30), channel_id=1, source_target_pairs={{0,2},{1,3},{2,0},{3,1},{4,6},{5,7},{6,4},{7,5},{8,10},{9,11},{10,... | collective-permute-start | bytes 983048 | tf_op jit(solution)/shard_map/ppermute | solution.py:80
  20.4 29.0 %collective-permute-start.4 = (bf16[256,640]{1,0:T(8,128)(2,1)S(1)}, bf16[256,640]{1,0:T(8,128)(2,1)}, u32[]{:S(2)}, u32[]{:S(2)}) collective-permute-start(bf16[256,640]{1,0:T(8,128)(2,1)S(1)} %fusion.30), channel_id=1, source_target_pairs={{0,3},{1,0},{2,1},{3,2},{4,7},{5,4},{6,5},{7,6},{8,11},{9,8},{10,9... | collective-permute-start | bytes 983048 | tf_op jit(solution)/shard_map/ppermute | solution.py:80
  29.4 4.6 %copy-start.1 = (f32[8,256,256]{1,2,0:T(8,128)}, f32[8,256,256]{1,2,0:T(8,128)S(1)}, u32[]{:S(2)}) copy-start(f32[8,256,256]{1,2,0:T(8,128)S(1)} %get-tuple-element.43) | copy-start | bytes 6291460
  29.4 10.0 %collective-permute-start.7 = (bf16[64,640]{1,0:T(8,128)(2,1)S(1)}, bf16[64,640]{1,0:T(8,128)(2,1)S(1)}, u32[]{:S(2)}, u32[]{:S(2)}) collective-permute-start(bf16[64,640]{1,0:T(8,128)(2,1)S(1)} %pad_maximum_fusion.3), channel_id=1, source_target_pairs={{0,16},{4,20},{8,24},{12,28},{16,0},{20,4},{24,8},{28,12},{32,48},... | collective-permute-start | bytes 245768 | tf_op jit(solution)/shard_map/ppermute | solution.py:51
  39.5 6.1 %collective-permute-start.8 = (bf16[128,640]{1,0:T(8,128)(2,1)S(1)}, bf16[128,640]{1,0:T(8,128)(2,1)S(1)}, u32[]{:S(2)}, u32[]{:S(2)}) collective-permute-start(bf16[128,640]{1,0:T(8,128)(2,1)S(1)} %pad_maximum_fusion.2), channel_id=1, source_target_pairs={{0,32},{4,36},{8,40},{12,44},{16,48},{20,52},{24,56},{28,60},{32,0... | collective-permute-start | bytes 491528 | tf_op jit(solution)/shard_map/ppermute | solution.py:51
  46.4 10.4 %collective-permute-start.9 = (bf16[256,640]{1,0:T(8,128)(2,1)}, bf16[256,640]{1,0:T(8,128)(2,1)S(1)}, u32[]{:S(2)}, u32[]{:S(2)}) collective-permute-start(bf16[256,640]{1,0:T(8,128)(2,1)} %get-tuple-element.27), channel_id=1, source_target_pairs={{0,64},{4,68},{8,72},{12,76},{16,80},{20,84},{24,88},{28,92},{32,9... | collective-permute-start | bytes 983048 | tf_op jit(solution)/shard_map/ppermute | solution.py:51
  57.7 16.6 %collective-permute-start.10 = (bf16[512,640]{1,0:T(8,128)(2,1)}, bf16[512,640]{1,0:T(8,128)(2,1)}, u32[]{:S(2)}, u32[]{:S(2)}) collective-permute-start(bf16[512,640]{1,0:T(8,128)(2,1)} %get-tuple-element.19), channel_id=1, source_target_pairs={{0,128},{4,132},{8,136},{12,140},{16,144},{20,148},{24,152},{28,15... | collective-permute-start | bytes 1966088 | tf_op jit(solution)/shard_map/ppermute | solution.py:51
  63.0 11.3 %copy-start.14 = (bf16[1024,640]{1,0:T(8,128)(2,1)S(1)}, bf16[1024,640]{1,0:T(8,128)(2,1)}, u32[]{:S(2)}) copy-start(bf16[1024,640]{1,0:T(8,128)(2,1)} %get-tuple-element.20) | copy-start | bytes 3932164
  63.0 12.5 %copy-start.6 = (bf16[640,1280]{1,0:T(8,128)(2,1)S(1)}, bf16[640,1280]{1,0:T(8,128)(2,1)}, u32[]{:S(2)}) copy-start(bf16[640,1280]{1,0:T(8,128)(2,1)} %copy-done.5) | copy-start | bytes 4915204
  79.5 8.7 %slice-start = ((s8[6291456]{0:T(1024)(128)(4,1)}), s8[2097152]{0:T(1024)(128)(4,1)S(1)}, s32[]{:S(2)}) async-start(s8[6291456]{0:T(1024)(128)(4,1)} %bitcast.127), calls=%async_computation | async-start | bytes 4194304
  82.2 6.1 %slice-start.1 = ((s8[6291456]{0:T(1024)(128)(4,1)}), s8[4194304]{0:T(1024)(128)(4,1)S(1)}, s32[]{:S(2)}) async-start(s8[6291456]{0:T(1024)(128)(4,1)} %bitcast.127), calls=%async_computation.1 | async-start | bytes 8388608
  88.2 1.5 %copy-start.4 = (bf16[768,640]{0,1:T(8,128)(2,1)S(1)}, bf16[768,640]{0,1:T(8,128)(2,1)}, u32[]{:S(2)}) copy-start(bf16[768,640]{0,1:T(8,128)(2,1)} %copy.26) | copy-start | bytes 2949124
  98.0 4.6 %copy-start.2 = (f32[8,256,256]{1,2,0:T(8,128)S(1)}, f32[8,256,256]{1,2,0:T(8,128)}, u32[]{:S(2)}) copy-start(f32[8,256,256]{1,2,0:T(8,128)} %copy-done.1) | copy-start | bytes 6291460
  98.0 4.6 %copy-start.10 = (f32[256,8,80]{0,2,1:T(8,128)S(1)}, f32[256,8,80]{0,2,1:T(8,128)}, u32[]{:S(2)}) copy-start(f32[256,8,80]{0,2,1:T(8,128)} %fusion.25) | copy-start | bytes 1966084
  98.0 4.6 %copy-start.12 = (bf16[256,640]{0,1:T(8,128)(2,1)S(1)}, bf16[256,640]{0,1:T(8,128)(2,1)}, u32[]{:S(2)}) copy-start(bf16[256,640]{0,1:T(8,128)(2,1)} %copy.23) | copy-start | bytes 983044
  102.7 1.1 %copy-start.15 = (bf16[640,640]{1,0:T(8,128)(2,1)S(1)}, bf16[640,640]{1,0:T(8,128)(2,1)}, u32[]{:S(2)}) copy-start(bf16[640,640]{1,0:T(8,128)(2,1)} %param.16) | copy-start | bytes 2457604
  102.7 1.1 %copy-start.16 = (f32[640]{0:T(1024)S(1)}, f32[640]{0:T(1024)}, u32[]{:S(2)}) copy-start(f32[640]{0:T(1024)} %param.17) | copy-start | bytes 7684

commit v4 on v3

--- a/solution.py
+++ b/solution.py
@@ -1,9 +1,96 @@
+import functools
+
 import jax
 import jax.numpy as jnp
+import numpy as np
 from jax import lax
+from jax.experimental import pallas as pl
+from jax.experimental.pallas import tpu as pltpu
+from jax.sharding import Mesh
 from jax.sharding import PartitionSpec as P
 
 HD = 80
+
+
+MESH = pl.DeviceIdType.MESH
+TM_PARTS = ("y_hi", "x", "z")
+ROW_PARTS = ("y_lo", "core")
+
+
+def distinct(values):
+    return len(set(values))
+
+
+def fine_mesh(mesh):
+    devices = np.asarray(mesh.devices)
+    tm, rows = devices.shape
+    try:
+        column = devices[:, 0]
+        nx = distinct(d.coords[0] for d in column)
+        nz = distinct(d.coords[2] for d in column)
+        cores = distinct(d.core_on_chip for d in devices[0])
+    except (AttributeError, IndexError, TypeError):
+        nx, nz, cores = tm, 1, rows
+    if tm % (nx * nz) or rows % cores:
+        nx, nz, cores = tm, 1, rows
+    shape = (tm // (nx * nz), nx, nz, rows // cores, cores)
+    return Mesh(devices.reshape(shape), TM_PARTS + ROW_PARTS)
+
+
+def staged_kernel(sizes, x_ref, out_ref, local_sem, *sems):
+    where = [lax.axis_index(axis) for axis in TM_PARTS]
+    strides = [sizes[1] * sizes[2], sizes[2], 1]
+    me = where[0] * strides[0] + where[1] * strides[1] + where[2]
+    barrier = pltpu.get_barrier_semaphore()
+    greeted = 0
+    for level in (2, 1, 0):
+        for shift in range(1, sizes[level]):
+            peer = lax.rem(where[level] + shift, sizes[level])
+            pl.semaphore_signal(
+                barrier, inc=1, device_id={TM_PARTS[level]: peer}, device_id_type=MESH
+            )
+            greeted += 1
+    pl.semaphore_wait(barrier, greeted)
+    local = pltpu.make_async_copy(x_ref, out_ref.at[pl.ds(me, 1)], local_sem)
+    local.start()
+    local.wait()
+    for stage, level in enumerate((2, 1, 0)):
+        span = strides[level]
+        first = me - lax.rem(me, span)
+        held = out_ref.at[pl.ds(first, span)]
+        send_sem, recv_sem = sems[2 * stage], sems[2 * stage + 1]
+        copies = []
+        for shift in range(1, sizes[level]):
+            peer = lax.rem(where[level] + shift, sizes[level])
+            copy = pltpu.make_async_remote_copy(
+                src_ref=held,
+                dst_ref=held,
+                send_sem=send_sem.at[shift],
+                recv_sem=recv_sem.at[shift],
+                device_id={TM_PARTS[level]: peer},
+                device_id_type=MESH,
+            )
+            copy.start()
+            copies.append(copy)
+        for copy in copies:
+            copy.wait()
+
+
+def staged_gather(value):
+    sizes = [lax.axis_size(axis) for axis in TM_PARTS]
+    total = sizes[0] * sizes[1] * sizes[2]
+    sems = []
+    for level in (2, 1, 0):
+        sems += [pltpu.SemaphoreType.DMA((sizes[level],))] * 2
+    gathered = pl.pallas_call(
+        functools.partial(staged_kernel, sizes),
+        out_shape=jax.ShapeDtypeStruct((total,) + value.shape, value.dtype),
+        in_specs=[pl.BlockSpec(memory_space=pl.ANY)],
+        out_specs=pl.BlockSpec(memory_space=pl.ANY),
+        scratch_shapes=[pltpu.SemaphoreType.DMA] + sems,
+        compiler_params=pltpu.CompilerParams(collective_id=0, has_side_effects=True),
+    )(value[None])
+    return gathered.reshape((total * value.shape[0],) + value.shape[1:])
 
 
 def extended(value, axis, dim, width):
@@ -58,9 +145,9 @@
     heads = channels // HD
     band = band_rows * width
     w_pair = jnp.concatenate([w_key, w_value], axis=1)
-    every_feature = doubling_gather(ref_features, "tm")
+    every_feature = staged_gather(ref_features)
     activated = jax.nn.silu(frames.astype(jnp.float32)).astype(jnp.bfloat16)
-    padded = extended(activated, "rows", 1, 1)
+    padded = extended(activated, ROW_PARTS, 1, 1)
     padded = jnp.pad(padded, ((0, 0), (0, 0), (1, 1), (0, 0)))
     convolved = jnp.zeros((count * band, channels), jnp.float32)
     for row_tap in range(3):
@@ -74,10 +161,10 @@
     hidden = (
         frames.reshape(count * band, channels).astype(jnp.float32) + convolved + conv_bias
     ).astype(jnp.bfloat16)
-    rows = lax.axis_size("rows")
+    rows = lax.axis_size(ROW_PARTS)
     others = jnp.concatenate(
         [
-            lax.ppermute(hidden, "rows", [(j, (j + shift) % rows) for j in range(rows)])
+            lax.ppermute(hidden, ROW_PARTS, [(j, (j + shift) % rows) for j in range(rows)])
             for shift in range(1, rows)
         ],
         axis=0,
@@ -101,11 +188,12 @@
 
 
 def solution(mesh):
-    blocks = P("tm", "rows", None, None)
+    fine = fine_mesh(mesh)
+    blocks = P(TM_PARTS, ROW_PARTS, None, None)
     return jax.shard_map(
         shards,
-        mesh=mesh,
-        in_specs=(blocks, P(), P(), P("tm", None), P(), P(), P(), P(), P()),
+        mesh=fine,
+        in_specs=(blocks, P(), P(), P(TM_PARTS, None), P(), P(), P(), P(), P()),
         out_specs=(blocks, blocks),
         check_vma=False,
     )

time: 105 us -> 116 us (1.10)
  the two profiles are of different devices: /device:TPU:56 before, /device:TPU:1 now
where the time goes in v4:
time: 116 us
  Pallas kernels  42.1 us (36%)
  matrix products  33.6 us (29%)
  local copies, waits for them, and re-layouts  18.7 us (16%)
  starting transfers between devices  10.4 us (9%)
  other arithmetic  10.1 us (9%)
    pallas_call x1, Pallas kernels, staged_gather(): pl.pallas_call(functools.partial(staged_kernel, sizes), out_shape=jax.Sha...  42.1 us
    dot_general x3, matrix products, attend_block(): jnp.einsum('qhd,khd->hqk', query_heads, key_heads, preferred_element_type...  10.1 us
    dot_general x3, matrix products, shards(): jnp.dot(source, w_pair, preferred_element_type=jnp.float32)  9.3 us
    reduce_sum x3, other arithmetic, attend_block(): block_total = jnp.sum(weights, axis=2)  8.54 us
    slice x4, local copies, waits for them, and re-layouts, shards(): pair[:, channels:]  6.64 us
    dot_general x3, matrix products, attend_block(): jnp.einsum('hqk,khd->hqd', weights.astype(jnp.bfloat16), value_heads, pre...  5.88 us
    slice x3, local copies, waits for them, and re-layouts, shards(): pair[:, :channels]  5.48 us
    ppermute x1, starting transfers between devices, extended(): after = lax.ppermute(initial, axis, down)  5.15 us
  transfers between devices with their start and end apart: 5, of which 0 were waited for; matrix products, arithmetic and copies ran while one was open for 19% of the time, Pallas kernels for 36%

profile of v4, /device:TPU:1, one launch (start us, length us, event | category | flops | bytes accessed | tf_op | source)
XLA Modules:
  0.0 115.8 jit_solution(13311234390260932230)
XLA Ops:
  0.6 0.0 copy-start
  0.7 1.3 %multiply_convert_fusion = bf16[1,8,32,640]{3,2,1,0:T(8,128)(2,1)S(1)} fusion(bf16[1,8,32,640]{3,2,1,0:T(8,128)(2,1)} %param.9), kind=kLoop, calls=%fused_computation.75 | loop fusion | flops 983040 | bytes 655360 | tf_op jit(solution)/shard_map/convert_element_type | solution.py:149
  2.0 5.1 %collective-permute-start.1 = (bf16[1,1,32,640]{3,2,1,0:T(8,128)(2,1)S(1)}, bf16[1,1,32,640]{3,2,1,0:T(8,128)(2,1)S(1)}, u32[]{:S(2)}, u32[]{:S(2)}) collective-permute-start(bf16[1,1,32,640]{3,2,1,0:T(8,128)(2,1)S(1)} %get-tuple-element.22), channel_id=1, source_target_pairs={{1,0},{2,1},{3,2},{5,4},{6,5},{7,6},{9,8},{10,9},{11,10},{13,12},{... | collective-permute-start | bytes 122888 | tf_op jit(solution)/shard_map/ppermute | solution.py:104
  7.1 1.9 %collective-permute-start = (bf16[1,1,32,640]{3,2,1,0:T(8,128)(2,1)S(1)}, bf16[1,1,32,640]{3,2,1,0:T(8,128)(2,1)S(1)}, u32[]{:S(2)}, u32[]{:S(2)}) collective-permute-start(bf16[1,1,32,640]{3,2,1,0:T(8,128)(2,1)S(1)} %get-tuple-element.21), channel_id=1, source_target_pairs={{0,1},{1,2},{2,3},{4,5},{5,6},{6,7},{8,9},{9,10},{10,11},{12,13},{... | collective-permute-start | bytes 122888 | tf_op jit(solution)/shard_map/ppermute | solution.py:103
  9.1 2.1 %constant_dynamic-update-slice_fusion.1 = bf16[640,1280]{1,0:T(8,128)(2,1)} fusion(bf16[640,640]{1,0:T(8,128)(2,1)} %param.14), kind=kLoop, calls=%fused_computation.93 | loop fusion | bytes 1638400
  11.2 42.1 %shard_map.104 = bf16[64,16,640]{2,1,0:T(8,128)(2,1)} custom-call(bf16[1,16,640]{2,1,0:T(8,128)(2,1)} %bitcast.155), custom_call_target="tpu_custom_call" | custom-call | tf_op jit(solution)/shard_map/pallas_call | solution.py:85
  53.3 1.0 constant_dynamic-update-slice_fusion
  54.3 4.2 %fusion.8 = bf16[1024,1280]{0,1:T(8,128)(2,1)S(1)} fusion(bf16[640,1280]{1,0:T(8,128)(2,1)} %constant_dynamic-update-slice_fusion, bf16[1024,640]{1,0:T(8,128)(2,1)} %bitcast.146), kind=kOutput, calls=%fused_computation.13 | convolution fusion | flops 1679032320 | bytes 5570560 | tf_op jit(solution)/shard_map/dot_general | solution.py:176
  58.5 1.3 %fusion.76 = (bf16[1024,640]{0,1:T(8,128)(2,1)S(1)}, bf16[1024,640]{0,1:T(8,128)(2,1)}) fusion(bf16[1024,1280]{0,1:T(8,128)(2,1)S(1)} %fusion.8), kind=kLoop, calls=%fused_computation.99 | loop fusion | bytes 5242880 | tf_op jit(solution)/shard_map/slice | solution.py:177
  59.9 0.2 fusion.65
  60.0 0.2 fusion.79
  60.3 0.5 fusion.41
  60.7 0.5 fusion.50
  61.2 0.1 pad_maximum_fusion
  61.3 0.5 convolution_add_fusion.7
  61.7 0.5 convolution_add_fusion.6
  62.2 0.5 convolution_add_fusion.5
  62.7 0.0 copy-start.4
  62.7 0.5 convolution_add_fusion.4
  63.2 0.5 convolution_add_fusion.3
  63.6 0.5 convolution_add_fusion.2
  64.1 1.2 %fusion.31 = bf16[256,640]{1,0:T(8,128)(2,1)} fusion(f32[256,640]{1,0:T(8,128)S(1)} %fusion.41, f32[256,640]{1,0:T(8,128)S(1)} %convolution_add_fusion.2, bf16[256,640]{1,0:T(8,128)(2,1)S(1)} %bitcast.144, bf16[3,3,640,640]{3,2,1,0:T(8,128)(2,1)S(1)} %bitcast.134, f32[640]{0:T(1024)S(1)} %copy-done.9, bf16[256,640]{1,0:T(8,128)(2,1)S(1)} %bitcast.143), kind=kOutput, calls=%fused_computation.45 | convolution fusion | flops 210698240 | bytes 3117056 | tf_op jit(solution)/shard_map/dot_general | solution.py:158
  65.3 1.7 %convolution_convert_fusion.2 = bf16[256,1280]{1,0:T(8,128)(2,1)S(1)} fusion(bf16[256,640]{1,0:T(8,128)(2,1)} %fusion.31, bf16[640,1280]{1,0:T(8,128)(2,1)S(1)} %copy-done.3), kind=kOutput, calls=%fused_computation.17 | convolution fusion | flops 419758080 | bytes 2621440 | tf_op jit(solution)/shard_map/dot_general | solution.py:176
  67.0 1.6 %collective-permute-start.4 = (bf16[256,640]{1,0:T(8,128)(2,1)}, bf16[256,640]{1,0:T(8,128)(2,1)}, u32[]{:S(2)}, u32[]{:S(2)}) collective-permute-start(bf16[256,640]{1,0:T(8,128)(2,1)} %fusion.31), channel_id=1, source_target_pairs={{0,3},{1,0},{2,1},{3,2},{4,7},{5,4},{6,5},{7,6},{8,11},{9,8},{10,9... | collective-permute-start | bytes 983048 | tf_op jit(solution)/shard_map/ppermute | solution.py:167
  68.6 1.7 %collective-permute-start.2 = (bf16[256,640]{1,0:T(8,128)(2,1)}, bf16[256,640]{1,0:T(8,128)(2,1)}, u32[]{:S(2)}, u32[]{:S(2)}) collective-permute-start(bf16[256,640]{1,0:T(8,128)(2,1)} %fusion.31), channel_id=1, source_target_pairs={{0,1},{1,2},{2,3},{3,0},{4,5},{5,6},{6,7},{7,4},{8,9},{9,10},{10,1... | collective-permute-start | bytes 983048 | tf_op jit(solution)/shard_map/ppermute | solution.py:167
  70.3 2.2 %convolution_convert_fusion.3 = bf16[256,640]{1,0:T(8,128)(2,1)} fusion(bf16[256,640]{1,0:T(8,128)(2,1)} %fusion.31, bf16[640,640]{1,0:T(8,128)(2,1)S(1)} %copy-done), kind=kOutput, calls=%fused_computation.46 | convolution fusion | flops 209879040 | bytes 1474560 | tf_op jit(solution)/shard_map/dot_general | solution.py:172
  72.5 1.1 copy.19
  73.6 0.9 fusion.78
  74.6 1.9 %copy.20 = bf16[256,640]{0,1:T(8,128)(2,1)} copy(bf16[256,640]{1,0:T(8,128)(2,1)} %get-tuple-element.12) | data formatting | bytes 655360 | tf_op jit(solution)/shard_map/slice | solution.py:177
  76.4 4.5 %multiply_reduce_fusion = (f32[8,256]{1,0:T(8,128)S(1)}, f32[8,256,1024]{2,1,0:T(8,128)}) fusion(bf16[256,8,80]{0,2,1:T(8,128)(2,1)S(1)} %bitcast.136, bf16[1024,8,80]{0,2,1:T(8,128)(2,1)S(1)} %bitcast.140), kind=kOutput, calls=%fused_computation.1 | convolution fusion | flops 339736576 | bytes 10035200 | tf_op jit(solution)/shard_map/qhd,khd->hqk/dot_general | solution.py:113
  81.0 0.5 multiply_reduce_fusion.2
  81.5 1.9 %copy.21 = bf16[256,640]{0,1:T(8,128)(2,1)} copy(bf16[256,640]{1,0:T(8,128)(2,1)} %get-tuple-element.11) | data formatting | bytes 655360 | tf_op jit(solution)/shard_map/slice | solution.py:177
  83.4 0.4 fusion.13
  83.8 3.4 %convolution_convert_fusion.1 = bf16[768,1280]{1,0:T(8,128)(2,1)S(1)} fusion(bf16[640,1280]{1,0:T(8,128)(2,1)} %constant_dynamic-update-slice_fusion, bf16[256,640]{1,0:T(8,128)(2,1)} %collective-permute-done.4, bf16[256,640]{1,0:T(8,128)(2,1)} %collective-permute-done.3, bf16[256,640]{1,0:T(8,128)(2,1)} %collective-permute-done.2), kind=kOutput, calls=%fused_computation.12 | convolution fusion | flops 1262223360 | bytes 4587520 | tf_op jit(solution)/shard_map/dot_general | solution.py:176
  87.2 1.5 %fusion.77 = (bf16[768,640]{1,0:T(8,128)(2,1)}, bf16[768,640]{1,0:T(8,128)(2,1)}) fusion(bf16[768,1280]{1,0:T(8,128)(2,1)S(1)} %convolution_convert_fusion.1), kind=kLoop, calls=%fused_computation.100 | loop fusion | bytes 3932160 | tf_op jit(solution)/shard_map/slice | solution.py:177
  88.8 2.3 %copy.23 = bf16[768,640]{0,1:T(8,128)(2,1)} copy(bf16[768,640]{1,0:T(8,128)(2,1)} %get-tuple-element.10) | data formatting | bytes 1966080 | tf_op jit(solution)/shard_map/slice | solution.py:177
  91.1 5.1 %multiply_reduce_fusion.1 = (f32[8,256]{1,0:T(8,128)S(1)}, f32[8,256,768]{2,1,0:T(8,128)}) fusion(bf16[256,8,80]{0,2,1:T(8,128)(2,1)S(1)} %bitcast.138, bf16[768,8,80]{0,2,1:T(8,128)(2,1)} %bitcast.142), kind=kOutput, calls=%fused_computation.5 | convolution fusion | flops 254801920 | bytes 7610368 | tf_op jit(solution)/shard_map/qhd,khd->hqk/dot_general | solution.py:113
  96.2 4.5 %fusion = f32[8,256]{1,0:T(8,128)S(1)} fusion(f32[8,256,1024]{2,1,0:T(8,128)} %get-tuple-element.24, f32[8,256]{1,0:T(8,128)S(1)} %get-tuple-element.5), kind=kLoop, calls=%fused_computation.2 | loop fusion | flops 6289408 | bytes 8404992 | tf_op jit(solution)/shard_map/reduce_sum | solution.py:120
  100.7 0.1 slice-done.1
  100.8 0.4 copy-done.2
  101.2 2.6 %fusion.15 = f32[256,8,80]{0,2,1:T(8,128)} fusion(bf16[1024,8,80]{0,2,1:T(8,128)(2,1)S(1)} %bitcast.139, f32[8,256,1024]{2,1,0:T(8,128)S(1)} %bitcast.132, f32[8,256]{1,0:T(8,128)S(1)} %get-tuple-element.5), kind=kOutput, calls=%fused_computation.24 | convolution fusion | flops 341835776 | bytes 10362880 | tf_op jit(solution)/shard_map/hqk,khd->hqd/dot_general | solution.py:121
  103.8 2.3 %copy.24 = bf16[768,640]{0,1:T(8,128)(2,1)} copy(bf16[768,640]{1,0:T(8,128)(2,1)} %get-tuple-element.9) | data formatting | bytes 1966080 | tf_op jit(solution)/shard_map/slice | solution.py:177
  106.1 3.7 %fusion.2 = f32[8,256]{1,0:T(8,128)S(1)} fusion(f32[8,256,768]{2,1,0:T(8,128)} %get-tuple-element.28, f32[8,256]{1,0:T(8,128)S(1)} %get-tuple-element.6), kind=kLoop, calls=%fused_computation.6 | loop fusion | flops 4716544 | bytes 6307840 | tf_op jit(solution)/shard_map/reduce_sum | solution.py:120
  109.8 0.9 copy-done.1
  110.7 2.8 %fusion.26 = f32[256,8,80]{0,2,1:T(8,128)S(1)} fusion(bf16[768,8,80]{0,2,1:T(8,128)(2,1)} %bitcast.141, f32[8,256,768]{2,1,0:T(8,128)S(1)} %copy-done.1, f32[8,256]{1,0:T(8,128)S(1)} %get-tuple-element.6), kind=kOutput, calls=%fused_computation.42 | convolution fusion | flops 256376832 | bytes 7938048 | tf_op jit(solution)/shard_map/hqk,khd->hqd/dot_general | solution.py:121
  113.5 0.5 fusion.30
  114.1 0.6 copy-done.10
  114.6 1.2 %fusion.29 = bf16[256,640]{1,0:T(8,128)(2,1)} fusion(bf16[256,640]{0,1:T(8,128)(2,1)S(1)} %bitcast.157, bf16[640,640]{1,0:T(8,128)(2,1)S(1)} %copy-done.10, f32[640]{0:T(1024)S(1)} %copy-done.11), kind=kOutput, calls=%fused_computation.43 | convolution fusion | flops 210042880 | bytes 1477120 | tf_op jit(solution)/shard_map/dot_general | solution.py:181
  (37 shorter events, 0.1 us)
Async XLA Ops:
  0.6 69.7 %copy-start = (bf16[640,640]{1,0:T(8,128)(2,1)S(1)}, bf16[640,640]{1,0:T(8,128)(2,1)}, u32[]{:S(2)}) copy-start(bf16[640,640]{1,0:T(8,128)(2,1)} %param.13) | copy-start | bytes 2457604
  0.6 52.7 %copy-start.6 = (bf16[640,640]{1,0:T(8,128)(2,1)S(1)}, bf16[640,640]{1,0:T(8,128)(2,1)}, u32[]{:S(2)}) copy-start(bf16[640,640]{1,0:T(8,128)(2,1)} %param.15) | copy-start | bytes 2457604
  2.0 57.9 %collective-permute-start.1 = (bf16[1,1,32,640]{3,2,1,0:T(8,128)(2,1)S(1)}, bf16[1,1,32,640]{3,2,1,0:T(8,128)(2,1)S(1)}, u32[]{:S(2)}, u32[]{:S(2)}) collective-permute-start(bf16[1,1,32,640]{3,2,1,0:T(8,128)(2,1)S(1)} %get-tuple-element.22), channel_id=1, source_target_pairs={{1,0},{2,1},{3,2},{5,4},{6,5},{7,6},{9,8},{10,9},{11,10},{13,12},{... | collective-permute-start | bytes 122888 | tf_op jit(solution)/shard_map/ppermute | solution.py:104
  7.1 52.7 %collective-permute-start = (bf16[1,1,32,640]{3,2,1,0:T(8,128)(2,1)S(1)}, bf16[1,1,32,640]{3,2,1,0:T(8,128)(2,1)S(1)}, u32[]{:S(2)}, u32[]{:S(2)}) collective-permute-start(bf16[1,1,32,640]{3,2,1,0:T(8,128)(2,1)S(1)} %get-tuple-element.21), channel_id=1, source_target_pairs={{0,1},{1,2},{2,3},{4,5},{5,6},{6,7},{8,9},{9,10},{10,11},{12,13},{... | collective-permute-start | bytes 122888 | tf_op jit(solution)/shard_map/ppermute | solution.py:103
  54.3 5.9 %slice-start.2 = ((s8[7372800]{0:T(1024)(128)(4,1)}), s8[4194304]{0:T(1024)(128)(4,1)S(1)}, s32[]{:S(2)}) async-start(s8[7372800]{0:T(1024)(128)(4,1)} %bitcast.133), calls=%async_computation.2 | async-start | bytes 8388608
  54.3 5.9 %slice-start.3 = ((s8[7372800]{0:T(1024)(128)(4,1)}), s8[3178496]{0:T(1024)(128)(4,1)S(1)}, s32[]{:S(2)}) async-start(s8[7372800]{0:T(1024)(128)(4,1)} %bitcast.133), calls=%async_computation.3 | async-start | bytes 6356992
  62.7 1.4 %copy-start.4 = (bf16[1,8,32,640]{3,2,1,0:T(8,128)(2,1)S(1)}, bf16[1,8,32,640]{3,2,1,0:T(8,128)(2,1)}, u32[]{:S(2)}) copy-start(bf16[1,8,32,640]{3,2,1,0:T(8,128)(2,1)} %param.9) | copy-start | bytes 983044
  62.7 1.4 %copy-start.9 = (f32[640]{0:T(1024)S(1)}, f32[640]{0:T(1024)}, u32[]{:S(2)}) copy-start(f32[640]{0:T(1024)} %param.11) | copy-start | bytes 7684
  63.6 1.7 %copy-start.3 = (bf16[640,1280]{1,0:T(8,128)(2,1)S(1)}, bf16[640,1280]{1,0:T(8,128)(2,1)}, u32[]{:S(2)}) copy-start(bf16[640,1280]{1,0:T(8,128)(2,1)} %constant_dynamic-update-slice_fusion) | copy-start | bytes 4915204
  67.0 16.8 %collective-permute-start.4 = (bf16[256,640]{1,0:T(8,128)(2,1)}, bf16[256,640]{1,0:T(8,128)(2,1)}, u32[]{:S(2)}, u32[]{:S(2)}) collective-permute-start(bf16[256,640]{1,0:T(8,128)(2,1)} %fusion.31), channel_id=1, source_target_pairs={{0,3},{1,0},{2,1},{3,2},{4,7},{5,4},{6,5},{7,6},{8,11},{9,8},{10,9... | collective-permute-start | bytes 983048 | tf_op jit(solution)/shard_map/ppermute | solution.py:167
  68.6 15.2 %collective-permute-start.3 = (bf16[256,640]{1,0:T(8,128)(2,1)}, bf16[256,640]{1,0:T(8,128)(2,1)}, u32[]{:S(2)}, u32[]{:S(2)}) collective-permute-start(bf16[256,640]{1,0:T(8,128)(2,1)} %fusion.31), channel_id=1, source_target_pairs={{0,2},{1,3},{2,0},{3,1},{4,6},{5,7},{6,4},{7,5},{8,10},{9,11},{10,... | collective-permute-start | bytes 983048 | tf_op jit(solution)/shard_map/ppermute | solution.py:167
  68.6 15.2 %collective-permute-start.2 = (bf16[256,640]{1,0:T(8,128)(2,1)}, bf16[256,640]{1,0:T(8,128)(2,1)}, u32[]{:S(2)}, u32[]{:S(2)}) collective-permute-start(bf16[256,640]{1,0:T(8,128)(2,1)} %fusion.31), channel_id=1, source_target_pairs={{0,1},{1,2},{2,3},{3,0},{4,5},{5,6},{6,7},{7,4},{8,9},{9,10},{10,1... | collective-permute-start | bytes 983048 | tf_op jit(solution)/shard_map/ppermute | solution.py:167
  76.4 4.5 %copy-start.5 = (bf16[256,640]{0,1:T(8,128)(2,1)S(1)}, bf16[256,640]{0,1:T(8,128)(2,1)}, u32[]{:S(2)}) copy-start(bf16[256,640]{0,1:T(8,128)(2,1)} %copy.20) | copy-start | bytes 983044
  91.1 9.6 %slice-start = ((s8[8388608]{0:T(1024)(128)(4,1)}), s8[4194304]{0:T(1024)(128)(4,1)S(1)}, s32[]{:S(2)}) async-start(s8[8388608]{0:T(1024)(128)(4,1)} %bitcast.131), calls=%async_computation | async-start | bytes 8388608
  96.2 4.6 %slice-start.1 = ((s8[8388608]{0:T(1024)(128)(4,1)}), s8[4194304]{0:T(1024)(128)(4,1)S(1)}, s32[]{:S(2)}) async-start(s8[8388608]{0:T(1024)(128)(4,1)} %bitcast.131), calls=%async_computation.1 | async-start | bytes 8388608
  96.2 5.0 %copy-start.2 = (bf16[1024,640]{0,1:T(8,128)(2,1)S(1)}, bf16[1024,640]{0,1:T(8,128)(2,1)}, u32[]{:S(2)}) copy-start(bf16[1024,640]{0,1:T(8,128)(2,1)} %get-tuple-element.8) | copy-start | bytes 3932164
  106.1 4.6 %copy-start.1 = (f32[8,256,768]{2,1,0:T(8,128)S(1)}, f32[8,256,768]{2,1,0:T(8,128)}, u32[]{:S(2)}) copy-start(f32[8,256,768]{2,1,0:T(8,128)} %get-tuple-element.28) | copy-start | bytes 18874372
  110.7 2.8 %copy-start.7 = (f32[256,8,80]{0,2,1:T(8,128)S(1)}, f32[256,8,80]{0,2,1:T(8,128)}, u32[]{:S(2)}) copy-start(f32[256,8,80]{0,2,1:T(8,128)} %fusion.15) | copy-start | bytes 1966084
  110.7 2.8 %copy-start.8 = (bf16[256,640]{0,1:T(8,128)(2,1)S(1)}, bf16[256,640]{0,1:T(8,128)(2,1)}, u32[]{:S(2)}) copy-start(bf16[256,640]{0,1:T(8,128)(2,1)} %copy.21) | copy-start | bytes 983044
  113.5 1.1 copy-start.10
  113.5 1.1 copy-start.11

commit v5 on v4

--- a/solution.py
+++ b/solution.py
@@ -38,36 +38,36 @@
 
 
 def staged_kernel(sizes, x_ref, out_ref, local_sem, *sems):
-    where = [lax.axis_index(axis) for axis in TM_PARTS]
-    strides = [sizes[1] * sizes[2], sizes[2], 1]
-    me = where[0] * strides[0] + where[1] * strides[1] + where[2]
+    high, across, along = sizes
+    half = along // 2
+    yh, xx, zz = [lax.axis_index(axis) for axis in TM_PARTS]
+    low, core = [lax.axis_index(axis) for axis in ROW_PARTS]
+    me = (yh * across + xx) * along + zz
+    mine = me - zz
+    other_core = 1 - core
+    z_peer = lambda shift: {"z": lax.rem(zz + shift, along)}
+    x_peer = lambda shift: {"x": lax.rem(xx + shift, across)}
+    y_peer = {"y_hi": 1 - yh, "y_lo": 1 - low}
+    c_peer = {"core": other_core}
+    peers = [z_peer(s) for s in range(1, along)] + [x_peer(s) for s in range(1, across)]
+    peers += [y_peer, c_peer]
     barrier = pltpu.get_barrier_semaphore()
-    greeted = 0
-    for level in (2, 1, 0):
-        for shift in range(1, sizes[level]):
-            peer = lax.rem(where[level] + shift, sizes[level])
-            pl.semaphore_signal(
-                barrier, inc=1, device_id={TM_PARTS[level]: peer}, device_id_type=MESH
-            )
-            greeted += 1
-    pl.semaphore_wait(barrier, greeted)
+    for peer in peers:
+        pl.semaphore_signal(barrier, inc=1, device_id=peer, device_id_type=MESH)
+    pl.semaphore_wait(barrier, len(peers))
     local = pltpu.make_async_copy(x_ref, out_ref.at[pl.ds(me, 1)], local_sem)
     local.start()
     local.wait()
-    for stage, level in enumerate((2, 1, 0)):
-        span = strides[level]
-        first = me - lax.rem(me, span)
-        held = out_ref.at[pl.ds(first, span)]
-        send_sem, recv_sem = sems[2 * stage], sems[2 * stage + 1]
+
+    def exchange(pairs, send_sem, recv_sem):
         copies = []
-        for shift in range(1, sizes[level]):
-            peer = lax.rem(where[level] + shift, sizes[level])
+        for index, (ref, peer) in enumerate(pairs):
             copy = pltpu.make_async_remote_copy(
-                src_ref=held,
-                dst_ref=held,
-                send_sem=send_sem.at[shift],
-                recv_sem=recv_sem.at[shift],
-                device_id={TM_PARTS[level]: peer},
+                src_ref=ref,
+                dst_ref=ref,
+                send_sem=send_sem.at[index],
+                recv_sem=recv_sem.at[index],
+                device_id=peer,
                 device_id_type=MESH,
             )
             copy.start()
@@ -75,13 +75,29 @@
         for copy in copies:
             copy.wait()
 
+    own = out_ref.at[pl.ds(me, 1)]
+    exchange([(own, z_peer(s)) for s in range(1, along)], sems[0], sems[1])
+    start = mine + core * half
+    part = out_ref.at[pl.ds(start, half)]
+    exchange([(part, x_peer(s)) for s in range(1, across)], sems[2], sems[3])
+    base = yh * across * along + core * half
+    chunks = [out_ref.at[pl.ds(base + g * along, half)] for g in range(across)]
+    exchange([(chunk, y_peer) for chunk in chunks], sems[4], sems[5])
+    regions = high * across
+    region = yh * across + xx
+    groups = []
+    for step in range(1, regions):
+        j = lax.rem(region + step, regions)
+        groups.append(out_ref.at[pl.ds(j * along + core * half, half)])
+    exchange([(chunk, c_peer) for chunk in groups], sems[6], sems[7])
+
 
 def staged_gather(value):
     sizes = [lax.axis_size(axis) for axis in TM_PARTS]
     total = sizes[0] * sizes[1] * sizes[2]
     sems = []
-    for level in (2, 1, 0):
-        sems += [pltpu.SemaphoreType.DMA((sizes[level],))] * 2
+    for count in (sizes[2], sizes[1], sizes[1], sizes[0] * sizes[1]):
+        sems += [pltpu.SemaphoreType.DMA((count,))] * 2
     gathered = pl.pallas_call(
         functools.partial(staged_kernel, sizes),
         out_shape=jax.ShapeDtypeStruct((total,) + value.shape, value.dtype),

time: 116 us -> 108 us (0.931)
  Pallas kernels: 42.1 us -> 31.6 us
  starting transfers between devices: 10.4 us -> 12.3 us
    pallas_call x1, Pallas kernels: 42.1 us -> 31.6 us  [staged_gather(): pl.pallas_call(functools.partial(staged_kernel, sizes), out_shape=jax.Sha...]
    ppermute x3, starting transfers between devices: 3.31 us -> 5.25 us  [shards(): lax.ppermute(hidden, ROW_PARTS, [(j, (j + shift) % rows) for j in range(r...]
  transfers between devices with their start and end apart: 5 -> 5, of which waited for: 0 -> 0; matrix products, arithmetic and copies ran while one was open for 19% -> 21% of each run, Pallas kernels for 36% -> 29%
where the time goes in v5:
time: 108 us; the launch traced here: 107 us
  matrix products  33.6 us (31%)
  Pallas kernels  31.6 us (29%)
  local copies, waits for them, and re-layouts  18.7 us (17%)
  starting transfers between devices  12.3 us (11%)
  other arithmetic  10.1 us (9%)
    pallas_call x1, Pallas kernels, staged_gather(): pl.pallas_call(functools.partial(staged_kernel, sizes), out_shape=jax.Sha...  31.6 us
    dot_general x3, matrix products, attend_block(): jnp.einsum('qhd,khd->hqk', query_heads, key_heads, preferred_element_type...  10.1 us
    dot_general x3, matrix products, shards(): jnp.dot(source, w_pair, preferred_element_type=jnp.float32)  9.3 us
    reduce_sum x3, other arithmetic, attend_block(): block_total = jnp.sum(weights, axis=2)  8.54 us
    slice x4, local copies, waits for them, and re-layouts, shards(): pair[:, channels:]  6.64 us
    dot_general x3, matrix products, attend_block(): jnp.einsum('hqk,khd->hqd', weights.astype(jnp.bfloat16), value_heads, pre...  5.88 us
    slice x3, local copies, waits for them, and re-layouts, shards(): pair[:, :channels]  5.48 us
    ppermute x3, starting transfers between devices, shards(): lax.ppermute(hidden, ROW_PARTS, [(j, (j + shift) % rows) for j in range(r...  5.25 us
  transfers between devices with their start and end apart: 5, of which 0 were waited for; matrix products, arithmetic and copies ran while one was open for 21% of the time, Pallas kernels for 29%

profile of v5, /device:TPU:1, one launch (start us, length us, event | category | flops | bytes accessed | tf_op | source)
XLA Modules:
  0.0 107.2 jit_solution(16027145054336883224)
XLA Ops:
  0.6 0.0 copy-start
  0.7 1.3 %multiply_convert_fusion = bf16[1,8,32,640]{3,2,1,0:T(8,128)(2,1)S(1)} fusion(bf16[1,8,32,640]{3,2,1,0:T(8,128)(2,1)} %param.9), kind=kLoop, calls=%fused_computation.75 | loop fusion | flops 983040 | bytes 655360 | tf_op jit(solution)/shard_map/convert_element_type | solution.py:165
  2.0 5.1 %collective-permute-start.1 = (bf16[1,1,32,640]{3,2,1,0:T(8,128)(2,1)S(1)}, bf16[1,1,32,640]{3,2,1,0:T(8,128)(2,1)S(1)}, u32[]{:S(2)}, u32[]{:S(2)}) collective-permute-start(bf16[1,1,32,640]{3,2,1,0:T(8,128)(2,1)S(1)} %get-tuple-element.22), channel_id=1, source_target_pairs={{1,0},{2,1},{3,2},{5,4},{6,5},{7,6},{9,8},{10,9},{11,10},{13,12},{... | collective-permute-start | bytes 122888 | tf_op jit(solution)/shard_map/ppermute | solution.py:120
  7.1 1.9 %collective-permute-start = (bf16[1,1,32,640]{3,2,1,0:T(8,128)(2,1)S(1)}, bf16[1,1,32,640]{3,2,1,0:T(8,128)(2,1)S(1)}, u32[]{:S(2)}, u32[]{:S(2)}) collective-permute-start(bf16[1,1,32,640]{3,2,1,0:T(8,128)(2,1)S(1)} %get-tuple-element.21), channel_id=1, source_target_pairs={{0,1},{1,2},{2,3},{4,5},{5,6},{6,7},{8,9},{9,10},{10,11},{12,13},{... | collective-permute-start | bytes 122888 | tf_op jit(solution)/shard_map/ppermute | solution.py:119
  9.1 2.1 %constant_dynamic-update-slice_fusion.1 = bf16[640,1280]{1,0:T(8,128)(2,1)} fusion(bf16[640,640]{1,0:T(8,128)(2,1)} %param.14), kind=kLoop, calls=%fused_computation.93 | loop fusion | bytes 1638400
  11.2 31.6 %shard_map.104 = bf16[64,16,640]{2,1,0:T(8,128)(2,1)} custom-call(bf16[1,16,640]{2,1,0:T(8,128)(2,1)} %bitcast.155), custom_call_target="tpu_custom_call" | custom-call | tf_op jit(solution)/shard_map/pallas_call | solution.py:101
  42.8 1.0 constant_dynamic-update-slice_fusion
  43.8 4.2 %fusion.8 = bf16[1024,1280]{0,1:T(8,128)(2,1)S(1)} fusion(bf16[640,1280]{1,0:T(8,128)(2,1)} %constant_dynamic-update-slice_fusion, bf16[1024,640]{1,0:T(8,128)(2,1)} %bitcast.146), kind=kOutput, calls=%fused_computation.13 | convolution fusion | flops 1679032320 | bytes 5570560 | tf_op jit(solution)/shard_map/dot_general | solution.py:192
  48.0 1.3 %fusion.76 = (bf16[1024,640]{0,1:T(8,128)(2,1)S(1)}, bf16[1024,640]{0,1:T(8,128)(2,1)}) fusion(bf16[1024,1280]{0,1:T(8,128)(2,1)S(1)} %fusion.8), kind=kLoop, calls=%fused_computation.99 | loop fusion | bytes 5242880 | tf_op jit(solution)/shard_map/slice | solution.py:193
  49.3 0.2 fusion.65
  49.5 0.2 fusion.79
  49.7 0.5 fusion.41
  50.2 0.5 fusion.50
  50.7 0.1 pad_maximum_fusion
  50.7 0.5 convolution_add_fusion.7
  51.2 0.5 convolution_add_fusion.6
  51.7 0.5 convolution_add_fusion.5
  52.2 0.5 convolution_add_fusion.4
  52.6 0.5 convolution_add_fusion.3
  53.1 0.5 convolution_add_fusion.2
  53.6 1.2 %fusion.31 = bf16[256,640]{1,0:T(8,128)(2,1)} fusion(f32[256,640]{1,0:T(8,128)S(1)} %fusion.41, f32[256,640]{1,0:T(8,128)S(1)} %convolution_add_fusion.2, bf16[256,640]{1,0:T(8,128)(2,1)S(1)} %bitcast.144, bf16[3,3,640,640]{3,2,1,0:T(8,128)(2,1)S(1)} %bitcast.134, f32[640]{0:T(1024)S(1)} %copy-done.9, bf16[256,640]{1,0:T(8,128)(2,1)S(1)} %bitcast.143), kind=kOutput, calls=%fused_computation.45 | convolution fusion | flops 210698240 | bytes 3117056 | tf_op jit(solution)/shard_map/dot_general | solution.py:174
  54.8 1.7 %convolution_convert_fusion.2 = bf16[256,1280]{1,0:T(8,128)(2,1)S(1)} fusion(bf16[256,640]{1,0:T(8,128)(2,1)} %fusion.31, bf16[640,1280]{1,0:T(8,128)(2,1)S(1)} %copy-done.3), kind=kOutput, calls=%fused_computation.17 | convolution fusion | flops 419758080 | bytes 2621440 | tf_op jit(solution)/shard_map/dot_general | solution.py:192
  56.5 0.2 collective-permute-start.4
  56.7 3.2 %collective-permute-start.3 = (bf16[256,640]{1,0:T(8,128)(2,1)}, bf16[256,640]{1,0:T(8,128)(2,1)}, u32[]{:S(2)}, u32[]{:S(2)}) collective-permute-start(bf16[256,640]{1,0:T(8,128)(2,1)} %fusion.31), channel_id=1, source_target_pairs={{0,2},{1,3},{2,0},{3,1},{4,6},{5,7},{6,4},{7,5},{8,10},{9,11},{10,... | collective-permute-start | bytes 983048 | tf_op jit(solution)/shard_map/ppermute | solution.py:183
  59.9 1.9 %collective-permute-start.2 = (bf16[256,640]{1,0:T(8,128)(2,1)}, bf16[256,640]{1,0:T(8,128)(2,1)}, u32[]{:S(2)}, u32[]{:S(2)}) collective-permute-start(bf16[256,640]{1,0:T(8,128)(2,1)} %fusion.31), channel_id=1, source_target_pairs={{0,1},{1,2},{2,3},{3,0},{4,5},{5,6},{6,7},{7,4},{8,9},{9,10},{10,1... | collective-permute-start | bytes 983048 | tf_op jit(solution)/shard_map/ppermute | solution.py:183
  61.7 2.2 %convolution_convert_fusion.3 = bf16[256,640]{1,0:T(8,128)(2,1)} fusion(bf16[256,640]{1,0:T(8,128)(2,1)} %fusion.31, bf16[640,640]{1,0:T(8,128)(2,1)S(1)} %copy-done), kind=kOutput, calls=%fused_computation.46 | convolution fusion | flops 209879040 | bytes 1474560 | tf_op jit(solution)/shard_map/dot_general | solution.py:188
  63.9 1.1 %copy.19 = bf16[256,640]{0,1:T(8,128)(2,1)S(1)} copy(bf16[256,640]{1,0:T(8,128)(2,1)} %convolution_convert_fusion.3) | data formatting | bytes 655360 | tf_op jit(solution)/shard_map/convert_element_type | solution.py:188
  65.1 0.9 fusion.78
  66.0 1.9 %copy.20 = bf16[256,640]{0,1:T(8,128)(2,1)} copy(bf16[256,640]{1,0:T(8,128)(2,1)} %get-tuple-element.12) | data formatting | bytes 655360 | tf_op jit(solution)/shard_map/slice | solution.py:193
  67.9 4.5 %multiply_reduce_fusion = (f32[8,256]{1,0:T(8,128)S(1)}, f32[8,256,1024]{2,1,0:T(8,128)}) fusion(bf16[256,8,80]{0,2,1:T(8,128)(2,1)S(1)} %bitcast.136, bf16[1024,8,80]{0,2,1:T(8,128)(2,1)S(1)} %bitcast.140), kind=kOutput, calls=%fused_computation.1 | convolution fusion | flops 339736576 | bytes 10035200 | tf_op jit(solution)/shard_map/qhd,khd->hqk/dot_general | solution.py:129
  72.4 0.5 multiply_reduce_fusion.2
  72.9 1.9 %copy.21 = bf16[256,640]{0,1:T(8,128)(2,1)} copy(bf16[256,640]{1,0:T(8,128)(2,1)} %get-tuple-element.11) | data formatting | bytes 655360 | tf_op jit(solution)/shard_map/slice | solution.py:193
  74.8 0.4 fusion.13
  75.2 3.4 %convolution_convert_fusion.1 = bf16[768,1280]{1,0:T(8,128)(2,1)S(1)} fusion(bf16[640,1280]{1,0:T(8,128)(2,1)} %constant_dynamic-update-slice_fusion, bf16[256,640]{1,0:T(8,128)(2,1)} %collective-permute-done.4, bf16[256,640]{1,0:T(8,128)(2,1)} %collective-permute-done.3, bf16[256,640]{1,0:T(8,128)(2,1)} %collective-permute-done.2), kind=kOutput, calls=%fused_computation.12 | convolution fusion | flops 1262223360 | bytes 4587520 | tf_op jit(solution)/shard_map/dot_general | solution.py:192
  78.7 1.5 %fusion.77 = (bf16[768,640]{1,0:T(8,128)(2,1)}, bf16[768,640]{1,0:T(8,128)(2,1)}) fusion(bf16[768,1280]{1,0:T(8,128)(2,1)S(1)} %convolution_convert_fusion.1), kind=kLoop, calls=%fused_computation.100 | loop fusion | bytes 3932160 | tf_op jit(solution)/shard_map/slice | solution.py:193
  80.2 2.3 %copy.23 = bf16[768,640]{0,1:T(8,128)(2,1)} copy(bf16[768,640]{1,0:T(8,128)(2,1)} %get-tuple-element.10) | data formatting | bytes 1966080 | tf_op jit(solution)/shard_map/slice | solution.py:193
  82.5 5.1 %multiply_reduce_fusion.1 = (f32[8,256]{1,0:T(8,128)S(1)}, f32[8,256,768]{2,1,0:T(8,128)}) fusion(bf16[256,8,80]{0,2,1:T(8,128)(2,1)S(1)} %bitcast.138, bf16[768,8,80]{0,2,1:T(8,128)(2,1)} %bitcast.142), kind=kOutput, calls=%fused_computation.5 | convolution fusion | flops 254801920 | bytes 7610368 | tf_op jit(solution)/shard_map/qhd,khd->hqk/dot_general | solution.py:129
  87.6 4.5 %fusion = f32[8,256]{1,0:T(8,128)S(1)} fusion(f32[8,256,1024]{2,1,0:T(8,128)} %get-tuple-element.24, f32[8,256]{1,0:T(8,128)S(1)} %get-tuple-element.5), kind=kLoop, calls=%fused_computation.2 | loop fusion | flops 6289408 | bytes 8404992 | tf_op jit(solution)/shard_map/reduce_sum | solution.py:136
  92.1 0.1 slice-done.1
  92.2 0.4 copy-done.2
  92.6 2.6 %fusion.15 = f32[256,8,80]{0,2,1:T(8,128)} fusion(bf16[1024,8,80]{0,2,1:T(8,128)(2,1)S(1)} %bitcast.139, f32[8,256,1024]{2,1,0:T(8,128)S(1)} %bitcast.132, f32[8,256]{1,0:T(8,128)S(1)} %get-tuple-element.5), kind=kOutput, calls=%fused_computation.24 | convolution fusion | flops 341835776 | bytes 10362880 | tf_op jit(solution)/shard_map/hqk,khd->hqd/dot_general | solution.py:137
  95.2 2.3 %copy.24 = bf16[768,640]{0,1:T(8,128)(2,1)} copy(bf16[768,640]{1,0:T(8,128)(2,1)} %get-tuple-element.9) | data formatting | bytes 1966080 | tf_op jit(solution)/shard_map/slice | solution.py:193
  97.5 3.7 %fusion.2 = f32[8,256]{1,0:T(8,128)S(1)} fusion(f32[8,256,768]{2,1,0:T(8,128)} %get-tuple-element.28, f32[8,256]{1,0:T(8,128)S(1)} %get-tuple-element.6), kind=kLoop, calls=%fused_computation.6 | loop fusion | flops 4716544 | bytes 6307840 | tf_op jit(solution)/shard_map/reduce_sum | solution.py:136
  101.2 0.9 copy-done.1
  102.1 2.8 %fusion.26 = f32[256,8,80]{0,2,1:T(8,128)S(1)} fusion(bf16[768,8,80]{0,2,1:T(8,128)(2,1)} %bitcast.141, f32[8,256,768]{2,1,0:T(8,128)S(1)} %copy-done.1, f32[8,256]{1,0:T(8,128)S(1)} %get-tuple-element.6), kind=kOutput, calls=%fused_computation.42 | convolution fusion | flops 256376832 | bytes 7938048 | tf_op jit(solution)/shard_map/hqk,khd->hqd/dot_general | solution.py:137
  105.0 0.5 fusion.30
  105.5 0.6 copy-done.10
  106.0 1.2 %fusion.29 = bf16[256,640]{1,0:T(8,128)(2,1)} fusion(bf16[256,640]{0,1:T(8,128)(2,1)S(1)} %bitcast.157, bf16[640,640]{1,0:T(8,128)(2,1)S(1)} %copy-done.10, f32[640]{0:T(1024)S(1)} %copy-done.11), kind=kOutput, calls=%fused_computation.43 | convolution fusion | flops 210042880 | bytes 1477120 | tf_op jit(solution)/shard_map/dot_general | solution.py:197
  (37 shorter events, 0.1 us)
Async XLA Ops:
  0.6 61.1 %copy-start = (bf16[640,640]{1,0:T(8,128)(2,1)S(1)}, bf16[640,640]{1,0:T(8,128)(2,1)}, u32[]{:S(2)}) copy-start(bf16[640,640]{1,0:T(8,128)(2,1)} %param.13) | copy-start | bytes 2457604
  0.6 42.1 %copy-start.6 = (bf16[640,640]{1,0:T(8,128)(2,1)S(1)}, bf16[640,640]{1,0:T(8,128)(2,1)}, u32[]{:S(2)}) copy-start(bf16[640,640]{1,0:T(8,128)(2,1)} %param.15) | copy-start | bytes 2457604
  2.0 47.4 %collective-permute-start.1 = (bf16[1,1,32,640]{3,2,1,0:T(8,128)(2,1)S(1)}, bf16[1,1,32,640]{3,2,1,0:T(8,128)(2,1)S(1)}, u32[]{:S(2)}, u32[]{:S(2)}) collective-permute-start(bf16[1,1,32,640]{3,2,1,0:T(8,128)(2,1)S(1)} %get-tuple-element.22), channel_id=1, source_target_pairs={{1,0},{2,1},{3,2},{5,4},{6,5},{7,6},{9,8},{10,9},{11,10},{13,12},{... | collective-permute-start | bytes 122888 | tf_op jit(solution)/shard_map/ppermute | solution.py:120
  7.1 42.2 %collective-permute-start = (bf16[1,1,32,640]{3,2,1,0:T(8,128)(2,1)S(1)}, bf16[1,1,32,640]{3,2,1,0:T(8,128)(2,1)S(1)}, u32[]{:S(2)}, u32[]{:S(2)}) collective-permute-start(bf16[1,1,32,640]{3,2,1,0:T(8,128)(2,1)S(1)} %get-tuple-element.21), channel_id=1, source_target_pairs={{0,1},{1,2},{2,3},{4,5},{5,6},{6,7},{8,9},{9,10},{10,11},{12,13},{... | collective-permute-start | bytes 122888 | tf_op jit(solution)/shard_map/ppermute | solution.py:119
  43.8 5.9 %slice-start.2 = ((s8[7372800]{0:T(1024)(128)(4,1)}), s8[4194304]{0:T(1024)(128)(4,1)S(1)}, s32[]{:S(2)}) async-start(s8[7372800]{0:T(1024)(128)(4,1)} %bitcast.133), calls=%async_computation.2 | async-start | bytes 8388608
  43.8 5.9 %slice-start.3 = ((s8[7372800]{0:T(1024)(128)(4,1)}), s8[3178496]{0:T(1024)(128)(4,1)S(1)}, s32[]{:S(2)}) async-start(s8[7372800]{0:T(1024)(128)(4,1)} %bitcast.133), calls=%async_computation.3 | async-start | bytes 6356992
  52.1 1.4 %copy-start.4 = (bf16[1,8,32,640]{3,2,1,0:T(8,128)(2,1)S(1)}, bf16[1,8,32,640]{3,2,1,0:T(8,128)(2,1)}, u32[]{:S(2)}) copy-start(bf16[1,8,32,640]{3,2,1,0:T(8,128)(2,1)} %param.9) | copy-start | bytes 983044
  52.2 1.4 %copy-start.9 = (f32[640]{0:T(1024)S(1)}, f32[640]{0:T(1024)}, u32[]{:S(2)}) copy-start(f32[640]{0:T(1024)} %param.11) | copy-start | bytes 7684
  53.1 1.7 %copy-start.3 = (bf16[640,1280]{1,0:T(8,128)(2,1)S(1)}, bf16[640,1280]{1,0:T(8,128)(2,1)}, u32[]{:S(2)}) copy-start(bf16[640,1280]{1,0:T(8,128)(2,1)} %constant_dynamic-update-slice_fusion) | copy-start | bytes 4915204
  56.5 18.7 %collective-permute-start.4 = (bf16[256,640]{1,0:T(8,128)(2,1)}, bf16[256,640]{1,0:T(8,128)(2,1)}, u32[]{:S(2)}, u32[]{:S(2)}) collective-permute-start(bf16[256,640]{1,0:T(8,128)(2,1)} %fusion.31), channel_id=1, source_target_pairs={{0,3},{1,0},{2,1},{3,2},{4,7},{5,4},{6,5},{7,6},{8,11},{9,8},{10,9... | collective-permute-start | bytes 983048 | tf_op jit(solution)/shard_map/ppermute | solution.py:183
  56.7 18.5 %collective-permute-start.3 = (bf16[256,640]{1,0:T(8,128)(2,1)}, bf16[256,640]{1,0:T(8,128)(2,1)}, u32[]{:S(2)}, u32[]{:S(2)}) collective-permute-start(bf16[256,640]{1,0:T(8,128)(2,1)} %fusion.31), channel_id=1, source_target_pairs={{0,2},{1,3},{2,0},{3,1},{4,6},{5,7},{6,4},{7,5},{8,10},{9,11},{10,... | collective-permute-start | bytes 983048 | tf_op jit(solution)/shard_map/ppermute | solution.py:183
  59.9 15.3 %collective-permute-start.2 = (bf16[256,640]{1,0:T(8,128)(2,1)}, bf16[256,640]{1,0:T(8,128)(2,1)}, u32[]{:S(2)}, u32[]{:S(2)}) collective-permute-start(bf16[256,640]{1,0:T(8,128)(2,1)} %fusion.31), channel_id=1, source_target_pairs={{0,1},{1,2},{2,3},{3,0},{4,5},{5,6},{6,7},{7,4},{8,9},{9,10},{10,1... | collective-permute-start | bytes 983048 | tf_op jit(solution)/shard_map/ppermute | solution.py:183
  67.9 4.5 %copy-start.5 = (bf16[256,640]{0,1:T(8,128)(2,1)S(1)}, bf16[256,640]{0,1:T(8,128)(2,1)}, u32[]{:S(2)}) copy-start(bf16[256,640]{0,1:T(8,128)(2,1)} %copy.20) | copy-start | bytes 983044
  82.5 9.6 %slice-start = ((s8[8388608]{0:T(1024)(128)(4,1)}), s8[4194304]{0:T(1024)(128)(4,1)S(1)}, s32[]{:S(2)}) async-start(s8[8388608]{0:T(1024)(128)(4,1)} %bitcast.131), calls=%async_computation | async-start | bytes 8388608
  87.6 4.6 %slice-start.1 = ((s8[8388608]{0:T(1024)(128)(4,1)}), s8[4194304]{0:T(1024)(128)(4,1)S(1)}, s32[]{:S(2)}) async-start(s8[8388608]{0:T(1024)(128)(4,1)} %bitcast.131), calls=%async_computation.1 | async-start | bytes 8388608
  87.6 5.0 %copy-start.2 = (bf16[1024,640]{0,1:T(8,128)(2,1)S(1)}, bf16[1024,640]{0,1:T(8,128)(2,1)}, u32[]{:S(2)}) copy-start(bf16[1024,640]{0,1:T(8,128)(2,1)} %get-tuple-element.8) | copy-start | bytes 3932164
  97.5 4.6 %copy-start.1 = (f32[8,256,768]{2,1,0:T(8,128)S(1)}, f32[8,256,768]{2,1,0:T(8,128)}, u32[]{:S(2)}) copy-start(f32[8,256,768]{2,1,0:T(8,128)} %get-tuple-element.28) | copy-start | bytes 18874372
  102.1 2.8 %copy-start.7 = (f32[256,8,80]{0,2,1:T(8,128)S(1)}, f32[256,8,80]{0,2,1:T(8,128)}, u32[]{:S(2)}) copy-start(f32[256,8,80]{0,2,1:T(8,128)} %fusion.15) | copy-start | bytes 1966084
  102.1 2.8 %copy-start.8 = (bf16[256,640]{0,1:T(8,128)(2,1)S(1)}, bf16[256,640]{0,1:T(8,128)(2,1)}, u32[]{:S(2)}) copy-start(bf16[256,640]{0,1:T(8,128)(2,1)} %copy.21) | copy-start | bytes 983044
  104.9 1.1 %copy-start.10 = (bf16[640,640]{1,0:T(8,128)(2,1)S(1)}, bf16[640,640]{1,0:T(8,128)(2,1)}, u32[]{:S(2)}) copy-start(bf16[640,640]{1,0:T(8,128)(2,1)} %param.16) | copy-start | bytes 2457604
  104.9 1.1 %copy-start.11 = (f32[640]{0:T(1024)S(1)}, f32[640]{0:T(1024)}, u32[]{:S(2)}) copy-start(f32[640]{0:T(1024)} %param.17) | copy-start | bytes 7684

commit v6 on v5

--- a/solution.py
+++ b/solution.py
@@ -146,6 +146,56 @@
     return (new_top, total * factor + block_total, summed * factor[..., None] + product)
 
 
+def attention_kernel(heads, q_ref, k_ref, v_ref, rk_ref, rv_ref, o_ref):
+    for head in range(heads):
+        lanes = slice(head * HD, (head + 1) * HD)
+        query = q_ref[:, lanes]
+        parts = []
+        for key_ref, value_ref in ((k_ref, v_ref), (rk_ref, rv_ref)):
+            scores = lax.dot_general(
+                query,
+                key_ref[:, lanes],
+                (((1,), (1,)), ((), ())),
+                preferred_element_type=jnp.float32,
+            )
+            parts.append((scores * HD ** (-0.5), value_ref))
+        top = jnp.maximum(
+            jnp.max(parts[0][0], axis=1, keepdims=True),
+            jnp.max(parts[1][0], axis=1, keepdims=True),
+        )
+        total = None
+        summed = None
+        for scores, value_ref in parts:
+            weights = jnp.exp(scores - top)
+            block_total = jnp.sum(weights, axis=1, keepdims=True)
+            product = jnp.dot(
+                weights.astype(jnp.bfloat16),
+                value_ref[:, lanes],
+                preferred_element_type=jnp.float32,
+            )
+            total = block_total if total is None else total + block_total
+            summed = product if summed is None else summed + product
+        o_ref[:, lanes] = (summed / total).astype(o_ref.dtype)
+
+
+def attention(query, keys, values, ref_keys, ref_values, heads, tile):
+    tokens, channels = query.shape
+    whole = lambda array: pl.BlockSpec(array.shape, lambda i: (0, 0))
+    return pl.pallas_call(
+        functools.partial(attention_kernel, heads),
+        out_shape=jax.ShapeDtypeStruct((tokens, channels), jnp.bfloat16),
+        grid=(tokens // tile,),
+        in_specs=[
+            pl.BlockSpec((tile, channels), lambda i: (i, 0)),
+            whole(keys),
+            whole(values),
+            whole(ref_keys),
+            whole(ref_values),
+        ],
+        out_specs=pl.BlockSpec((tile, channels), lambda i: (i, 0)),
+    )(query, keys, values, ref_keys, ref_values)
+
+
 def doubling_gather(value, axis):
     size = lax.axis_size(axis)
     step = 1
@@ -160,7 +210,6 @@
     count, band_rows, width, channels = frames.shape
     heads = channels // HD
     band = band_rows * width
-    w_pair = jnp.concatenate([w_key, w_value], axis=1)
     every_feature = staged_gather(ref_features)
     activated = jax.nn.silu(frames.astype(jnp.float32)).astype(jnp.bfloat16)
     padded = extended(activated, ROW_PARTS, 1, 1)
@@ -186,14 +235,19 @@
         axis=0,
     )
     query = jnp.dot(hidden, w_query, preferred_element_type=jnp.float32).astype(jnp.bfloat16)
-    query_heads = query.reshape(band, heads, HD)
-    state = (None, None, None)
-    for source in (hidden, others, every_feature):
-        pair = jnp.dot(source, w_pair, preferred_element_type=jnp.float32).astype(jnp.bfloat16)
-        state = attend_block(state, query_heads, pair[:, :channels], pair[:, channels:], heads)
-    top, total, summed = state
-    mixed = summed / total[..., None]
-    mixed = jnp.transpose(mixed, (1, 0, 2)).reshape(band, channels).astype(jnp.bfloat16)
+    source = jnp.concatenate([hidden, others], axis=0)
+    project = lambda rows, weight: jnp.dot(
+        rows, weight, preferred_element_type=jnp.float32
+    ).astype(jnp.bfloat16)
+    mixed = attention(
+        query,
+        project(source, w_key),
+        project(source, w_value),
+        project(every_feature, w_key),
+        project(every_feature, w_value),
+        heads,
+        128,
+    )
     attended = (jnp.dot(mixed, w_out, preferred_element_type=jnp.float32) + out_bias).astype(
         jnp.bfloat16
     )

time: 108 us -> 92.6 us (0.86)
  Pallas kernels: 31.6 us -> 51 us
  local copies, waits for them, and re-layouts: 18.7 us -> 0.27 us
  matrix products: 33.6 us -> 18.5 us
  waiting for transfers between devices: 0.01 us -> 8.77 us
  other arithmetic: 10.1 us -> 1.46 us
    pallas_call x0 -> x1, Pallas kernels: none -> 18.6 us  [attention(): pl.pallas_call(functools.partial(attention_kernel, heads), out_shape=jax....]
    dot_general x9 -> x4, matrix products: 25.3 us -> 11.1 us  [shards(): jnp.dot(rows, weight, preferred_element_type=jnp.float32)]
    slice x7 -> x0, local copies, waits for them, and re-layouts: 12.1 us -> none  [the longest x4 6.64 us: shards(): pair[:, channels:]]
    ppermute x3, waiting for transfers between devices: 0.01 us -> 8.76 us  [shards(): lax.ppermute(hidden, ROW_PARTS, [(j, (j + shift) % rows) for j in range(r...]
    reduce_sum x3 -> x0, other arithmetic: 8.54 us -> none  [attend_block(): block_total = jnp.sum(weights, axis=2)]
    unnamed x33 -> x20, local copies, waits for them, and re-layouts: 4.21 us -> 0.06 us
    ppermute x1, starting transfers between devices: 5.15 us -> 1.92 us  [extended(): after = lax.ppermute(initial, axis, down)]
    ppermute x1, starting transfers between devices: 1.92 us -> 4.59 us  [extended(): before = lax.ppermute(last, axis, up)]
  transfers between devices with their start and end apart: 5 -> 5, of which waited for: 0 -> 2; matrix products, arithmetic and copies ran while one was open for 21% -> 8% of each run, Pallas kernels for 29% -> 35%
where the time goes in v6:
time: 92.6 us; the launch traced here: 92.2 us
  Pallas kernels  51 us (55%)
  matrix products  18.5 us (20%)
  starting transfers between devices  11.3 us (12%)
  waiting for transfers between devices  8.77 us (9%)
  other arithmetic  1.46 us (2%)
    pallas_call x1, Pallas kernels, staged_gather(): pl.pallas_call(functools.partial(staged_kernel, sizes), out_shape=jax.Sha...  32.5 us
    pallas_call x1, Pallas kernels, attention(): pl.pallas_call(functools.partial(attention_kernel, heads), out_shape=jax....  18.6 us
    dot_general x4, matrix products, shards(): jnp.dot(rows, weight, preferred_element_type=jnp.float32)  11.1 us
    ppermute x3, waiting for transfers between devices, shards(): lax.ppermute(hidden, ROW_PARTS, [(j, (j + shift) % rows) for j in range(r...  8.76 us
    ppermute x3, starting transfers between devices, shards(): lax.ppermute(hidden, ROW_PARTS, [(j, (j + shift) % rows) for j in range(r...  4.8 us
    ppermute x1, starting transfers between devices, extended(): before = lax.ppermute(last, axis, up)  4.59 us
    dot_general x9, matrix products, shards(): jnp.dot(window, conv_weight[row_tap, col_tap], preferred_element_type=jnp...  4.13 us
    dot_general x1, matrix products, shards(): jnp.dot(mixed, w_out, preferred_element_type=jnp.float32) + out_bias  2.16 us
  transfers between devices with their start and end apart: 5, of which 2 were waited for; matrix products, arithmetic and copies ran while one was open for 8% of the time, Pallas kernels for 35%

profile of v6, /device:TPU:1, one launch (start us, length us, event | category | flops | bytes accessed | tf_op | source)
XLA Modules:
  0.0 92.2 jit_solution(14704440980727250415)
XLA Ops:
  0.6 0.0 copy-start
  0.6 1.2 %multiply_convert_fusion = bf16[1,8,32,640]{3,2,1,0:T(8,128)(2,1)S(1)} fusion(bf16[1,8,32,640]{3,2,1,0:T(8,128)(2,1)} %param.9), kind=kLoop, calls=%fused_computation.42 | loop fusion | flops 983040 | bytes 655360 | tf_op jit(solution)/shard_map/convert_element_type | solution.py:214
  1.9 4.6 %collective-permute-start = (bf16[1,1,32,640]{3,2,1,0:T(8,128)(2,1)S(1)}, bf16[1,1,32,640]{3,2,1,0:T(8,128)(2,1)S(1)}, u32[]{:S(2)}, u32[]{:S(2)}) collective-permute-start(bf16[1,1,32,640]{3,2,1,0:T(8,128)(2,1)S(1)} %get-tuple-element.10), channel_id=1, source_target_pairs={{0,1},{1,2},{2,3},{4,5},{5,6},{6,7},{8,9},{9,10},{10,11},{12,13},{... | collective-permute-start | bytes 122888 | tf_op jit(solution)/shard_map/ppermute | solution.py:119
  6.5 1.9 %collective-permute-start.1 = (bf16[1,1,32,640]{3,2,1,0:T(8,128)(2,1)S(1)}, bf16[1,1,32,640]{3,2,1,0:T(8,128)(2,1)S(1)}, u32[]{:S(2)}, u32[]{:S(2)}) collective-permute-start(bf16[1,1,32,640]{3,2,1,0:T(8,128)(2,1)S(1)} %get-tuple-element.11), channel_id=1, source_target_pairs={{1,0},{2,1},{3,2},{5,4},{6,5},{7,6},{9,8},{10,9},{11,10},{13,12},{... | collective-permute-start | bytes 122888 | tf_op jit(solution)/shard_map/ppermute | solution.py:120
  8.4 32.5 %shard_map.104 = bf16[64,16,640]{2,1,0:T(8,128)(2,1)} custom-call(bf16[1,16,640]{2,1,0:T(8,128)(2,1)} %bitcast.74), custom_call_target="tpu_custom_call" | custom-call | tf_op jit(solution)/shard_map/pallas_call | solution.py:101
  40.9 0.0 copy-done
  40.9 0.0 copy-start.1
  41.0 3.9 %convolution_convert_fusion.rv_ref = bf16[1024,640]{1,0:T(8,128)(2,1)} fusion(bf16[1024,640]{1,0:T(8,128)(2,1)} %bitcast.66, bf16[640,640]{1,0:T(8,128)(2,1)S(1)} %copy-done), kind=kOutput, calls=%fused_computation | convolution fusion | flops 839516160 | bytes 3440640 | tf_op jit(solution)/shard_map/dot_general | solution.py:239
  44.8 0.0 collective-permute-done
  44.8 0.0 collective-permute-done.1
  44.8 0.2 fusion.30
  45.0 0.2 fusion.33
  45.2 0.0 copy-done.1
  45.2 0.5 fusion.15
  45.7 0.5 fusion.6
  46.1 0.1 pad_maximum_fusion.1
  46.2 0.5 convolution_add_fusion.7
  46.7 0.5 convolution_add_fusion.6
  47.1 0.5 convolution_add_fusion.5
  47.6 0.5 convolution_add_fusion.4
  48.1 0.0 copy-start.2
  48.1 0.0 copy-start.6
  48.1 0.5 convolution_add_fusion.3
  48.5 0.0 copy-start.4
  48.6 0.0 copy-start.7
  48.6 0.5 convolution_add_fusion.2
  49.0 0.0 copy-done.2
  49.0 0.0 copy-done.6
  49.1 0.5 fusion.4
  49.5 0.0 copy-start.3
  49.5 0.0 copy-start.5
  49.6 0.2 collective-permute-start.4
  49.8 2.7 %collective-permute-start.3 = (bf16[256,640]{1,0:T(8,128)(2,1)S(1)}, bf16[256,640]{1,0:T(8,128)(2,1)S(1)}, u32[]{:S(2)}, u32[]{:S(2)}) collective-permute-start(bf16[256,640]{1,0:T(8,128)(2,1)S(1)} %fusion.4), channel_id=1, source_target_pairs={{0,2},{1,3},{2,0},{3,1},{4,6},{5,7},{6,4},{7,5},{8,10},{9,11},{10,... | collective-permute-start | bytes 983048 | tf_op jit(solution)/shard_map/ppermute | solution.py:232
  52.5 1.9 %collective-permute-start.2 = (bf16[256,640]{1,0:T(8,128)(2,1)S(1)}, bf16[256,640]{1,0:T(8,128)(2,1)S(1)}, u32[]{:S(2)}, u32[]{:S(2)}) collective-permute-start(bf16[256,640]{1,0:T(8,128)(2,1)S(1)} %fusion.4), channel_id=1, source_target_pairs={{0,1},{1,2},{2,3},{3,0},{4,5},{5,6},{6,7},{7,4},{8,9},{9,10},{10,1... | collective-permute-start | bytes 983048 | tf_op jit(solution)/shard_map/ppermute | solution.py:232
  54.4 0.0 copy-done.4
  54.4 0.0 copy-done.7
  54.4 2.4 %convolution_convert_fusion.1.rk_ref = bf16[1024,640]{1,0:T(8,128)(2,1)} fusion(bf16[1024,640]{1,0:T(8,128)(2,1)S(1)} %bitcast.67, bf16[640,640]{1,0:T(8,128)(2,1)S(1)} %copy-done.7), kind=kOutput, calls=%fused_computation.1 | convolution fusion | flops 839516160 | bytes 3440640 | tf_op jit(solution)/shard_map/dot_general | solution.py:239
  56.7 0.0 copy-done.5
  56.7 1.2 %convolution_convert_fusion.4.q_ref = bf16[256,640]{1,0:T(8,128)(2,1)} fusion(bf16[256,640]{1,0:T(8,128)(2,1)S(1)} %fusion.4, bf16[640,640]{1,0:T(8,128)(2,1)S(1)} %copy-done.5), kind=kOutput, calls=%fused_computation.20 | convolution fusion | flops 209879040 | bytes 1474560 | tf_op jit(solution)/shard_map/dot_general | solution.py:237
  57.9 3.0 %collective-permute-done.4 = bf16[256,640]{1,0:T(8,128)(2,1)S(1)} collective-permute-done((bf16[256,640]{1,0:T(8,128)(2,1)S(1)}, bf16[256,640]{1,0:T(8,128)(2,1)S(1)}, u32[]{:S(2)}, u32[]{:S(2)}) %collective-permute-start.4) | collective-permute-done | bytes 327712 | tf_op jit(solution)/shard_map/ppermute | solution.py:232
  60.9 0.0 collective-permute-done.3
  60.9 5.8 %collective-permute-done.2 = bf16[256,640]{1,0:T(8,128)(2,1)S(1)} collective-permute-done((bf16[256,640]{1,0:T(8,128)(2,1)S(1)}, bf16[256,640]{1,0:T(8,128)(2,1)S(1)}, u32[]{:S(2)}, u32[]{:S(2)}) %collective-permute-start.2) | collective-permute-done | bytes 327712 | tf_op jit(solution)/shard_map/ppermute | solution.py:232
  66.7 2.4 %convolution_convert_fusion.2.v_ref = bf16[1024,640]{1,0:T(8,128)(2,1)} fusion(bf16[640,640]{1,0:T(8,128)(2,1)S(1)} %copy-done, bf16[256,640]{1,0:T(8,128)(2,1)S(1)} %collective-permute-done.4, bf16[256,640]{1,0:T(8,128)(2,1)S(1)} %collective-permute-done.3, bf16[256,640]{1,0:T(8,128)(2,1)S(1)} %collective-permute-done.2, bf16[256,640]{1,0:T(8,128)(2,1)S(1)} %fusion.4), kind=kOutput, calls=%fused_computation.2 | convolution fusion | flops 844759040 | bytes 3440640 | tf_op jit(solution)/shard_map/dot_general | solution.py:239
  69.1 0.0 copy-done.3
  69.1 2.4 %convolution_convert_fusion.3.k_ref = bf16[1024,640]{1,0:T(8,128)(2,1)} fusion(bf16[640,640]{1,0:T(8,128)(2,1)S(1)} %copy-done.7, bf16[256,640]{1,0:T(8,128)(2,1)S(1)} %collective-permute-done.4, bf16[256,640]{1,0:T(8,128)(2,1)S(1)} %collective-permute-done.3, bf16[256,640]{1,0:T(8,128)(2,1)S(1)} %collective-permute-done.2, bf16[256,640]{1,0:T(8,128)(2,1)S(1)} %fusion.4), kind=kOutput, calls=%fused_computation.3 | convolution fusion | flops 844759040 | bytes 3440640 | tf_op jit(solution)/shard_map/dot_general | solution.py:239
  71.5 18.6 %shard_map.105 = bf16[256,640]{1,0:T(8,128)(2,1)} custom-call(bf16[256,640]{1,0:T(8,128)(2,1)} %convolution_convert_fusion.4.q_ref, bf16[1024,640]{1,0:T(8,128)(2,1)} %convolution_convert_fusion.3.k_ref, bf16[1024,640]{1,0:T(8,128)(2,1)} %convolution_convert_fusion.2.v_ref, bf16[1024,640]{1,0:T(8,128)(2,1)} %convolution_convert_fusion.1.rk_ref, ...), custom_call_target="tpu_custom_call" | custom-call | tf_op jit(solution)/shard_map/pallas_call | solution.py:184
  90.1 0.0 copy-done.8
  90.1 2.2 %fusion.3 = bf16[256,640]{1,0:T(8,128)(2,1)} fusion(bf16[256,640]{1,0:T(8,128)(2,1)} %shard_map.105, bf16[640,640]{1,0:T(8,128)(2,1)S(1)} %copy-done.8, f32[640]{0:T(1024)S(1)} %copy-done.9), kind=kOutput, calls=%fused_computation.18 | convolution fusion | flops 210042880 | bytes 1477120 | tf_op jit(solution)/shard_map/dot_general | solution.py:251
  (4 shorter events, 0.0 us)
Async XLA Ops:
  0.6 40.3 %copy-start = (bf16[640,640]{1,0:T(8,128)(2,1)S(1)}, bf16[640,640]{1,0:T(8,128)(2,1)}, u32[]{:S(2)}) copy-start(bf16[640,640]{1,0:T(8,128)(2,1)} %param.15) | copy-start | bytes 2457604
  1.9 42.9 %collective-permute-start = (bf16[1,1,32,640]{3,2,1,0:T(8,128)(2,1)S(1)}, bf16[1,1,32,640]{3,2,1,0:T(8,128)(2,1)S(1)}, u32[]{:S(2)}, u32[]{:S(2)}) collective-permute-start(bf16[1,1,32,640]{3,2,1,0:T(8,128)(2,1)S(1)} %get-tuple-element.10), channel_id=1, source_target_pairs={{0,1},{1,2},{2,3},{4,5},{5,6},{6,7},{8,9},{9,10},{10,11},{12,13},{... | collective-permute-start | bytes 122888 | tf_op jit(solution)/shard_map/ppermute | solution.py:119
  6.5 38.3 %collective-permute-start.1 = (bf16[1,1,32,640]{3,2,1,0:T(8,128)(2,1)S(1)}, bf16[1,1,32,640]{3,2,1,0:T(8,128)(2,1)S(1)}, u32[]{:S(2)}, u32[]{:S(2)}) collective-permute-start(bf16[1,1,32,640]{3,2,1,0:T(8,128)(2,1)S(1)} %get-tuple-element.11), channel_id=1, source_target_pairs={{1,0},{2,1},{3,2},{5,4},{6,5},{7,6},{9,8},{10,9},{11,10},{13,12},{... | collective-permute-start | bytes 122888 | tf_op jit(solution)/shard_map/ppermute | solution.py:120
  40.9 4.3 %copy-start.1 = (bf16[3,3,640,640]{3,2,1,0:T(8,128)(2,1)S(1)}, bf16[3,3,640,640]{3,2,1,0:T(8,128)(2,1)}, u32[]{:S(2)}) copy-start(bf16[3,3,640,640]{3,2,1,0:T(8,128)(2,1)} %param.10) | copy-start | bytes 22118404
  48.1 1.0 %copy-start.2 = (bf16[1,8,32,640]{3,2,1,0:T(8,128)(2,1)S(1)}, bf16[1,8,32,640]{3,2,1,0:T(8,128)(2,1)}, u32[]{:S(2)}) copy-start(bf16[1,8,32,640]{3,2,1,0:T(8,128)(2,1)} %param.9) | copy-start | bytes 983044
  48.1 1.0 %copy-start.6 = (f32[640]{0:T(1024)S(1)}, f32[640]{0:T(1024)}, u32[]{:S(2)}) copy-start(f32[640]{0:T(1024)} %param.11) | copy-start | bytes 7684
  48.5 5.8 %copy-start.4 = (bf16[64,16,640]{2,1,0:T(8,128)(2,1)S(1)}, bf16[64,16,640]{2,1,0:T(8,128)(2,1)}, u32[]{:S(2)}) copy-start(bf16[64,16,640]{2,1,0:T(8,128)(2,1)} %shard_map.104) | copy-start | bytes 3932164
  48.6 5.8 %copy-start.7 = (bf16[640,640]{1,0:T(8,128)(2,1)S(1)}, bf16[640,640]{1,0:T(8,128)(2,1)}, u32[]{:S(2)}) copy-start(bf16[640,640]{1,0:T(8,128)(2,1)} %param.14) | copy-start | bytes 2457604
  49.5 19.6 %copy-start.3 = (bf16[256,640]{1,0:T(8,128)(2,1)}, bf16[256,640]{1,0:T(8,128)(2,1)S(1)}, u32[]{:S(2)}) copy-start(bf16[256,640]{1,0:T(8,128)(2,1)S(1)} %fusion.4) | copy-start | bytes 983044
  49.5 7.2 %copy-start.5 = (bf16[640,640]{1,0:T(8,128)(2,1)S(1)}, bf16[640,640]{1,0:T(8,128)(2,1)}, u32[]{:S(2)}) copy-start(bf16[640,640]{1,0:T(8,128)(2,1)} %param.13) | copy-start | bytes 2457604
  49.6 11.4 %collective-permute-start.4 = (bf16[256,640]{1,0:T(8,128)(2,1)S(1)}, bf16[256,640]{1,0:T(8,128)(2,1)S(1)}, u32[]{:S(2)}, u32[]{:S(2)}) collective-permute-start(bf16[256,640]{1,0:T(8,128)(2,1)S(1)} %fusion.4), channel_id=1, source_target_pairs={{0,3},{1,0},{2,1},{3,2},{4,7},{5,4},{6,5},{7,6},{8,11},{9,8},{10,9... | collective-permute-start | bytes 983048 | tf_op jit(solution)/shard_map/ppermute | solution.py:232
  49.8 11.1 %collective-permute-start.3 = (bf16[256,640]{1,0:T(8,128)(2,1)S(1)}, bf16[256,640]{1,0:T(8,128)(2,1)S(1)}, u32[]{:S(2)}, u32[]{:S(2)}) collective-permute-start(bf16[256,640]{1,0:T(8,128)(2,1)S(1)} %fusion.4), channel_id=1, source_target_pairs={{0,2},{1,3},{2,0},{3,1},{4,6},{5,7},{6,4},{7,5},{8,10},{9,11},{10,... | collective-permute-start | bytes 983048 | tf_op jit(solution)/shard_map/ppermute | solution.py:232
  52.5 14.2 %collective-permute-start.2 = (bf16[256,640]{1,0:T(8,128)(2,1)S(1)}, bf16[256,640]{1,0:T(8,128)(2,1)S(1)}, u32[]{:S(2)}, u32[]{:S(2)}) collective-permute-start(bf16[256,640]{1,0:T(8,128)(2,1)S(1)} %fusion.4), channel_id=1, source_target_pairs={{0,1},{1,2},{2,3},{3,0},{4,5},{5,6},{6,7},{7,4},{8,9},{9,10},{10,1... | collective-permute-start | bytes 983048 | tf_op jit(solution)/shard_map/ppermute | solution.py:232
  71.5 18.6 %copy-start.8 = (bf16[640,640]{1,0:T(8,128)(2,1)S(1)}, bf16[640,640]{1,0:T(8,128)(2,1)}, u32[]{:S(2)}) copy-start(bf16[640,640]{1,0:T(8,128)(2,1)} %param.16) | copy-start | bytes 2457604
  71.5 18.6 %copy-start.9 = (f32[640]{0:T(1024)S(1)}, f32[640]{0:T(1024)}, u32[]{:S(2)}) copy-start(f32[640]{0:T(1024)} %param.17) | copy-start | bytes 7684

commit v7 on v6

--- a/solution.py
+++ b/solution.py
@@ -37,7 +37,7 @@
     return Mesh(devices.reshape(shape), TM_PARTS + ROW_PARTS)
 
 
-def staged_kernel(sizes, x_ref, out_ref, local_sem, *sems):
+def staged_kernel(sizes, x_ref, band_ref, out_ref, whole_ref, local_sem, band_sem, *sems):
     high, across, along = sizes
     half = along // 2
     yh, xx, zz = [lax.axis_index(axis) for axis in TM_PARTS]
@@ -51,10 +51,32 @@
     c_peer = {"core": other_core}
     peers = [z_peer(s) for s in range(1, along)] + [x_peer(s) for s in range(1, across)]
     peers += [y_peer, c_peer]
+    cores = lax.axis_size("core")
+    bands = lax.axis_size("y_lo") * cores
+    band = low * cores + core
+    band_peer = lambda shift: {
+        "y_lo": lax.rem(band + shift, bands) // cores,
+        "core": lax.rem(band + shift, bands) % cores,
+    }
+    peers += [band_peer(shift) for shift in range(1, bands)]
     barrier = pltpu.get_barrier_semaphore()
     for peer in peers:
         pl.semaphore_signal(barrier, inc=1, device_id=peer, device_id_type=MESH)
     pl.semaphore_wait(barrier, len(peers))
+    band_copies = []
+    for shift in range(1, bands):
+        copy = pltpu.make_async_remote_copy(
+            src_ref=band_ref,
+            dst_ref=whole_ref.at[band],
+            send_sem=sems[8].at[shift],
+            recv_sem=sems[9].at[shift],
+            device_id=band_peer(shift),
+            device_id_type=MESH,
+        )
+        copy.start()
+        band_copies.append(copy)
+    own_band = pltpu.make_async_copy(band_ref, whole_ref.at[band], band_sem)
+    own_band.start()
     local = pltpu.make_async_copy(x_ref, out_ref.at[pl.ds(me, 1)], local_sem)
     local.start()
     local.wait()
@@ -90,23 +112,31 @@
         j = lax.rem(region + step, regions)
         groups.append(out_ref.at[pl.ds(j * along + core * half, half)])
     exchange([(chunk, c_peer) for chunk in groups], sems[6], sems[7])
-
-
-def staged_gather(value):
+    own_band.wait()
+    for copy in band_copies:
+        copy.wait()
+
+
+def staged_gather(value, hidden):
     sizes = [lax.axis_size(axis) for axis in TM_PARTS]
     total = sizes[0] * sizes[1] * sizes[2]
+    bands = lax.axis_size(ROW_PARTS)
     sems = []
-    for count in (sizes[2], sizes[1], sizes[1], sizes[0] * sizes[1]):
+    for count in (sizes[2], sizes[1], sizes[1], sizes[0] * sizes[1], bands):
         sems += [pltpu.SemaphoreType.DMA((count,))] * 2
-    gathered = pl.pallas_call(
+    gathered, whole = pl.pallas_call(
         functools.partial(staged_kernel, sizes),
-        out_shape=jax.ShapeDtypeStruct((total,) + value.shape, value.dtype),
-        in_specs=[pl.BlockSpec(memory_space=pl.ANY)],
-        out_specs=pl.BlockSpec(memory_space=pl.ANY),
-        scratch_shapes=[pltpu.SemaphoreType.DMA] + sems,
+        out_shape=(
+            jax.ShapeDtypeStruct((total,) + value.shape, value.dtype),
+            jax.ShapeDtypeStruct((bands,) + hidden.shape, hidden.dtype),
+        ),
+        in_specs=[pl.BlockSpec(memory_space=pl.ANY)] * 2,
+        out_specs=(pl.BlockSpec(memory_space=pl.ANY),) * 2,
+        scratch_shapes=[pltpu.SemaphoreType.DMA] * 2 + sems,
         compiler_params=pltpu.CompilerParams(collective_id=0, has_side_effects=True),
-    )(value[None])
-    return gathered.reshape((total * value.shape[0],) + value.shape[1:])
+    )(value[None], hidden)
+    every = gathered.reshape((total * value.shape[0],) + value.shape[1:])
+    return every, whole.reshape((bands * hidden.shape[0],) + hidden.shape[1:])
 
 
 def extended(value, axis, dim, width):
@@ -210,7 +240,6 @@
     count, band_rows, width, channels = frames.shape
     heads = channels // HD
     band = band_rows * width
-    every_feature = staged_gather(ref_features)
     activated = jax.nn.silu(frames.astype(jnp.float32)).astype(jnp.bfloat16)
     padded = extended(activated, ROW_PARTS, 1, 1)
     padded = jnp.pad(padded, ((0, 0), (0, 0), (1, 1), (0, 0)))
@@ -226,16 +255,8 @@
     hidden = (
         frames.reshape(count * band, channels).astype(jnp.float32) + convolved + conv_bias
     ).astype(jnp.bfloat16)
-    rows = lax.axis_size(ROW_PARTS)
-    others = jnp.concatenate(
-        [
-            lax.ppermute(hidden, ROW_PARTS, [(j, (j + shift) % rows) for j in range(rows)])
-            for shift in range(1, rows)
-        ],
-        axis=0,
-    )
+    every_feature, source = staged_gather(ref_features, hidden)
     query = jnp.dot(hidden, w_query, preferred_element_type=jnp.float32).astype(jnp.bfloat16)
-    source = jnp.concatenate([hidden, others], axis=0)
     project = lambda rows, weight: jnp.dot(
         rows, weight, preferred_element_type=jnp.float32
     ).astype(jnp.bfloat16)

time: 92.6 us -> 95 us (1.026)
  Pallas kernels: 51 us -> 61.6 us
  waiting for transfers between devices: 8.77 us -> 3.38 us
  starting transfers between devices: 11.3 us -> 6.78 us
  matrix products: 18.5 us -> 20.3 us
    pallas_call x1, Pallas kernels: 32.5 us -> 42.9 us  [staged_gather(): pl.pallas_call(functools.partial(staged_kernel, sizes), out_shape=(jax.Sh...]
    ppermute x3 -> x0, waiting for transfers between devices: 8.76 us -> none  [shards(): lax.ppermute(hidden, ROW_PARTS, [(j, (j + shift) % rows) for j in range(r...]
    ppermute x3 -> x0, starting transfers between devices: 4.8 us -> none  [shards(): lax.ppermute(hidden, ROW_PARTS, [(j, (j + shift) % rows) for j in range(r...]
    ppermute x1, waiting for transfers between devices: 0.01 us -> 3.38 us  [extended(): after = lax.ppermute(initial, axis, down)]
    dot_general x9, matrix products: 4.13 us -> 6 us  [shards(): jnp.dot(window, conv_weight[row_tap, col_tap], preferred_element_type=jnp...]
  transfers between devices with their start and end apart: 5 -> 2, of which waited for: 2 -> 1; matrix products, arithmetic and copies ran while one was open for 8% -> 0% of each run, Pallas kernels for 35% -> 0%
where the time goes in v7:
time: 95 us; the launch traced here: 94.8 us
  Pallas kernels  61.6 us (65%)
  matrix products  20.3 us (21%)
  starting transfers between devices  6.78 us (7%)
  waiting for transfers between devices  3.38 us (4%)
  other arithmetic  1.54 us (2%)
    pallas_call x1, Pallas kernels, staged_gather(): pl.pallas_call(functools.partial(staged_kernel, sizes), out_shape=(jax.Sh...  42.9 us
    pallas_call x1, Pallas kernels, attention(): pl.pallas_call(functools.partial(attention_kernel, heads), out_shape=jax....  18.8 us
    dot_general x4, matrix products, shards(): jnp.dot(rows, weight, preferred_element_type=jnp.float32)  11 us
    dot_general x9, matrix products, shards(): jnp.dot(window, conv_weight[row_tap, col_tap], preferred_element_type=jnp...  6 us
    ppermute x1, starting transfers between devices, extended(): before = lax.ppermute(last, axis, up)  4.86 us
    ppermute x1, waiting for transfers between devices, extended(): after = lax.ppermute(initial, axis, down)  3.38 us
    dot_general x1, matrix products, shards(): jnp.dot(mixed, w_out, preferred_element_type=jnp.float32) + out_bias  2.16 us
    ppermute x1, starting transfers between devices, extended(): after = lax.ppermute(initial, axis, down)  1.92 us
  transfers between devices with their start and end apart: 2, of which 1 were waited for; matrix products, arithmetic and copies ran while one was open for 0% of the time, Pallas kernels for 0%

profile of v7, /device:TPU:1, one launch (start us, length us, event | category | flops | bytes accessed | tf_op | source)
XLA Modules:
  0.0 94.8 jit_solution(189268374783370384)
XLA Ops:
  0.6 0.0 copy-start
  0.6 0.0 copy-start.1
  0.7 1.3 %multiply_convert_fusion = bf16[1,8,32,640]{3,2,1,0:T(8,128)(2,1)S(1)} fusion(bf16[1,8,32,640]{3,2,1,0:T(8,128)(2,1)} %param.9), kind=kLoop, calls=%fused_computation.41 | loop fusion | flops 983040 | bytes 655360 | tf_op jit(solution)/shard_map/convert_element_type | solution.py:243
  2.0 4.9 %collective-permute-start = (bf16[1,1,32,640]{3,2,1,0:T(8,128)(2,1)S(1)}, bf16[1,1,32,640]{3,2,1,0:T(8,128)(2,1)S(1)}, u32[]{:S(2)}, u32[]{:S(2)}) collective-permute-start(bf16[1,1,32,640]{3,2,1,0:T(8,128)(2,1)S(1)} %get-tuple-element.14), channel_id=1, source_target_pairs={{0,1},{1,2},{2,3},{4,5},{5,6},{6,7},{8,9},{9,10},{10,11},{12,13},{... | collective-permute-start | bytes 122888 | tf_op jit(solution)/shard_map/ppermute | solution.py:149
  6.9 1.9 %collective-permute-start.1 = (bf16[1,1,32,640]{3,2,1,0:T(8,128)(2,1)S(1)}, bf16[1,1,32,640]{3,2,1,0:T(8,128)(2,1)S(1)}, u32[]{:S(2)}, u32[]{:S(2)}) collective-permute-start(bf16[1,1,32,640]{3,2,1,0:T(8,128)(2,1)S(1)} %get-tuple-element.15), channel_id=1, source_target_pairs={{1,0},{2,1},{3,2},{5,4},{6,5},{7,6},{9,8},{10,9},{11,10},{13,12},{... | collective-permute-start | bytes 122888 | tf_op jit(solution)/shard_map/ppermute | solution.py:150
  8.8 0.0 collective-permute-done
  8.8 3.4 %collective-permute-done.1 = bf16[1,1,32,640]{3,2,1,0:T(8,128)(2,1)S(1)} collective-permute-done((bf16[1,1,32,640]{3,2,1,0:T(8,128)(2,1)S(1)}, bf16[1,1,32,640]{3,2,1,0:T(8,128)(2,1)S(1)}, u32[]{:S(2)}, u32[]{:S(2)}) %collective-permute-start.1) | collective-permute-done | bytes 40992 | tf_op jit(solution)/shard_map/ppermute | solution.py:150
  12.2 0.2 fusion.30
  12.4 0.2 fusion.31
  12.6 1.6 %fusion.15 = f32[256,640]{1,0:T(8,128)S(1)} fusion(bf16[256,640]{1,0:T(8,128)(2,1)S(1)} %bitcast.74, bf16[3,3,640,640]{3,2,1,0:T(8,128)(2,1)} %param.10), kind=kOutput, calls=%fused_computation.30 | convolution fusion | flops 209715200 | bytes 1802240 | tf_op jit(solution)/shard_map/dot_general | solution.py:252
  14.2 0.0 copy-done.1
  14.2 0.5 fusion.6
  14.6 0.1 pad_maximum_fusion
  14.7 0.5 convolution_add_fusion.7
  15.2 0.5 convolution_add_fusion.6
  15.6 0.5 convolution_add_fusion.5
  16.1 0.5 convolution_add_fusion.4
  16.6 0.0 copy-start.3
  16.6 0.0 copy-start.5
  16.6 0.5 convolution_add_fusion.3
  17.1 0.5 convolution_add_fusion.2
  17.5 0.0 copy-done.3
  17.5 0.0 copy-done.5
  17.5 1.2 %fusion.4.band_ref = bf16[256,640]{1,0:T(8,128)(2,1)} fusion(f32[256,640]{1,0:T(8,128)S(1)} %fusion.6, f32[256,640]{1,0:T(8,128)S(1)} %convolution_add_fusion.2, bf16[256,640]{1,0:T(8,128)(2,1)S(1)} %bitcast.67, bf16[3,3,640,640]{3,2,1,0:T(8,128)(2,1)S(1)} %copy-done.1, f32[640]{0:T(1024)S(1)} %copy-done.5, bf16[256,640]{1,0:T(8,128)(2,1)S(1)} %bitcast.66), kind=kOutput, calls=%fused_computation.18 | convolution fusion | flops 210698240 | bytes 3117056 | tf_op jit(solution)/shard_map/dot_general | solution.py:252
  18.7 0.0 copy-start.8
  18.7 42.9 %shard_map.104 = (bf16[64,16,640]{2,1,0:T(8,128)(2,1)}, bf16[4,256,640]{2,1,0:T(8,128)(2,1)}) custom-call(bf16[1,16,640]{2,1,0:T(8,128)(2,1)} %bitcast.75, bf16[256,640]{1,0:T(8,128)(2,1)} %fusion.4.band_ref), custom_call_target="tpu_custom_call" | custom-call | tf_op jit(solution)/shard_map/pallas_call | solution.py:127
  61.6 0.0 copy-start.7
  61.6 0.0 copy-done
  61.6 3.8 %convolution_convert_fusion.rv_ref = bf16[1024,640]{1,0:T(8,128)(2,1)} fusion(bf16[1024,640]{1,0:T(8,128)(2,1)} %bitcast.78, bf16[640,640]{1,0:T(8,128)(2,1)S(1)} %copy-done), kind=kOutput, calls=%fused_computation | convolution fusion | flops 839516160 | bytes 3440640 | tf_op jit(solution)/shard_map/dot_general | solution.py:260
  65.4 0.0 copy-done.8
  65.4 0.0 copy-done.7
  65.4 0.0 copy-start.6
  65.4 2.4 %convolution_convert_fusion.1.rk_ref = bf16[1024,640]{1,0:T(8,128)(2,1)} fusion(bf16[1024,640]{1,0:T(8,128)(2,1)S(1)} %bitcast.79, bf16[640,640]{1,0:T(8,128)(2,1)S(1)} %copy-done.8), kind=kOutput, calls=%fused_computation.1 | convolution fusion | flops 839516160 | bytes 3440640 | tf_op jit(solution)/shard_map/dot_general | solution.py:260
  67.8 0.0 copy-done.6
  67.8 2.4 %convolution_convert_fusion.2.v_ref = bf16[1024,640]{1,0:T(8,128)(2,1)} fusion(bf16[1024,640]{1,0:T(8,128)(2,1)S(1)} %bitcast.76, bf16[640,640]{1,0:T(8,128)(2,1)S(1)} %copy-done), kind=kOutput, calls=%fused_computation.2 | convolution fusion | flops 839516160 | bytes 3440640 | tf_op jit(solution)/shard_map/dot_general | solution.py:260
  70.2 0.0 copy-start.2
  70.2 0.0 copy-start.4
  70.2 2.4 %convolution_convert_fusion.3.k_ref = bf16[1024,640]{1,0:T(8,128)(2,1)} fusion(bf16[1024,640]{1,0:T(8,128)(2,1)S(1)} %bitcast.77, bf16[640,640]{1,0:T(8,128)(2,1)S(1)} %copy-done.8), kind=kOutput, calls=%fused_computation.3 | convolution fusion | flops 839516160 | bytes 3440640 | tf_op jit(solution)/shard_map/dot_general | solution.py:260
  72.6 0.0 copy-done.2
  72.6 0.0 copy-done.4
  72.6 1.2 %convolution_convert_fusion.4.q_ref = bf16[256,640]{1,0:T(8,128)(2,1)} fusion(bf16[256,640]{1,0:T(8,128)(2,1)S(1)} %copy-done.2, bf16[640,640]{1,0:T(8,128)(2,1)S(1)} %copy-done.4), kind=kOutput, calls=%fused_computation.19 | convolution fusion | flops 209879040 | bytes 1474560 | tf_op jit(solution)/shard_map/dot_general | solution.py:259
  73.8 0.0 copy-start.9
  73.8 0.0 copy-start.10
  73.8 18.8 %shard_map.105 = bf16[256,640]{1,0:T(8,128)(2,1)} custom-call(bf16[256,640]{1,0:T(8,128)(2,1)} %convolution_convert_fusion.4.q_ref, bf16[1024,640]{1,0:T(8,128)(2,1)} %convolution_convert_fusion.3.k_ref, bf16[1024,640]{1,0:T(8,128)(2,1)} %convolution_convert_fusion.2.v_ref, bf16[1024,640]{1,0:T(8,128)(2,1)} %convolution_convert_fusion.1.rk_ref, ...), custom_call_target="tpu_custom_call" | custom-call | tf_op jit(solution)/shard_map/pallas_call | solution.py:214
  92.6 0.0 copy-done.9
  92.6 0.0 copy-done.10
  92.6 2.2 %fusion.3 = bf16[256,640]{1,0:T(8,128)(2,1)} fusion(bf16[256,640]{1,0:T(8,128)(2,1)} %shard_map.105, bf16[640,640]{1,0:T(8,128)(2,1)S(1)} %copy-done.9, f32[640]{0:T(1024)S(1)} %copy-done.10), kind=kOutput, calls=%fused_computation.17 | convolution fusion | flops 210042880 | bytes 1477120 | tf_op jit(solution)/shard_map/dot_general | solution.py:272
  (1 shorter events, 0.0 us)
Async XLA Ops:
  0.6 61.0 %copy-start = (bf16[640,640]{1,0:T(8,128)(2,1)S(1)}, bf16[640,640]{1,0:T(8,128)(2,1)}, u32[]{:S(2)}) copy-start(bf16[640,640]{1,0:T(8,128)(2,1)} %param.15) | copy-start | bytes 2457604
  0.6 13.5 %copy-start.1 = (bf16[3,3,640,640]{3,2,1,0:T(8,128)(2,1)S(1)}, bf16[3,3,640,640]{3,2,1,0:T(8,128)(2,1)}, u32[]{:S(2)}) copy-start(bf16[3,3,640,640]{3,2,1,0:T(8,128)(2,1)} %param.10) | copy-start | bytes 22118404
  2.0 6.8 %collective-permute-start = (bf16[1,1,32,640]{3,2,1,0:T(8,128)(2,1)S(1)}, bf16[1,1,32,640]{3,2,1,0:T(8,128)(2,1)S(1)}, u32[]{:S(2)}, u32[]{:S(2)}) collective-permute-start(bf16[1,1,32,640]{3,2,1,0:T(8,128)(2,1)S(1)} %get-tuple-element.14), channel_id=1, source_target_pairs={{0,1},{1,2},{2,3},{4,5},{5,6},{6,7},{8,9},{9,10},{10,11},{12,13},{... | collective-permute-start | bytes 122888 | tf_op jit(solution)/shard_map/ppermute | solution.py:149
  6.9 5.3 %collective-permute-start.1 = (bf16[1,1,32,640]{3,2,1,0:T(8,128)(2,1)S(1)}, bf16[1,1,32,640]{3,2,1,0:T(8,128)(2,1)S(1)}, u32[]{:S(2)}, u32[]{:S(2)}) collective-permute-start(bf16[1,1,32,640]{3,2,1,0:T(8,128)(2,1)S(1)} %get-tuple-element.15), channel_id=1, source_target_pairs={{1,0},{2,1},{3,2},{5,4},{6,5},{7,6},{9,8},{10,9},{11,10},{13,12},{... | collective-permute-start | bytes 122888 | tf_op jit(solution)/shard_map/ppermute | solution.py:150
  16.6 1.0 %copy-start.3 = (bf16[1,8,32,640]{3,2,1,0:T(8,128)(2,1)S(1)}, bf16[1,8,32,640]{3,2,1,0:T(8,128)(2,1)}, u32[]{:S(2)}) copy-start(bf16[1,8,32,640]{3,2,1,0:T(8,128)(2,1)} %param.9) | copy-start | bytes 983044
  16.6 1.0 %copy-start.5 = (f32[640]{0:T(1024)S(1)}, f32[640]{0:T(1024)}, u32[]{:S(2)}) copy-start(f32[640]{0:T(1024)} %param.11) | copy-start | bytes 7684
  18.7 46.7 %copy-start.8 = (bf16[640,640]{1,0:T(8,128)(2,1)S(1)}, bf16[640,640]{1,0:T(8,128)(2,1)}, u32[]{:S(2)}) copy-start(bf16[640,640]{1,0:T(8,128)(2,1)} %param.14) | copy-start | bytes 2457604
  61.6 3.8 %copy-start.7 = (bf16[64,16,640]{2,1,0:T(8,128)(2,1)S(1)}, bf16[64,16,640]{2,1,0:T(8,128)(2,1)}, u32[]{:S(2)}) copy-start(bf16[64,16,640]{2,1,0:T(8,128)(2,1)} %get-tuple-element.5) | copy-start | bytes 3932164
  65.4 2.4 %copy-start.6 = (bf16[4,256,640]{2,1,0:T(8,128)(2,1)S(1)}, bf16[4,256,640]{2,1,0:T(8,128)(2,1)}, u32[]{:S(2)}) copy-start(bf16[4,256,640]{2,1,0:T(8,128)(2,1)} %get-tuple-element.4) | copy-start | bytes 3932164
  70.2 2.4 %copy-start.2 = (bf16[256,640]{1,0:T(8,128)(2,1)S(1)}, bf16[256,640]{1,0:T(8,128)(2,1)}, u32[]{:S(2)}) copy-start(bf16[256,640]{1,0:T(8,128)(2,1)} %fusion.4.band_ref) | copy-start | bytes 983044
  70.2 2.4 %copy-start.4 = (bf16[640,640]{1,0:T(8,128)(2,1)S(1)}, bf16[640,640]{1,0:T(8,128)(2,1)}, u32[]{:S(2)}) copy-start(bf16[640,640]{1,0:T(8,128)(2,1)} %param.13) | copy-start | bytes 2457604
  73.8 18.8 %copy-start.9 = (bf16[640,640]{1,0:T(8,128)(2,1)S(1)}, bf16[640,640]{1,0:T(8,128)(2,1)}, u32[]{:S(2)}) copy-start(bf16[640,640]{1,0:T(8,128)(2,1)} %param.16) | copy-start | bytes 2457604
  73.8 18.8 %copy-start.10 = (f32[640]{0:T(1024)S(1)}, f32[640]{0:T(1024)}, u32[]{:S(2)}) copy-start(f32[640]{0:T(1024)} %param.17) | copy-start | bytes 7684

commit v8 on v6

--- a/solution.py
+++ b/solution.py
@@ -152,11 +152,8 @@
         query = q_ref[:, lanes]
         parts = []
         for key_ref, value_ref in ((k_ref, v_ref), (rk_ref, rv_ref)):
-            scores = lax.dot_general(
-                query,
-                key_ref[:, lanes],
-                (((1,), (1,)), ((), ())),
-                preferred_element_type=jnp.float32,
+            scores = jnp.dot(
+                query, key_ref[lanes, :], preferred_element_type=jnp.float32
             )
             parts.append((scores * HD ** (-0.5), value_ref))
         top = jnp.maximum(
@@ -178,22 +175,17 @@
         o_ref[:, lanes] = (summed / total).astype(o_ref.dtype)
 
 
-def attention(query, keys, values, ref_keys, ref_values, heads, tile):
+def attention(query, keys, values, ref_keys, ref_values, heads):
     tokens, channels = query.shape
     whole = lambda array: pl.BlockSpec(array.shape, lambda i: (0, 0))
+    operands = (query, keys, values, ref_keys, ref_values)
     return pl.pallas_call(
         functools.partial(attention_kernel, heads),
         out_shape=jax.ShapeDtypeStruct((tokens, channels), jnp.bfloat16),
-        grid=(tokens // tile,),
-        in_specs=[
-            pl.BlockSpec((tile, channels), lambda i: (i, 0)),
-            whole(keys),
-            whole(values),
-            whole(ref_keys),
-            whole(ref_values),
-        ],
-        out_specs=pl.BlockSpec((tile, channels), lambda i: (i, 0)),
-    )(query, keys, values, ref_keys, ref_values)
+        grid=(1,),
+        in_specs=[whole(array) for array in operands],
+        out_specs=pl.BlockSpec((tokens, channels), lambda i: (0, 0)),
+    )(*operands)
 
 
 def doubling_gather(value, axis):
@@ -239,14 +231,16 @@
     project = lambda rows, weight: jnp.dot(
         rows, weight, preferred_element_type=jnp.float32
     ).astype(jnp.bfloat16)
+    flipped = lambda rows, weight: jnp.einsum(
+        "tc,cd->dt", rows, weight, preferred_element_type=jnp.float32
+    ).astype(jnp.bfloat16)
     mixed = attention(
         query,
-        project(source, w_key),
+        flipped(source, w_key),
         project(source, w_value),
-        project(every_feature, w_key),
+        flipped(every_feature, w_key),
         project(every_feature, w_value),
         heads,
-        128,
     )
     attended = (jnp.dot(mixed, w_out, preferred_element_type=jnp.float32) + out_bias).astype(
         jnp.bfloat16

time: 92.6 us -> 85.1 us (0.919)
  Pallas kernels: 51 us -> 43.7 us
    pallas_call x1, Pallas kernels: 18.6 us -> 11.2 us  [attention(): pl.pallas_call(functools.partial(attention_kernel, heads), out_shape=jax....]
    dot_general x4 -> x2, matrix products: 11.1 us -> 6.25 us  [shards(): jnp.dot(rows, weight, preferred_element_type=jnp.float32)]
    dot_general x0 -> x2, matrix products: none -> 4.63 us  [shards(): jnp.einsum('tc,cd->dt', rows, weight, preferred_element_type=jnp.float32)]
  transfers between devices with their start and end apart: 5 -> 5, of which waited for: 2 -> 2; matrix products, arithmetic and copies ran while one was open for 8% -> 9% of each run, Pallas kernels for 35% -> 38%
where the time goes in v8:
time: 85.1 us; the launch traced here: 84.8 us
  Pallas kernels  43.7 us (51%)
  matrix products  18.4 us (22%)
  starting transfers between devices  11.3 us (13%)
  waiting for transfers between devices  8.85 us (10%)
  other arithmetic  1.46 us (2%)
    pallas_call x1, Pallas kernels, staged_gather(): pl.pallas_call(functools.partial(staged_kernel, sizes), out_shape=jax.Sha...  32.5 us
    pallas_call x1, Pallas kernels, attention(): pl.pallas_call(functools.partial(attention_kernel, heads), out_shape=jax....  11.2 us
    ppermute x3, waiting for transfers between devices, shards(): lax.ppermute(hidden, ROW_PARTS, [(j, (j + shift) % rows) for j in range(r...  8.85 us
    dot_general x2, matrix products, shards(): jnp.dot(rows, weight, preferred_element_type=jnp.float32)  6.25 us
    ppermute x3, starting transfers between devices, shards(): lax.ppermute(hidden, ROW_PARTS, [(j, (j + shift) % rows) for j in range(r...  4.8 us
    dot_general x2, matrix products, shards(): jnp.einsum('tc,cd->dt', rows, weight, preferred_element_type=jnp.float32)  4.63 us
    ppermute x1, starting transfers between devices, extended(): before = lax.ppermute(last, axis, up)  4.59 us
    dot_general x9, matrix products, shards(): jnp.dot(window, conv_weight[row_tap, col_tap], preferred_element_type=jnp...  4.13 us
  transfers between devices with their start and end apart: 5, of which 2 were waited for; matrix products, arithmetic and copies ran while one was open for 9% of the time, Pallas kernels for 38%

profile of v8, /device:TPU:1, one launch (start us, length us, event | category | flops | bytes accessed | tf_op | source)
XLA Modules:
  0.0 84.8 jit_solution(1267239146651922387)
XLA Ops:
  0.6 0.0 copy-start
  0.6 1.2 %multiply_convert_fusion = bf16[1,8,32,640]{3,2,1,0:T(8,128)(2,1)S(1)} fusion(bf16[1,8,32,640]{3,2,1,0:T(8,128)(2,1)} %param.9), kind=kLoop, calls=%fused_computation.43 | loop fusion | flops 983040 | bytes 655360 | tf_op jit(solution)/shard_map/convert_element_type | solution.py:206
  1.9 4.6 %collective-permute-start = (bf16[1,1,32,640]{3,2,1,0:T(8,128)(2,1)S(1)}, bf16[1,1,32,640]{3,2,1,0:T(8,128)(2,1)S(1)}, u32[]{:S(2)}, u32[]{:S(2)}) collective-permute-start(bf16[1,1,32,640]{3,2,1,0:T(8,128)(2,1)S(1)} %get-tuple-element.10), channel_id=1, source_target_pairs={{0,1},{1,2},{2,3},{4,5},{5,6},{6,7},{8,9},{9,10},{10,11},{12,13},{... | collective-permute-start | bytes 122888 | tf_op jit(solution)/shard_map/ppermute | solution.py:119
  6.5 1.9 %collective-permute-start.1 = (bf16[1,1,32,640]{3,2,1,0:T(8,128)(2,1)S(1)}, bf16[1,1,32,640]{3,2,1,0:T(8,128)(2,1)S(1)}, u32[]{:S(2)}, u32[]{:S(2)}) collective-permute-start(bf16[1,1,32,640]{3,2,1,0:T(8,128)(2,1)S(1)} %get-tuple-element.11), channel_id=1, source_target_pairs={{1,0},{2,1},{3,2},{5,4},{6,5},{7,6},{9,8},{10,9},{11,10},{13,12},{... | collective-permute-start | bytes 122888 | tf_op jit(solution)/shard_map/ppermute | solution.py:120
  8.4 32.5 %shard_map.104 = bf16[64,16,640]{2,1,0:T(8,128)(2,1)} custom-call(bf16[1,16,640]{2,1,0:T(8,128)(2,1)} %bitcast.76), custom_call_target="tpu_custom_call" | custom-call | tf_op jit(solution)/shard_map/pallas_call | solution.py:101
  40.9 0.0 copy-done
  40.9 0.0 copy-start.1
  41.0 3.9 %convolution_convert_fusion.rv_ref = bf16[1024,640]{1,0:T(8,128)(2,1)} fusion(bf16[1024,640]{1,0:T(8,128)(2,1)} %bitcast.68, bf16[640,640]{1,0:T(8,128)(2,1)S(1)} %copy-done), kind=kOutput, calls=%fused_computation | convolution fusion | flops 839516160 | bytes 3440640 | tf_op jit(solution)/shard_map/dot_general | solution.py:231
  44.8 0.0 collective-permute-done
  44.8 0.0 collective-permute-done.1
  44.8 0.2 fusion.31
  45.0 0.2 fusion.34
  45.2 0.0 copy-done.1
  45.2 0.5 fusion.16
  45.7 0.5 fusion.7
  46.1 0.1 pad_maximum_fusion.1
  46.2 0.5 convolution_add_fusion.7
  46.7 0.5 convolution_add_fusion.6
  47.1 0.5 convolution_add_fusion.5
  47.6 0.5 convolution_add_fusion.4
  48.1 0.0 copy-start.2
  48.1 0.0 copy-start.6
  48.1 0.5 convolution_add_fusion.3
  48.5 0.0 copy-start.4
  48.6 0.0 copy-start.7
  48.6 0.5 convolution_add_fusion.2
  49.0 0.0 copy-done.2
  49.0 0.0 copy-done.6
  49.1 0.5 fusion.5
  49.5 0.0 copy-start.3
  49.5 0.0 copy-start.5
  49.6 0.2 collective-permute-start.4
  49.8 2.7 %collective-permute-start.3 = (bf16[256,640]{1,0:T(8,128)(2,1)S(1)}, bf16[256,640]{1,0:T(8,128)(2,1)S(1)}, u32[]{:S(2)}, u32[]{:S(2)}) collective-permute-start(bf16[256,640]{1,0:T(8,128)(2,1)S(1)} %fusion.5), channel_id=1, source_target_pairs={{0,2},{1,3},{2,0},{3,1},{4,6},{5,7},{6,4},{7,5},{8,10},{9,11},{10,... | collective-permute-start | bytes 983048 | tf_op jit(solution)/shard_map/ppermute | solution.py:224
  52.5 1.9 %collective-permute-start.2 = (bf16[256,640]{1,0:T(8,128)(2,1)S(1)}, bf16[256,640]{1,0:T(8,128)(2,1)S(1)}, u32[]{:S(2)}, u32[]{:S(2)}) collective-permute-start(bf16[256,640]{1,0:T(8,128)(2,1)S(1)} %fusion.5), channel_id=1, source_target_pairs={{0,1},{1,2},{2,3},{3,0},{4,5},{5,6},{6,7},{7,4},{8,9},{9,10},{10,1... | collective-permute-start | bytes 983048 | tf_op jit(solution)/shard_map/ppermute | solution.py:224
  54.4 0.0 copy-done.4
  54.4 0.0 copy-done.7
  54.4 2.3 %convolution_convert_fusion.1.rk_ref = bf16[640,1024]{1,0:T(8,128)(2,1)} fusion(bf16[640,640]{1,0:T(8,128)(2,1)S(1)} %copy-done.7, bf16[1024,640]{1,0:T(8,128)(2,1)S(1)} %bitcast.69), kind=kOutput, calls=%fused_computation.1 | convolution fusion | flops 839516160 | bytes 3440640 | tf_op jit(solution)/shard_map/tc,cd->dt/dot_general | solution.py:234
  56.7 0.0 copy-done.5
  56.7 1.2 %convolution_convert_fusion.4.q_ref = bf16[256,640]{1,0:T(8,128)(2,1)} fusion(bf16[256,640]{1,0:T(8,128)(2,1)S(1)} %fusion.5, bf16[640,640]{1,0:T(8,128)(2,1)S(1)} %copy-done.5), kind=kOutput, calls=%fused_computation.21 | convolution fusion | flops 209879040 | bytes 1474560 | tf_op jit(solution)/shard_map/dot_general | solution.py:229
  57.8 3.1 %collective-permute-done.4 = bf16[256,640]{1,0:T(8,128)(2,1)S(1)} collective-permute-done((bf16[256,640]{1,0:T(8,128)(2,1)S(1)}, bf16[256,640]{1,0:T(8,128)(2,1)S(1)}, u32[]{:S(2)}, u32[]{:S(2)}) %collective-permute-start.4) | collective-permute-done | bytes 327712 | tf_op jit(solution)/shard_map/ppermute | solution.py:224
  60.9 0.0 collective-permute-done.3
  60.9 5.8 %collective-permute-done.2 = bf16[256,640]{1,0:T(8,128)(2,1)S(1)} collective-permute-done((bf16[256,640]{1,0:T(8,128)(2,1)S(1)}, bf16[256,640]{1,0:T(8,128)(2,1)S(1)}, u32[]{:S(2)}, u32[]{:S(2)}) %collective-permute-start.2) | collective-permute-done | bytes 327712 | tf_op jit(solution)/shard_map/ppermute | solution.py:224
  66.7 2.4 %convolution_convert_fusion.2.v_ref = bf16[1024,640]{1,0:T(8,128)(2,1)} fusion(bf16[640,640]{1,0:T(8,128)(2,1)S(1)} %copy-done, bf16[256,640]{1,0:T(8,128)(2,1)S(1)} %collective-permute-done.4, bf16[256,640]{1,0:T(8,128)(2,1)S(1)} %collective-permute-done.3, bf16[256,640]{1,0:T(8,128)(2,1)S(1)} %collective-permute-done.2, bf16[256,640]{1,0:T(8,128)(2,1)S(1)} %fusion.5), kind=kOutput, calls=%fused_computation.2 | convolution fusion | flops 844759040 | bytes 3440640 | tf_op jit(solution)/shard_map/dot_general | solution.py:231
  69.1 0.0 copy-done.3
  69.1 2.3 %fusion.k_ref = bf16[640,1024]{1,0:T(8,128)(2,1)} fusion(bf16[640,640]{1,0:T(8,128)(2,1)S(1)} %copy-done.7, bf16[256,640]{1,0:T(8,128)(2,1)S(1)} %collective-permute-done.4, bf16[256,640]{1,0:T(8,128)(2,1)S(1)} %collective-permute-done.3, bf16[256,640]{1,0:T(8,128)(2,1)S(1)} %collective-permute-done.2, bf16[256,640]{1,0:T(8,128)(2,1)S(1)} %fusion.5), kind=kOutput, calls=%fused_computation.6 | convolution fusion | flops 844759040 | bytes 3440640 | tf_op jit(solution)/shard_map/tc,cd->dt/dot_general | solution.py:234
  71.4 11.2 %shard_map.105 = bf16[256,640]{1,0:T(8,128)(2,1)} custom-call(bf16[256,640]{1,0:T(8,128)(2,1)} %convolution_convert_fusion.4.q_ref, bf16[640,1024]{1,0:T(8,128)(2,1)} %fusion.k_ref, bf16[1024,640]{1,0:T(8,128)(2,1)} %convolution_convert_fusion.2.v_ref, bf16[640,1024]{1,0:T(8,128)(2,1)} %convolution_convert_fusion.1.rk_ref, ...), custom_call_target="tpu_custom_call" | custom-call | tf_op jit(solution)/shard_map/pallas_call | solution.py:182
  82.6 0.0 copy-done.8
  82.6 2.2 %fusion.4 = bf16[256,640]{1,0:T(8,128)(2,1)} fusion(bf16[256,640]{1,0:T(8,128)(2,1)} %shard_map.105, bf16[640,640]{1,0:T(8,128)(2,1)S(1)} %copy-done.8, f32[640]{0:T(1024)S(1)} %copy-done.9), kind=kOutput, calls=%fused_computation.19 | convolution fusion | flops 210042880 | bytes 1477120 | tf_op jit(solution)/shard_map/dot_general | solution.py:245
  (4 shorter events, 0.0 us)
Async XLA Ops:
  0.6 40.3 %copy-start = (bf16[640,640]{1,0:T(8,128)(2,1)S(1)}, bf16[640,640]{1,0:T(8,128)(2,1)}, u32[]{:S(2)}) copy-start(bf16[640,640]{1,0:T(8,128)(2,1)} %param.15) | copy-start | bytes 2457604
  1.9 42.9 %collective-permute-start = (bf16[1,1,32,640]{3,2,1,0:T(8,128)(2,1)S(1)}, bf16[1,1,32,640]{3,2,1,0:T(8,128)(2,1)S(1)}, u32[]{:S(2)}, u32[]{:S(2)}) collective-permute-start(bf16[1,1,32,640]{3,2,1,0:T(8,128)(2,1)S(1)} %get-tuple-element.10), channel_id=1, source_target_pairs={{0,1},{1,2},{2,3},{4,5},{5,6},{6,7},{8,9},{9,10},{10,11},{12,13},{... | collective-permute-start | bytes 122888 | tf_op jit(solution)/shard_map/ppermute | solution.py:119
  6.5 38.3 %collective-permute-start.1 = (bf16[1,1,32,640]{3,2,1,0:T(8,128)(2,1)S(1)}, bf16[1,1,32,640]{3,2,1,0:T(8,128)(2,1)S(1)}, u32[]{:S(2)}, u32[]{:S(2)}) collective-permute-start(bf16[1,1,32,640]{3,2,1,0:T(8,128)(2,1)S(1)} %get-tuple-element.11), channel_id=1, source_target_pairs={{1,0},{2,1},{3,2},{5,4},{6,5},{7,6},{9,8},{10,9},{11,10},{13,12},{... | collective-permute-start | bytes 122888 | tf_op jit(solution)/shard_map/ppermute | solution.py:120
  40.9 4.3 %copy-start.1 = (bf16[3,3,640,640]{3,2,1,0:T(8,128)(2,1)S(1)}, bf16[3,3,640,640]{3,2,1,0:T(8,128)(2,1)}, u32[]{:S(2)}) copy-start(bf16[3,3,640,640]{3,2,1,0:T(8,128)(2,1)} %param.10) | copy-start | bytes 22118404
  48.1 1.0 %copy-start.2 = (bf16[1,8,32,640]{3,2,1,0:T(8,128)(2,1)S(1)}, bf16[1,8,32,640]{3,2,1,0:T(8,128)(2,1)}, u32[]{:S(2)}) copy-start(bf16[1,8,32,640]{3,2,1,0:T(8,128)(2,1)} %param.9) | copy-start | bytes 983044
  48.1 1.0 %copy-start.6 = (f32[640]{0:T(1024)S(1)}, f32[640]{0:T(1024)}, u32[]{:S(2)}) copy-start(f32[640]{0:T(1024)} %param.11) | copy-start | bytes 7684
  48.5 5.8 %copy-start.4 = (bf16[64,16,640]{2,1,0:T(8,128)(2,1)S(1)}, bf16[64,16,640]{2,1,0:T(8,128)(2,1)}, u32[]{:S(2)}) copy-start(bf16[64,16,640]{2,1,0:T(8,128)(2,1)} %shard_map.104) | copy-start | bytes 3932164
  48.6 5.8 %copy-start.7 = (bf16[640,640]{1,0:T(8,128)(2,1)S(1)}, bf16[640,640]{1,0:T(8,128)(2,1)}, u32[]{:S(2)}) copy-start(bf16[640,640]{1,0:T(8,128)(2,1)} %param.14) | copy-start | bytes 2457604
  49.5 19.6 %copy-start.3 = (bf16[256,640]{1,0:T(8,128)(2,1)}, bf16[256,640]{1,0:T(8,128)(2,1)S(1)}, u32[]{:S(2)}) copy-start(bf16[256,640]{1,0:T(8,128)(2,1)S(1)} %fusion.5) | copy-start | bytes 983044
  49.5 7.1 %copy-start.5 = (bf16[640,640]{1,0:T(8,128)(2,1)S(1)}, bf16[640,640]{1,0:T(8,128)(2,1)}, u32[]{:S(2)}) copy-start(bf16[640,640]{1,0:T(8,128)(2,1)} %param.13) | copy-start | bytes 2457604
  49.6 11.4 %collective-permute-start.4 = (bf16[256,640]{1,0:T(8,128)(2,1)S(1)}, bf16[256,640]{1,0:T(8,128)(2,1)S(1)}, u32[]{:S(2)}, u32[]{:S(2)}) collective-permute-start(bf16[256,640]{1,0:T(8,128)(2,1)S(1)} %fusion.5), channel_id=1, source_target_pairs={{0,3},{1,0},{2,1},{3,2},{4,7},{5,4},{6,5},{7,6},{8,11},{9,8},{10,9... | collective-permute-start | bytes 983048 | tf_op jit(solution)/shard_map/ppermute | solution.py:224
  49.8 11.1 %collective-permute-start.3 = (bf16[256,640]{1,0:T(8,128)(2,1)S(1)}, bf16[256,640]{1,0:T(8,128)(2,1)S(1)}, u32[]{:S(2)}, u32[]{:S(2)}) collective-permute-start(bf16[256,640]{1,0:T(8,128)(2,1)S(1)} %fusion.5), channel_id=1, source_target_pairs={{0,2},{1,3},{2,0},{3,1},{4,6},{5,7},{6,4},{7,5},{8,10},{9,11},{10,... | collective-permute-start | bytes 983048 | tf_op jit(solution)/shard_map/ppermute | solution.py:224
  52.5 14.2 %collective-permute-start.2 = (bf16[256,640]{1,0:T(8,128)(2,1)S(1)}, bf16[256,640]{1,0:T(8,128)(2,1)S(1)}, u32[]{:S(2)}, u32[]{:S(2)}) collective-permute-start(bf16[256,640]{1,0:T(8,128)(2,1)S(1)} %fusion.5), channel_id=1, source_target_pairs={{0,1},{1,2},{2,3},{3,0},{4,5},{5,6},{6,7},{7,4},{8,9},{9,10},{10,1... | collective-permute-start | bytes 983048 | tf_op jit(solution)/shard_map/ppermute | solution.py:224
  71.4 11.2 %copy-start.8 = (bf16[640,640]{1,0:T(8,128)(2,1)S(1)}, bf16[640,640]{1,0:T(8,128)(2,1)}, u32[]{:S(2)}) copy-start(bf16[640,640]{1,0:T(8,128)(2,1)} %param.16) | copy-start | bytes 2457604
  71.4 11.2 %copy-start.9 = (f32[640]{0:T(1024)S(1)}, f32[640]{0:T(1024)}, u32[]{:S(2)}) copy-start(f32[640]{0:T(1024)} %param.17) | copy-start | bytes 7684

commit v9 on v8

--- a/solution.py
+++ b/solution.py
@@ -37,7 +37,7 @@
     return Mesh(devices.reshape(shape), TM_PARTS + ROW_PARTS)
 
 
-def staged_kernel(sizes, x_ref, out_ref, local_sem, *sems):
+def staged_kernel(sizes, x_ref, after_ref, out_ref, local_sem, *sems):
     high, across, along = sizes
     half = along // 2
     yh, xx, zz = [lax.axis_index(axis) for axis in TM_PARTS]
@@ -92,7 +92,7 @@
     exchange([(chunk, c_peer) for chunk in groups], sems[6], sems[7])
 
 
-def staged_gather(value):
+def staged_gather(value, after):
     sizes = [lax.axis_size(axis) for axis in TM_PARTS]
     total = sizes[0] * sizes[1] * sizes[2]
     sems = []
@@ -101,11 +101,11 @@
     gathered = pl.pallas_call(
         functools.partial(staged_kernel, sizes),
         out_shape=jax.ShapeDtypeStruct((total,) + value.shape, value.dtype),
-        in_specs=[pl.BlockSpec(memory_space=pl.ANY)],
+        in_specs=[pl.BlockSpec(memory_space=pl.ANY)] * 2,
         out_specs=pl.BlockSpec(memory_space=pl.ANY),
         scratch_shapes=[pltpu.SemaphoreType.DMA] + sems,
         compiler_params=pltpu.CompilerParams(collective_id=0, has_side_effects=True),
-    )(value[None])
+    )(value[None], after)
     return gathered.reshape((total * value.shape[0],) + value.shape[1:])
 
 
@@ -202,7 +202,6 @@
     count, band_rows, width, channels = frames.shape
     heads = channels // HD
     band = band_rows * width
-    every_feature = staged_gather(ref_features)
     activated = jax.nn.silu(frames.astype(jnp.float32)).astype(jnp.bfloat16)
     padded = extended(activated, ROW_PARTS, 1, 1)
     padded = jnp.pad(padded, ((0, 0), (0, 0), (1, 1), (0, 0)))
@@ -226,6 +225,7 @@
         ],
         axis=0,
     )
+    every_feature = staged_gather(ref_features, hidden)
     query = jnp.dot(hidden, w_query, preferred_element_type=jnp.float32).astype(jnp.bfloat16)
     source = jnp.concatenate([hidden, others], axis=0)
     project = lambda rows, weight: jnp.dot(

time: 85.1 us -> 82.4 us (0.968)
  waiting for transfers between devices: 8.85 us -> 3.39 us
  matrix products: 18.4 us -> 23.1 us
  starting transfers between devices: 11.3 us -> 7.29 us
  Pallas kernels: 43.7 us -> 45.6 us
    ppermute x3, waiting for transfers between devices: 8.85 us -> 0.01 us  [shards(): lax.ppermute(hidden, ROW_PARTS, [(j, (j + shift) % rows) for j in range(r...]
    ppermute x3, starting transfers between devices: 4.8 us -> 0.51 us  [shards(): lax.ppermute(hidden, ROW_PARTS, [(j, (j + shift) % rows) for j in range(r...]
    ppermute x1, waiting for transfers between devices: 0.01 us -> 3.38 us  [extended(): after = lax.ppermute(initial, axis, down)]
    pallas_call x1, Pallas kernels: 32.5 us -> 34.4 us  [staged_gather(): pl.pallas_call(functools.partial(staged_kernel, sizes), out_shape=jax.Sha...]
    dot_general x9, matrix products: 4.13 us -> 6.01 us  [shards(): jnp.dot(window, conv_weight[row_tap, col_tap], preferred_element_type=jnp...]
    dot_general x1, matrix products: 1.18 us -> 2.16 us  [shards(): jnp.dot(hidden, w_query, preferred_element_type=jnp.float32)]
    dot_general x2, matrix products: 4.63 us -> 5.6 us  [shards(): jnp.einsum('tc,cd->dt', rows, weight, preferred_element_type=jnp.float32)]
    dot_general x2, matrix products: 6.25 us -> 7.2 us  [shards(): jnp.dot(rows, weight, preferred_element_type=jnp.float32)]
  transfers between devices with their start and end apart: 5 -> 5, of which waited for: 2 -> 1; matrix products, arithmetic and copies ran while one was open for 9% -> 10% of each run, Pallas kernels for 38% -> 42%
where the time goes in v9:
time: 82.4 us; the launch traced here: 82 us
  Pallas kernels  45.6 us (55%)
  matrix products  23.1 us (28%)
  starting transfers between devices  7.29 us (9%)
  waiting for transfers between devices  3.39 us (4%)
  other arithmetic  1.54 us (2%)
  between operations  0.83 us (1%)
    pallas_call x1, Pallas kernels, staged_gather(): pl.pallas_call(functools.partial(staged_kernel, sizes), out_shape=jax.Sha...  34.4 us
    pallas_call x1, Pallas kernels, attention(): pl.pallas_call(functools.partial(attention_kernel, heads), out_shape=jax....  11.2 us
    dot_general x2, matrix products, shards(): jnp.dot(rows, weight, preferred_element_type=jnp.float32)  7.2 us
    dot_general x9, matrix products, shards(): jnp.dot(window, conv_weight[row_tap, col_tap], preferred_element_type=jnp...  6.01 us
    dot_general x2, matrix products, shards(): jnp.einsum('tc,cd->dt', rows, weight, preferred_element_type=jnp.float32)  5.6 us
    ppermute x1, starting transfers between devices, extended(): before = lax.ppermute(last, axis, up)  4.86 us
    ppermute x1, waiting for transfers between devices, extended(): after = lax.ppermute(initial, axis, down)  3.38 us
    dot_general x1, matrix products, shards(): jnp.dot(mixed, w_out, preferred_element_type=jnp.float32) + out_bias  2.16 us
  transfers between devices with their start and end apart: 5, of which 1 were waited for; matrix products, arithmetic and copies ran while one was open for 10% of the time, Pallas kernels for 42%

profile of v9, /device:TPU:1, one launch (start us, length us, event | category | flops | bytes accessed | tf_op | source)
XLA Modules:
  0.0 82.0 jit_solution(15596958165171057401)
XLA Ops:
  0.6 0.0 copy-start
  0.6 0.0 copy-start.1
  0.7 1.3 %multiply_convert_fusion = bf16[1,8,32,640]{3,2,1,0:T(8,128)(2,1)S(1)} fusion(bf16[1,8,32,640]{3,2,1,0:T(8,128)(2,1)} %param.9), kind=kLoop, calls=%fused_computation.44 | loop fusion | flops 983040 | bytes 655360 | tf_op jit(solution)/shard_map/convert_element_type | solution.py:205
  2.0 4.9 %collective-permute-start = (bf16[1,1,32,640]{3,2,1,0:T(8,128)(2,1)S(1)}, bf16[1,1,32,640]{3,2,1,0:T(8,128)(2,1)S(1)}, u32[]{:S(2)}, u32[]{:S(2)}) collective-permute-start(bf16[1,1,32,640]{3,2,1,0:T(8,128)(2,1)S(1)} %get-tuple-element.10), channel_id=1, source_target_pairs={{0,1},{1,2},{2,3},{4,5},{5,6},{6,7},{8,9},{9,10},{10,11},{12,13},{... | collective-permute-start | bytes 122888 | tf_op jit(solution)/shard_map/ppermute | solution.py:119
  6.9 1.9 %collective-permute-start.1 = (bf16[1,1,32,640]{3,2,1,0:T(8,128)(2,1)S(1)}, bf16[1,1,32,640]{3,2,1,0:T(8,128)(2,1)S(1)}, u32[]{:S(2)}, u32[]{:S(2)}) collective-permute-start(bf16[1,1,32,640]{3,2,1,0:T(8,128)(2,1)S(1)} %get-tuple-element.11), channel_id=1, source_target_pairs={{1,0},{2,1},{3,2},{5,4},{6,5},{7,6},{9,8},{10,9},{11,10},{13,12},{... | collective-permute-start | bytes 122888 | tf_op jit(solution)/shard_map/ppermute | solution.py:120
  8.8 0.0 collective-permute-done
  8.8 3.4 %collective-permute-done.1 = bf16[1,1,32,640]{3,2,1,0:T(8,128)(2,1)S(1)} collective-permute-done((bf16[1,1,32,640]{3,2,1,0:T(8,128)(2,1)S(1)}, bf16[1,1,32,640]{3,2,1,0:T(8,128)(2,1)S(1)}, u32[]{:S(2)}, u32[]{:S(2)}) %collective-permute-start.1) | collective-permute-done | bytes 40992 | tf_op jit(solution)/shard_map/ppermute | solution.py:120
  12.2 0.2 fusion.32
  12.4 0.2 fusion.35
  12.6 1.6 %fusion.17 = f32[256,640]{1,0:T(8,128)S(1)} fusion(bf16[256,640]{1,0:T(8,128)(2,1)S(1)} %bitcast.76, bf16[3,3,640,640]{3,2,1,0:T(8,128)(2,1)} %param.10), kind=kOutput, calls=%fused_computation.33 | convolution fusion | flops 209715200 | bytes 1802240 | tf_op jit(solution)/shard_map/dot_general | solution.py:214
  14.2 0.0 copy-done.1
  14.2 0.5 fusion.8
  14.6 0.1 pad_maximum_fusion.1
  14.7 0.5 convolution_add_fusion.7
  15.2 0.5 convolution_add_fusion.6
  15.6 0.5 convolution_add_fusion.5
  16.1 0.5 convolution_add_fusion.4
  16.6 0.0 copy-start.2
  16.6 0.0 copy-start.5
  16.6 0.5 convolution_add_fusion.3
  17.1 0.5 convolution_add_fusion.2
  17.5 0.0 copy-done.2
  17.5 0.0 copy-done.5
  17.6 1.2 %fusion.6.after_ref = bf16[256,640]{1,0:T(8,128)(2,1)} fusion(f32[256,640]{1,0:T(8,128)S(1)} %fusion.8, f32[256,640]{1,0:T(8,128)S(1)} %convolution_add_fusion.2, bf16[256,640]{1,0:T(8,128)(2,1)S(1)} %bitcast.67, bf16[3,3,640,640]{3,2,1,0:T(8,128)(2,1)S(1)} %copy-done.1, f32[640]{0:T(1024)S(1)} %copy-done.5, bf16[256,640]{1,0:T(8,128)(2,1)S(1)} %bitcast.66), kind=kOutput, calls=%fused_computation.21 | convolution fusion | flops 210698240 | bytes 3117056 | tf_op jit(solution)/shard_map/dot_general | solution.py:214
  18.7 0.0 collective-permute-start.2
  18.8 0.0 collective-permute-start.3
  18.8 0.5 collective-permute-start.4
  19.3 34.4 %shard_map.104 = bf16[64,16,640]{2,1,0:T(8,128)(2,1)} custom-call(bf16[1,16,640]{2,1,0:T(8,128)(2,1)} %bitcast.77, bf16[256,640]{1,0:T(8,128)(2,1)} %fusion.6.after_ref), custom_call_target="tpu_custom_call" | custom-call | tf_op jit(solution)/shard_map/pallas_call | solution.py:101
  53.7 0.0 copy-start.4
  53.7 0.0 copy-done
  53.7 0.0 copy-start.3
  53.7 0.0 copy-start.6
  53.7 3.8 %convolution_convert_fusion.rv_ref = bf16[1024,640]{1,0:T(8,128)(2,1)} fusion(bf16[1024,640]{1,0:T(8,128)(2,1)} %bitcast.69, bf16[640,640]{1,0:T(8,128)(2,1)S(1)} %copy-done), kind=kOutput, calls=%fused_computation | convolution fusion | flops 839516160 | bytes 3440640 | tf_op jit(solution)/shard_map/dot_general | solution.py:231
  57.6 0.0 copy-done.4
  57.6 2.2 %convolution_convert_fusion.4.q_ref = bf16[256,640]{1,0:T(8,128)(2,1)} fusion(bf16[256,640]{1,0:T(8,128)(2,1)} %fusion.6.after_ref, bf16[640,640]{1,0:T(8,128)(2,1)S(1)} %copy-done.4), kind=kOutput, calls=%fused_computation.22 | convolution fusion | flops 209879040 | bytes 1474560 | tf_op jit(solution)/shard_map/dot_general | solution.py:229
  59.7 0.0 copy-done.3
  59.7 0.0 copy-done.6
  59.7 2.3 %fusion.1.rk_ref = bf16[640,1024]{1,0:T(8,128)(2,1)} fusion(bf16[1024,640]{1,0:T(8,128)(2,1)S(1)} %bitcast.70, bf16[640,640]{1,0:T(8,128)(2,1)S(1)} %copy-done.6), kind=kOutput, calls=%fused_computation.7 | convolution fusion | flops 839516160 | bytes 3440640 | tf_op jit(solution)/shard_map/tc,cd->dt/dot_general | solution.py:234
  62.0 0.0 collective-permute-done.2
  62.0 0.0 collective-permute-done.3
  62.0 0.0 collective-permute-done.4
  62.0 3.4 %convolution_convert_fusion.2.v_ref = bf16[1024,640]{1,0:T(8,128)(2,1)} fusion(bf16[640,640]{1,0:T(8,128)(2,1)S(1)} %copy-done, bf16[256,640]{1,0:T(8,128)(2,1)S(1)} %collective-permute-done.4, bf16[256,640]{1,0:T(8,128)(2,1)S(1)} %collective-permute-done.3, bf16[256,640]{1,0:T(8,128)(2,1)S(1)} %collective-permute-done.2, bf16[256,640]{1,0:T(8,128)(2,1)} %fusion.6.after_ref), kind=kOutput, calls=%fused_computation.2 | convolution fusion | flops 844759040 | bytes 3440640 | tf_op jit(solution)/shard_map/dot_general | solution.py:231
  65.4 3.3 %fusion.k_ref = bf16[640,1024]{1,0:T(8,128)(2,1)} fusion(bf16[640,640]{1,0:T(8,128)(2,1)S(1)} %copy-done.6, bf16[256,640]{1,0:T(8,128)(2,1)S(1)} %collective-permute-done.4, bf16[256,640]{1,0:T(8,128)(2,1)S(1)} %collective-permute-done.3, bf16[256,640]{1,0:T(8,128)(2,1)S(1)} %collective-permute-done.2, bf16[256,640]{1,0:T(8,128)(2,1)} %fusion.6.after_ref), kind=kOutput, calls=%fused_computation.6 | convolution fusion | flops 844759040 | bytes 3440640 | tf_op jit(solution)/shard_map/tc,cd->dt/dot_general | solution.py:234
  68.7 0.0 copy-start.7
  68.7 11.2 %shard_map.105 = bf16[256,640]{1,0:T(8,128)(2,1)} custom-call(bf16[256,640]{1,0:T(8,128)(2,1)} %convolution_convert_fusion.4.q_ref, bf16[640,1024]{1,0:T(8,128)(2,1)} %fusion.k_ref, bf16[1024,640]{1,0:T(8,128)(2,1)} %convolution_convert_fusion.2.v_ref, bf16[640,1024]{1,0:T(8,128)(2,1)} %fusion.1.rk_ref, bf16[1024,640]{1,0:T(8,128)(2,1)} %convolution_convert_fusion.rv_ref), custom_call_target="tpu_custom_call" | custom-call | tf_op jit(solution)/shard_map/pallas_call | solution.py:182
  79.9 0.0 copy-done.7
  79.9 0.0 copy-done.8
  79.9 2.2 %fusion.5 = bf16[256,640]{1,0:T(8,128)(2,1)} fusion(bf16[256,640]{1,0:T(8,128)(2,1)} %shard_map.105, bf16[640,640]{1,0:T(8,128)(2,1)S(1)} %copy-done.7, f32[640]{0:T(1024)S(1)} %copy-done.8), kind=kOutput, calls=%fused_computation.20 | convolution fusion | flops 210042880 | bytes 1477120 | tf_op jit(solution)/shard_map/dot_general | solution.py:245
  (2 shorter events, 0.0 us)
Async XLA Ops:
  0.6 53.0 %copy-start = (bf16[640,640]{1,0:T(8,128)(2,1)S(1)}, bf16[640,640]{1,0:T(8,128)(2,1)}, u32[]{:S(2)}) copy-start(bf16[640,640]{1,0:T(8,128)(2,1)} %param.15) | copy-start | bytes 2457604
  0.6 13.5 %copy-start.1 = (bf16[3,3,640,640]{3,2,1,0:T(8,128)(2,1)S(1)}, bf16[3,3,640,640]{3,2,1,0:T(8,128)(2,1)}, u32[]{:S(2)}) copy-start(bf16[3,3,640,640]{3,2,1,0:T(8,128)(2,1)} %param.10) | copy-start | bytes 22118404
  2.0 6.8 %collective-permute-start = (bf16[1,1,32,640]{3,2,1,0:T(8,128)(2,1)S(1)}, bf16[1,1,32,640]{3,2,1,0:T(8,128)(2,1)S(1)}, u32[]{:S(2)}, u32[]{:S(2)}) collective-permute-start(bf16[1,1,32,640]{3,2,1,0:T(8,128)(2,1)S(1)} %get-tuple-element.10), channel_id=1, source_target_pairs={{0,1},{1,2},{2,3},{4,5},{5,6},{6,7},{8,9},{9,10},{10,11},{12,13},{... | collective-permute-start | bytes 122888 | tf_op jit(solution)/shard_map/ppermute | solution.py:119
  6.9 5.3 %collective-permute-start.1 = (bf16[1,1,32,640]{3,2,1,0:T(8,128)(2,1)S(1)}, bf16[1,1,32,640]{3,2,1,0:T(8,128)(2,1)S(1)}, u32[]{:S(2)}, u32[]{:S(2)}) collective-permute-start(bf16[1,1,32,640]{3,2,1,0:T(8,128)(2,1)S(1)} %get-tuple-element.11), channel_id=1, source_target_pairs={{1,0},{2,1},{3,2},{5,4},{6,5},{7,6},{9,8},{10,9},{11,10},{13,12},{... | collective-permute-start | bytes 122888 | tf_op jit(solution)/shard_map/ppermute | solution.py:120
  16.6 1.0 %copy-start.2 = (bf16[1,8,32,640]{3,2,1,0:T(8,128)(2,1)S(1)}, bf16[1,8,32,640]{3,2,1,0:T(8,128)(2,1)}, u32[]{:S(2)}) copy-start(bf16[1,8,32,640]{3,2,1,0:T(8,128)(2,1)} %param.9) | copy-start | bytes 983044
  16.6 1.0 %copy-start.5 = (f32[640]{0:T(1024)S(1)}, f32[640]{0:T(1024)}, u32[]{:S(2)}) copy-start(f32[640]{0:T(1024)} %param.11) | copy-start | bytes 7684
  18.7 43.3 %collective-permute-start.2 = (bf16[256,640]{1,0:T(8,128)(2,1)}, bf16[256,640]{1,0:T(8,128)(2,1)S(1)}, u32[]{:S(2)}, u32[]{:S(2)}) collective-permute-start(bf16[256,640]{1,0:T(8,128)(2,1)} %fusion.6.after_ref), channel_id=1, source_target_pairs={{0,1},{1,2},{2,3},{3,0},{4,5},{5,6},{6,7},{7,4},{8,9},{9,10},{10,1... | collective-permute-start | bytes 983048 | tf_op jit(solution)/shard_map/ppermute | solution.py:223
  18.8 43.3 %collective-permute-start.3 = (bf16[256,640]{1,0:T(8,128)(2,1)}, bf16[256,640]{1,0:T(8,128)(2,1)S(1)}, u32[]{:S(2)}, u32[]{:S(2)}) collective-permute-start(bf16[256,640]{1,0:T(8,128)(2,1)} %fusion.6.after_ref), channel_id=1, source_target_pairs={{0,2},{1,3},{2,0},{3,1},{4,6},{5,7},{6,4},{7,5},{8,10},{9,11},{10,... | collective-permute-start | bytes 983048 | tf_op jit(solution)/shard_map/ppermute | solution.py:223
  18.8 43.3 %collective-permute-start.4 = (bf16[256,640]{1,0:T(8,128)(2,1)}, bf16[256,640]{1,0:T(8,128)(2,1)S(1)}, u32[]{:S(2)}, u32[]{:S(2)}) collective-permute-start(bf16[256,640]{1,0:T(8,128)(2,1)} %fusion.6.after_ref), channel_id=1, source_target_pairs={{0,3},{1,0},{2,1},{3,2},{4,7},{5,4},{6,5},{7,6},{8,11},{9,8},{10,9... | collective-permute-start | bytes 983048 | tf_op jit(solution)/shard_map/ppermute | solution.py:223
  53.7 3.9 %copy-start.4 = (bf16[640,640]{1,0:T(8,128)(2,1)S(1)}, bf16[640,640]{1,0:T(8,128)(2,1)}, u32[]{:S(2)}) copy-start(bf16[640,640]{1,0:T(8,128)(2,1)} %param.13) | copy-start | bytes 2457604
  53.7 6.0 %copy-start.3 = (bf16[64,16,640]{2,1,0:T(8,128)(2,1)S(1)}, bf16[64,16,640]{2,1,0:T(8,128)(2,1)}, u32[]{:S(2)}) copy-start(bf16[64,16,640]{2,1,0:T(8,128)(2,1)} %shard_map.104) | copy-start | bytes 3932164
  53.7 6.0 %copy-start.6 = (bf16[640,640]{1,0:T(8,128)(2,1)S(1)}, bf16[640,640]{1,0:T(8,128)(2,1)}, u32[]{:S(2)}) copy-start(bf16[640,640]{1,0:T(8,128)(2,1)} %param.14) | copy-start | bytes 2457604
  68.7 11.2 %copy-start.7 = (bf16[640,640]{1,0:T(8,128)(2,1)S(1)}, bf16[640,640]{1,0:T(8,128)(2,1)}, u32[]{:S(2)}) copy-start(bf16[640,640]{1,0:T(8,128)(2,1)} %param.16) | copy-start | bytes 2457604
  68.7 11.2 %copy-start.8 = (f32[640]{0:T(1024)S(1)}, f32[640]{0:T(1024)}, u32[]{:S(2)}) copy-start(f32[640]{0:T(1024)} %param.17) | copy-start | bytes 7684

commit v10 on v5

--- a/solution.py
+++ b/solution.py
@@ -37,7 +37,7 @@
     return Mesh(devices.reshape(shape), TM_PARTS + ROW_PARTS)
 
 
-def staged_kernel(sizes, x_ref, out_ref, local_sem, *sems):
+def staged_kernel(sizes, x_ref, after_ref, out_ref, local_sem, *sems):
     high, across, along = sizes
     half = along // 2
     yh, xx, zz = [lax.axis_index(axis) for axis in TM_PARTS]
@@ -92,7 +92,7 @@
     exchange([(chunk, c_peer) for chunk in groups], sems[6], sems[7])
 
 
-def staged_gather(value):
+def staged_gather(value, after):
     sizes = [lax.axis_size(axis) for axis in TM_PARTS]
     total = sizes[0] * sizes[1] * sizes[2]
     sems = []
@@ -101,11 +101,11 @@
     gathered = pl.pallas_call(
         functools.partial(staged_kernel, sizes),
         out_shape=jax.ShapeDtypeStruct((total,) + value.shape, value.dtype),
-        in_specs=[pl.BlockSpec(memory_space=pl.ANY)],
+        in_specs=[pl.BlockSpec(memory_space=pl.ANY)] * 2,
         out_specs=pl.BlockSpec(memory_space=pl.ANY),
         scratch_shapes=[pltpu.SemaphoreType.DMA] + sems,
         compiler_params=pltpu.CompilerParams(collective_id=0, has_side_effects=True),
-    )(value[None])
+    )(value[None], after)
     return gathered.reshape((total * value.shape[0],) + value.shape[1:])
 
 
@@ -146,6 +146,33 @@
     return (new_top, total * factor + block_total, summed * factor[..., None] + product)
 
 
+def attention_kernel(heads, q_ref, k_ref, v_ref, o_ref):
+    for head in range(heads):
+        lanes = slice(head * HD, (head + 1) * HD)
+        scores = jnp.dot(q_ref[:, lanes], k_ref[lanes, :], preferred_element_type=jnp.float32)
+        scores = scores * HD ** (-0.5)
+        top = jnp.max(scores, axis=1, keepdims=True)
+        weights = jnp.exp(scores - top)
+        total = jnp.sum(weights, axis=1, keepdims=True)
+        summed = jnp.dot(
+            weights.astype(jnp.bfloat16), v_ref[:, lanes], preferred_element_type=jnp.float32
+        )
+        o_ref[:, lanes] = (summed / total).astype(o_ref.dtype)
+
+
+def attention(query, keys, values, heads):
+    tokens, channels = query.shape
+    whole = lambda array: pl.BlockSpec(array.shape, lambda i: (0, 0))
+    operands = (query, keys, values)
+    return pl.pallas_call(
+        functools.partial(attention_kernel, heads),
+        out_shape=jax.ShapeDtypeStruct((tokens, channels), jnp.bfloat16),
+        grid=(1,),
+        in_specs=[whole(array) for array in operands],
+        out_specs=pl.BlockSpec((tokens, channels), lambda i: (0, 0)),
+    )(*operands)
+
+
 def doubling_gather(value, axis):
     size = lax.axis_size(axis)
     step = 1
@@ -160,8 +187,6 @@
     count, band_rows, width, channels = frames.shape
     heads = channels // HD
     band = band_rows * width
-    w_pair = jnp.concatenate([w_key, w_value], axis=1)
-    every_feature = staged_gather(ref_features)
     activated = jax.nn.silu(frames.astype(jnp.float32)).astype(jnp.bfloat16)
     padded = extended(activated, ROW_PARTS, 1, 1)
     padded = jnp.pad(padded, ((0, 0), (0, 0), (1, 1), (0, 0)))
@@ -186,14 +211,11 @@
         axis=0,
     )
     query = jnp.dot(hidden, w_query, preferred_element_type=jnp.float32).astype(jnp.bfloat16)
-    query_heads = query.reshape(band, heads, HD)
-    state = (None, None, None)
-    for source in (hidden, others, every_feature):
-        pair = jnp.dot(source, w_pair, preferred_element_type=jnp.float32).astype(jnp.bfloat16)
-        state = attend_block(state, query_heads, pair[:, :channels], pair[:, channels:], heads)
-    top, total, summed = state
-    mixed = summed / total[..., None]
-    mixed = jnp.transpose(mixed, (1, 0, 2)).reshape(band, channels).astype(jnp.bfloat16)
+    every_feature = staged_gather(ref_features, query)
+    source = jnp.concatenate([hidden, others, every_feature], axis=0)
+    keys = jnp.einsum("tc,cd->dt", source, w_key, preferred_element_type=jnp.float32)
+    values = jnp.dot(source, w_value, preferred_element_type=jnp.float32)
+    mixed = attention(query, keys.astype(jnp.bfloat16), values.astype(jnp.bfloat16), heads)
     attended = (jnp.dot(mixed, w_out, preferred_element_type=jnp.float32) + out_bias).astype(
         jnp.bfloat16
     )

time: 108 us -> 80.3 us (0.74)
  local copies, waits for them, and re-layouts: 18.7 us -> 3.71 us
  matrix products: 33.6 us -> 19 us
  Pallas kernels: 31.6 us -> 44.3 us
  other arithmetic: 10.1 us -> 1.54 us
  starting transfers between devices: 12.3 us -> 7.29 us
  waiting for transfers between devices: 0.01 us -> 3.39 us
    dot_general x9 -> x2, matrix products: 25.3 us -> 9.63 us  [the longest x1 5.86 us: shards(): values = jnp.dot(source, w_value, preferred_element_type=jnp.float32)]
    slice x7 -> x0, local copies, waits for them, and re-layouts: 12.1 us -> none  [the longest x4 6.64 us: shards(): pair[:, channels:]]
    pallas_call x0 -> x1, Pallas kernels: none -> 11 us  [attention(): pl.pallas_call(functools.partial(attention_kernel, heads), out_shape=jax....]
    reduce_sum x3 -> x0, other arithmetic: 8.54 us -> none  [attend_block(): block_total = jnp.sum(weights, axis=2)]
    ppermute x3, starting transfers between devices: 5.25 us -> 0.51 us  [shards(): lax.ppermute(hidden, ROW_PARTS, [(j, (j + shift) % rows) for j in range(r...]
    ppermute x1, waiting for transfers between devices: 0.01 us -> 3.38 us  [extended(): after = lax.ppermute(initial, axis, down)]
    ppermute x1, starting transfers between devices: 5.15 us -> 1.92 us  [extended(): after = lax.ppermute(initial, axis, down)]
    ppermute x1, starting transfers between devices: 1.92 us -> 4.86 us  [extended(): before = lax.ppermute(last, axis, up)]
  transfers between devices with their start and end apart: 5 -> 5, of which waited for: 0 -> 1; matrix products, arithmetic and copies ran while one was open for 21% -> 3% of each run, Pallas kernels for 29% -> 42%
where the time goes in v10:
time: 80.3 us; the launch traced here: 80 us
  Pallas kernels  44.3 us (55%)
  matrix products  19 us (24%)
  starting transfers between devices  7.29 us (9%)
  local copies, waits for them, and re-layouts  3.71 us (5%)
  waiting for transfers between devices  3.39 us (4%)
  other arithmetic  1.54 us (2%)
  between operations  0.84 us (1%)
    pallas_call x1, Pallas kernels, staged_gather(): pl.pallas_call(functools.partial(staged_kernel, sizes), out_shape=jax.Sha...  33.3 us
    pallas_call x1, Pallas kernels, attention(): pl.pallas_call(functools.partial(attention_kernel, heads), out_shape=jax....  11 us
    dot_general x9, matrix products, shards(): jnp.dot(window, conv_weight[row_tap, col_tap], preferred_element_type=jnp...  6.02 us
    dot_general x1, matrix products, shards(): values = jnp.dot(source, w_value, preferred_element_type=jnp.float32)  5.86 us
    ppermute x1, starting transfers between devices, extended(): before = lax.ppermute(last, axis, up)  4.86 us
    dot_general x1, matrix products, shards(): jnp.einsum('tc,cd->dt', source, w_key, preferred_element_type=jnp.float32)  3.77 us
    ppermute x1, waiting for transfers between devices, extended(): after = lax.ppermute(initial, axis, down)  3.38 us
    unnamed x25, local copies, waits for them, and re-layouts  2.33 us
  transfers between devices with their start and end apart: 5, of which 1 were waited for; matrix products, arithmetic and copies ran while one was open for 3% of the time, Pallas kernels for 42%

profile of v10, /device:TPU:1, one launch (start us, length us, event | category | flops | bytes accessed | tf_op | source)
XLA Modules:
  0.0 80.0 jit_solution(15585364621565201482)
XLA Ops:
  0.6 0.0 copy-start
  0.6 0.0 copy-start.1
  0.7 1.3 %multiply_convert_fusion = bf16[1,8,32,640]{3,2,1,0:T(8,128)(2,1)S(1)} fusion(bf16[1,8,32,640]{3,2,1,0:T(8,128)(2,1)} %param.9), kind=kLoop, calls=%fused_computation.40 | loop fusion | flops 983040 | bytes 655360 | tf_op jit(solution)/shard_map/convert_element_type | solution.py:190
  2.0 4.9 %collective-permute-start = (bf16[1,1,32,640]{3,2,1,0:T(8,128)(2,1)S(1)}, bf16[1,1,32,640]{3,2,1,0:T(8,128)(2,1)S(1)}, u32[]{:S(2)}, u32[]{:S(2)}) collective-permute-start(bf16[1,1,32,640]{3,2,1,0:T(8,128)(2,1)S(1)} %get-tuple-element.10), channel_id=1, source_target_pairs={{0,1},{1,2},{2,3},{4,5},{5,6},{6,7},{8,9},{9,10},{10,11},{12,13},{... | collective-permute-start | bytes 122888 | tf_op jit(solution)/shard_map/ppermute | solution.py:119
  6.9 1.9 %collective-permute-start.1 = (bf16[1,1,32,640]{3,2,1,0:T(8,128)(2,1)S(1)}, bf16[1,1,32,640]{3,2,1,0:T(8,128)(2,1)S(1)}, u32[]{:S(2)}, u32[]{:S(2)}) collective-permute-start(bf16[1,1,32,640]{3,2,1,0:T(8,128)(2,1)S(1)} %get-tuple-element.11), channel_id=1, source_target_pairs={{1,0},{2,1},{3,2},{5,4},{6,5},{7,6},{9,8},{10,9},{11,10},{13,12},{... | collective-permute-start | bytes 122888 | tf_op jit(solution)/shard_map/ppermute | solution.py:120
  8.8 0.0 collective-permute-done
  8.8 3.4 %collective-permute-done.1 = bf16[1,1,32,640]{3,2,1,0:T(8,128)(2,1)S(1)} collective-permute-done((bf16[1,1,32,640]{3,2,1,0:T(8,128)(2,1)S(1)}, bf16[1,1,32,640]{3,2,1,0:T(8,128)(2,1)S(1)}, u32[]{:S(2)}, u32[]{:S(2)}) %collective-permute-start.1) | collective-permute-done | bytes 40992 | tf_op jit(solution)/shard_map/ppermute | solution.py:120
  12.2 0.2 fusion.31
  12.4 0.2 fusion.32
  12.6 1.6 %fusion.16 = f32[256,640]{1,0:T(8,128)S(1)} fusion(bf16[256,640]{1,0:T(8,128)(2,1)S(1)} %bitcast.71, bf16[3,3,640,640]{3,2,1,0:T(8,128)(2,1)} %param.10), kind=kOutput, calls=%fused_computation.29 | convolution fusion | flops 209715200 | bytes 1802240 | tf_op jit(solution)/shard_map/dot_general | solution.py:199
  14.2 0.0 copy-done.1
  14.2 0.5 fusion.7
  14.6 0.1 pad_maximum_fusion
  14.7 0.5 convolution_add_fusion.7
  15.2 0.5 convolution_add_fusion.6
  15.6 0.5 convolution_add_fusion.5
  16.1 0.5 convolution_add_fusion.4
  16.6 0.0 copy-start.3
  16.6 0.0 copy-start.7
  16.6 0.5 convolution_add_fusion.3
  17.1 0.0 copy-start.5
  17.1 0.5 convolution_add_fusion.2
  17.5 0.0 copy-done.3
  17.5 0.0 copy-done.7
  17.6 1.2 %constant_dynamic-update-slice_fusion.4 = (bf16[2048,640]{1,0:T(8,128)(2,1)}, bf16[256,640]{1,0:T(8,128)(2,1)S(1)}) fusion(f32[640]{0:T(1024)S(1)} %copy-done.7, f32[256,640]{1,0:T(8,128)S(1)} %fusion.7, f32[256,640]{1,0:T(8,128)S(1)} %convolution_add_fusion.2, bf16[256,640]{1,0:T(8,128)(2,1)S(1)} %bitcast.73, bf16[3,3,640,640]{3,2,1,0:T(8,128)(2,1)S(1)} %copy-done.1, ...), kind=kOutput, calls=%fused_computation.52 | convolution fusion | flops 210698240 | bytes 3444736 | tf_op jit(solution)/shard_map/dot_general | solution.py:199
  18.8 0.0 collective-permute-start.2
  18.8 0.5 collective-permute-start.4
  19.3 0.0 collective-permute-start.3
  19.3 0.0 copy-done.5
  19.3 1.2 %convolution_convert_fusion.2.after_ref.q_ref = bf16[256,640]{1,0:T(8,128)(2,1)} fusion(bf16[256,640]{1,0:T(8,128)(2,1)S(1)} %get-tuple-element.13, bf16[640,640]{1,0:T(8,128)(2,1)S(1)} %copy-done.5), kind=kOutput, calls=%fused_computation.18 | convolution fusion | flops 209879040 | bytes 1474560 | tf_op jit(solution)/shard_map/dot_general | solution.py:213
  20.5 33.3 %shard_map.104 = bf16[64,16,640]{2,1,0:T(8,128)(2,1)} custom-call(bf16[1,16,640]{2,1,0:T(8,128)(2,1)} %bitcast.75, bf16[256,640]{1,0:T(8,128)(2,1)} %convolution_convert_fusion.2.after_ref.q_ref), custom_call_target="tpu_custom_call" | custom-call | tf_op jit(solution)/shard_map/pallas_call | solution.py:101
  53.8 0.0 copy-start.2
  53.8 0.0 collective-permute-done.2
  53.8 0.8 constant_dynamic-update-slice_fusion.3
  54.6 0.0 collective-permute-done.3
  54.6 0.8 constant_dynamic-update-slice_fusion.2
  55.4 0.0 collective-permute-done.4
  55.4 0.8 constant_dynamic-update-slice_fusion.1
  56.1 0.0 copy-done.2
  56.1 1.2 %constant_dynamic-update-slice_fusion = bf16[2048,640]{1,0:T(8,128)(2,1)} fusion(bf16[2048,640]{1,0:T(8,128)(2,1)} %constant_dynamic-update-slice_fusion.1, bf16[1024,640]{1,0:T(8,128)(2,1)S(1)} %bitcast.64), kind=kLoop, calls=%fused_computation.48 | loop fusion | bytes 2621440 | tf_op jit(solution)/shard_map/concatenate | solution.py:215
  57.3 0.0 copy-done.4
  57.3 0.0 copy-done
  57.3 5.9 %convolution_convert_fusion.v_ref = bf16[2048,640]{1,0:T(8,128)(2,1)} fusion(bf16[2048,640]{1,0:T(8,128)(2,1)} %constant_dynamic-update-slice_fusion, bf16[640,640]{1,0:T(8,128)(2,1)S(1)} %copy-done), kind=kOutput, calls=%fused_computation | convolution fusion | flops 1679032320 | bytes 6062080 | tf_op jit(solution)/shard_map/dot_general | solution.py:217
  63.2 0.0 copy-done.6
  63.2 0.0 copy-done.8
  63.2 3.8 %fusion.k_ref = bf16[640,2048]{1,0:T(8,128)(2,1)} fusion(bf16[2048,640]{1,0:T(8,128)(2,1)S(1)} %copy-done.6, bf16[640,640]{1,0:T(8,128)(2,1)S(1)} %copy-done.8), kind=kOutput, calls=%fused_computation.2 | convolution fusion | flops 1679032320 | bytes 6062080 | tf_op jit(solution)/shard_map/tc,cd->dt/dot_general | solution.py:216
  66.9 11.0 %shard_map.105 = bf16[256,640]{1,0:T(8,128)(2,1)} custom-call(bf16[256,640]{1,0:T(8,128)(2,1)} %convolution_convert_fusion.2.after_ref.q_ref, bf16[640,2048]{1,0:T(8,128)(2,1)} %fusion.k_ref, bf16[2048,640]{1,0:T(8,128)(2,1)} %convolution_convert_fusion.v_ref), custom_call_target="tpu_custom_call" | custom-call | tf_op jit(solution)/shard_map/pallas_call | solution.py:167
  77.9 2.2 %fusion.4 = bf16[256,640]{1,0:T(8,128)(2,1)} fusion(bf16[256,640]{1,0:T(8,128)(2,1)} %shard_map.105, bf16[640,640]{1,0:T(8,128)(2,1)S(1)} %copy-done.9, f32[640]{0:T(1024)S(1)} %copy-done.10), kind=kOutput, calls=%fused_computation.16 | convolution fusion | flops 210042880 | bytes 1477120 | tf_op jit(solution)/shard_map/dot_general | solution.py:219
  (8 shorter events, 0.0 us)
Async XLA Ops:
  0.6 56.7 %copy-start = (bf16[640,640]{1,0:T(8,128)(2,1)S(1)}, bf16[640,640]{1,0:T(8,128)(2,1)}, u32[]{:S(2)}) copy-start(bf16[640,640]{1,0:T(8,128)(2,1)} %param.15) | copy-start | bytes 2457604
  0.6 13.5 %copy-start.1 = (bf16[3,3,640,640]{3,2,1,0:T(8,128)(2,1)S(1)}, bf16[3,3,640,640]{3,2,1,0:T(8,128)(2,1)}, u32[]{:S(2)}) copy-start(bf16[3,3,640,640]{3,2,1,0:T(8,128)(2,1)} %param.10) | copy-start | bytes 22118404
  2.0 6.8 %collective-permute-start = (bf16[1,1,32,640]{3,2,1,0:T(8,128)(2,1)S(1)}, bf16[1,1,32,640]{3,2,1,0:T(8,128)(2,1)S(1)}, u32[]{:S(2)}, u32[]{:S(2)}) collective-permute-start(bf16[1,1,32,640]{3,2,1,0:T(8,128)(2,1)S(1)} %get-tuple-element.10), channel_id=1, source_target_pairs={{0,1},{1,2},{2,3},{4,5},{5,6},{6,7},{8,9},{9,10},{10,11},{12,13},{... | collective-permute-start | bytes 122888 | tf_op jit(solution)/shard_map/ppermute | solution.py:119
  6.9 5.3 %collective-permute-start.1 = (bf16[1,1,32,640]{3,2,1,0:T(8,128)(2,1)S(1)}, bf16[1,1,32,640]{3,2,1,0:T(8,128)(2,1)S(1)}, u32[]{:S(2)}, u32[]{:S(2)}) collective-permute-start(bf16[1,1,32,640]{3,2,1,0:T(8,128)(2,1)S(1)} %get-tuple-element.11), channel_id=1, source_target_pairs={{1,0},{2,1},{3,2},{5,4},{6,5},{7,6},{9,8},{10,9},{11,10},{13,12},{... | collective-permute-start | bytes 122888 | tf_op jit(solution)/shard_map/ppermute | solution.py:120
  16.6 1.0 %copy-start.3 = (bf16[1,8,32,640]{3,2,1,0:T(8,128)(2,1)S(1)}, bf16[1,8,32,640]{3,2,1,0:T(8,128)(2,1)}, u32[]{:S(2)}) copy-start(bf16[1,8,32,640]{3,2,1,0:T(8,128)(2,1)} %param.9) | copy-start | bytes 983044
  16.6 1.0 %copy-start.7 = (f32[640]{0:T(1024)S(1)}, f32[640]{0:T(1024)}, u32[]{:S(2)}) copy-start(f32[640]{0:T(1024)} %param.11) | copy-start | bytes 7684
  17.1 2.2 %copy-start.5 = (bf16[640,640]{1,0:T(8,128)(2,1)S(1)}, bf16[640,640]{1,0:T(8,128)(2,1)}, u32[]{:S(2)}) copy-start(bf16[640,640]{1,0:T(8,128)(2,1)} %param.13) | copy-start | bytes 2457604
  18.8 38.5 %copy-start.4 = (bf16[256,640]{1,0:T(8,128)(2,1)}, bf16[256,640]{1,0:T(8,128)(2,1)S(1)}, u32[]{:S(2)}) copy-start(bf16[256,640]{1,0:T(8,128)(2,1)S(1)} %get-tuple-element.13) | copy-start | bytes 983044
  18.8 35.1 %collective-permute-start.2 = (bf16[256,640]{1,0:T(8,128)(2,1)S(1)}, bf16[256,640]{1,0:T(8,128)(2,1)S(1)}, u32[]{:S(2)}, u32[]{:S(2)}) collective-permute-start(bf16[256,640]{1,0:T(8,128)(2,1)S(1)} %get-tuple-element.13), channel_id=1, source_target_pairs={{0,1},{1,2},{2,3},{3,0},{4,5},{5,6},{6,7},{7,4},{8,9},{9,10},{10,1... | collective-permute-start | bytes 983048 | tf_op jit(solution)/shard_map/ppermute | solution.py:208
  18.8 36.6 %collective-permute-start.4 = (bf16[256,640]{1,0:T(8,128)(2,1)S(1)}, bf16[256,640]{1,0:T(8,128)(2,1)S(1)}, u32[]{:S(2)}, u32[]{:S(2)}) collective-permute-start(bf16[256,640]{1,0:T(8,128)(2,1)S(1)} %get-tuple-element.13), channel_id=1, source_target_pairs={{0,3},{1,0},{2,1},{3,2},{4,7},{5,4},{6,5},{7,6},{8,11},{9,8},{10,9... | collective-permute-start | bytes 983048 | tf_op jit(solution)/shard_map/ppermute | solution.py:208
  19.3 35.3 %collective-permute-start.3 = (bf16[256,640]{1,0:T(8,128)(2,1)S(1)}, bf16[256,640]{1,0:T(8,128)(2,1)S(1)}, u32[]{:S(2)}, u32[]{:S(2)}) collective-permute-start(bf16[256,640]{1,0:T(8,128)(2,1)S(1)} %get-tuple-element.13), channel_id=1, source_target_pairs={{0,2},{1,3},{2,0},{3,1},{4,6},{5,7},{6,4},{7,5},{8,10},{9,11},{10,... | collective-permute-start | bytes 983048 | tf_op jit(solution)/shard_map/ppermute | solution.py:208
  53.8 2.3 %copy-start.2 = (bf16[64,16,640]{2,1,0:T(8,128)(2,1)S(1)}, bf16[64,16,640]{2,1,0:T(8,128)(2,1)}, u32[]{:S(2)}) copy-start(bf16[64,16,640]{2,1,0:T(8,128)(2,1)} %shard_map.104) | copy-start | bytes 3932164
  57.3 5.9 %copy-start.6 = (bf16[2048,640]{1,0:T(8,128)(2,1)S(1)}, bf16[2048,640]{1,0:T(8,128)(2,1)}, u32[]{:S(2)}) copy-start(bf16[2048,640]{1,0:T(8,128)(2,1)} %constant_dynamic-update-slice_fusion) | copy-start | bytes 7864324
  57.3 5.9 %copy-start.8 = (bf16[640,640]{1,0:T(8,128)(2,1)S(1)}, bf16[640,640]{1,0:T(8,128)(2,1)}, u32[]{:S(2)}) copy-start(bf16[640,640]{1,0:T(8,128)(2,1)} %param.14) | copy-start | bytes 2457604
  66.9 11.0 %copy-start.9 = (bf16[640,640]{1,0:T(8,128)(2,1)S(1)}, bf16[640,640]{1,0:T(8,128)(2,1)}, u32[]{:S(2)}) copy-start(bf16[640,640]{1,0:T(8,128)(2,1)} %param.16) | copy-start | bytes 2457604
  66.9 11.0 %copy-start.10 = (f32[640]{0:T(1024)S(1)}, f32[640]{0:T(1024)}, u32[]{:S(2)}) copy-start(f32[640]{0:T(1024)} %param.17) | copy-start | bytes 7684

commit v11 on v10

--- a/solution.py
+++ b/solution.py
@@ -146,7 +146,10 @@
     return (new_top, total * factor + block_total, summed * factor[..., None] + product)
 
 
-def attention_kernel(heads, q_ref, k_ref, v_ref, o_ref):
+def attention_kernel(heads, q_ref, k_ref, s_ref, w_ref, o_ref, v_ref):
+    v_ref[...] = jnp.dot(
+        s_ref[...], w_ref[...], preferred_element_type=jnp.float32
+    ).astype(v_ref.dtype)
     for head in range(heads):
         lanes = slice(head * HD, (head + 1) * HD)
         scores = jnp.dot(q_ref[:, lanes], k_ref[lanes, :], preferred_element_type=jnp.float32)
@@ -160,16 +163,17 @@
         o_ref[:, lanes] = (summed / total).astype(o_ref.dtype)
 
 
-def attention(query, keys, values, heads):
+def attention(query, keys, source, w_value, heads):
     tokens, channels = query.shape
     whole = lambda array: pl.BlockSpec(array.shape, lambda i: (0, 0))
-    operands = (query, keys, values)
+    operands = (query, keys, source, w_value)
     return pl.pallas_call(
         functools.partial(attention_kernel, heads),
         out_shape=jax.ShapeDtypeStruct((tokens, channels), jnp.bfloat16),
         grid=(1,),
         in_specs=[whole(array) for array in operands],
         out_specs=pl.BlockSpec((tokens, channels), lambda i: (0, 0)),
+        scratch_shapes=[pltpu.VMEM((source.shape[0], w_value.shape[1]), jnp.bfloat16)],
     )(*operands)
 
 
@@ -214,8 +218,7 @@
     every_feature = staged_gather(ref_features, query)
     source = jnp.concatenate([hidden, others, every_feature], axis=0)
     keys = jnp.einsum("tc,cd->dt", source, w_key, preferred_element_type=jnp.float32)
-    values = jnp.dot(source, w_value, preferred_element_type=jnp.float32)
-    mixed = attention(query, keys.astype(jnp.bfloat16), values.astype(jnp.bfloat16), heads)
+    mixed = attention(query, keys.astype(jnp.bfloat16), source, w_value, heads)
     attended = (jnp.dot(mixed, w_out, preferred_element_type=jnp.float32) + out_bias).astype(
         jnp.bfloat16
     )

time: 80.3 us -> 78.2 us (0.974)
  matrix products: 19 us -> 14.4 us
  Pallas kernels: 44.3 us -> 46.7 us
    dot_general x1 -> x0, matrix products: 5.86 us -> none  [shards(): values = jnp.dot(source, w_value, preferred_element_type=jnp.float32)]
    pallas_call x1, Pallas kernels: 11 us -> 13.4 us  [attention(): pl.pallas_call(functools.partial(attention_kernel, heads), out_shape=jax....]
    dot_general x1, matrix products: 1.18 us -> 2.19 us  [shards(): jnp.dot(hidden, w_query, preferred_element_type=jnp.float32)]
    concatenate x1, local copies, waits for them, and re-layouts: 1.17 us -> 0.23 us  [shards(): source = jnp.concatenate([hidden, others, every_feature], axis=0)]
    unnamed x25 -> x19, local copies, waits for them, and re-layouts: 2.33 us -> 3.2 us
  transfers between devices with their start and end apart: 5 -> 5, of which waited for: 1 -> 1; matrix products, arithmetic and copies ran while one was open for 3% -> 6% of each run, Pallas kernels for 42% -> 43%
where the time goes in v11:
time: 78.2 us; the launch traced here: 77.8 us
  Pallas kernels  46.7 us (60%)
  matrix products  14.4 us (18%)
  starting transfers between devices  7.29 us (9%)
  local copies, waits for them, and re-layouts  3.63 us (5%)
  waiting for transfers between devices  3.39 us (4%)
  other arithmetic  1.54 us (2%)
  between operations  0.88 us (1%)
    pallas_call x1, Pallas kernels, staged_gather(): pl.pallas_call(functools.partial(staged_kernel, sizes), out_shape=jax.Sha...  33.3 us
    pallas_call x1, Pallas kernels, attention(): pl.pallas_call(functools.partial(attention_kernel, heads), out_shape=jax....  13.4 us
    dot_general x9, matrix products, shards(): jnp.dot(window, conv_weight[row_tap, col_tap], preferred_element_type=jnp...  6 us
    ppermute x1, starting transfers between devices, extended(): before = lax.ppermute(last, axis, up)  4.86 us
    dot_general x1, matrix products, shards(): jnp.einsum('tc,cd->dt', source, w_key, preferred_element_type=jnp.float32)  3.75 us
    ppermute x1, waiting for transfers between devices, extended(): after = lax.ppermute(initial, axis, down)  3.38 us
    unnamed x19, local copies, waits for them, and re-layouts  3.2 us
    dot_general x1, matrix products, shards(): jnp.dot(mixed, w_out, preferred_element_type=jnp.float32) + out_bias  2.43 us
  transfers between devices with their start and end apart: 5, of which 1 were waited for; matrix products, arithmetic and copies ran while one was open for 6% of the time, Pallas kernels for 43%

profile of v11, /device:TPU:1, one launch (start us, length us, event | category | flops | bytes accessed | tf_op | source)
XLA Modules:
  0.0 77.8 jit_solution(13671375662641511966)
XLA Ops:
  0.6 0.0 copy-start
  0.6 0.0 copy-start.1
  0.7 1.3 %multiply_convert_fusion = bf16[1,8,32,640]{3,2,1,0:T(8,128)(2,1)S(1)} fusion(bf16[1,8,32,640]{3,2,1,0:T(8,128)(2,1)} %param.9), kind=kLoop, calls=%fused_computation.39 | loop fusion | flops 983040 | bytes 655360 | tf_op jit(solution)/shard_map/convert_element_type | solution.py:194
  2.0 4.9 %collective-permute-start = (bf16[1,1,32,640]{3,2,1,0:T(8,128)(2,1)S(1)}, bf16[1,1,32,640]{3,2,1,0:T(8,128)(2,1)S(1)}, u32[]{:S(2)}, u32[]{:S(2)}) collective-permute-start(bf16[1,1,32,640]{3,2,1,0:T(8,128)(2,1)S(1)} %get-tuple-element.10), channel_id=1, source_target_pairs={{0,1},{1,2},{2,3},{4,5},{5,6},{6,7},{8,9},{9,10},{10,11},{12,13},{... | collective-permute-start | bytes 122888 | tf_op jit(solution)/shard_map/ppermute | solution.py:119
  6.9 1.9 %collective-permute-start.1 = (bf16[1,1,32,640]{3,2,1,0:T(8,128)(2,1)S(1)}, bf16[1,1,32,640]{3,2,1,0:T(8,128)(2,1)S(1)}, u32[]{:S(2)}, u32[]{:S(2)}) collective-permute-start(bf16[1,1,32,640]{3,2,1,0:T(8,128)(2,1)S(1)} %get-tuple-element.11), channel_id=1, source_target_pairs={{1,0},{2,1},{3,2},{5,4},{6,5},{7,6},{9,8},{10,9},{11,10},{13,12},{... | collective-permute-start | bytes 122888 | tf_op jit(solution)/shard_map/ppermute | solution.py:120
  8.8 0.0 collective-permute-done
  8.8 3.4 %collective-permute-done.1 = bf16[1,1,32,640]{3,2,1,0:T(8,128)(2,1)S(1)} collective-permute-done((bf16[1,1,32,640]{3,2,1,0:T(8,128)(2,1)S(1)}, bf16[1,1,32,640]{3,2,1,0:T(8,128)(2,1)S(1)}, u32[]{:S(2)}, u32[]{:S(2)}) %collective-permute-start.1) | collective-permute-done | bytes 40992 | tf_op jit(solution)/shard_map/ppermute | solution.py:120
  12.2 0.2 fusion.31
  12.4 0.2 fusion.32
  12.6 1.6 %fusion.16 = f32[256,640]{1,0:T(8,128)S(1)} fusion(bf16[256,640]{1,0:T(8,128)(2,1)S(1)} %bitcast.69, bf16[3,3,640,640]{3,2,1,0:T(8,128)(2,1)} %param.10), kind=kOutput, calls=%fused_computation.28 | convolution fusion | flops 209715200 | bytes 1802240 | tf_op jit(solution)/shard_map/dot_general | solution.py:203
  14.2 0.0 copy-done.1
  14.2 0.5 fusion.7
  14.6 0.1 pad_maximum_fusion
  14.7 0.5 convolution_add_fusion.7
  15.2 0.5 convolution_add_fusion.6
  15.6 0.5 convolution_add_fusion.5
  16.1 0.5 convolution_add_fusion.4
  16.6 0.0 copy-start.4
  16.6 0.0 copy-start.6
  16.6 0.5 convolution_add_fusion.3
  17.1 0.0 copy-start.5
  17.1 0.5 convolution_add_fusion.2
  17.5 0.0 copy-done.4
  17.5 0.0 copy-done.6
  17.5 1.2 %constant_dynamic-update-slice_fusion.4 = (bf16[2048,640]{1,0:T(8,128)(2,1)S(1)}, bf16[256,640]{1,0:T(8,128)(2,1)}) fusion(f32[640]{0:T(1024)S(1)} %copy-done.6, f32[256,640]{1,0:T(8,128)S(1)} %fusion.7, f32[256,640]{1,0:T(8,128)S(1)} %convolution_add_fusion.2, bf16[256,640]{1,0:T(8,128)(2,1)S(1)} %bitcast.71, bf16[3,3,640,640]{3,2,1,0:T(8,128)(2,1)S(1)} %copy-done.1, ...), kind=kOutput, calls=%fused_computation.51 | convolution fusion | flops 210698240 | bytes 3444736 | tf_op jit(solution)/shard_map/dot_general | solution.py:203
  18.7 0.0 collective-permute-start.2
  18.8 0.5 collective-permute-start.4
  19.3 0.0 collective-permute-start.3
  19.3 0.0 copy-done.5
  19.3 2.2 %convolution_convert_fusion.1.after_ref.q_ref = bf16[256,640]{1,0:T(8,128)(2,1)} fusion(bf16[256,640]{1,0:T(8,128)(2,1)} %get-tuple-element.13, bf16[640,640]{1,0:T(8,128)(2,1)S(1)} %copy-done.5), kind=kOutput, calls=%fused_computation.17 | convolution fusion | flops 209879040 | bytes 1474560 | tf_op jit(solution)/shard_map/dot_general | solution.py:217
  21.5 33.3 %shard_map.104 = bf16[64,16,640]{2,1,0:T(8,128)(2,1)} custom-call(bf16[1,16,640]{2,1,0:T(8,128)(2,1)} %bitcast.72, bf16[256,640]{1,0:T(8,128)(2,1)} %convolution_convert_fusion.1.after_ref.q_ref), custom_call_target="tpu_custom_call" | custom-call | tf_op jit(solution)/shard_map/pallas_call | solution.py:101
  54.8 0.0 copy-start.2
  54.8 0.0 collective-permute-done.2
  54.8 1.1 %constant_dynamic-update-slice_fusion.3 = bf16[2048,640]{1,0:T(8,128)(2,1)S(1)} fusion(bf16[2048,640]{1,0:T(8,128)(2,1)S(1)} %get-tuple-element.12, bf16[256,640]{1,0:T(8,128)(2,1)} %collective-permute-done.2), kind=kLoop, calls=%fused_computation.50 | loop fusion | bytes 655360
  55.9 0.0 collective-permute-done.3
  55.9 1.0 %constant_dynamic-update-slice_fusion.2 = bf16[2048,640]{1,0:T(8,128)(2,1)S(1)} fusion(bf16[2048,640]{1,0:T(8,128)(2,1)S(1)} %constant_dynamic-update-slice_fusion.3, bf16[256,640]{1,0:T(8,128)(2,1)} %collective-permute-done.3), kind=kLoop, calls=%fused_computation.49 | loop fusion | bytes 655360
  57.0 0.0 collective-permute-done.4
  57.0 1.0 %constant_dynamic-update-slice_fusion.1 = bf16[2048,640]{1,0:T(8,128)(2,1)S(1)} fusion(bf16[2048,640]{1,0:T(8,128)(2,1)S(1)} %constant_dynamic-update-slice_fusion.2, bf16[256,640]{1,0:T(8,128)(2,1)} %collective-permute-done.4), kind=kLoop, calls=%fused_computation.48 | loop fusion | bytes 655360
  58.0 0.0 copy-done.2
  58.0 0.2 constant_dynamic-update-slice_fusion.s_ref
  58.2 0.0 copy-done
  58.2 0.0 copy-start.3
  58.2 3.7 %fusion.k_ref = bf16[640,2048]{1,0:T(8,128)(2,1)} fusion(bf16[2048,640]{1,0:T(8,128)(2,1)S(1)} %constant_dynamic-update-slice_fusion.s_ref, bf16[640,640]{1,0:T(8,128)(2,1)S(1)} %copy-done), kind=kOutput, calls=%fused_computation.1 | convolution fusion | flops 1679032320 | bytes 6062080 | tf_op jit(solution)/shard_map/tc,cd->dt/dot_general | solution.py:220
  62.0 0.0 copy-done.3
  62.0 0.0 copy-start.7
  62.0 13.4 %shard_map.105 = bf16[256,640]{1,0:T(8,128)(2,1)} custom-call(bf16[256,640]{1,0:T(8,128)(2,1)} %convolution_convert_fusion.1.after_ref.q_ref, bf16[640,2048]{1,0:T(8,128)(2,1)} %fusion.k_ref, bf16[2048,640]{1,0:T(8,128)(2,1)} %copy-done.3, bf16[640,640]{1,0:T(8,128)(2,1)} %w_ref.1), custom_call_target="tpu_custom_call" | custom-call | tf_op jit(solution)/shard_map/pallas_call | solution.py:170
  75.4 0.0 copy-done.7
  75.4 2.4 %fusion.4 = bf16[256,640]{1,0:T(8,128)(2,1)} fusion(bf16[256,640]{1,0:T(8,128)(2,1)} %shard_map.105, bf16[640,640]{1,0:T(8,128)(2,1)} %param.16, f32[640]{0:T(1024)S(1)} %copy-done.7), kind=kOutput, calls=%fused_computation.15 | convolution fusion | flops 210042880 | bytes 1477120 | tf_op jit(solution)/shard_map/dot_general | solution.py:222
  (1 shorter events, 0.0 us)
Async XLA Ops:
  0.6 57.6 %copy-start = (bf16[640,640]{1,0:T(8,128)(2,1)S(1)}, bf16[640,640]{1,0:T(8,128)(2,1)}, u32[]{:S(2)}) copy-start(bf16[640,640]{1,0:T(8,128)(2,1)} %param.14) | copy-start | bytes 2457604
  0.6 13.5 %copy-start.1 = (bf16[3,3,640,640]{3,2,1,0:T(8,128)(2,1)S(1)}, bf16[3,3,640,640]{3,2,1,0:T(8,128)(2,1)}, u32[]{:S(2)}) copy-start(bf16[3,3,640,640]{3,2,1,0:T(8,128)(2,1)} %param.10) | copy-start | bytes 22118404
  2.0 6.8 %collective-permute-start = (bf16[1,1,32,640]{3,2,1,0:T(8,128)(2,1)S(1)}, bf16[1,1,32,640]{3,2,1,0:T(8,128)(2,1)S(1)}, u32[]{:S(2)}, u32[]{:S(2)}) collective-permute-start(bf16[1,1,32,640]{3,2,1,0:T(8,128)(2,1)S(1)} %get-tuple-element.10), channel_id=1, source_target_pairs={{0,1},{1,2},{2,3},{4,5},{5,6},{6,7},{8,9},{9,10},{10,11},{12,13},{... | collective-permute-start | bytes 122888 | tf_op jit(solution)/shard_map/ppermute | solution.py:119
  6.9 5.3 %collective-permute-start.1 = (bf16[1,1,32,640]{3,2,1,0:T(8,128)(2,1)S(1)}, bf16[1,1,32,640]{3,2,1,0:T(8,128)(2,1)S(1)}, u32[]{:S(2)}, u32[]{:S(2)}) collective-permute-start(bf16[1,1,32,640]{3,2,1,0:T(8,128)(2,1)S(1)} %get-tuple-element.11), channel_id=1, source_target_pairs={{1,0},{2,1},{3,2},{5,4},{6,5},{7,6},{9,8},{10,9},{11,10},{13,12},{... | collective-permute-start | bytes 122888 | tf_op jit(solution)/shard_map/ppermute | solution.py:120
  16.6 1.0 %copy-start.4 = (bf16[1,8,32,640]{3,2,1,0:T(8,128)(2,1)S(1)}, bf16[1,8,32,640]{3,2,1,0:T(8,128)(2,1)}, u32[]{:S(2)}) copy-start(bf16[1,8,32,640]{3,2,1,0:T(8,128)(2,1)} %param.9) | copy-start | bytes 983044
  16.6 1.0 %copy-start.6 = (f32[640]{0:T(1024)S(1)}, f32[640]{0:T(1024)}, u32[]{:S(2)}) copy-start(f32[640]{0:T(1024)} %param.11) | copy-start | bytes 7684
  17.1 2.2 %copy-start.5 = (bf16[640,640]{1,0:T(8,128)(2,1)S(1)}, bf16[640,640]{1,0:T(8,128)(2,1)}, u32[]{:S(2)}) copy-start(bf16[640,640]{1,0:T(8,128)(2,1)} %param.13) | copy-start | bytes 2457604
  18.7 36.0 %collective-permute-start.2 = (bf16[256,640]{1,0:T(8,128)(2,1)}, bf16[256,640]{1,0:T(8,128)(2,1)}, u32[]{:S(2)}, u32[]{:S(2)}) collective-permute-start(bf16[256,640]{1,0:T(8,128)(2,1)} %get-tuple-element.13), channel_id=1, source_target_pairs={{0,1},{1,2},{2,3},{3,0},{4,5},{5,6},{6,7},{7,4},{8,9},{9,10},{10,1... | collective-permute-start | bytes 983048 | tf_op jit(solution)/shard_map/ppermute | solution.py:212
  18.8 38.2 %collective-permute-start.4 = (bf16[256,640]{1,0:T(8,128)(2,1)}, bf16[256,640]{1,0:T(8,128)(2,1)}, u32[]{:S(2)}, u32[]{:S(2)}) collective-permute-start(bf16[256,640]{1,0:T(8,128)(2,1)} %get-tuple-element.13), channel_id=1, source_target_pairs={{0,3},{1,0},{2,1},{3,2},{4,7},{5,4},{6,5},{7,6},{8,11},{9,8},{10,9... | collective-permute-start | bytes 983048 | tf_op jit(solution)/shard_map/ppermute | solution.py:212
  19.3 36.7 %collective-permute-start.3 = (bf16[256,640]{1,0:T(8,128)(2,1)}, bf16[256,640]{1,0:T(8,128)(2,1)}, u32[]{:S(2)}, u32[]{:S(2)}) collective-permute-start(bf16[256,640]{1,0:T(8,128)(2,1)} %get-tuple-element.13), channel_id=1, source_target_pairs={{0,2},{1,3},{2,0},{3,1},{4,6},{5,7},{6,4},{7,5},{8,10},{9,11},{10,... | collective-permute-start | bytes 983048 | tf_op jit(solution)/shard_map/ppermute | solution.py:212
  54.8 3.2 %copy-start.2 = (bf16[64,16,640]{2,1,0:T(8,128)(2,1)S(1)}, bf16[64,16,640]{2,1,0:T(8,128)(2,1)}, u32[]{:S(2)}) copy-start(bf16[64,16,640]{2,1,0:T(8,128)(2,1)} %shard_map.104) | copy-start | bytes 3932164
  58.2 3.8 %copy-start.3 = (bf16[2048,640]{1,0:T(8,128)(2,1)}, bf16[2048,640]{1,0:T(8,128)(2,1)S(1)}, u32[]{:S(2)}) copy-start(bf16[2048,640]{1,0:T(8,128)(2,1)S(1)} %constant_dynamic-update-slice_fusion.s_ref) | copy-start | bytes 7864324
  62.0 13.4 %copy-start.7 = (f32[640]{0:T(1024)S(1)}, f32[640]{0:T(1024)}, u32[]{:S(2)}) copy-start(f32[640]{0:T(1024)} %param.17) | copy-start | bytes 7684

commit v12 on v10

--- a/solution.py
+++ b/solution.py
@@ -146,7 +146,20 @@
     return (new_top, total * factor + block_total, summed * factor[..., None] + product)
 
 
-def attention_kernel(heads, q_ref, k_ref, v_ref, o_ref):
+def attention_kernel(heads, parts, *refs):
+    q_ref, wk_ref, wv_ref = refs[:3]
+    sources = refs[3 : 3 + parts]
+    o_ref, k_ref, v_ref = refs[3 + parts :]
+    offset = 0
+    for source in sources:
+        rows = source.shape[0]
+        k_ref[:, offset : offset + rows] = lax.dot_general(
+            wk_ref[...], source[...], (((1,), (1,)), ((), ())), preferred_element_type=jnp.float32
+        ).astype(k_ref.dtype)
+        v_ref[offset : offset + rows, :] = jnp.dot(
+            source[...], wv_ref[...], preferred_element_type=jnp.float32
+        ).astype(v_ref.dtype)
+        offset += rows
     for head in range(heads):
         lanes = slice(head * HD, (head + 1) * HD)
         scores = jnp.dot(q_ref[:, lanes], k_ref[lanes, :], preferred_element_type=jnp.float32)
@@ -160,16 +173,21 @@
         o_ref[:, lanes] = (summed / total).astype(o_ref.dtype)
 
 
-def attention(query, keys, values, heads):
+def attention(query, w_key_t, w_value, sources, heads):
     tokens, channels = query.shape
+    length = sum(source.shape[0] for source in sources)
     whole = lambda array: pl.BlockSpec(array.shape, lambda i: (0, 0))
-    operands = (query, keys, values)
+    operands = (query, w_key_t, w_value) + tuple(sources)
     return pl.pallas_call(
-        functools.partial(attention_kernel, heads),
+        functools.partial(attention_kernel, heads, len(sources)),
         out_shape=jax.ShapeDtypeStruct((tokens, channels), jnp.bfloat16),
         grid=(1,),
         in_specs=[whole(array) for array in operands],
         out_specs=pl.BlockSpec((tokens, channels), lambda i: (0, 0)),
+        scratch_shapes=[
+            pltpu.VMEM((channels, length), jnp.bfloat16),
+            pltpu.VMEM((length, channels), jnp.bfloat16),
+        ],
     )(*operands)
 
 
@@ -203,19 +221,14 @@
         frames.reshape(count * band, channels).astype(jnp.float32) + convolved + conv_bias
     ).astype(jnp.bfloat16)
     rows = lax.axis_size(ROW_PARTS)
-    others = jnp.concatenate(
-        [
-            lax.ppermute(hidden, ROW_PARTS, [(j, (j + shift) % rows) for j in range(rows)])
-            for shift in range(1, rows)
-        ],
-        axis=0,
-    )
+    others = [
+        lax.ppermute(hidden, ROW_PARTS, [(j, (j + shift) % rows) for j in range(rows)])
+        for shift in range(1, rows)
+    ]
     query = jnp.dot(hidden, w_query, preferred_element_type=jnp.float32).astype(jnp.bfloat16)
     every_feature = staged_gather(ref_features, query)
-    source = jnp.concatenate([hidden, others, every_feature], axis=0)
-    keys = jnp.einsum("tc,cd->dt", source, w_key, preferred_element_type=jnp.float32)
-    values = jnp.dot(source, w_value, preferred_element_type=jnp.float32)
-    mixed = attention(query, keys.astype(jnp.bfloat16), values.astype(jnp.bfloat16), heads)
+    sources = [hidden] + others + [every_feature]
+    mixed = attention(query, jnp.transpose(w_key), w_value, sources, heads)
     attended = (jnp.dot(mixed, w_out, preferred_element_type=jnp.float32) + out_bias).astype(
         jnp.bfloat16
     )

time: 80.3 us -> 73.9 us (0.920)
  matrix products: 19 us -> 8.61 us
  Pallas kernels: 44.3 us -> 49.4 us
  local copies, waits for them, and re-layouts: 3.71 us -> 2.47 us
    dot_general x2 -> x0, matrix products: 9.63 us -> none  [the longest x1 5.86 us: shards(): values = jnp.dot(source, w_value, preferred_element_type=jnp.float32)]
    pallas_call x1, Pallas kernels: 11 us -> 15 us  [attention(): pl.pallas_call(functools.partial(attention_kernel, heads, len(sources)),...]
    concatenate x1 -> x0, local copies, waits for them, and re-layouts: 1.17 us -> none  [shards(): source = jnp.concatenate([hidden, others, every_feature], axis=0)]
    pallas_call x1, Pallas kernels: 33.3 us -> 34.4 us  [staged_gather(): pl.pallas_call(functools.partial(staged_kernel, sizes), out_shape=jax.Sha...]
    unnamed x25 -> x23, local copies, waits for them, and re-layouts: 2.33 us -> 2.26 us
  transfers between devices with their start and end apart: 5 -> 5, of which waited for: 1 -> 1; matrix products, arithmetic and copies ran while one was open for 3% -> 3% of each run, Pallas kernels for 42% -> 47%
where the time goes in v12:
time: 73.9 us; the launch traced here: 73.7 us
  Pallas kernels  49.4 us (67%)
  matrix products  8.61 us (12%)
  starting transfers between devices  7.35 us (10%)
  waiting for transfers between devices  3.39 us (5%)
  local copies, waits for them, and re-layouts  2.47 us (3%)
  other arithmetic  1.54 us (2%)
  between operations  0.91 us (1%)
    pallas_call x1, Pallas kernels, staged_gather(): pl.pallas_call(functools.partial(staged_kernel, sizes), out_shape=jax.Sha...  34.4 us
    pallas_call x1, Pallas kernels, attention(): pl.pallas_call(functools.partial(attention_kernel, heads, len(sources)),...  15 us
    dot_general x9, matrix products, shards(): jnp.dot(window, conv_weight[row_tap, col_tap], preferred_element_type=jnp...  5.27 us
    ppermute x1, starting transfers between devices, extended(): before = lax.ppermute(last, axis, up)  4.86 us
    ppermute x1, waiting for transfers between devices, extended(): after = lax.ppermute(initial, axis, down)  3.38 us
    unnamed x23, local copies, waits for them, and re-layouts  2.26 us
    dot_general x1, matrix products, shards(): jnp.dot(mixed, w_out, preferred_element_type=jnp.float32) + out_bias  2.16 us
    ppermute x1, starting transfers between devices, extended(): after = lax.ppermute(initial, axis, down)  1.92 us
  transfers between devices with their start and end apart: 5, of which 1 were waited for; matrix products, arithmetic and copies ran while one was open for 3% of the time, Pallas kernels for 47%

profile of v12, /device:TPU:1, one launch (start us, length us, event | category | flops | bytes accessed | tf_op | source)
XLA Modules:
  0.0 73.7 jit_solution(17467540774030235076)
XLA Ops:
  0.6 0.0 copy-start
  0.6 0.0 copy-start.1
  0.7 1.3 %multiply_convert_fusion = bf16[1,8,32,640]{3,2,1,0:T(8,128)(2,1)S(1)} fusion(bf16[1,8,32,640]{3,2,1,0:T(8,128)(2,1)} %param.9), kind=kLoop, calls=%fused_computation.37 | loop fusion | flops 983040 | bytes 655360 | tf_op jit(solution)/shard_map/convert_element_type | solution.py:208
  2.0 4.9 %collective-permute-start = (bf16[1,1,32,640]{3,2,1,0:T(8,128)(2,1)S(1)}, bf16[1,1,32,640]{3,2,1,0:T(8,128)(2,1)S(1)}, u32[]{:S(2)}, u32[]{:S(2)}) collective-permute-start(bf16[1,1,32,640]{3,2,1,0:T(8,128)(2,1)S(1)} %get-tuple-element.10), channel_id=1, source_target_pairs={{0,1},{1,2},{2,3},{4,5},{5,6},{6,7},{8,9},{9,10},{10,11},{12,13},{... | collective-permute-start | bytes 122888 | tf_op jit(solution)/shard_map/ppermute | solution.py:119
  6.9 1.9 %collective-permute-start.1 = (bf16[1,1,32,640]{3,2,1,0:T(8,128)(2,1)S(1)}, bf16[1,1,32,640]{3,2,1,0:T(8,128)(2,1)S(1)}, u32[]{:S(2)}, u32[]{:S(2)}) collective-permute-start(bf16[1,1,32,640]{3,2,1,0:T(8,128)(2,1)S(1)} %get-tuple-element.11), channel_id=1, source_target_pairs={{1,0},{2,1},{3,2},{5,4},{6,5},{7,6},{9,8},{10,9},{11,10},{13,12},{... | collective-permute-start | bytes 122888 | tf_op jit(solution)/shard_map/ppermute | solution.py:120
  8.8 0.0 collective-permute-done
  8.8 3.4 %collective-permute-done.1 = bf16[1,1,32,640]{3,2,1,0:T(8,128)(2,1)S(1)} collective-permute-done((bf16[1,1,32,640]{3,2,1,0:T(8,128)(2,1)S(1)}, bf16[1,1,32,640]{3,2,1,0:T(8,128)(2,1)S(1)}, u32[]{:S(2)}, u32[]{:S(2)}) %collective-permute-start.1) | collective-permute-done | bytes 40992 | tf_op jit(solution)/shard_map/ppermute | solution.py:120
  12.2 0.2 fusion.30
  12.4 0.2 fusion.31
  12.6 1.6 %fusion.15 = f32[256,640]{1,0:T(8,128)S(1)} fusion(bf16[256,640]{1,0:T(8,128)(2,1)S(1)} %bitcast.68, bf16[3,3,640,640]{3,2,1,0:T(8,128)(2,1)} %param.10), kind=kOutput, calls=%fused_computation.26 | convolution fusion | flops 209715200 | bytes 1802240 | tf_op jit(solution)/shard_map/dot_general | solution.py:217
  14.2 0.0 copy-done.1
  14.2 0.5 fusion.6
  14.6 0.1 pad_maximum_fusion
  14.7 0.0 copy-start.3
  14.7 0.0 copy-start.8
  14.7 0.5 convolution_add_fusion.7
  15.2 0.0 copy-start.4
  15.2 0.5 convolution_add_fusion.6
  15.7 0.5 convolution_add_fusion.5
  16.1 0.5 convolution_add_fusion.4
  16.6 0.5 convolution_add_fusion.3
  17.1 0.0 copy-start.10
  17.1 0.5 convolution_add_fusion.2
  17.5 0.0 copy-done.3
  17.5 0.0 copy-done.8
  17.6 0.5 fusion.4.refs_3_
  18.0 0.0 copy-start.2
  18.0 0.1 collective-permute-start.2
  18.1 0.1 collective-permute-start.3
  18.2 0.4 collective-permute-start.4
  18.6 0.0 copy-done.4
  18.6 1.3 %copy.11 = bf16[640,640]{0,1:T(8,128)(2,1)} copy(bf16[640,640]{1,0:T(8,128)(2,1)S(1)} %copy-done.4) | data formatting | bytes 1638400 | tf_op args[5]
  20.0 0.0 copy-done
  20.0 1.2 %convolution_convert_fusion.after_ref.refs_0_ = bf16[256,640]{1,0:T(8,128)(2,1)} fusion(bf16[256,640]{1,0:T(8,128)(2,1)S(1)} %fusion.4.refs_3_, bf16[640,640]{1,0:T(8,128)(2,1)S(1)} %copy-done), kind=kOutput, calls=%fused_computation.15 | convolution fusion | flops 209879040 | bytes 1474560 | tf_op jit(solution)/shard_map/dot_general | solution.py:228
  21.1 34.4 %shard_map.104 = bf16[64,16,640]{2,1,0:T(8,128)(2,1)} custom-call(bf16[1,16,640]{2,1,0:T(8,128)(2,1)} %bitcast.69, bf16[256,640]{1,0:T(8,128)(2,1)} %convolution_convert_fusion.after_ref.refs_0_), custom_call_target="tpu_custom_call" | custom-call | tf_op jit(solution)/shard_map/pallas_call | solution.py:101
  55.6 0.0 collective-permute-done.2.refs_4_
  55.6 0.0 copy-start.5
  55.6 0.0 collective-permute-done.3.refs_5_
  55.6 0.0 copy-start.6
  55.6 0.0 collective-permute-done.4.refs_6_
  55.6 0.0 copy-start.7
  55.6 0.0 copy-done.2
  55.6 0.7 copy-done.5
  56.3 0.1 copy-done.6
  56.4 0.1 copy-done.7
  56.5 15.0 %shard_map.105 = bf16[256,640]{1,0:T(8,128)(2,1)} custom-call(bf16[256,640]{1,0:T(8,128)(2,1)} %convolution_convert_fusion.after_ref.refs_0_, bf16[640,640]{1,0:T(8,128)(2,1)} %bitcast.58, bf16[640,640]{1,0:T(8,128)(2,1)} %refs_2_.1, bf16[256,640]{1,0:T(8,128)(2,1)} %copy-done.2, bf16[256,640]{1,0:T(8,128)(2,1)} %copy-done.5, bf16[256,640]{1,0:T(8,128)(2,1)} %copy-done.6, ...), custom_call_target="tpu_custom_call" | custom-call | tf_op jit(solution)/shard_map/pallas_call | solution.py:181
  71.5 0.0 copy-done.9
  71.5 2.2 %fusion.3 = bf16[256,640]{1,0:T(8,128)(2,1)} fusion(bf16[256,640]{1,0:T(8,128)(2,1)} %shard_map.105, bf16[640,640]{1,0:T(8,128)(2,1)S(1)} %copy-done.9, f32[640]{0:T(1024)S(1)} %copy-done.10), kind=kOutput, calls=%fused_computation.13 | convolution fusion | flops 210042880 | bytes 1477120 | tf_op jit(solution)/shard_map/dot_general | solution.py:232
  (3 shorter events, 0.0 us)
Async XLA Ops:
  0.6 19.3 %copy-start = (bf16[640,640]{1,0:T(8,128)(2,1)S(1)}, bf16[640,640]{1,0:T(8,128)(2,1)}, u32[]{:S(2)}) copy-start(bf16[640,640]{1,0:T(8,128)(2,1)} %param.13) | copy-start | bytes 2457604
  0.6 13.5 %copy-start.1 = (bf16[3,3,640,640]{3,2,1,0:T(8,128)(2,1)S(1)}, bf16[3,3,640,640]{3,2,1,0:T(8,128)(2,1)}, u32[]{:S(2)}) copy-start(bf16[3,3,640,640]{3,2,1,0:T(8,128)(2,1)} %param.10) | copy-start | bytes 22118404
  2.0 6.8 %collective-permute-start = (bf16[1,1,32,640]{3,2,1,0:T(8,128)(2,1)S(1)}, bf16[1,1,32,640]{3,2,1,0:T(8,128)(2,1)S(1)}, u32[]{:S(2)}, u32[]{:S(2)}) collective-permute-start(bf16[1,1,32,640]{3,2,1,0:T(8,128)(2,1)S(1)} %get-tuple-element.10), channel_id=1, source_target_pairs={{0,1},{1,2},{2,3},{4,5},{5,6},{6,7},{8,9},{9,10},{10,11},{12,13},{... | collective-permute-start | bytes 122888 | tf_op jit(solution)/shard_map/ppermute | solution.py:119
  6.9 5.3 %collective-permute-start.1 = (bf16[1,1,32,640]{3,2,1,0:T(8,128)(2,1)S(1)}, bf16[1,1,32,640]{3,2,1,0:T(8,128)(2,1)S(1)}, u32[]{:S(2)}, u32[]{:S(2)}) collective-permute-start(bf16[1,1,32,640]{3,2,1,0:T(8,128)(2,1)S(1)} %get-tuple-element.11), channel_id=1, source_target_pairs={{1,0},{2,1},{3,2},{5,4},{6,5},{7,6},{9,8},{10,9},{11,10},{13,12},{... | collective-permute-start | bytes 122888 | tf_op jit(solution)/shard_map/ppermute | solution.py:120
  14.7 2.8 %copy-start.3 = (bf16[1,8,32,640]{3,2,1,0:T(8,128)(2,1)S(1)}, bf16[1,8,32,640]{3,2,1,0:T(8,128)(2,1)}, u32[]{:S(2)}) copy-start(bf16[1,8,32,640]{3,2,1,0:T(8,128)(2,1)} %param.9) | copy-start | bytes 983044
  14.7 2.8 %copy-start.8 = (f32[640]{0:T(1024)S(1)}, f32[640]{0:T(1024)}, u32[]{:S(2)}) copy-start(f32[640]{0:T(1024)} %param.11) | copy-start | bytes 7684
  15.2 3.4 %copy-start.4 = (bf16[640,640]{1,0:T(8,128)(2,1)S(1)}, bf16[640,640]{1,0:T(8,128)(2,1)}, u32[]{:S(2)}) copy-start(bf16[640,640]{1,0:T(8,128)(2,1)} %param.14) | copy-start | bytes 2457604
  17.1 54.5 %copy-start.10 = (f32[640]{0:T(1024)S(1)}, f32[640]{0:T(1024)}, u32[]{:S(2)}) copy-start(f32[640]{0:T(1024)} %param.17) | copy-start | bytes 7684
  18.0 37.6 %copy-start.2 = (bf16[256,640]{1,0:T(8,128)(2,1)}, bf16[256,640]{1,0:T(8,128)(2,1)S(1)}, u32[]{:S(2)}) copy-start(bf16[256,640]{1,0:T(8,128)(2,1)S(1)} %fusion.4.refs_3_) | copy-start | bytes 983044
  18.0 37.5 %collective-permute-start.2 = (bf16[256,640]{1,0:T(8,128)(2,1)S(1)}, bf16[256,640]{1,0:T(8,128)(2,1)S(1)}, u32[]{:S(2)}, u32[]{:S(2)}) collective-permute-start(bf16[256,640]{1,0:T(8,128)(2,1)S(1)} %fusion.4.refs_3_), channel_id=1, source_target_pairs={{0,1},{1,2},{2,3},{3,0},{4,5},{5,6},{6,7},{7,4},{8,9},{9,10},{10,1... | collective-permute-start | bytes 983048 | tf_op jit(solution)/shard_map/ppermute | solution.py:225
  18.1 37.4 %collective-permute-start.3 = (bf16[256,640]{1,0:T(8,128)(2,1)S(1)}, bf16[256,640]{1,0:T(8,128)(2,1)S(1)}, u32[]{:S(2)}, u32[]{:S(2)}) collective-permute-start(bf16[256,640]{1,0:T(8,128)(2,1)S(1)} %fusion.4.refs_3_), channel_id=1, source_target_pairs={{0,2},{1,3},{2,0},{3,1},{4,6},{5,7},{6,4},{7,5},{8,10},{9,11},{10,... | collective-permute-start | bytes 983048 | tf_op jit(solution)/shard_map/ppermute | solution.py:225
  18.2 37.4 %collective-permute-start.4 = (bf16[256,640]{1,0:T(8,128)(2,1)S(1)}, bf16[256,640]{1,0:T(8,128)(2,1)S(1)}, u32[]{:S(2)}, u32[]{:S(2)}) collective-permute-start(bf16[256,640]{1,0:T(8,128)(2,1)S(1)} %fusion.4.refs_3_), channel_id=1, source_target_pairs={{0,3},{1,0},{2,1},{3,2},{4,7},{5,4},{6,5},{7,6},{8,11},{9,8},{10,9... | collective-permute-start | bytes 983048 | tf_op jit(solution)/shard_map/ppermute | solution.py:225
  20.0 51.6 %copy-start.9 = (bf16[640,640]{1,0:T(8,128)(2,1)S(1)}, bf16[640,640]{1,0:T(8,128)(2,1)}, u32[]{:S(2)}) copy-start(bf16[640,640]{1,0:T(8,128)(2,1)} %param.16) | copy-start | bytes 2457604
  55.6 0.7 copy-start.5
  55.6 0.8 %copy-start.6 = (bf16[256,640]{1,0:T(8,128)(2,1)}, bf16[256,640]{1,0:T(8,128)(2,1)S(1)}, u32[]{:S(2)}) copy-start(bf16[256,640]{1,0:T(8,128)(2,1)S(1)} %collective-permute-done.3.refs_5_) | copy-start | bytes 983044
  55.6 0.9 %copy-start.7 = (bf16[256,640]{1,0:T(8,128)(2,1)}, bf16[256,640]{1,0:T(8,128)(2,1)S(1)}, u32[]{:S(2)}) copy-start(bf16[256,640]{1,0:T(8,128)(2,1)S(1)} %collective-permute-done.4.refs_6_) | copy-start | bytes 983044

commit v13 on v12

--- a/solution.py
+++ b/solution.py
@@ -39,23 +39,26 @@
 
 def staged_kernel(sizes, x_ref, after_ref, out_ref, local_sem, *sems):
     high, across, along = sizes
-    half = along // 2
+    plane = across * along
+    half = plane // 2
     yh, xx, zz = [lax.axis_index(axis) for axis in TM_PARTS]
     low, core = [lax.axis_index(axis) for axis in ROW_PARTS]
-    me = (yh * across + xx) * along + zz
-    mine = me - zz
-    other_core = 1 - core
-    z_peer = lambda shift: {"z": lax.rem(zz + shift, along)}
-    x_peer = lambda shift: {"x": lax.rem(xx + shift, across)}
+    spot = xx * along + zz
+    me = yh * plane + spot
+
+    def plane_peer(shift):
+        place = lax.rem(spot + shift, plane)
+        return {"x": place // along, "z": lax.rem(place, along)}
+
     y_peer = {"y_hi": 1 - yh, "y_lo": 1 - low}
-    c_peer = {"core": other_core}
-    peers = [z_peer(s) for s in range(1, along)] + [x_peer(s) for s in range(1, across)]
-    peers += [y_peer, c_peer]
+    c_peer = {"core": 1 - core}
+    peers = [plane_peer(shift) for shift in range(1, plane)] + [y_peer, c_peer]
     barrier = pltpu.get_barrier_semaphore()
     for peer in peers:
         pl.semaphore_signal(barrier, inc=1, device_id=peer, device_id_type=MESH)
     pl.semaphore_wait(barrier, len(peers))
-    local = pltpu.make_async_copy(x_ref, out_ref.at[pl.ds(me, 1)], local_sem)
+    own = out_ref.at[pl.ds(me, 1)]
+    local = pltpu.make_async_copy(x_ref, own, local_sem)
     local.start()
     local.wait()
 
@@ -75,28 +78,18 @@
         for copy in copies:
             copy.wait()
 
-    own = out_ref.at[pl.ds(me, 1)]
-    exchange([(own, z_peer(s)) for s in range(1, along)], sems[0], sems[1])
-    start = mine + core * half
-    part = out_ref.at[pl.ds(start, half)]
-    exchange([(part, x_peer(s)) for s in range(1, across)], sems[2], sems[3])
-    base = yh * across * along + core * half
-    chunks = [out_ref.at[pl.ds(base + g * along, half)] for g in range(across)]
-    exchange([(chunk, y_peer) for chunk in chunks], sems[4], sems[5])
-    regions = high * across
-    region = yh * across + xx
-    groups = []
-    for step in range(1, regions):
-        j = lax.rem(region + step, regions)
-        groups.append(out_ref.at[pl.ds(j * along + core * half, half)])
-    exchange([(chunk, c_peer) for chunk in groups], sems[6], sems[7])
+    exchange([(own, plane_peer(shift)) for shift in range(1, plane)], sems[0], sems[1])
+    mine = out_ref.at[pl.ds(yh * plane + core * half, half)]
+    exchange([(mine, y_peer)], sems[2], sems[3])
+    theirs = out_ref.at[pl.ds((1 - yh) * plane + core * half, half)]
+    exchange([(theirs, c_peer)], sems[4], sems[5])
 
 
 def staged_gather(value, after):
     sizes = [lax.axis_size(axis) for axis in TM_PARTS]
     total = sizes[0] * sizes[1] * sizes[2]
     sems = []
-    for count in (sizes[2], sizes[1], sizes[1], sizes[0] * sizes[1]):
+    for count in (sizes[1] * sizes[2], 1, 1):
         sems += [pltpu.SemaphoreType.DMA((count,))] * 2
     gathered = pl.pallas_call(
         functools.partial(staged_kernel, sizes),

time: 73.9 us -> 80.5 us (1.089)
  Pallas kernels: 49.4 us -> 56.1 us
    pallas_call x1, Pallas kernels: 34.4 us -> 41 us  [staged_gather(): pl.pallas_call(functools.partial(staged_kernel, sizes), out_shape=jax.Sha...]
  transfers between devices with their start and end apart: 5 -> 5, of which waited for: 1 -> 1; matrix products, arithmetic and copies ran while one was open for 3% -> 3% of each run, Pallas kernels for 47% -> 51%
where the time goes in v13:
time: 80.5 us; the launch traced here: 80.4 us
  Pallas kernels  56.1 us (70%)
  matrix products  8.61 us (11%)
  starting transfers between devices  7.35 us (9%)
  waiting for transfers between devices  3.39 us (4%)
  local copies, waits for them, and re-layouts  2.47 us (3%)
  other arithmetic  1.54 us (2%)
  between operations  0.91 us (1%)
    pallas_call x1, Pallas kernels, staged_gather(): pl.pallas_call(functools.partial(staged_kernel, sizes), out_shape=jax.Sha...  41 us
    pallas_call x1, Pallas kernels, attention(): pl.pallas_call(functools.partial(attention_kernel, heads, len(sources)),...  15 us
    dot_general x9, matrix products, shards(): jnp.dot(window, conv_weight[row_tap, col_tap], preferred_element_type=jnp...  5.27 us
    ppermute x1, starting transfers between devices, extended(): before = lax.ppermute(last, axis, up)  4.86 us
    ppermute x1, waiting for transfers between devices, extended(): after = lax.ppermute(initial, axis, down)  3.38 us
    unnamed x23, local copies, waits for them, and re-layouts  2.26 us
    dot_general x1, matrix products, shards(): jnp.dot(mixed, w_out, preferred_element_type=jnp.float32) + out_bias  2.16 us
    ppermute x1, starting transfers between devices, extended(): after = lax.ppermute(initial, axis, down)  1.92 us
  transfers between devices with their start and end apart: 5, of which 1 were waited for; matrix products, arithmetic and copies ran while one was open for 3% of the time, Pallas kernels for 51%

profile of v13, /device:TPU:1, one launch (start us, length us, event | category | flops | bytes accessed | tf_op | source)
XLA Modules:
  0.0 80.4 jit_solution(4881517155507924054)
XLA Ops:
  0.6 0.0 copy-start
  0.6 0.0 copy-start.1
  0.7 1.3 %multiply_convert_fusion = bf16[1,8,32,640]{3,2,1,0:T(8,128)(2,1)S(1)} fusion(bf16[1,8,32,640]{3,2,1,0:T(8,128)(2,1)} %param.9), kind=kLoop, calls=%fused_computation.37 | loop fusion | flops 983040 | bytes 655360 | tf_op jit(solution)/shard_map/convert_element_type | solution.py:201
  2.0 4.9 %collective-permute-start = (bf16[1,1,32,640]{3,2,1,0:T(8,128)(2,1)S(1)}, bf16[1,1,32,640]{3,2,1,0:T(8,128)(2,1)S(1)}, u32[]{:S(2)}, u32[]{:S(2)}) collective-permute-start(bf16[1,1,32,640]{3,2,1,0:T(8,128)(2,1)S(1)} %get-tuple-element.10), channel_id=1, source_target_pairs={{0,1},{1,2},{2,3},{4,5},{5,6},{6,7},{8,9},{9,10},{10,11},{12,13},{... | collective-permute-start | bytes 122888 | tf_op jit(solution)/shard_map/ppermute | solution.py:112
  6.9 1.9 %collective-permute-start.1 = (bf16[1,1,32,640]{3,2,1,0:T(8,128)(2,1)S(1)}, bf16[1,1,32,640]{3,2,1,0:T(8,128)(2,1)S(1)}, u32[]{:S(2)}, u32[]{:S(2)}) collective-permute-start(bf16[1,1,32,640]{3,2,1,0:T(8,128)(2,1)S(1)} %get-tuple-element.11), channel_id=1, source_target_pairs={{1,0},{2,1},{3,2},{5,4},{6,5},{7,6},{9,8},{10,9},{11,10},{13,12},{... | collective-permute-start | bytes 122888 | tf_op jit(solution)/shard_map/ppermute | solution.py:113
  8.8 0.0 collective-permute-done
  8.8 3.4 %collective-permute-done.1 = bf16[1,1,32,640]{3,2,1,0:T(8,128)(2,1)S(1)} collective-permute-done((bf16[1,1,32,640]{3,2,1,0:T(8,128)(2,1)S(1)}, bf16[1,1,32,640]{3,2,1,0:T(8,128)(2,1)S(1)}, u32[]{:S(2)}, u32[]{:S(2)}) %collective-permute-start.1) | collective-permute-done | bytes 40992 | tf_op jit(solution)/shard_map/ppermute | solution.py:113
  12.2 0.2 fusion.30
  12.4 0.2 fusion.31
  12.6 1.6 %fusion.15 = f32[256,640]{1,0:T(8,128)S(1)} fusion(bf16[256,640]{1,0:T(8,128)(2,1)S(1)} %bitcast.68, bf16[3,3,640,640]{3,2,1,0:T(8,128)(2,1)} %param.10), kind=kOutput, calls=%fused_computation.26 | convolution fusion | flops 209715200 | bytes 1802240 | tf_op jit(solution)/shard_map/dot_general | solution.py:210
  14.2 0.0 copy-done.1
  14.2 0.5 fusion.6
  14.6 0.1 pad_maximum_fusion
  14.7 0.0 copy-start.3
  14.7 0.0 copy-start.8
  14.7 0.5 convolution_add_fusion.7
  15.2 0.0 copy-start.4
  15.2 0.5 convolution_add_fusion.6
  15.7 0.5 convolution_add_fusion.5
  16.1 0.5 convolution_add_fusion.4
  16.6 0.5 convolution_add_fusion.3
  17.1 0.0 copy-start.10
  17.1 0.5 convolution_add_fusion.2
  17.5 0.0 copy-done.3
  17.5 0.0 copy-done.8
  17.6 0.5 fusion.4.refs_3_
  18.0 0.0 copy-start.2
  18.0 0.1 collective-permute-start.2
  18.1 0.1 collective-permute-start.3
  18.2 0.4 collective-permute-start.4
  18.6 0.0 copy-done.4
  18.6 1.3 %copy.11 = bf16[640,640]{0,1:T(8,128)(2,1)} copy(bf16[640,640]{1,0:T(8,128)(2,1)S(1)} %copy-done.4) | data formatting | bytes 1638400 | tf_op args[5]
  20.0 0.0 copy-done
  20.0 1.2 %convolution_convert_fusion.after_ref.refs_0_ = bf16[256,640]{1,0:T(8,128)(2,1)} fusion(bf16[256,640]{1,0:T(8,128)(2,1)S(1)} %fusion.4.refs_3_, bf16[640,640]{1,0:T(8,128)(2,1)S(1)} %copy-done), kind=kOutput, calls=%fused_computation.15 | convolution fusion | flops 209879040 | bytes 1474560 | tf_op jit(solution)/shard_map/dot_general | solution.py:221
  21.1 41.0 %shard_map.104 = bf16[64,16,640]{2,1,0:T(8,128)(2,1)} custom-call(bf16[1,16,640]{2,1,0:T(8,128)(2,1)} %bitcast.69, bf16[256,640]{1,0:T(8,128)(2,1)} %convolution_convert_fusion.after_ref.refs_0_), custom_call_target="tpu_custom_call" | custom-call | tf_op jit(solution)/shard_map/pallas_call | solution.py:94
  62.2 0.0 collective-permute-done.2.refs_4_
  62.2 0.0 copy-start.5
  62.2 0.0 collective-permute-done.3.refs_5_
  62.2 0.0 copy-start.6
  62.2 0.0 collective-permute-done.4.refs_6_
  62.3 0.0 copy-start.7
  62.3 0.0 copy-done.2
  62.3 0.7 copy-done.5
  62.9 0.1 copy-done.6
  63.1 0.1 copy-done.7
  63.2 15.0 %shard_map.105 = bf16[256,640]{1,0:T(8,128)(2,1)} custom-call(bf16[256,640]{1,0:T(8,128)(2,1)} %convolution_convert_fusion.after_ref.refs_0_, bf16[640,640]{1,0:T(8,128)(2,1)} %bitcast.58, bf16[640,640]{1,0:T(8,128)(2,1)} %refs_2_.1, bf16[256,640]{1,0:T(8,128)(2,1)} %copy-done.2, bf16[256,640]{1,0:T(8,128)(2,1)} %copy-done.5, bf16[256,640]{1,0:T(8,128)(2,1)} %copy-done.6, ...), custom_call_target="tpu_custom_call" | custom-call | tf_op jit(solution)/shard_map/pallas_call | solution.py:174
  78.2 0.0 copy-done.10
  78.2 2.2 %fusion.3 = bf16[256,640]{1,0:T(8,128)(2,1)} fusion(bf16[256,640]{1,0:T(8,128)(2,1)} %shard_map.105, bf16[640,640]{1,0:T(8,128)(2,1)S(1)} %copy-done.9, f32[640]{0:T(1024)S(1)} %copy-done.10), kind=kOutput, calls=%fused_computation.13 | convolution fusion | flops 210042880 | bytes 1477120 | tf_op jit(solution)/shard_map/dot_general | solution.py:225
  (3 shorter events, 0.0 us)
Async XLA Ops:
  0.6 19.3 %copy-start = (bf16[640,640]{1,0:T(8,128)(2,1)S(1)}, bf16[640,640]{1,0:T(8,128)(2,1)}, u32[]{:S(2)}) copy-start(bf16[640,640]{1,0:T(8,128)(2,1)} %param.13) | copy-start | bytes 2457604
  0.6 13.5 %copy-start.1 = (bf16[3,3,640,640]{3,2,1,0:T(8,128)(2,1)S(1)}, bf16[3,3,640,640]{3,2,1,0:T(8,128)(2,1)}, u32[]{:S(2)}) copy-start(bf16[3,3,640,640]{3,2,1,0:T(8,128)(2,1)} %param.10) | copy-start | bytes 22118404
  2.0 6.8 %collective-permute-start = (bf16[1,1,32,640]{3,2,1,0:T(8,128)(2,1)S(1)}, bf16[1,1,32,640]{3,2,1,0:T(8,128)(2,1)S(1)}, u32[]{:S(2)}, u32[]{:S(2)}) collective-permute-start(bf16[1,1,32,640]{3,2,1,0:T(8,128)(2,1)S(1)} %get-tuple-element.10), channel_id=1, source_target_pairs={{0,1},{1,2},{2,3},{4,5},{5,6},{6,7},{8,9},{9,10},{10,11},{12,13},{... | collective-permute-start | bytes 122888 | tf_op jit(solution)/shard_map/ppermute | solution.py:112
  6.9 5.3 %collective-permute-start.1 = (bf16[1,1,32,640]{3,2,1,0:T(8,128)(2,1)S(1)}, bf16[1,1,32,640]{3,2,1,0:T(8,128)(2,1)S(1)}, u32[]{:S(2)}, u32[]{:S(2)}) collective-permute-start(bf16[1,1,32,640]{3,2,1,0:T(8,128)(2,1)S(1)} %get-tuple-element.11), channel_id=1, source_target_pairs={{1,0},{2,1},{3,2},{5,4},{6,5},{7,6},{9,8},{10,9},{11,10},{13,12},{... | collective-permute-start | bytes 122888 | tf_op jit(solution)/shard_map/ppermute | solution.py:113
  14.7 2.8 %copy-start.3 = (bf16[1,8,32,640]{3,2,1,0:T(8,128)(2,1)S(1)}, bf16[1,8,32,640]{3,2,1,0:T(8,128)(2,1)}, u32[]{:S(2)}) copy-start(bf16[1,8,32,640]{3,2,1,0:T(8,128)(2,1)} %param.9) | copy-start | bytes 983044
  14.7 2.8 %copy-start.8 = (f32[640]{0:T(1024)S(1)}, f32[640]{0:T(1024)}, u32[]{:S(2)}) copy-start(f32[640]{0:T(1024)} %param.11) | copy-start | bytes 7684
  15.2 3.4 %copy-start.4 = (bf16[640,640]{1,0:T(8,128)(2,1)S(1)}, bf16[640,640]{1,0:T(8,128)(2,1)}, u32[]{:S(2)}) copy-start(bf16[640,640]{1,0:T(8,128)(2,1)} %param.14) | copy-start | bytes 2457604
  17.1 61.1 %copy-start.10 = (f32[640]{0:T(1024)S(1)}, f32[640]{0:T(1024)}, u32[]{:S(2)}) copy-start(f32[640]{0:T(1024)} %param.17) | copy-start | bytes 7684
  18.0 44.2 %copy-start.2 = (bf16[256,640]{1,0:T(8,128)(2,1)}, bf16[256,640]{1,0:T(8,128)(2,1)S(1)}, u32[]{:S(2)}) copy-start(bf16[256,640]{1,0:T(8,128)(2,1)S(1)} %fusion.4.refs_3_) | copy-start | bytes 983044
  18.0 44.2 %collective-permute-start.2 = (bf16[256,640]{1,0:T(8,128)(2,1)S(1)}, bf16[256,640]{1,0:T(8,128)(2,1)S(1)}, u32[]{:S(2)}, u32[]{:S(2)}) collective-permute-start(bf16[256,640]{1,0:T(8,128)(2,1)S(1)} %fusion.4.refs_3_), channel_id=1, source_target_pairs={{0,1},{1,2},{2,3},{3,0},{4,5},{5,6},{6,7},{7,4},{8,9},{9,10},{10,1... | collective-permute-start | bytes 983048 | tf_op jit(solution)/shard_map/ppermute | solution.py:218
  18.1 44.1 %collective-permute-start.3 = (bf16[256,640]{1,0:T(8,128)(2,1)S(1)}, bf16[256,640]{1,0:T(8,128)(2,1)S(1)}, u32[]{:S(2)}, u32[]{:S(2)}) collective-permute-start(bf16[256,640]{1,0:T(8,128)(2,1)S(1)} %fusion.4.refs_3_), channel_id=1, source_target_pairs={{0,2},{1,3},{2,0},{3,1},{4,6},{5,7},{6,4},{7,5},{8,10},{9,11},{10,... | collective-permute-start | bytes 983048 | tf_op jit(solution)/shard_map/ppermute | solution.py:218
  18.2 44.0 %collective-permute-start.4 = (bf16[256,640]{1,0:T(8,128)(2,1)S(1)}, bf16[256,640]{1,0:T(8,128)(2,1)S(1)}, u32[]{:S(2)}, u32[]{:S(2)}) collective-permute-start(bf16[256,640]{1,0:T(8,128)(2,1)S(1)} %fusion.4.refs_3_), channel_id=1, source_target_pairs={{0,3},{1,0},{2,1},{3,2},{4,7},{5,4},{6,5},{7,6},{8,11},{9,8},{10,9... | collective-permute-start | bytes 983048 | tf_op jit(solution)/shard_map/ppermute | solution.py:218
  20.0 58.2 %copy-start.9 = (bf16[640,640]{1,0:T(8,128)(2,1)S(1)}, bf16[640,640]{1,0:T(8,128)(2,1)}, u32[]{:S(2)}) copy-start(bf16[640,640]{1,0:T(8,128)(2,1)} %param.16) | copy-start | bytes 2457604
  62.2 0.7 copy-start.5
  62.2 0.8 %copy-start.6 = (bf16[256,640]{1,0:T(8,128)(2,1)}, bf16[256,640]{1,0:T(8,128)(2,1)S(1)}, u32[]{:S(2)}) copy-start(bf16[256,640]{1,0:T(8,128)(2,1)S(1)} %collective-permute-done.3.refs_5_) | copy-start | bytes 983044
  62.3 0.9 %copy-start.7 = (bf16[256,640]{1,0:T(8,128)(2,1)}, bf16[256,640]{1,0:T(8,128)(2,1)S(1)}, u32[]{:S(2)}) copy-start(bf16[256,640]{1,0:T(8,128)(2,1)S(1)} %collective-permute-done.4.refs_6_) | copy-start | bytes 983044

commit v14 on v12

--- a/solution.py
+++ b/solution.py
@@ -147,14 +147,14 @@
 
 
 def attention_kernel(heads, parts, *refs):
-    q_ref, wk_ref, wv_ref = refs[:3]
-    sources = refs[3 : 3 + parts]
-    o_ref, k_ref, v_ref = refs[3 + parts :]
+    q_ref, wk_ref, wv_ref, wo_ref, bias_ref = refs[:5]
+    sources = refs[5 : 5 + parts]
+    o_ref, k_ref, v_ref, mixed_ref = refs[5 + parts :]
     offset = 0
     for source in sources:
         rows = source.shape[0]
         k_ref[:, offset : offset + rows] = lax.dot_general(
-            wk_ref[...], source[...], (((1,), (1,)), ((), ())), preferred_element_type=jnp.float32
+            wk_ref[...], source[...], (((0,), (1,)), ((), ())), preferred_element_type=jnp.float32
         ).astype(k_ref.dtype)
         v_ref[offset : offset + rows, :] = jnp.dot(
             source[...], wv_ref[...], preferred_element_type=jnp.float32
@@ -170,14 +170,16 @@
         summed = jnp.dot(
             weights.astype(jnp.bfloat16), v_ref[:, lanes], preferred_element_type=jnp.float32
         )
-        o_ref[:, lanes] = (summed / total).astype(o_ref.dtype)
-
-
-def attention(query, w_key_t, w_value, sources, heads):
+        mixed_ref[:, lanes] = (summed / total).astype(mixed_ref.dtype)
+    attended = jnp.dot(mixed_ref[...], wo_ref[...], preferred_element_type=jnp.float32)
+    o_ref[...] = (attended + bias_ref[...]).astype(o_ref.dtype)
+
+
+def attention(query, w_key, w_value, w_out, out_bias, sources, heads):
     tokens, channels = query.shape
     length = sum(source.shape[0] for source in sources)
     whole = lambda array: pl.BlockSpec(array.shape, lambda i: (0, 0))
-    operands = (query, w_key_t, w_value) + tuple(sources)
+    operands = (query, w_key, w_value, w_out, out_bias.reshape(1, -1)) + tuple(sources)
     return pl.pallas_call(
         functools.partial(attention_kernel, heads, len(sources)),
         out_shape=jax.ShapeDtypeStruct((tokens, channels), jnp.bfloat16),
@@ -187,6 +189,7 @@
         scratch_shapes=[
             pltpu.VMEM((channels, length), jnp.bfloat16),
             pltpu.VMEM((length, channels), jnp.bfloat16),
+            pltpu.VMEM((tokens, channels), jnp.bfloat16),
         ],
     )(*operands)
 
@@ -228,10 +231,7 @@
     query = jnp.dot(hidden, w_query, preferred_element_type=jnp.float32).astype(jnp.bfloat16)
     every_feature = staged_gather(ref_features, query)
     sources = [hidden] + others + [every_feature]
-    mixed = attention(query, jnp.transpose(w_key), w_value, sources, heads)
-    attended = (jnp.dot(mixed, w_out, preferred_element_type=jnp.float32) + out_bias).astype(
-        jnp.bfloat16
-    )
+    attended = attention(query, w_key, w_value, w_out, out_bias, sources, heads)
     return (
         hidden.reshape(count, band_rows, width, channels),
         attended.reshape(count, band_rows, width, channels),

time: 73.9 us -> 71.5 us (0.968)
  matrix products: 8.61 us -> 6.45 us
    dot_general x1 -> x0, matrix products: 2.16 us -> none  [shards(): jnp.dot(mixed, w_out, preferred_element_type=jnp.float32) + out_bias]
    unnamed x23 -> x18, local copies, waits for them, and re-layouts: 2.26 us -> 0.97 us
  transfers between devices with their start and end apart: 5 -> 5, of which waited for: 1 -> 1; matrix products, arithmetic and copies ran while one was open for 3% -> 2% of each run, Pallas kernels for 47% -> 48%
where the time goes in v14:
time: 71.5 us; the launch traced here: 71.3 us
  Pallas kernels  49.9 us (70%)
  starting transfers between devices  7.35 us (10%)
  matrix products  6.45 us (9%)
  waiting for transfers between devices  3.39 us (5%)
  local copies, waits for them, and re-layouts  1.77 us (2%)
  other arithmetic  1.54 us (2%)
  between operations  0.9 us (1%)
    pallas_call x1, Pallas kernels, staged_gather(): pl.pallas_call(functools.partial(staged_kernel, sizes), out_shape=jax.Sha...  34.4 us
    pallas_call x1, Pallas kernels, attention(): pl.pallas_call(functools.partial(attention_kernel, heads, len(sources)),...  15.5 us
    dot_general x9, matrix products, shards(): jnp.dot(window, conv_weight[row_tap, col_tap], preferred_element_type=jnp...  5.27 us
    ppermute x1, starting transfers between devices, extended(): before = lax.ppermute(last, axis, up)  4.86 us
    ppermute x1, waiting for transfers between devices, extended(): after = lax.ppermute(initial, axis, down)  3.38 us
    ppermute x1, starting transfers between devices, extended(): after = lax.ppermute(initial, axis, down)  1.92 us
  transfers between devices with their start and end apart: 5, of which 1 were waited for; matrix products, arithmetic and copies ran while one was open for 2% of the time, Pallas kernels for 48%

profile of v14, /device:TPU:1, one launch (start us, length us, event | category | flops | bytes accessed | tf_op | source)
XLA Modules:
  0.0 71.3 jit_solution(4818333217328094460)
XLA Ops:
  0.6 0.0 copy-start
  0.6 0.0 copy-start.1
  0.7 1.3 %multiply_convert_fusion = bf16[1,8,32,640]{3,2,1,0:T(8,128)(2,1)S(1)} fusion(bf16[1,8,32,640]{3,2,1,0:T(8,128)(2,1)} %param.9), kind=kLoop, calls=%fused_computation.35 | loop fusion | flops 983040 | bytes 655360 | tf_op jit(solution)/shard_map/convert_element_type | solution.py:211
  2.0 4.9 %collective-permute-start = (bf16[1,1,32,640]{3,2,1,0:T(8,128)(2,1)S(1)}, bf16[1,1,32,640]{3,2,1,0:T(8,128)(2,1)S(1)}, u32[]{:S(2)}, u32[]{:S(2)}) collective-permute-start(bf16[1,1,32,640]{3,2,1,0:T(8,128)(2,1)S(1)} %get-tuple-element.10), channel_id=1, source_target_pairs={{0,1},{1,2},{2,3},{4,5},{5,6},{6,7},{8,9},{9,10},{10,11},{12,13},{... | collective-permute-start | bytes 122888 | tf_op jit(solution)/shard_map/ppermute | solution.py:119
  6.9 1.9 %collective-permute-start.1 = (bf16[1,1,32,640]{3,2,1,0:T(8,128)(2,1)S(1)}, bf16[1,1,32,640]{3,2,1,0:T(8,128)(2,1)S(1)}, u32[]{:S(2)}, u32[]{:S(2)}) collective-permute-start(bf16[1,1,32,640]{3,2,1,0:T(8,128)(2,1)S(1)} %get-tuple-element.11), channel_id=1, source_target_pairs={{1,0},{2,1},{3,2},{5,4},{6,5},{7,6},{9,8},{10,9},{11,10},{13,12},{... | collective-permute-start | bytes 122888 | tf_op jit(solution)/shard_map/ppermute | solution.py:120
  8.8 0.0 collective-permute-done
  8.8 3.4 %collective-permute-done.1 = bf16[1,1,32,640]{3,2,1,0:T(8,128)(2,1)S(1)} collective-permute-done((bf16[1,1,32,640]{3,2,1,0:T(8,128)(2,1)S(1)}, bf16[1,1,32,640]{3,2,1,0:T(8,128)(2,1)S(1)}, u32[]{:S(2)}, u32[]{:S(2)}) %collective-permute-start.1) | collective-permute-done | bytes 40992 | tf_op jit(solution)/shard_map/ppermute | solution.py:120
  12.2 0.2 fusion.29
  12.4 0.2 fusion.30
  12.6 1.6 %fusion.14 = f32[256,640]{1,0:T(8,128)S(1)} fusion(bf16[256,640]{1,0:T(8,128)(2,1)S(1)} %bitcast.64, bf16[3,3,640,640]{3,2,1,0:T(8,128)(2,1)} %param.10), kind=kOutput, calls=%fused_computation.24 | convolution fusion | flops 209715200 | bytes 1802240 | tf_op jit(solution)/shard_map/dot_general | solution.py:220
  14.2 0.0 copy-done.1
  14.2 0.5 fusion.5
  14.6 0.1 pad_maximum_fusion
  14.7 0.0 copy-start.3
  14.7 0.0 copy-start.7
  14.7 0.5 convolution_add_fusion.6
  15.2 0.0 copy-start.8
  15.2 0.5 convolution_add_fusion.5
  15.7 0.5 convolution_add_fusion.4
  16.1 0.5 convolution_add_fusion.3
  16.6 0.5 convolution_add_fusion.2
  17.1 0.5 convolution_add_fusion.1
  17.5 0.0 copy-done.3
  17.5 0.0 copy-done.7
  17.5 0.5 fusion.3.refs_5_
  18.0 0.0 copy-start.2
  18.0 0.1 collective-permute-start.2
  18.1 0.1 collective-permute-start.3
  18.2 0.4 collective-permute-start.4
  18.6 0.0 copy-done.8
  18.6 0.6 reshape.57.refs_4_
  19.2 0.0 copy-done
  19.2 1.2 %convolution_convert_fusion.after_ref.refs_0_ = bf16[256,640]{1,0:T(8,128)(2,1)} fusion(bf16[256,640]{1,0:T(8,128)(2,1)S(1)} %fusion.3.refs_5_, bf16[640,640]{1,0:T(8,128)(2,1)S(1)} %copy-done), kind=kOutput, calls=%fused_computation.13 | convolution fusion | flops 209879040 | bytes 1474560 | tf_op jit(solution)/shard_map/dot_general | solution.py:231
  20.4 34.4 %shard_map.104 = bf16[64,16,640]{2,1,0:T(8,128)(2,1)} custom-call(bf16[1,16,640]{2,1,0:T(8,128)(2,1)} %bitcast.66, bf16[256,640]{1,0:T(8,128)(2,1)} %convolution_convert_fusion.after_ref.refs_0_), custom_call_target="tpu_custom_call" | custom-call | tf_op jit(solution)/shard_map/pallas_call | solution.py:101
  54.8 0.0 collective-permute-done.2.refs_6_
  54.8 0.0 copy-start.4
  54.8 0.0 collective-permute-done.3.refs_7_
  54.9 0.0 copy-start.5
  54.9 0.0 collective-permute-done.4.refs_8_
  54.9 0.0 copy-start.6
  54.9 0.0 copy-done.2
  54.9 0.7 copy-done.4
  55.6 0.1 copy-done.5
  55.7 0.2 copy-done.6
  55.8 15.5 %shard_map.105 = bf16[256,640]{1,0:T(8,128)(2,1)} custom-call(bf16[256,640]{1,0:T(8,128)(2,1)} %convolution_convert_fusion.after_ref.refs_0_, bf16[640,640]{1,0:T(8,128)(2,1)} %refs_1_.1, bf16[640,640]{1,0:T(8,128)(2,1)} %refs_2_.1, bf16[640,640]{1,0:T(8,128)(2,1)} %refs_3_.1, f32[1,640]{1,0:T(1,128)} %reshape.57.refs_4_, bf16[256,640]{1,0:T(8,128)(2,1)} %copy-done.2, ...), custom_call_target="tpu_custom_call" | custom-call | tf_op jit(solution)/shard_map/pallas_call | solution.py:183
  (1 shorter events, 0.0 us)
Async XLA Ops:
  0.6 18.6 %copy-start = (bf16[640,640]{1,0:T(8,128)(2,1)S(1)}, bf16[640,640]{1,0:T(8,128)(2,1)}, u32[]{:S(2)}) copy-start(bf16[640,640]{1,0:T(8,128)(2,1)} %param.13) | copy-start | bytes 2457604
  0.6 13.5 %copy-start.1 = (bf16[3,3,640,640]{3,2,1,0:T(8,128)(2,1)S(1)}, bf16[3,3,640,640]{3,2,1,0:T(8,128)(2,1)}, u32[]{:S(2)}) copy-start(bf16[3,3,640,640]{3,2,1,0:T(8,128)(2,1)} %param.10) | copy-start | bytes 22118404
  2.0 6.8 %collective-permute-start = (bf16[1,1,32,640]{3,2,1,0:T(8,128)(2,1)S(1)}, bf16[1,1,32,640]{3,2,1,0:T(8,128)(2,1)S(1)}, u32[]{:S(2)}, u32[]{:S(2)}) collective-permute-start(bf16[1,1,32,640]{3,2,1,0:T(8,128)(2,1)S(1)} %get-tuple-element.10), channel_id=1, source_target_pairs={{0,1},{1,2},{2,3},{4,5},{5,6},{6,7},{8,9},{9,10},{10,11},{12,13},{... | collective-permute-start | bytes 122888 | tf_op jit(solution)/shard_map/ppermute | solution.py:119
  6.9 5.3 %collective-permute-start.1 = (bf16[1,1,32,640]{3,2,1,0:T(8,128)(2,1)S(1)}, bf16[1,1,32,640]{3,2,1,0:T(8,128)(2,1)S(1)}, u32[]{:S(2)}, u32[]{:S(2)}) collective-permute-start(bf16[1,1,32,640]{3,2,1,0:T(8,128)(2,1)S(1)} %get-tuple-element.11), channel_id=1, source_target_pairs={{1,0},{2,1},{3,2},{5,4},{6,5},{7,6},{9,8},{10,9},{11,10},{13,12},{... | collective-permute-start | bytes 122888 | tf_op jit(solution)/shard_map/ppermute | solution.py:120
  14.7 2.8 %copy-start.3 = (bf16[1,8,32,640]{3,2,1,0:T(8,128)(2,1)S(1)}, bf16[1,8,32,640]{3,2,1,0:T(8,128)(2,1)}, u32[]{:S(2)}) copy-start(bf16[1,8,32,640]{3,2,1,0:T(8,128)(2,1)} %param.9) | copy-start | bytes 983044
  14.7 2.8 %copy-start.7 = (f32[640]{0:T(1024)S(1)}, f32[640]{0:T(1024)}, u32[]{:S(2)}) copy-start(f32[640]{0:T(1024)} %param.11) | copy-start | bytes 7684
  15.2 3.4 %copy-start.8 = (f32[640]{0:T(1024)S(1)}, f32[640]{0:T(1024)}, u32[]{:S(2)}) copy-start(f32[640]{0:T(1024)} %param.17) | copy-start | bytes 7684
  18.0 36.9 %copy-start.2 = (bf16[256,640]{1,0:T(8,128)(2,1)}, bf16[256,640]{1,0:T(8,128)(2,1)S(1)}, u32[]{:S(2)}) copy-start(bf16[256,640]{1,0:T(8,128)(2,1)S(1)} %fusion.3.refs_5_) | copy-start | bytes 983044
  18.0 36.8 %collective-permute-start.2 = (bf16[256,640]{1,0:T(8,128)(2,1)S(1)}, bf16[256,640]{1,0:T(8,128)(2,1)S(1)}, u32[]{:S(2)}, u32[]{:S(2)}) collective-permute-start(bf16[256,640]{1,0:T(8,128)(2,1)S(1)} %fusion.3.refs_5_), channel_id=1, source_target_pairs={{0,1},{1,2},{2,3},{3,0},{4,5},{5,6},{6,7},{7,4},{8,9},{9,10},{10,1... | collective-permute-start | bytes 983048 | tf_op jit(solution)/shard_map/ppermute | solution.py:228
  18.1 36.7 %collective-permute-start.3 = (bf16[256,640]{1,0:T(8,128)(2,1)S(1)}, bf16[256,640]{1,0:T(8,128)(2,1)S(1)}, u32[]{:S(2)}, u32[]{:S(2)}) collective-permute-start(bf16[256,640]{1,0:T(8,128)(2,1)S(1)} %fusion.3.refs_5_), channel_id=1, source_target_pairs={{0,2},{1,3},{2,0},{3,1},{4,6},{5,7},{6,4},{7,5},{8,10},{9,11},{10,... | collective-permute-start | bytes 983048 | tf_op jit(solution)/shard_map/ppermute | solution.py:228
  18.2 36.6 %collective-permute-start.4 = (bf16[256,640]{1,0:T(8,128)(2,1)S(1)}, bf16[256,640]{1,0:T(8,128)(2,1)S(1)}, u32[]{:S(2)}, u32[]{:S(2)}) collective-permute-start(bf16[256,640]{1,0:T(8,128)(2,1)S(1)} %fusion.3.refs_5_), channel_id=1, source_target_pairs={{0,3},{1,0},{2,1},{3,2},{4,7},{5,4},{6,5},{7,6},{8,11},{9,8},{10,9... | collective-permute-start | bytes 983048 | tf_op jit(solution)/shard_map/ppermute | solution.py:228
  54.8 0.7 %copy-start.4 = (bf16[256,640]{1,0:T(8,128)(2,1)}, bf16[256,640]{1,0:T(8,128)(2,1)S(1)}, u32[]{:S(2)}) copy-start(bf16[256,640]{1,0:T(8,128)(2,1)S(1)} %collective-permute-done.2.refs_6_) | copy-start | bytes 983044
  54.9 0.8 %copy-start.5 = (bf16[256,640]{1,0:T(8,128)(2,1)}, bf16[256,640]{1,0:T(8,128)(2,1)S(1)}, u32[]{:S(2)}) copy-start(bf16[256,640]{1,0:T(8,128)(2,1)S(1)} %collective-permute-done.3.refs_7_) | copy-start | bytes 983044
  54.9 0.9 %copy-start.6 = (bf16[256,640]{1,0:T(8,128)(2,1)}, bf16[256,640]{1,0:T(8,128)(2,1)S(1)}, u32[]{:S(2)}) copy-start(bf16[256,640]{1,0:T(8,128)(2,1)S(1)} %collective-permute-done.4.refs_8_) | copy-start | bytes 983044

commit v15 on v14

--- a/solution.py
+++ b/solution.py
@@ -147,9 +147,12 @@
 
 
 def attention_kernel(heads, parts, *refs):
-    q_ref, wk_ref, wv_ref, wo_ref, bias_ref = refs[:5]
+    wq_ref, wk_ref, wv_ref, wo_ref, bias_ref = refs[:5]
     sources = refs[5 : 5 + parts]
-    o_ref, k_ref, v_ref, mixed_ref = refs[5 + parts :]
+    o_ref, k_ref, v_ref, mixed_ref, q_ref = refs[5 + parts :]
+    q_ref[...] = jnp.dot(
+        sources[0][...], wq_ref[...], preferred_element_type=jnp.float32
+    ).astype(q_ref.dtype)
     offset = 0
     for source in sources:
         rows = source.shape[0]
@@ -175,11 +178,11 @@
     o_ref[...] = (attended + bias_ref[...]).astype(o_ref.dtype)
 
 
-def attention(query, w_key, w_value, w_out, out_bias, sources, heads):
-    tokens, channels = query.shape
+def attention(w_query, w_key, w_value, w_out, out_bias, sources, heads):
+    tokens, channels = sources[0].shape
     length = sum(source.shape[0] for source in sources)
     whole = lambda array: pl.BlockSpec(array.shape, lambda i: (0, 0))
-    operands = (query, w_key, w_value, w_out, out_bias.reshape(1, -1)) + tuple(sources)
+    operands = (w_query, w_key, w_value, w_out, out_bias.reshape(1, -1)) + tuple(sources)
     return pl.pallas_call(
         functools.partial(attention_kernel, heads, len(sources)),
         out_shape=jax.ShapeDtypeStruct((tokens, channels), jnp.bfloat16),
@@ -189,6 +192,7 @@
         scratch_shapes=[
             pltpu.VMEM((channels, length), jnp.bfloat16),
             pltpu.VMEM((length, channels), jnp.bfloat16),
+            pltpu.VMEM((tokens, channels), jnp.bfloat16),
             pltpu.VMEM((tokens, channels), jnp.bfloat16),
         ],
     )(*operands)
@@ -228,10 +232,9 @@
         lax.ppermute(hidden, ROW_PARTS, [(j, (j + shift) % rows) for j in range(rows)])
         for shift in range(1, rows)
     ]
-    query = jnp.dot(hidden, w_query, preferred_element_type=jnp.float32).astype(jnp.bfloat16)
-    every_feature = staged_gather(ref_features, query)
+    every_feature = staged_gather(ref_features, hidden)
     sources = [hidden] + others + [every_feature]
-    attended = attention(query, w_key, w_value, w_out, out_bias, sources, heads)
+    attended = attention(w_query, w_key, w_value, w_out, out_bias, sources, heads)
     return (
         hidden.reshape(count, band_rows, width, channels),
         attended.reshape(count, band_rows, width, channels),

time: 71.5 us -> 70.7 us (0.989)
  matrix products: 6.45 us -> 5.27 us
    dot_general x1 -> x0, matrix products: 1.18 us -> none  [shards(): jnp.dot(hidden, w_query, preferred_element_type=jnp.float32)]
  transfers between devices with their start and end apart: 5 -> 5, of which waited for: 1 -> 1; matrix products, arithmetic and copies ran while one was open for 2% -> 1% of each run, Pallas kernels for 48% -> 49%
where the time goes in v15:
time: 70.7 us; the launch traced here: 70.5 us
  Pallas kernels  50.4 us (71%)
  starting transfers between devices  7.35 us (10%)
  matrix products  5.27 us (7%)
  waiting for transfers between devices  3.39 us (5%)
  local copies, waits for them, and re-layouts  1.71 us (2%)
  other arithmetic  1.54 us (2%)
  between operations  0.88 us (1%)
    pallas_call x1, Pallas kernels, staged_gather(): pl.pallas_call(functools.partial(staged_kernel, sizes), out_shape=jax.Sha...  34.4 us
    pallas_call x1, Pallas kernels, attention(): pl.pallas_call(functools.partial(attention_kernel, heads, len(sources)),...  16 us
    dot_general x9, matrix products, shards(): jnp.dot(window, conv_weight[row_tap, col_tap], preferred_element_type=jnp...  5.27 us
    ppermute x1, starting transfers between devices, extended(): before = lax.ppermute(last, axis, up)  4.86 us
    ppermute x1, waiting for transfers between devices, extended(): after = lax.ppermute(initial, axis, down)  3.38 us
    ppermute x1, starting transfers between devices, extended(): after = lax.ppermute(initial, axis, down)  1.92 us
  transfers between devices with their start and end apart: 5, of which 1 were waited for; matrix products, arithmetic and copies ran while one was open for 1% of the time, Pallas kernels for 49%

profile of v15, /device:TPU:1, one launch (start us, length us, event | category | flops | bytes accessed | tf_op | source)
XLA Modules:
  0.0 70.5 jit_solution(41141359391841020)
XLA Ops:
  0.6 0.0 copy-start
  0.6 1.3 %multiply_convert_fusion = bf16[1,8,32,640]{3,2,1,0:T(8,128)(2,1)S(1)} fusion(bf16[1,8,32,640]{3,2,1,0:T(8,128)(2,1)} %param.9), kind=kLoop, calls=%fused_computation.34 | loop fusion | flops 983040 | bytes 655360 | tf_op jit(solution)/shard_map/convert_element_type | solution.py:215
  2.0 4.9 %collective-permute-start = (bf16[1,1,32,640]{3,2,1,0:T(8,128)(2,1)S(1)}, bf16[1,1,32,640]{3,2,1,0:T(8,128)(2,1)S(1)}, u32[]{:S(2)}, u32[]{:S(2)}) collective-permute-start(bf16[1,1,32,640]{3,2,1,0:T(8,128)(2,1)S(1)} %get-tuple-element.10), channel_id=1, source_target_pairs={{0,1},{1,2},{2,3},{4,5},{5,6},{6,7},{8,9},{9,10},{10,11},{12,13},{... | collective-permute-start | bytes 122888 | tf_op jit(solution)/shard_map/ppermute | solution.py:119
  6.8 1.9 %collective-permute-start.1 = (bf16[1,1,32,640]{3,2,1,0:T(8,128)(2,1)S(1)}, bf16[1,1,32,640]{3,2,1,0:T(8,128)(2,1)S(1)}, u32[]{:S(2)}, u32[]{:S(2)}) collective-permute-start(bf16[1,1,32,640]{3,2,1,0:T(8,128)(2,1)S(1)} %get-tuple-element.11), channel_id=1, source_target_pairs={{1,0},{2,1},{3,2},{5,4},{6,5},{7,6},{9,8},{10,9},{11,10},{13,12},{... | collective-permute-start | bytes 122888 | tf_op jit(solution)/shard_map/ppermute | solution.py:120
  8.8 0.0 collective-permute-done
  8.8 3.4 %collective-permute-done.1 = bf16[1,1,32,640]{3,2,1,0:T(8,128)(2,1)S(1)} collective-permute-done((bf16[1,1,32,640]{3,2,1,0:T(8,128)(2,1)S(1)}, bf16[1,1,32,640]{3,2,1,0:T(8,128)(2,1)S(1)}, u32[]{:S(2)}, u32[]{:S(2)}) %collective-permute-start.1) | collective-permute-done | bytes 40992 | tf_op jit(solution)/shard_map/ppermute | solution.py:120
  12.2 0.2 fusion.29
  12.3 0.2 fusion.30
  12.5 1.6 %fusion.14 = f32[256,640]{1,0:T(8,128)S(1)} fusion(bf16[256,640]{1,0:T(8,128)(2,1)S(1)} %bitcast.62, bf16[3,3,640,640]{3,2,1,0:T(8,128)(2,1)} %param.10), kind=kOutput, calls=%fused_computation.23 | convolution fusion | flops 209715200 | bytes 1802240 | tf_op jit(solution)/shard_map/dot_general | solution.py:224
  14.2 0.0 copy-done
  14.2 0.5 fusion.5
  14.6 0.1 pad_maximum_fusion
  14.7 0.0 copy-start.2
  14.7 0.0 copy-start.6
  14.7 0.5 convolution_add_fusion.6
  15.2 0.0 copy-start.7
  15.2 0.5 convolution_add_fusion.5
  15.7 0.5 convolution_add_fusion.4
  16.1 0.5 convolution_add_fusion.3
  16.6 0.5 convolution_add_fusion.2
  17.0 0.5 convolution_add_fusion.1
  17.5 0.0 copy-done.2
  17.5 0.0 copy-done.6
  17.5 0.5 fusion.3.after_ref.refs_5_
  18.0 0.0 copy-start.1
  18.0 0.1 collective-permute-start.2
  18.1 0.1 collective-permute-start.3
  18.2 0.4 collective-permute-start.4
  18.6 0.0 copy-done.7
  18.6 0.6 reshape.57.refs_4_
  19.2 0.0 copy-done.1
  19.2 34.4 %shard_map.104 = bf16[64,16,640]{2,1,0:T(8,128)(2,1)} custom-call(bf16[1,16,640]{2,1,0:T(8,128)(2,1)} %bitcast.64, bf16[256,640]{1,0:T(8,128)(2,1)} %copy-done.1), custom_call_target="tpu_custom_call" | custom-call | tf_op jit(solution)/shard_map/pallas_call | solution.py:101
  53.6 0.0 collective-permute-done.2.refs_6_
  53.6 0.0 copy-start.3
  53.6 0.0 collective-permute-done.3.refs_7_
  53.7 0.0 copy-start.4
  53.7 0.0 collective-permute-done.4.refs_8_
  53.7 0.0 copy-start.5
  53.7 0.7 copy-done.3
  54.4 0.1 copy-done.4
  54.5 0.1 copy-done.5
  54.6 16.0 %shard_map.105 = bf16[256,640]{1,0:T(8,128)(2,1)} custom-call(bf16[640,640]{1,0:T(8,128)(2,1)} %refs_0_.1, bf16[640,640]{1,0:T(8,128)(2,1)} %refs_1_.1, bf16[640,640]{1,0:T(8,128)(2,1)} %refs_2_.1, bf16[640,640]{1,0:T(8,128)(2,1)} %refs_3_.1, f32[1,640]{1,0:T(1,128)} %reshape.57.refs_4_, bf16[256,640]{1,0:T(8,128)(2,1)} %copy-done.1, ...), custom_call_target="tpu_custom_call" | custom-call | tf_op jit(solution)/shard_map/pallas_call | solution.py:186
  (1 shorter events, 0.0 us)
Async XLA Ops:
  0.6 13.5 %copy-start = (bf16[3,3,640,640]{3,2,1,0:T(8,128)(2,1)S(1)}, bf16[3,3,640,640]{3,2,1,0:T(8,128)(2,1)}, u32[]{:S(2)}) copy-start(bf16[3,3,640,640]{3,2,1,0:T(8,128)(2,1)} %param.10) | copy-start | bytes 22118404
  2.0 6.8 %collective-permute-start = (bf16[1,1,32,640]{3,2,1,0:T(8,128)(2,1)S(1)}, bf16[1,1,32,640]{3,2,1,0:T(8,128)(2,1)S(1)}, u32[]{:S(2)}, u32[]{:S(2)}) collective-permute-start(bf16[1,1,32,640]{3,2,1,0:T(8,128)(2,1)S(1)} %get-tuple-element.10), channel_id=1, source_target_pairs={{0,1},{1,2},{2,3},{4,5},{5,6},{6,7},{8,9},{9,10},{10,11},{12,13},{... | collective-permute-start | bytes 122888 | tf_op jit(solution)/shard_map/ppermute | solution.py:119
  6.8 5.3 %collective-permute-start.1 = (bf16[1,1,32,640]{3,2,1,0:T(8,128)(2,1)S(1)}, bf16[1,1,32,640]{3,2,1,0:T(8,128)(2,1)S(1)}, u32[]{:S(2)}, u32[]{:S(2)}) collective-permute-start(bf16[1,1,32,640]{3,2,1,0:T(8,128)(2,1)S(1)} %get-tuple-element.11), channel_id=1, source_target_pairs={{1,0},{2,1},{3,2},{5,4},{6,5},{7,6},{9,8},{10,9},{11,10},{13,12},{... | collective-permute-start | bytes 122888 | tf_op jit(solution)/shard_map/ppermute | solution.py:120
  14.7 2.8 %copy-start.2 = (bf16[1,8,32,640]{3,2,1,0:T(8,128)(2,1)S(1)}, bf16[1,8,32,640]{3,2,1,0:T(8,128)(2,1)}, u32[]{:S(2)}) copy-start(bf16[1,8,32,640]{3,2,1,0:T(8,128)(2,1)} %param.9) | copy-start | bytes 983044
  14.7 2.8 %copy-start.6 = (f32[640]{0:T(1024)S(1)}, f32[640]{0:T(1024)}, u32[]{:S(2)}) copy-start(f32[640]{0:T(1024)} %param.11) | copy-start | bytes 7684
  15.2 3.4 %copy-start.7 = (f32[640]{0:T(1024)S(1)}, f32[640]{0:T(1024)}, u32[]{:S(2)}) copy-start(f32[640]{0:T(1024)} %param.17) | copy-start | bytes 7684
  18.0 1.2 %copy-start.1 = (bf16[256,640]{1,0:T(8,128)(2,1)}, bf16[256,640]{1,0:T(8,128)(2,1)S(1)}, u32[]{:S(2)}) copy-start(bf16[256,640]{1,0:T(8,128)(2,1)S(1)} %fusion.3.after_ref.refs_5_) | copy-start | bytes 983044
  18.0 35.6 %collective-permute-start.2 = (bf16[256,640]{1,0:T(8,128)(2,1)S(1)}, bf16[256,640]{1,0:T(8,128)(2,1)S(1)}, u32[]{:S(2)}, u32[]{:S(2)}) collective-permute-start(bf16[256,640]{1,0:T(8,128)(2,1)S(1)} %fusion.3.after_ref.refs_5_), channel_id=1, source_target_pairs={{0,1},{1,2},{2,3},{3,0},{4,5},{5,6},{6,7},{7,4},{8,9},{9,10},{10,1... | collective-permute-start | bytes 983048 | tf_op jit(solution)/shard_map/ppermute | solution.py:232
  18.1 35.5 %collective-permute-start.3 = (bf16[256,640]{1,0:T(8,128)(2,1)S(1)}, bf16[256,640]{1,0:T(8,128)(2,1)S(1)}, u32[]{:S(2)}, u32[]{:S(2)}) collective-permute-start(bf16[256,640]{1,0:T(8,128)(2,1)S(1)} %fusion.3.after_ref.refs_5_), channel_id=1, source_target_pairs={{0,2},{1,3},{2,0},{3,1},{4,6},{5,7},{6,4},{7,5},{8,10},{9,11},{10,... | collective-permute-start | bytes 983048 | tf_op jit(solution)/shard_map/ppermute | solution.py:232
  18.2 35.5 %collective-permute-start.4 = (bf16[256,640]{1,0:T(8,128)(2,1)S(1)}, bf16[256,640]{1,0:T(8,128)(2,1)S(1)}, u32[]{:S(2)}, u32[]{:S(2)}) collective-permute-start(bf16[256,640]{1,0:T(8,128)(2,1)S(1)} %fusion.3.after_ref.refs_5_), channel_id=1, source_target_pairs={{0,3},{1,0},{2,1},{3,2},{4,7},{5,4},{6,5},{7,6},{8,11},{9,8},{10,9... | collective-permute-start | bytes 983048 | tf_op jit(solution)/shard_map/ppermute | solution.py:232
  53.6 0.7 %copy-start.3 = (bf16[256,640]{1,0:T(8,128)(2,1)}, bf16[256,640]{1,0:T(8,128)(2,1)S(1)}, u32[]{:S(2)}) copy-start(bf16[256,640]{1,0:T(8,128)(2,1)S(1)} %collective-permute-done.2.refs_6_) | copy-start | bytes 983044
  53.7 0.8 %copy-start.4 = (bf16[256,640]{1,0:T(8,128)(2,1)}, bf16[256,640]{1,0:T(8,128)(2,1)S(1)}, u32[]{:S(2)}) copy-start(bf16[256,640]{1,0:T(8,128)(2,1)S(1)} %collective-permute-done.3.refs_7_) | copy-start | bytes 983044
  53.7 0.9 %copy-start.5 = (bf16[256,640]{1,0:T(8,128)(2,1)}, bf16[256,640]{1,0:T(8,128)(2,1)S(1)}, u32[]{:S(2)}) copy-start(bf16[256,640]{1,0:T(8,128)(2,1)S(1)} %collective-permute-done.4.refs_8_) | copy-start | bytes 983044

commit v16 on v15

--- a/solution.py
+++ b/solution.py
@@ -42,61 +42,75 @@
     half = along // 2
     yh, xx, zz = [lax.axis_index(axis) for axis in TM_PARTS]
     low, core = [lax.axis_index(axis) for axis in ROW_PARTS]
-    me = (yh * across + xx) * along + zz
-    mine = me - zz
-    other_core = 1 - core
     z_peer = lambda shift: {"z": lax.rem(zz + shift, along)}
     x_peer = lambda shift: {"x": lax.rem(xx + shift, across)}
     y_peer = {"y_hi": 1 - yh, "y_lo": 1 - low}
-    c_peer = {"core": other_core}
+    c_peer = {"core": 1 - core}
     peers = [z_peer(s) for s in range(1, along)] + [x_peer(s) for s in range(1, across)]
     peers += [y_peer, c_peer]
     barrier = pltpu.get_barrier_semaphore()
     for peer in peers:
         pl.semaphore_signal(barrier, inc=1, device_id=peer, device_id_type=MESH)
     pl.semaphore_wait(barrier, len(peers))
-    local = pltpu.make_async_copy(x_ref, out_ref.at[pl.ds(me, 1)], local_sem)
-    local.start()
-    local.wait()
+
+    def block_of(z):
+        return ((z // half * high + yh) * across + xx) * half + lax.rem(z, half)
+
+    own = out_ref.at[pl.ds(block_of(zz), 1)]
+    mine = zz // half == core
+
+    @pl.when(mine)
+    def _():
+        local = pltpu.make_async_copy(x_ref, own, local_sem)
+        local.start()
+        local.wait()
+
+    def remote(ref, peer, send_sem, recv_sem):
+        return pltpu.make_async_remote_copy(
+            src_ref=ref,
+            dst_ref=ref,
+            send_sem=send_sem,
+            recv_sem=recv_sem,
+            device_id=peer,
+            device_id_type=MESH,
+        )
+
+    z_copies = [remote(own, z_peer(s), sems[0].at[s], sems[1].at[s]) for s in range(1, along)]
+
+    @pl.when(mine)
+    def _():
+        for copy in z_copies:
+            copy.start()
+        for copy in z_copies:
+            copy.wait_send()
+
+    for s, copy in zip(range(1, along), z_copies):
+        sender = lax.rem(zz + along - s, along)
+
+        @pl.when(sender // half == core)
+        def _():
+            copy.wait_recv()
 
     def exchange(pairs, send_sem, recv_sem):
-        copies = []
-        for index, (ref, peer) in enumerate(pairs):
-            copy = pltpu.make_async_remote_copy(
-                src_ref=ref,
-                dst_ref=ref,
-                send_sem=send_sem.at[index],
-                recv_sem=recv_sem.at[index],
-                device_id=peer,
-                device_id_type=MESH,
-            )
+        copies = [remote(ref, peer, send_sem.at[i], recv_sem.at[i]) for i, (ref, peer) in enumerate(pairs)]
+        for copy in copies:
             copy.start()
-            copies.append(copy)
         for copy in copies:
             copy.wait()
 
-    own = out_ref.at[pl.ds(me, 1)]
-    exchange([(own, z_peer(s)) for s in range(1, along)], sems[0], sems[1])
-    start = mine + core * half
-    part = out_ref.at[pl.ds(start, half)]
-    exchange([(part, x_peer(s)) for s in range(1, across)], sems[2], sems[3])
-    base = yh * across * along + core * half
-    chunks = [out_ref.at[pl.ds(base + g * along, half)] for g in range(across)]
-    exchange([(chunk, y_peer) for chunk in chunks], sems[4], sems[5])
-    regions = high * across
-    region = yh * across + xx
-    groups = []
-    for step in range(1, regions):
-        j = lax.rem(region + step, regions)
-        groups.append(out_ref.at[pl.ds(j * along + core * half, half)])
-    exchange([(chunk, c_peer) for chunk in groups], sems[6], sems[7])
+    group = out_ref.at[pl.ds(((core * high + yh) * across + xx) * half, half)]
+    exchange([(group, x_peer(s)) for s in range(1, across)], sems[2], sems[3])
+    row = out_ref.at[pl.ds((core * high + yh) * across * half, across * half)]
+    exchange([(row, y_peer)], sems[4], sems[5])
+    whole = out_ref.at[pl.ds(core * high * across * half, high * across * half)]
+    exchange([(whole, c_peer)], sems[6], sems[7])
 
 
 def staged_gather(value, after):
     sizes = [lax.axis_size(axis) for axis in TM_PARTS]
     total = sizes[0] * sizes[1] * sizes[2]
     sems = []
-    for count in (sizes[2], sizes[1], sizes[1], sizes[0] * sizes[1]):
+    for count in (sizes[2], sizes[1], 1, 1):
         sems += [pltpu.SemaphoreType.DMA((count,))] * 2
     gathered = pl.pallas_call(
         functools.partial(staged_kernel, sizes),

time: 70.7 us -> 69.1 us (0.977)
  Pallas kernels: 50.4 us -> 48.8 us
    pallas_call x1, Pallas kernels: 34.4 us -> 32.8 us  [staged_gather(): pl.pallas_call(functools.partial(staged_kernel, sizes), out_shape=jax.Sha...]
  transfers between devices with their start and end apart: 5 -> 5, of which waited for: 1 -> 1; matrix products, arithmetic and copies ran while one was open for 1% -> 1% of each run, Pallas kernels for 49% -> 48%
where the time goes in v16:
time: 69.1 us; the launch traced here: 68.9 us
  Pallas kernels  48.8 us (71%)
  starting transfers between devices  7.35 us (11%)
  matrix products  5.27 us (8%)
  waiting for transfers between devices  3.39 us (5%)
  local copies, waits for them, and re-layouts  1.71 us (2%)
  other arithmetic  1.54 us (2%)
  between operations  0.88 us (1%)
    pallas_call x1, Pallas kernels, staged_gather(): pl.pallas_call(functools.partial(staged_kernel, sizes), out_shape=jax.Sha...  32.8 us
    pallas_call x1, Pallas kernels, attention(): pl.pallas_call(functools.partial(attention_kernel, heads, len(sources)),...  16 us
    dot_general x9, matrix products, shards(): jnp.dot(window, conv_weight[row_tap, col_tap], preferred_element_type=jnp...  5.27 us
    ppermute x1, starting transfers between devices, extended(): before = lax.ppermute(last, axis, up)  4.86 us
    ppermute x1, waiting for transfers between devices, extended(): after = lax.ppermute(initial, axis, down)  3.38 us
    ppermute x1, starting transfers between devices, extended(): after = lax.ppermute(initial, axis, down)  1.92 us
  transfers between devices with their start and end apart: 5, of which 1 were waited for; matrix products, arithmetic and copies ran while one was open for 1% of the time, Pallas kernels for 48%

profile of v16, /device:TPU:1, one launch (start us, length us, event | category | flops | bytes accessed | tf_op | source)
XLA Modules:
  0.0 68.9 jit_solution(10869808349914681515)
XLA Ops:
  0.6 0.0 copy-start
  0.6 1.3 %multiply_convert_fusion = bf16[1,8,32,640]{3,2,1,0:T(8,128)(2,1)S(1)} fusion(bf16[1,8,32,640]{3,2,1,0:T(8,128)(2,1)} %param.9), kind=kLoop, calls=%fused_computation.34 | loop fusion | flops 983040 | bytes 655360 | tf_op jit(solution)/shard_map/convert_element_type | solution.py:229
  2.0 4.9 %collective-permute-start = (bf16[1,1,32,640]{3,2,1,0:T(8,128)(2,1)S(1)}, bf16[1,1,32,640]{3,2,1,0:T(8,128)(2,1)S(1)}, u32[]{:S(2)}, u32[]{:S(2)}) collective-permute-start(bf16[1,1,32,640]{3,2,1,0:T(8,128)(2,1)S(1)} %get-tuple-element.10), channel_id=1, source_target_pairs={{0,1},{1,2},{2,3},{4,5},{5,6},{6,7},{8,9},{9,10},{10,11},{12,13},{... | collective-permute-start | bytes 122888 | tf_op jit(solution)/shard_map/ppermute | solution.py:133
  6.8 1.9 %collective-permute-start.1 = (bf16[1,1,32,640]{3,2,1,0:T(8,128)(2,1)S(1)}, bf16[1,1,32,640]{3,2,1,0:T(8,128)(2,1)S(1)}, u32[]{:S(2)}, u32[]{:S(2)}) collective-permute-start(bf16[1,1,32,640]{3,2,1,0:T(8,128)(2,1)S(1)} %get-tuple-element.11), channel_id=1, source_target_pairs={{1,0},{2,1},{3,2},{5,4},{6,5},{7,6},{9,8},{10,9},{11,10},{13,12},{... | collective-permute-start | bytes 122888 | tf_op jit(solution)/shard_map/ppermute | solution.py:134
  8.8 0.0 collective-permute-done
  8.8 3.4 %collective-permute-done.1 = bf16[1,1,32,640]{3,2,1,0:T(8,128)(2,1)S(1)} collective-permute-done((bf16[1,1,32,640]{3,2,1,0:T(8,128)(2,1)S(1)}, bf16[1,1,32,640]{3,2,1,0:T(8,128)(2,1)S(1)}, u32[]{:S(2)}, u32[]{:S(2)}) %collective-permute-start.1) | collective-permute-done | bytes 40992 | tf_op jit(solution)/shard_map/ppermute | solution.py:134
  12.2 0.2 fusion.29
  12.3 0.2 fusion.30
  12.5 1.6 %fusion.14 = f32[256,640]{1,0:T(8,128)S(1)} fusion(bf16[256,640]{1,0:T(8,128)(2,1)S(1)} %bitcast.62, bf16[3,3,640,640]{3,2,1,0:T(8,128)(2,1)} %param.10), kind=kOutput, calls=%fused_computation.23 | convolution fusion | flops 209715200 | bytes 1802240 | tf_op jit(solution)/shard_map/dot_general | solution.py:238
  14.2 0.0 copy-done
  14.2 0.5 fusion.5
  14.6 0.1 pad_maximum_fusion
  14.7 0.0 copy-start.2
  14.7 0.0 copy-start.6
  14.7 0.5 convolution_add_fusion.6
  15.2 0.0 copy-start.7
  15.2 0.5 convolution_add_fusion.5
  15.7 0.5 convolution_add_fusion.4
  16.1 0.5 convolution_add_fusion.3
  16.6 0.5 convolution_add_fusion.2
  17.0 0.5 convolution_add_fusion.1
  17.5 0.0 copy-done.2
  17.5 0.0 copy-done.6
  17.5 0.5 fusion.3.after_ref.refs_5_
  18.0 0.0 copy-start.1
  18.0 0.1 collective-permute-start.2
  18.1 0.1 collective-permute-start.3
  18.2 0.4 collective-permute-start.4
  18.6 0.0 copy-done.7
  18.6 0.6 reshape.57.refs_4_
  19.2 0.0 copy-done.1
  19.2 32.8 %shard_map.104 = bf16[64,16,640]{2,1,0:T(8,128)(2,1)} custom-call(bf16[1,16,640]{2,1,0:T(8,128)(2,1)} %bitcast.64, bf16[256,640]{1,0:T(8,128)(2,1)} %copy-done.1), custom_call_target="tpu_custom_call" | custom-call | tf_op jit(solution)/shard_map/pallas_call | solution.py:115
  52.0 0.0 collective-permute-done.2.refs_6_
  52.0 0.0 copy-start.3
  52.0 0.0 collective-permute-done.3.refs_7_
  52.0 0.0 copy-start.4
  52.1 0.0 collective-permute-done.4.refs_8_
  52.1 0.0 copy-start.5
  52.1 0.7 copy-done.3
  52.8 0.1 copy-done.4
  52.9 0.1 copy-done.5
  53.0 16.0 %shard_map.105 = bf16[256,640]{1,0:T(8,128)(2,1)} custom-call(bf16[640,640]{1,0:T(8,128)(2,1)} %refs_0_.1, bf16[640,640]{1,0:T(8,128)(2,1)} %refs_1_.1, bf16[640,640]{1,0:T(8,128)(2,1)} %refs_2_.1, bf16[640,640]{1,0:T(8,128)(2,1)} %refs_3_.1, f32[1,640]{1,0:T(1,128)} %reshape.57.refs_4_, bf16[256,640]{1,0:T(8,128)(2,1)} %copy-done.1, ...), custom_call_target="tpu_custom_call" | custom-call | tf_op jit(solution)/shard_map/pallas_call | solution.py:200
  (1 shorter events, 0.0 us)
Async XLA Ops:
  0.6 13.5 %copy-start = (bf16[3,3,640,640]{3,2,1,0:T(8,128)(2,1)S(1)}, bf16[3,3,640,640]{3,2,1,0:T(8,128)(2,1)}, u32[]{:S(2)}) copy-start(bf16[3,3,640,640]{3,2,1,0:T(8,128)(2,1)} %param.10) | copy-start | bytes 22118404
  2.0 6.8 %collective-permute-start = (bf16[1,1,32,640]{3,2,1,0:T(8,128)(2,1)S(1)}, bf16[1,1,32,640]{3,2,1,0:T(8,128)(2,1)S(1)}, u32[]{:S(2)}, u32[]{:S(2)}) collective-permute-start(bf16[1,1,32,640]{3,2,1,0:T(8,128)(2,1)S(1)} %get-tuple-element.10), channel_id=1, source_target_pairs={{0,1},{1,2},{2,3},{4,5},{5,6},{6,7},{8,9},{9,10},{10,11},{12,13},{... | collective-permute-start | bytes 122888 | tf_op jit(solution)/shard_map/ppermute | solution.py:133
  6.8 5.3 %collective-permute-start.1 = (bf16[1,1,32,640]{3,2,1,0:T(8,128)(2,1)S(1)}, bf16[1,1,32,640]{3,2,1,0:T(8,128)(2,1)S(1)}, u32[]{:S(2)}, u32[]{:S(2)}) collective-permute-start(bf16[1,1,32,640]{3,2,1,0:T(8,128)(2,1)S(1)} %get-tuple-element.11), channel_id=1, source_target_pairs={{1,0},{2,1},{3,2},{5,4},{6,5},{7,6},{9,8},{10,9},{11,10},{13,12},{... | collective-permute-start | bytes 122888 | tf_op jit(solution)/shard_map/ppermute | solution.py:134
  14.7 2.8 %copy-start.2 = (bf16[1,8,32,640]{3,2,1,0:T(8,128)(2,1)S(1)}, bf16[1,8,32,640]{3,2,1,0:T(8,128)(2,1)}, u32[]{:S(2)}) copy-start(bf16[1,8,32,640]{3,2,1,0:T(8,128)(2,1)} %param.9) | copy-start | bytes 983044
  14.7 2.8 %copy-start.6 = (f32[640]{0:T(1024)S(1)}, f32[640]{0:T(1024)}, u32[]{:S(2)}) copy-start(f32[640]{0:T(1024)} %param.11) | copy-start | bytes 7684
  15.2 3.4 %copy-start.7 = (f32[640]{0:T(1024)S(1)}, f32[640]{0:T(1024)}, u32[]{:S(2)}) copy-start(f32[640]{0:T(1024)} %param.17) | copy-start | bytes 7684
  18.0 1.2 %copy-start.1 = (bf16[256,640]{1,0:T(8,128)(2,1)}, bf16[256,640]{1,0:T(8,128)(2,1)S(1)}, u32[]{:S(2)}) copy-start(bf16[256,640]{1,0:T(8,128)(2,1)S(1)} %fusion.3.after_ref.refs_5_) | copy-start | bytes 983044
  18.0 34.0 %collective-permute-start.2 = (bf16[256,640]{1,0:T(8,128)(2,1)S(1)}, bf16[256,640]{1,0:T(8,128)(2,1)S(1)}, u32[]{:S(2)}, u32[]{:S(2)}) collective-permute-start(bf16[256,640]{1,0:T(8,128)(2,1)S(1)} %fusion.3.after_ref.refs_5_), channel_id=1, source_target_pairs={{0,1},{1,2},{2,3},{3,0},{4,5},{5,6},{6,7},{7,4},{8,9},{9,10},{10,1... | collective-permute-start | bytes 983048 | tf_op jit(solution)/shard_map/ppermute | solution.py:246
  18.1 33.9 %collective-permute-start.3 = (bf16[256,640]{1,0:T(8,128)(2,1)S(1)}, bf16[256,640]{1,0:T(8,128)(2,1)S(1)}, u32[]{:S(2)}, u32[]{:S(2)}) collective-permute-start(bf16[256,640]{1,0:T(8,128)(2,1)S(1)} %fusion.3.after_ref.refs_5_), channel_id=1, source_target_pairs={{0,2},{1,3},{2,0},{3,1},{4,6},{5,7},{6,4},{7,5},{8,10},{9,11},{10,... | collective-permute-start | bytes 983048 | tf_op jit(solution)/shard_map/ppermute | solution.py:246
  18.2 33.8 %collective-permute-start.4 = (bf16[256,640]{1,0:T(8,128)(2,1)S(1)}, bf16[256,640]{1,0:T(8,128)(2,1)S(1)}, u32[]{:S(2)}, u32[]{:S(2)}) collective-permute-start(bf16[256,640]{1,0:T(8,128)(2,1)S(1)} %fusion.3.after_ref.refs_5_), channel_id=1, source_target_pairs={{0,3},{1,0},{2,1},{3,2},{4,7},{5,4},{6,5},{7,6},{8,11},{9,8},{10,9... | collective-permute-start | bytes 983048 | tf_op jit(solution)/shard_map/ppermute | solution.py:246
  52.0 0.7 %copy-start.3 = (bf16[256,640]{1,0:T(8,128)(2,1)}, bf16[256,640]{1,0:T(8,128)(2,1)S(1)}, u32[]{:S(2)}) copy-start(bf16[256,640]{1,0:T(8,128)(2,1)S(1)} %collective-permute-done.2.refs_6_) | copy-start | bytes 983044
  52.0 0.8 %copy-start.4 = (bf16[256,640]{1,0:T(8,128)(2,1)}, bf16[256,640]{1,0:T(8,128)(2,1)S(1)}, u32[]{:S(2)}) copy-start(bf16[256,640]{1,0:T(8,128)(2,1)S(1)} %collective-permute-done.3.refs_7_) | copy-start | bytes 983044
  52.1 0.9 %copy-start.5 = (bf16[256,640]{1,0:T(8,128)(2,1)}, bf16[256,640]{1,0:T(8,128)(2,1)S(1)}, u32[]{:S(2)}) copy-start(bf16[256,640]{1,0:T(8,128)(2,1)S(1)} %collective-permute-done.4.refs_8_) | copy-start | bytes 983044

commit v17 on v16

--- a/solution.py
+++ b/solution.py
@@ -177,17 +177,23 @@
             source[...], wv_ref[...], preferred_element_type=jnp.float32
         ).astype(v_ref.dtype)
         offset += rows
+    tokens = q_ref.shape[0]
+    tile = tokens // 2 if tokens % 16 == 0 else tokens
     for head in range(heads):
         lanes = slice(head * HD, (head + 1) * HD)
-        scores = jnp.dot(q_ref[:, lanes], k_ref[lanes, :], preferred_element_type=jnp.float32)
-        scores = scores * HD ** (-0.5)
-        top = jnp.max(scores, axis=1, keepdims=True)
-        weights = jnp.exp(scores - top)
-        total = jnp.sum(weights, axis=1, keepdims=True)
-        summed = jnp.dot(
-            weights.astype(jnp.bfloat16), v_ref[:, lanes], preferred_element_type=jnp.float32
-        )
-        mixed_ref[:, lanes] = (summed / total).astype(mixed_ref.dtype)
+        for first in range(0, tokens, tile):
+            rows = slice(first, first + tile)
+            scores = jnp.dot(
+                q_ref[rows, lanes], k_ref[lanes, :], preferred_element_type=jnp.float32
+            )
+            scores = scores * HD ** (-0.5)
+            top = jnp.max(scores, axis=1, keepdims=True)
+            weights = jnp.exp(scores - top)
+            total = jnp.sum(weights, axis=1, keepdims=True)
+            summed = jnp.dot(
+                weights.astype(jnp.bfloat16), v_ref[:, lanes], preferred_element_type=jnp.float32
+            )
+            mixed_ref[rows, lanes] = (summed / total).astype(mixed_ref.dtype)
     attended = jnp.dot(mixed_ref[...], wo_ref[...], preferred_element_type=jnp.float32)
     o_ref[...] = (attended + bias_ref[...]).astype(o_ref.dtype)
 

time: 69.1 us -> 70.6 us (1.022)
  Pallas kernels: 48.8 us -> 50.3 us
    pallas_call x1, Pallas kernels: 16 us -> 17.5 us  [attention(): pl.pallas_call(functools.partial(attention_kernel, heads, len(sources)),...]
  transfers between devices with their start and end apart: 5 -> 5, of which waited for: 1 -> 1; matrix products, arithmetic and copies ran while one was open for 1% -> 1% of each run, Pallas kernels for 48% -> 47%
where the time goes in v17:
time: 70.6 us; the launch traced here: 70.4 us
  Pallas kernels  50.3 us (71%)
  starting transfers between devices  7.35 us (10%)
  matrix products  5.27 us (7%)
  waiting for transfers between devices  3.39 us (5%)
  local copies, waits for them, and re-layouts  1.71 us (2%)
  other arithmetic  1.54 us (2%)
  between operations  0.88 us (1%)
    pallas_call x1, Pallas kernels, staged_gather(): pl.pallas_call(functools.partial(staged_kernel, sizes), out_shape=jax.Sha...  32.8 us
    pallas_call x1, Pallas kernels, attention(): pl.pallas_call(functools.partial(attention_kernel, heads, len(sources)),...  17.5 us
    dot_general x9, matrix products, shards(): jnp.dot(window, conv_weight[row_tap, col_tap], preferred_element_type=jnp...  5.27 us
    ppermute x1, starting transfers between devices, extended(): before = lax.ppermute(last, axis, up)  4.86 us
    ppermute x1, waiting for transfers between devices, extended(): after = lax.ppermute(initial, axis, down)  3.38 us
    ppermute x1, starting transfers between devices, extended(): after = lax.ppermute(initial, axis, down)  1.92 us
  transfers between devices with their start and end apart: 5, of which 1 were waited for; matrix products, arithmetic and copies ran while one was open for 1% of the time, Pallas kernels for 47%

profile of v17, /device:TPU:1, one launch (start us, length us, event | category | flops | bytes accessed | tf_op | source)
XLA Modules:
  0.0 70.4 jit_solution(4749267699410509421)
XLA Ops:
  0.6 0.0 copy-start
  0.6 1.3 %multiply_convert_fusion = bf16[1,8,32,640]{3,2,1,0:T(8,128)(2,1)S(1)} fusion(bf16[1,8,32,640]{3,2,1,0:T(8,128)(2,1)} %param.9), kind=kLoop, calls=%fused_computation.34 | loop fusion | flops 983040 | bytes 655360 | tf_op jit(solution)/shard_map/convert_element_type | solution.py:235
  2.0 4.9 %collective-permute-start = (bf16[1,1,32,640]{3,2,1,0:T(8,128)(2,1)S(1)}, bf16[1,1,32,640]{3,2,1,0:T(8,128)(2,1)S(1)}, u32[]{:S(2)}, u32[]{:S(2)}) collective-permute-start(bf16[1,1,32,640]{3,2,1,0:T(8,128)(2,1)S(1)} %get-tuple-element.10), channel_id=1, source_target_pairs={{0,1},{1,2},{2,3},{4,5},{5,6},{6,7},{8,9},{9,10},{10,11},{12,13},{... | collective-permute-start | bytes 122888 | tf_op jit(solution)/shard_map/ppermute | solution.py:133
  6.8 1.9 %collective-permute-start.1 = (bf16[1,1,32,640]{3,2,1,0:T(8,128)(2,1)S(1)}, bf16[1,1,32,640]{3,2,1,0:T(8,128)(2,1)S(1)}, u32[]{:S(2)}, u32[]{:S(2)}) collective-permute-start(bf16[1,1,32,640]{3,2,1,0:T(8,128)(2,1)S(1)} %get-tuple-element.11), channel_id=1, source_target_pairs={{1,0},{2,1},{3,2},{5,4},{6,5},{7,6},{9,8},{10,9},{11,10},{13,12},{... | collective-permute-start | bytes 122888 | tf_op jit(solution)/shard_map/ppermute | solution.py:134
  8.8 0.0 collective-permute-done
  8.8 3.4 %collective-permute-done.1 = bf16[1,1,32,640]{3,2,1,0:T(8,128)(2,1)S(1)} collective-permute-done((bf16[1,1,32,640]{3,2,1,0:T(8,128)(2,1)S(1)}, bf16[1,1,32,640]{3,2,1,0:T(8,128)(2,1)S(1)}, u32[]{:S(2)}, u32[]{:S(2)}) %collective-permute-start.1) | collective-permute-done | bytes 40992 | tf_op jit(solution)/shard_map/ppermute | solution.py:134
  12.2 0.2 fusion.29
  12.3 0.2 fusion.30
  12.5 1.6 %fusion.14 = f32[256,640]{1,0:T(8,128)S(1)} fusion(bf16[256,640]{1,0:T(8,128)(2,1)S(1)} %bitcast.62, bf16[3,3,640,640]{3,2,1,0:T(8,128)(2,1)} %param.10), kind=kOutput, calls=%fused_computation.23 | convolution fusion | flops 209715200 | bytes 1802240 | tf_op jit(solution)/shard_map/dot_general | solution.py:244
  14.2 0.0 copy-done
  14.2 0.5 fusion.5
  14.6 0.1 pad_maximum_fusion
  14.7 0.0 copy-start.2
  14.7 0.0 copy-start.6
  14.7 0.5 convolution_add_fusion.6
  15.2 0.0 copy-start.7
  15.2 0.5 convolution_add_fusion.5
  15.7 0.5 convolution_add_fusion.4
  16.1 0.5 convolution_add_fusion.3
  16.6 0.5 convolution_add_fusion.2
  17.0 0.5 convolution_add_fusion.1
  17.5 0.0 copy-done.2
  17.5 0.0 copy-done.6
  17.5 0.5 fusion.3.after_ref.refs_5_
  18.0 0.0 copy-start.1
  18.0 0.1 collective-permute-start.2
  18.1 0.1 collective-permute-start.3
  18.2 0.4 collective-permute-start.4
  18.6 0.0 copy-done.7
  18.6 0.6 reshape.57.refs_4_
  19.2 0.0 copy-done.1
  19.2 32.8 %shard_map.104 = bf16[64,16,640]{2,1,0:T(8,128)(2,1)} custom-call(bf16[1,16,640]{2,1,0:T(8,128)(2,1)} %bitcast.64, bf16[256,640]{1,0:T(8,128)(2,1)} %copy-done.1), custom_call_target="tpu_custom_call" | custom-call | tf_op jit(solution)/shard_map/pallas_call | solution.py:115
  52.0 0.0 collective-permute-done.2.refs_6_
  52.0 0.0 copy-start.3
  52.0 0.0 collective-permute-done.3.refs_7_
  52.0 0.0 copy-start.4
  52.1 0.0 collective-permute-done.4.refs_8_
  52.1 0.0 copy-start.5
  52.1 0.7 copy-done.3
  52.8 0.1 copy-done.4
  52.9 0.1 copy-done.5
  53.0 17.5 %shard_map.105 = bf16[256,640]{1,0:T(8,128)(2,1)} custom-call(bf16[640,640]{1,0:T(8,128)(2,1)} %refs_0_.1, bf16[640,640]{1,0:T(8,128)(2,1)} %refs_1_.1, bf16[640,640]{1,0:T(8,128)(2,1)} %refs_2_.1, bf16[640,640]{1,0:T(8,128)(2,1)} %refs_3_.1, f32[1,640]{1,0:T(1,128)} %reshape.57.refs_4_, bf16[256,640]{1,0:T(8,128)(2,1)} %copy-done.1, ...), custom_call_target="tpu_custom_call" | custom-call | tf_op jit(solution)/shard_map/pallas_call | solution.py:206
  (1 shorter events, 0.0 us)
Async XLA Ops:
  0.6 13.5 %copy-start = (bf16[3,3,640,640]{3,2,1,0:T(8,128)(2,1)S(1)}, bf16[3,3,640,640]{3,2,1,0:T(8,128)(2,1)}, u32[]{:S(2)}) copy-start(bf16[3,3,640,640]{3,2,1,0:T(8,128)(2,1)} %param.10) | copy-start | bytes 22118404
  2.0 6.8 %collective-permute-start = (bf16[1,1,32,640]{3,2,1,0:T(8,128)(2,1)S(1)}, bf16[1,1,32,640]{3,2,1,0:T(8,128)(2,1)S(1)}, u32[]{:S(2)}, u32[]{:S(2)}) collective-permute-start(bf16[1,1,32,640]{3,2,1,0:T(8,128)(2,1)S(1)} %get-tuple-element.10), channel_id=1, source_target_pairs={{0,1},{1,2},{2,3},{4,5},{5,6},{6,7},{8,9},{9,10},{10,11},{12,13},{... | collective-permute-start | bytes 122888 | tf_op jit(solution)/shard_map/ppermute | solution.py:133
  6.8 5.3 %collective-permute-start.1 = (bf16[1,1,32,640]{3,2,1,0:T(8,128)(2,1)S(1)}, bf16[1,1,32,640]{3,2,1,0:T(8,128)(2,1)S(1)}, u32[]{:S(2)}, u32[]{:S(2)}) collective-permute-start(bf16[1,1,32,640]{3,2,1,0:T(8,128)(2,1)S(1)} %get-tuple-element.11), channel_id=1, source_target_pairs={{1,0},{2,1},{3,2},{5,4},{6,5},{7,6},{9,8},{10,9},{11,10},{13,12},{... | collective-permute-start | bytes 122888 | tf_op jit(solution)/shard_map/ppermute | solution.py:134
  14.7 2.8 %copy-start.2 = (bf16[1,8,32,640]{3,2,1,0:T(8,128)(2,1)S(1)}, bf16[1,8,32,640]{3,2,1,0:T(8,128)(2,1)}, u32[]{:S(2)}) copy-start(bf16[1,8,32,640]{3,2,1,0:T(8,128)(2,1)} %param.9) | copy-start | bytes 983044
  14.7 2.8 %copy-start.6 = (f32[640]{0:T(1024)S(1)}, f32[640]{0:T(1024)}, u32[]{:S(2)}) copy-start(f32[640]{0:T(1024)} %param.11) | copy-start | bytes 7684
  15.2 3.4 %copy-start.7 = (f32[640]{0:T(1024)S(1)}, f32[640]{0:T(1024)}, u32[]{:S(2)}) copy-start(f32[640]{0:T(1024)} %param.17) | copy-start | bytes 7684
  18.0 1.2 %copy-start.1 = (bf16[256,640]{1,0:T(8,128)(2,1)}, bf16[256,640]{1,0:T(8,128)(2,1)S(1)}, u32[]{:S(2)}) copy-start(bf16[256,640]{1,0:T(8,128)(2,1)S(1)} %fusion.3.after_ref.refs_5_) | copy-start | bytes 983044
  18.0 34.0 %collective-permute-start.2 = (bf16[256,640]{1,0:T(8,128)(2,1)S(1)}, bf16[256,640]{1,0:T(8,128)(2,1)S(1)}, u32[]{:S(2)}, u32[]{:S(2)}) collective-permute-start(bf16[256,640]{1,0:T(8,128)(2,1)S(1)} %fusion.3.after_ref.refs_5_), channel_id=1, source_target_pairs={{0,1},{1,2},{2,3},{3,0},{4,5},{5,6},{6,7},{7,4},{8,9},{9,10},{10,1... | collective-permute-start | bytes 983048 | tf_op jit(solution)/shard_map/ppermute | solution.py:252
  18.1 33.9 %collective-permute-start.3 = (bf16[256,640]{1,0:T(8,128)(2,1)S(1)}, bf16[256,640]{1,0:T(8,128)(2,1)S(1)}, u32[]{:S(2)}, u32[]{:S(2)}) collective-permute-start(bf16[256,640]{1,0:T(8,128)(2,1)S(1)} %fusion.3.after_ref.refs_5_), channel_id=1, source_target_pairs={{0,2},{1,3},{2,0},{3,1},{4,6},{5,7},{6,4},{7,5},{8,10},{9,11},{10,... | collective-permute-start | bytes 983048 | tf_op jit(solution)/shard_map/ppermute | solution.py:252
  18.2 33.8 %collective-permute-start.4 = (bf16[256,640]{1,0:T(8,128)(2,1)S(1)}, bf16[256,640]{1,0:T(8,128)(2,1)S(1)}, u32[]{:S(2)}, u32[]{:S(2)}) collective-permute-start(bf16[256,640]{1,0:T(8,128)(2,1)S(1)} %fusion.3.after_ref.refs_5_), channel_id=1, source_target_pairs={{0,3},{1,0},{2,1},{3,2},{4,7},{5,4},{6,5},{7,6},{8,11},{9,8},{10,9... | collective-permute-start | bytes 983048 | tf_op jit(solution)/shard_map/ppermute | solution.py:252
  52.0 0.7 %copy-start.3 = (bf16[256,640]{1,0:T(8,128)(2,1)}, bf16[256,640]{1,0:T(8,128)(2,1)S(1)}, u32[]{:S(2)}) copy-start(bf16[256,640]{1,0:T(8,128)(2,1)S(1)} %collective-permute-done.2.refs_6_) | copy-start | bytes 983044
  52.0 0.8 %copy-start.4 = (bf16[256,640]{1,0:T(8,128)(2,1)}, bf16[256,640]{1,0:T(8,128)(2,1)S(1)}, u32[]{:S(2)}) copy-start(bf16[256,640]{1,0:T(8,128)(2,1)S(1)} %collective-permute-done.3.refs_7_) | copy-start | bytes 983044
  52.1 0.9 %copy-start.5 = (bf16[256,640]{1,0:T(8,128)(2,1)}, bf16[256,640]{1,0:T(8,128)(2,1)S(1)}, u32[]{:S(2)}) copy-start(bf16[256,640]{1,0:T(8,128)(2,1)S(1)} %collective-permute-done.4.refs_8_) | copy-start | bytes 983044

commit v18 on v16

--- a/solution.py
+++ b/solution.py
@@ -226,8 +226,8 @@
     count, band_rows, width, channels = frames.shape
     heads = channels // HD
     band = band_rows * width
-    activated = jax.nn.silu(frames.astype(jnp.float32)).astype(jnp.bfloat16)
-    padded = extended(activated, ROW_PARTS, 1, 1)
+    padded = extended(frames, ROW_PARTS, 1, 1)
+    padded = jax.nn.silu(padded.astype(jnp.float32)).astype(jnp.bfloat16)
     padded = jnp.pad(padded, ((0, 0), (0, 0), (1, 1), (0, 0)))
     convolved = jnp.zeros((count * band, channels), jnp.float32)
     for row_tap in range(3):

time: 69.1 us -> 71 us (1.027)
  matrix products: 5.27 us -> 6.43 us
  local copies, waits for them, and re-layouts: 1.71 us -> 2.75 us
    dot_general x9, matrix products: 5.27 us -> 6.43 us  [shards(): jnp.dot(window, conv_weight[row_tap, col_tap], preferred_element_type=jnp...]
    slice x1, local copies, waits for them, and re-layouts: 0.01 us -> 0.96 us  [extended(): last = lax.slice_in_dim(value, length - width, length, axis=dim)]
  transfers between devices with their start and end apart: 5 -> 5, of which waited for: 1 -> 1; matrix products, arithmetic and copies ran while one was open for 1% -> 1% of each run, Pallas kernels for 48% -> 46%
where the time goes in v18:
time: 71 us; the launch traced here: 70.8 us
  Pallas kernels  48.8 us (69%)
  starting transfers between devices  7.34 us (10%)
  matrix products  6.43 us (9%)
  waiting for transfers between devices  3.39 us (5%)
  local copies, waits for them, and re-layouts  2.75 us (4%)
  other arithmetic  1.21 us (2%)
  between operations  0.86 us (1%)
    pallas_call x1, Pallas kernels, staged_gather(): pl.pallas_call(functools.partial(staged_kernel, sizes), out_shape=jax.Sha...  32.8 us
    pallas_call x1, Pallas kernels, attention(): pl.pallas_call(functools.partial(attention_kernel, heads, len(sources)),...  16 us
    dot_general x9, matrix products, shards(): jnp.dot(window, conv_weight[row_tap, col_tap], preferred_element_type=jnp...  6.43 us
    ppermute x1, starting transfers between devices, extended(): before = lax.ppermute(last, axis, up)  4.85 us
    ppermute x1, waiting for transfers between devices, extended(): after = lax.ppermute(initial, axis, down)  3.38 us
    ppermute x1, starting transfers between devices, extended(): after = lax.ppermute(initial, axis, down)  1.92 us
  transfers between devices with their start and end apart: 5, of which 1 were waited for; matrix products, arithmetic and copies ran while one was open for 1% of the time, Pallas kernels for 46%

profile of v18, /device:TPU:1, one launch (start us, length us, event | category | flops | bytes accessed | tf_op | source)
XLA Modules:
  0.0 70.8 jit_solution(12461226426174173224)
XLA Ops:
  0.6 0.0 copy-start
  0.6 1.0 %fusion.26 = (bf16[1,1,32,640]{3,2,1,0:T(8,128)(2,1)S(1)}, bf16[1,1,32,640]{3,2,1,0:T(8,128)(2,1)S(1)}) fusion(bf16[1,8,32,640]{3,2,1,0:T(8,128)(2,1)} %param.9), kind=kLoop, calls=%fused_computation.42 | loop fusion | bytes 163840 | tf_op jit(solution)/shard_map/slice | solution.py:131
  1.6 4.8 %collective-permute-start = (bf16[1,1,32,640]{3,2,1,0:T(8,128)(2,1)S(1)}, bf16[1,1,32,640]{3,2,1,0:T(8,128)(2,1)S(1)}, u32[]{:S(2)}, u32[]{:S(2)}) collective-permute-start(bf16[1,1,32,640]{3,2,1,0:T(8,128)(2,1)S(1)} %get-tuple-element.11), channel_id=1, source_target_pairs={{0,1},{1,2},{2,3},{4,5},{5,6},{6,7},{8,9},{9,10},{10,11},{12,13},{... | collective-permute-start | bytes 122888 | tf_op jit(solution)/shard_map/ppermute | solution.py:133
  6.5 1.9 %collective-permute-start.1 = (bf16[1,1,32,640]{3,2,1,0:T(8,128)(2,1)S(1)}, bf16[1,1,32,640]{3,2,1,0:T(8,128)(2,1)S(1)}, u32[]{:S(2)}, u32[]{:S(2)}) collective-permute-start(bf16[1,1,32,640]{3,2,1,0:T(8,128)(2,1)S(1)} %get-tuple-element.12), channel_id=1, source_target_pairs={{1,0},{2,1},{3,2},{5,4},{6,5},{7,6},{9,8},{10,9},{11,10},{13,12},{... | collective-permute-start | bytes 122888 | tf_op jit(solution)/shard_map/ppermute | solution.py:134
  8.4 0.0 collective-permute-done
  8.4 3.4 %collective-permute-done.1 = bf16[1,1,32,640]{3,2,1,0:T(8,128)(2,1)S(1)} collective-permute-done((bf16[1,1,32,640]{3,2,1,0:T(8,128)(2,1)S(1)}, bf16[1,1,32,640]{3,2,1,0:T(8,128)(2,1)S(1)}, u32[]{:S(2)}, u32[]{:S(2)}) %collective-permute-start.1) | collective-permute-done | bytes 40992 | tf_op jit(solution)/shard_map/ppermute | solution.py:134
  11.8 1.2 %fusion.6 = bf16[1,10,32,640]{3,2,1,0:T(8,128)(2,1)S(1)} fusion(bf16[1,1,32,640]{3,2,1,0:T(8,128)(2,1)S(1)} %collective-permute-done.1, bf16[1,8,32,640]{3,2,1,0:T(8,128)(2,1)} %param.9, bf16[1,1,32,640]{3,2,1,0:T(8,128)(2,1)S(1)} %collective-permute-done), kind=kLoop, calls=%fused_computation.16 | loop fusion | flops 1638400 | bytes 819200 | tf_op jit(solution)/shard_map/convert_element_type | solution.py:230
  13.0 0.3 pad_slice_fusion
  13.3 1.6 %fusion.15 = f32[256,640]{1,0:T(8,128)S(1)} fusion(bf16[256,640]{1,0:T(8,128)(2,1)S(1)} %bitcast.62, bf16[3,3,640,640]{3,2,1,0:T(8,128)(2,1)} %param.10), kind=kOutput, calls=%fused_computation.25 | convolution fusion | flops 209715200 | bytes 1802240 | tf_op jit(solution)/shard_map/dot_general | solution.py:238
  14.9 1.6 %convolution_add_fusion.7 = f32[256,640]{1,0:T(8,128)S(1)} fusion(f32[256,640]{1,0:T(8,128)S(1)} %fusion.15, bf16[256,640]{1,0:T(8,128)(2,1)S(1)} %bitcast.61, bf16[3,3,640,640]{3,2,1,0:T(8,128)(2,1)} %param.10), kind=kOutput, calls=%fused_computation.7 | convolution fusion | flops 209879040 | bytes 2457600 | tf_op jit(solution)/shard_map/dot_general | solution.py:238
  16.6 0.0 copy-done
  16.6 0.0 copy-start.2
  16.6 0.0 copy-start.6
  16.6 0.5 convolution_add_fusion.6
  17.1 0.0 copy-start.7
  17.1 0.5 convolution_add_fusion.5
  17.5 0.5 convolution_add_fusion.4
  18.0 0.5 convolution_add_fusion.3
  18.5 0.5 convolution_add_fusion.2
  18.9 0.5 convolution_add_fusion.1
  19.4 0.0 copy-done.2
  19.4 0.0 copy-done.6
  19.4 0.5 fusion.2.after_ref.refs_5_
  19.9 0.0 copy-start.1
  19.9 0.1 collective-permute-start.2
  20.0 0.1 collective-permute-start.3
  20.1 0.4 collective-permute-start.4
  20.5 0.0 copy-done.7
  20.5 0.5 reshape.121.refs_4_
  21.0 0.0 copy-done.1
  21.0 32.8 %shard_map.104 = bf16[64,16,640]{2,1,0:T(8,128)(2,1)} custom-call(bf16[1,16,640]{2,1,0:T(8,128)(2,1)} %bitcast.64, bf16[256,640]{1,0:T(8,128)(2,1)} %copy-done.1), custom_call_target="tpu_custom_call" | custom-call | tf_op jit(solution)/shard_map/pallas_call | solution.py:115
  53.9 0.0 collective-permute-done.2.refs_6_
  53.9 0.0 copy-start.3
  53.9 0.0 collective-permute-done.3.refs_7_
  53.9 0.0 copy-start.4
  53.9 0.0 collective-permute-done.4.refs_8_
  53.9 0.0 copy-start.5
  53.9 0.7 copy-done.3
  54.6 0.1 copy-done.4
  54.7 0.1 copy-done.5
  54.8 16.0 %shard_map.105 = bf16[256,640]{1,0:T(8,128)(2,1)} custom-call(bf16[640,640]{1,0:T(8,128)(2,1)} %refs_0_.1, bf16[640,640]{1,0:T(8,128)(2,1)} %refs_1_.1, bf16[640,640]{1,0:T(8,128)(2,1)} %refs_2_.1, bf16[640,640]{1,0:T(8,128)(2,1)} %refs_3_.1, f32[1,640]{1,0:T(1,128)} %reshape.121.refs_4_, bf16[256,640]{1,0:T(8,128)(2,1)} %copy-done.1, ...), custom_call_target="tpu_custom_call" | custom-call | tf_op jit(solution)/shard_map/pallas_call | solution.py:200
Async XLA Ops:
  0.6 15.9 %copy-start = (bf16[3,3,640,640]{3,2,1,0:T(8,128)(2,1)S(1)}, bf16[3,3,640,640]{3,2,1,0:T(8,128)(2,1)}, u32[]{:S(2)}) copy-start(bf16[3,3,640,640]{3,2,1,0:T(8,128)(2,1)} %param.10) | copy-start | bytes 22118404
  1.6 6.8 %collective-permute-start = (bf16[1,1,32,640]{3,2,1,0:T(8,128)(2,1)S(1)}, bf16[1,1,32,640]{3,2,1,0:T(8,128)(2,1)S(1)}, u32[]{:S(2)}, u32[]{:S(2)}) collective-permute-start(bf16[1,1,32,640]{3,2,1,0:T(8,128)(2,1)S(1)} %get-tuple-element.11), channel_id=1, source_target_pairs={{0,1},{1,2},{2,3},{4,5},{5,6},{6,7},{8,9},{9,10},{10,11},{12,13},{... | collective-permute-start | bytes 122888 | tf_op jit(solution)/shard_map/ppermute | solution.py:133
  6.5 5.3 %collective-permute-start.1 = (bf16[1,1,32,640]{3,2,1,0:T(8,128)(2,1)S(1)}, bf16[1,1,32,640]{3,2,1,0:T(8,128)(2,1)S(1)}, u32[]{:S(2)}, u32[]{:S(2)}) collective-permute-start(bf16[1,1,32,640]{3,2,1,0:T(8,128)(2,1)S(1)} %get-tuple-element.12), channel_id=1, source_target_pairs={{1,0},{2,1},{3,2},{5,4},{6,5},{7,6},{9,8},{10,9},{11,10},{13,12},{... | collective-permute-start | bytes 122888 | tf_op jit(solution)/shard_map/ppermute | solution.py:134
  16.6 2.8 %copy-start.2 = (bf16[1,8,32,640]{3,2,1,0:T(8,128)(2,1)S(1)}, bf16[1,8,32,640]{3,2,1,0:T(8,128)(2,1)}, u32[]{:S(2)}) copy-start(bf16[1,8,32,640]{3,2,1,0:T(8,128)(2,1)} %param.9) | copy-start | bytes 983044
  16.6 2.8 %copy-start.6 = (f32[640]{0:T(1024)S(1)}, f32[640]{0:T(1024)}, u32[]{:S(2)}) copy-start(f32[640]{0:T(1024)} %param.11) | copy-start | bytes 7684
  17.1 3.4 %copy-start.7 = (f32[640]{0:T(1024)S(1)}, f32[640]{0:T(1024)}, u32[]{:S(2)}) copy-start(f32[640]{0:T(1024)} %param.17) | copy-start | bytes 7684
  19.9 1.2 %copy-start.1 = (bf16[256,640]{1,0:T(8,128)(2,1)}, bf16[256,640]{1,0:T(8,128)(2,1)S(1)}, u32[]{:S(2)}) copy-start(bf16[256,640]{1,0:T(8,128)(2,1)S(1)} %fusion.2.after_ref.refs_5_) | copy-start | bytes 983044
  19.9 34.0 %collective-permute-start.2 = (bf16[256,640]{1,0:T(8,128)(2,1)S(1)}, bf16[256,640]{1,0:T(8,128)(2,1)S(1)}, u32[]{:S(2)}, u32[]{:S(2)}) collective-permute-start(bf16[256,640]{1,0:T(8,128)(2,1)S(1)} %fusion.2.after_ref.refs_5_), channel_id=1, source_target_pairs={{0,1},{1,2},{2,3},{3,0},{4,5},{5,6},{6,7},{7,4},{8,9},{9,10},{10,1... | collective-permute-start | bytes 983048 | tf_op jit(solution)/shard_map/ppermute | solution.py:246
  20.0 33.9 %collective-permute-start.3 = (bf16[256,640]{1,0:T(8,128)(2,1)S(1)}, bf16[256,640]{1,0:T(8,128)(2,1)S(1)}, u32[]{:S(2)}, u32[]{:S(2)}) collective-permute-start(bf16[256,640]{1,0:T(8,128)(2,1)S(1)} %fusion.2.after_ref.refs_5_), channel_id=1, source_target_pairs={{0,2},{1,3},{2,0},{3,1},{4,6},{5,7},{6,4},{7,5},{8,10},{9,11},{10,... | collective-permute-start | bytes 983048 | tf_op jit(solution)/shard_map/ppermute | solution.py:246
  20.1 33.8 %collective-permute-start.4 = (bf16[256,640]{1,0:T(8,128)(2,1)S(1)}, bf16[256,640]{1,0:T(8,128)(2,1)S(1)}, u32[]{:S(2)}, u32[]{:S(2)}) collective-permute-start(bf16[256,640]{1,0:T(8,128)(2,1)S(1)} %fusion.2.after_ref.refs_5_), channel_id=1, source_target_pairs={{0,3},{1,0},{2,1},{3,2},{4,7},{5,4},{6,5},{7,6},{8,11},{9,8},{10,9... | collective-permute-start | bytes 983048 | tf_op jit(solution)/shard_map/ppermute | solution.py:246
  53.9 0.7 %copy-start.3 = (bf16[256,640]{1,0:T(8,128)(2,1)}, bf16[256,640]{1,0:T(8,128)(2,1)S(1)}, u32[]{:S(2)}) copy-start(bf16[256,640]{1,0:T(8,128)(2,1)S(1)} %collective-permute-done.2.refs_6_) | copy-start | bytes 983044
  53.9 0.8 %copy-start.4 = (bf16[256,640]{1,0:T(8,128)(2,1)}, bf16[256,640]{1,0:T(8,128)(2,1)S(1)}, u32[]{:S(2)}) copy-start(bf16[256,640]{1,0:T(8,128)(2,1)S(1)} %collective-permute-done.3.refs_7_) | copy-start | bytes 983044
  53.9 0.9 %copy-start.5 = (bf16[256,640]{1,0:T(8,128)(2,1)}, bf16[256,640]{1,0:T(8,128)(2,1)S(1)}, u32[]{:S(2)}) copy-start(bf16[256,640]{1,0:T(8,128)(2,1)S(1)} %collective-permute-done.4.refs_8_) | copy-start | bytes 983044

commit v19 on v16

--- a/solution.py
+++ b/solution.py
@@ -37,7 +37,7 @@
     return Mesh(devices.reshape(shape), TM_PARTS + ROW_PARTS)
 
 
-def staged_kernel(sizes, x_ref, after_ref, out_ref, local_sem, *sems):
+def staged_kernel(sizes, x_ref, h_ref, wq_ref, wk_ref, wv_ref, out_ref, q_ref, k_ref, v_ref, local_sem, *sems):
     high, across, along = sizes
     half = along // 2
     yh, xx, zz = [lax.axis_index(axis) for axis in TM_PARTS]
@@ -81,6 +81,16 @@
     def _():
         for copy in z_copies:
             copy.start()
+
+    band = h_ref[...]
+    q_ref[...] = jnp.dot(band, wq_ref[...], preferred_element_type=jnp.float32).astype(q_ref.dtype)
+    k_ref[...] = lax.dot_general(
+        wk_ref[...], band, (((0,), (1,)), ((), ())), preferred_element_type=jnp.float32
+    ).astype(k_ref.dtype)
+    v_ref[...] = jnp.dot(band, wv_ref[...], preferred_element_type=jnp.float32).astype(v_ref.dtype)
+
+    @pl.when(mine)
+    def _():
         for copy in z_copies:
             copy.wait_send()
 
@@ -106,21 +116,29 @@
     exchange([(whole, c_peer)], sems[6], sems[7])
 
 
-def staged_gather(value, after):
+def staged_gather(value, band, w_query, w_key, w_value):
     sizes = [lax.axis_size(axis) for axis in TM_PARTS]
     total = sizes[0] * sizes[1] * sizes[2]
+    tokens, channels = band.shape
     sems = []
     for count in (sizes[2], sizes[1], 1, 1):
         sems += [pltpu.SemaphoreType.DMA((count,))] * 2
-    gathered = pl.pallas_call(
+    vmem = pl.BlockSpec(memory_space=pltpu.VMEM)
+    gathered, query, key, value_part = pl.pallas_call(
         functools.partial(staged_kernel, sizes),
-        out_shape=jax.ShapeDtypeStruct((total,) + value.shape, value.dtype),
-        in_specs=[pl.BlockSpec(memory_space=pl.ANY)] * 2,
-        out_specs=pl.BlockSpec(memory_space=pl.ANY),
+        out_shape=(
+            jax.ShapeDtypeStruct((total,) + value.shape, value.dtype),
+            jax.ShapeDtypeStruct((tokens, w_query.shape[1]), jnp.bfloat16),
+            jax.ShapeDtypeStruct((w_key.shape[1], tokens), jnp.bfloat16),
+            jax.ShapeDtypeStruct((tokens, w_value.shape[1]), jnp.bfloat16),
+        ),
+        in_specs=[pl.BlockSpec(memory_space=pl.ANY)] + [vmem] * 4,
+        out_specs=(pl.BlockSpec(memory_space=pl.ANY), vmem, vmem, vmem),
         scratch_shapes=[pltpu.SemaphoreType.DMA] + sems,
         compiler_params=pltpu.CompilerParams(collective_id=0, has_side_effects=True),
-    )(value[None], after)
-    return gathered.reshape((total * value.shape[0],) + value.shape[1:])
+    )(value[None], band, w_query, w_key, w_value)
+    every = gathered.reshape((total * value.shape[0],) + value.shape[1:])
+    return every, query, key, value_part
 
 
 def extended(value, axis, dim, width):
@@ -161,13 +179,12 @@
 
 
 def attention_kernel(heads, parts, *refs):
-    wq_ref, wk_ref, wv_ref, wo_ref, bias_ref = refs[:5]
-    sources = refs[5 : 5 + parts]
-    o_ref, k_ref, v_ref, mixed_ref, q_ref = refs[5 + parts :]
-    q_ref[...] = jnp.dot(
-        sources[0][...], wq_ref[...], preferred_element_type=jnp.float32
-    ).astype(q_ref.dtype)
-    offset = 0
+    q_ref, ko_ref, vo_ref, wk_ref, wv_ref, wo_ref, bias_ref = refs[:7]
+    sources = refs[7 : 7 + parts]
+    o_ref, k_ref, v_ref, mixed_ref = refs[7 + parts :]
+    offset = vo_ref.shape[0]
+    k_ref[:, :offset] = ko_ref[...]
+    v_ref[:offset, :] = vo_ref[...]
     for source in sources:
         rows = source.shape[0]
         k_ref[:, offset : offset + rows] = lax.dot_general(
@@ -192,11 +209,12 @@
     o_ref[...] = (attended + bias_ref[...]).astype(o_ref.dtype)
 
 
-def attention(w_query, w_key, w_value, w_out, out_bias, sources, heads):
-    tokens, channels = sources[0].shape
-    length = sum(source.shape[0] for source in sources)
+def attention(query, own_key, own_value, w_key, w_value, w_out, out_bias, sources, heads):
+    tokens, channels = query.shape
+    length = own_value.shape[0] + sum(source.shape[0] for source in sources)
     whole = lambda array: pl.BlockSpec(array.shape, lambda i: (0, 0))
-    operands = (w_query, w_key, w_value, w_out, out_bias.reshape(1, -1)) + tuple(sources)
+    operands = (query, own_key, own_value, w_key, w_value, w_out, out_bias.reshape(1, -1))
+    operands += tuple(sources)
     return pl.pallas_call(
         functools.partial(attention_kernel, heads, len(sources)),
         out_shape=jax.ShapeDtypeStruct((tokens, channels), jnp.bfloat16),
@@ -206,7 +224,6 @@
         scratch_shapes=[
             pltpu.VMEM((channels, length), jnp.bfloat16),
             pltpu.VMEM((length, channels), jnp.bfloat16),
-            pltpu.VMEM((tokens, channels), jnp.bfloat16),
             pltpu.VMEM((tokens, channels), jnp.bfloat16),
         ],
     )(*operands)
@@ -246,9 +263,11 @@
         lax.ppermute(hidden, ROW_PARTS, [(j, (j + shift) % rows) for j in range(rows)])
         for shift in range(1, rows)
     ]
-    every_feature = staged_gather(ref_features, hidden)
-    sources = [hidden] + others + [every_feature]
-    attended = attention(w_query, w_key, w_value, w_out, out_bias, sources, heads)
+    every_feature, query, own_key, own_value = staged_gather(
+        ref_features, hidden, w_query, w_key, w_value
+    )
+    sources = others + [every_feature]
+    attended = attention(query, own_key, own_value, w_key, w_value, w_out, out_bias, sources, heads)
     return (
         hidden.reshape(count, band_rows, width, channels),
         attended.reshape(count, band_rows, width, channels),

time: 69.1 us -> 74 us (1.071)
  Pallas kernels: 48.8 us -> 52.3 us
  starting transfers between devices: 7.35 us -> 8.62 us
    pallas_call x1, Pallas kernels: 32.8 us -> 37.2 us  [staged_gather(): pl.pallas_call(functools.partial(staged_kernel, sizes), out_shape=(jax.Sh...]
    ppermute x3, starting transfers between devices: 0.58 us -> 1.84 us  [shards(): lax.ppermute(hidden, ROW_PARTS, [(j, (j + shift) % rows) for j in range(r...]
    pallas_call x1, Pallas kernels: 16 us -> 15.1 us  [attention(): pl.pallas_call(functools.partial(attention_kernel, heads, len(sources)),...]
  transfers between devices with their start and end apart: 5 -> 5, of which waited for: 1 -> 1; matrix products, arithmetic and copies ran while one was open for 1% -> 1% of each run, Pallas kernels for 48% -> 50%
where the time goes in v19:
time: 74 us; the launch traced here: 73.8 us
  Pallas kernels  52.3 us (71%)
  starting transfers between devices  8.62 us (12%)
  matrix products  5.27 us (7%)
  waiting for transfers between devices  3.39 us (5%)
  local copies, waits for them, and re-layouts  1.75 us (2%)
  other arithmetic  1.54 us (2%)
  between operations  0.88 us (1%)
    pallas_call x1, Pallas kernels, staged_gather(): pl.pallas_call(functools.partial(staged_kernel, sizes), out_shape=(jax.Sh...  37.2 us
    pallas_call x1, Pallas kernels, attention(): pl.pallas_call(functools.partial(attention_kernel, heads, len(sources)),...  15.1 us
    dot_general x9, matrix products, shards(): jnp.dot(window, conv_weight[row_tap, col_tap], preferred_element_type=jnp...  5.27 us
    ppermute x1, starting transfers between devices, extended(): before = lax.ppermute(last, axis, up)  4.86 us
    ppermute x1, waiting for transfers between devices, extended(): after = lax.ppermute(initial, axis, down)  3.38 us
    ppermute x1, starting transfers between devices, extended(): after = lax.ppermute(initial, axis, down)  1.92 us
    ppermute x3, starting transfers between devices, shards(): lax.ppermute(hidden, ROW_PARTS, [(j, (j + shift) % rows) for j in range(r...  1.84 us
  transfers between devices with their start and end apart: 5, of which 1 were waited for; matrix products, arithmetic and copies ran while one was open for 1% of the time, Pallas kernels for 50%

profile of v19, /device:TPU:1, one launch (start us, length us, event | category | flops | bytes accessed | tf_op | source)
XLA Modules:
  0.0 73.8 jit_solution(4471048837609506616)
XLA Ops:
  0.6 0.0 copy-start
  0.6 1.3 %multiply_convert_fusion = bf16[1,8,32,640]{3,2,1,0:T(8,128)(2,1)S(1)} fusion(bf16[1,8,32,640]{3,2,1,0:T(8,128)(2,1)} %param.9), kind=kLoop, calls=%fused_computation.34 | loop fusion | flops 983040 | bytes 655360 | tf_op jit(solution)/shard_map/convert_element_type | solution.py:246
  2.0 4.9 %collective-permute-start = (bf16[1,1,32,640]{3,2,1,0:T(8,128)(2,1)S(1)}, bf16[1,1,32,640]{3,2,1,0:T(8,128)(2,1)S(1)}, u32[]{:S(2)}, u32[]{:S(2)}) collective-permute-start(bf16[1,1,32,640]{3,2,1,0:T(8,128)(2,1)S(1)} %get-tuple-element.18), channel_id=1, source_target_pairs={{0,1},{1,2},{2,3},{4,5},{5,6},{6,7},{8,9},{9,10},{10,11},{12,13},{... | collective-permute-start | bytes 122888 | tf_op jit(solution)/shard_map/ppermute | solution.py:151
  6.8 1.9 %collective-permute-start.1 = (bf16[1,1,32,640]{3,2,1,0:T(8,128)(2,1)S(1)}, bf16[1,1,32,640]{3,2,1,0:T(8,128)(2,1)S(1)}, u32[]{:S(2)}, u32[]{:S(2)}) collective-permute-start(bf16[1,1,32,640]{3,2,1,0:T(8,128)(2,1)S(1)} %get-tuple-element.19), channel_id=1, source_target_pairs={{1,0},{2,1},{3,2},{5,4},{6,5},{7,6},{9,8},{10,9},{11,10},{13,12},{... | collective-permute-start | bytes 122888 | tf_op jit(solution)/shard_map/ppermute | solution.py:152
  8.8 0.0 collective-permute-done
  8.8 3.4 %collective-permute-done.1 = bf16[1,1,32,640]{3,2,1,0:T(8,128)(2,1)S(1)} collective-permute-done((bf16[1,1,32,640]{3,2,1,0:T(8,128)(2,1)S(1)}, bf16[1,1,32,640]{3,2,1,0:T(8,128)(2,1)S(1)}, u32[]{:S(2)}, u32[]{:S(2)}) %collective-permute-start.1) | collective-permute-done | bytes 40992 | tf_op jit(solution)/shard_map/ppermute | solution.py:152
  12.2 0.2 fusion.29
  12.3 0.2 fusion.30
  12.5 1.6 %fusion.14 = f32[256,640]{1,0:T(8,128)S(1)} fusion(bf16[256,640]{1,0:T(8,128)(2,1)S(1)} %bitcast.62, bf16[3,3,640,640]{3,2,1,0:T(8,128)(2,1)} %param.10), kind=kOutput, calls=%fused_computation.23 | convolution fusion | flops 209715200 | bytes 1802240 | tf_op jit(solution)/shard_map/dot_general | solution.py:255
  14.2 0.0 copy-done
  14.2 0.5 fusion.5
  14.6 0.1 pad_maximum_fusion
  14.7 0.0 copy-start.1
  14.7 0.0 copy-start.6
  14.7 0.5 convolution_add_fusion.6
  15.2 0.0 copy-start.7
  15.2 0.5 convolution_add_fusion.5
  15.7 0.5 convolution_add_fusion.4
  16.1 0.5 convolution_add_fusion.3
  16.6 0.5 convolution_add_fusion.2
  17.0 0.5 convolution_add_fusion.1
  17.5 0.0 copy-done.1
  17.5 0.0 copy-done.6
  17.5 0.5 fusion.3.h_ref
  18.0 0.0 copy-start.2
  18.0 0.1 collective-permute-start.4
  18.1 0.1 collective-permute-start.3
  18.2 1.7 %collective-permute-start.2 = (bf16[256,640]{1,0:T(8,128)(2,1)S(1)}, bf16[256,640]{1,0:T(8,128)(2,1)S(1)}, u32[]{:S(2)}, u32[]{:S(2)}) collective-permute-start(bf16[256,640]{1,0:T(8,128)(2,1)S(1)} %fusion.3.h_ref), channel_id=1, source_target_pairs={{0,1},{1,2},{2,3},{3,0},{4,5},{5,6},{6,7},{7,4},{8,9},{9,10},{10,1... | collective-permute-start | bytes 983048 | tf_op jit(solution)/shard_map/ppermute | solution.py:263
  19.9 0.0 copy-done.7
  19.9 0.6 reshape.57.refs_6_
  20.5 0.0 copy-done.2
  20.5 37.2 %shard_map.104 = (bf16[64,16,640]{2,1,0:T(8,128)(2,1)}, bf16[256,640]{1,0:T(8,128)(2,1)}, bf16[640,256]{1,0:T(8,128)(2,1)}, bf16[256,640]{1,0:T(8,128)(2,1)}) custom-call(bf16[1,16,640]{2,1,0:T(8,128)(2,1)} %bitcast.64, bf16[256,640]{1,0:T(8,128)(2,1)} %copy-done.2, bf16[640,640]{1,0:T(8,128)(2,1)} %wq_ref.1, bf16[640,640]{1,0:T(8,128)(2,1)} %refs_3_.1, ...), custom_call_target="tpu_custom_call" | custom-call | tf_op jit(solution)/shard_map/pallas_call | solution.py:127
  57.7 0.0 collective-permute-done.4.refs_9_
  57.7 0.0 copy-start.3
  57.7 0.0 collective-permute-done.3.refs_8_
  57.7 0.0 copy-start.4
  57.7 0.0 collective-permute-done.2.refs_7_
  57.7 0.0 copy-start.5
  57.8 0.7 copy-done.3
  58.4 0.1 copy-done.4
  58.6 0.1 copy-done.5
  58.7 15.1 %shard_map.105 = bf16[256,640]{1,0:T(8,128)(2,1)} custom-call(bf16[256,640]{1,0:T(8,128)(2,1)} %get-tuple-element.6.refs_0_, bf16[640,256]{1,0:T(8,128)(2,1)} %get-tuple-element.7.refs_1_, bf16[256,640]{1,0:T(8,128)(2,1)} %get-tuple-element.8.refs_2_, bf16[640,640]{1,0:T(8,128)(2,1)} %refs_3_.1, bf16[640,640]{1,0:T(8,128)(2,1)} %refs_4_.1, ...), custom_call_target="tpu_custom_call" | custom-call | tf_op jit(solution)/shard_map/pallas_call | solution.py:218
  (1 shorter events, 0.0 us)
Async XLA Ops:
  0.6 13.5 %copy-start = (bf16[3,3,640,640]{3,2,1,0:T(8,128)(2,1)S(1)}, bf16[3,3,640,640]{3,2,1,0:T(8,128)(2,1)}, u32[]{:S(2)}) copy-start(bf16[3,3,640,640]{3,2,1,0:T(8,128)(2,1)} %param.10) | copy-start | bytes 22118404
  2.0 6.8 %collective-permute-start = (bf16[1,1,32,640]{3,2,1,0:T(8,128)(2,1)S(1)}, bf16[1,1,32,640]{3,2,1,0:T(8,128)(2,1)S(1)}, u32[]{:S(2)}, u32[]{:S(2)}) collective-permute-start(bf16[1,1,32,640]{3,2,1,0:T(8,128)(2,1)S(1)} %get-tuple-element.18), channel_id=1, source_target_pairs={{0,1},{1,2},{2,3},{4,5},{5,6},{6,7},{8,9},{9,10},{10,11},{12,13},{... | collective-permute-start | bytes 122888 | tf_op jit(solution)/shard_map/ppermute | solution.py:151
  6.8 5.3 %collective-permute-start.1 = (bf16[1,1,32,640]{3,2,1,0:T(8,128)(2,1)S(1)}, bf16[1,1,32,640]{3,2,1,0:T(8,128)(2,1)S(1)}, u32[]{:S(2)}, u32[]{:S(2)}) collective-permute-start(bf16[1,1,32,640]{3,2,1,0:T(8,128)(2,1)S(1)} %get-tuple-element.19), channel_id=1, source_target_pairs={{1,0},{2,1},{3,2},{5,4},{6,5},{7,6},{9,8},{10,9},{11,10},{13,12},{... | collective-permute-start | bytes 122888 | tf_op jit(solution)/shard_map/ppermute | solution.py:152
  14.7 2.8 %copy-start.1 = (bf16[1,8,32,640]{3,2,1,0:T(8,128)(2,1)S(1)}, bf16[1,8,32,640]{3,2,1,0:T(8,128)(2,1)}, u32[]{:S(2)}) copy-start(bf16[1,8,32,640]{3,2,1,0:T(8,128)(2,1)} %param.9) | copy-start | bytes 983044
  14.7 2.8 %copy-start.6 = (f32[640]{0:T(1024)S(1)}, f32[640]{0:T(1024)}, u32[]{:S(2)}) copy-start(f32[640]{0:T(1024)} %param.11) | copy-start | bytes 7684
  15.2 4.7 %copy-start.7 = (f32[640]{0:T(1024)S(1)}, f32[640]{0:T(1024)}, u32[]{:S(2)}) copy-start(f32[640]{0:T(1024)} %param.17) | copy-start | bytes 7684
  18.0 2.5 %copy-start.2 = (bf16[256,640]{1,0:T(8,128)(2,1)}, bf16[256,640]{1,0:T(8,128)(2,1)S(1)}, u32[]{:S(2)}) copy-start(bf16[256,640]{1,0:T(8,128)(2,1)S(1)} %fusion.3.h_ref) | copy-start | bytes 983044
  18.0 39.7 %collective-permute-start.4 = (bf16[256,640]{1,0:T(8,128)(2,1)S(1)}, bf16[256,640]{1,0:T(8,128)(2,1)S(1)}, u32[]{:S(2)}, u32[]{:S(2)}) collective-permute-start(bf16[256,640]{1,0:T(8,128)(2,1)S(1)} %fusion.3.h_ref), channel_id=1, source_target_pairs={{0,3},{1,0},{2,1},{3,2},{4,7},{5,4},{6,5},{7,6},{8,11},{9,8},{10,9... | collective-permute-start | bytes 983048 | tf_op jit(solution)/shard_map/ppermute | solution.py:263
  18.1 39.6 %collective-permute-start.3 = (bf16[256,640]{1,0:T(8,128)(2,1)S(1)}, bf16[256,640]{1,0:T(8,128)(2,1)S(1)}, u32[]{:S(2)}, u32[]{:S(2)}) collective-permute-start(bf16[256,640]{1,0:T(8,128)(2,1)S(1)} %fusion.3.h_ref), channel_id=1, source_target_pairs={{0,2},{1,3},{2,0},{3,1},{4,6},{5,7},{6,4},{7,5},{8,10},{9,11},{10,... | collective-permute-start | bytes 983048 | tf_op jit(solution)/shard_map/ppermute | solution.py:263
  18.2 39.5 %collective-permute-start.2 = (bf16[256,640]{1,0:T(8,128)(2,1)S(1)}, bf16[256,640]{1,0:T(8,128)(2,1)S(1)}, u32[]{:S(2)}, u32[]{:S(2)}) collective-permute-start(bf16[256,640]{1,0:T(8,128)(2,1)S(1)} %fusion.3.h_ref), channel_id=1, source_target_pairs={{0,1},{1,2},{2,3},{3,0},{4,5},{5,6},{6,7},{7,4},{8,9},{9,10},{10,1... | collective-permute-start | bytes 983048 | tf_op jit(solution)/shard_map/ppermute | solution.py:263
  57.7 0.7 copy-start.3
  57.7 0.8 %copy-start.4 = (bf16[256,640]{1,0:T(8,128)(2,1)}, bf16[256,640]{1,0:T(8,128)(2,1)S(1)}, u32[]{:S(2)}) copy-start(bf16[256,640]{1,0:T(8,128)(2,1)S(1)} %collective-permute-done.3.refs_8_) | copy-start | bytes 983044
  57.7 0.9 %copy-start.5 = (bf16[256,640]{1,0:T(8,128)(2,1)}, bf16[256,640]{1,0:T(8,128)(2,1)S(1)}, u32[]{:S(2)}) copy-start(bf16[256,640]{1,0:T(8,128)(2,1)S(1)} %collective-permute-done.2.refs_7_) | copy-start | bytes 983044

commit v20 on v16

--- a/solution.py
+++ b/solution.py
@@ -161,14 +161,30 @@
 
 
 def attention_kernel(heads, parts, *refs):
-    wq_ref, wk_ref, wv_ref, wo_ref, bias_ref = refs[:5]
-    sources = refs[5 : 5 + parts]
-    o_ref, k_ref, v_ref, mixed_ref, q_ref = refs[5 + parts :]
+    bias_ref = refs[0]
+    weights_in = refs[1:5]
+    sources_in = refs[5 : 5 + parts]
+    o_ref = refs[5 + parts]
+    scratch = refs[6 + parts :]
+    wq_ref, wk_ref, wv_ref, wo_ref = scratch[:4]
+    sources = scratch[4 : 4 + parts]
+    k_ref, v_ref, mixed_ref, q_ref, sems = scratch[4 + parts :]
+    pairs = [(sources_in[0], sources[0])] + list(zip(weights_in[:3], (wq_ref, wk_ref, wv_ref)))
+    pairs += list(zip(sources_in[1:], sources[1:])) + [(weights_in[3], wo_ref)]
+    copies = []
+    for index, (src_ref, dst_ref) in enumerate(pairs):
+        copy = pltpu.make_async_copy(src_ref, dst_ref, sems.at[index])
+        copy.start()
+        copies.append(copy)
+    for copy in copies[:4]:
+        copy.wait()
     q_ref[...] = jnp.dot(
         sources[0][...], wq_ref[...], preferred_element_type=jnp.float32
     ).astype(q_ref.dtype)
     offset = 0
-    for source in sources:
+    for index, source in enumerate(sources):
+        if index:
+            copies[3 + index].wait()
         rows = source.shape[0]
         k_ref[:, offset : offset + rows] = lax.dot_general(
             wk_ref[...], source[...], (((0,), (1,)), ((), ())), preferred_element_type=jnp.float32
@@ -188,6 +204,7 @@
             weights.astype(jnp.bfloat16), v_ref[:, lanes], preferred_element_type=jnp.float32
         )
         mixed_ref[:, lanes] = (summed / total).astype(mixed_ref.dtype)
+    copies[-1].wait()
     attended = jnp.dot(mixed_ref[...], wo_ref[...], preferred_element_type=jnp.float32)
     o_ref[...] = (attended + bias_ref[...]).astype(o_ref.dtype)
 
@@ -195,19 +212,22 @@
 def attention(w_query, w_key, w_value, w_out, out_bias, sources, heads):
     tokens, channels = sources[0].shape
     length = sum(source.shape[0] for source in sources)
-    whole = lambda array: pl.BlockSpec(array.shape, lambda i: (0, 0))
-    operands = (w_query, w_key, w_value, w_out, out_bias.reshape(1, -1)) + tuple(sources)
+    weights = (w_query, w_key, w_value, w_out)
+    operands = (out_bias.reshape(1, -1),) + weights + tuple(sources)
+    anywhere = pl.BlockSpec(memory_space=pl.ANY)
     return pl.pallas_call(
         functools.partial(attention_kernel, heads, len(sources)),
         out_shape=jax.ShapeDtypeStruct((tokens, channels), jnp.bfloat16),
         grid=(1,),
-        in_specs=[whole(array) for array in operands],
+        in_specs=[pl.BlockSpec((1, channels), lambda i: (0, 0))] + [anywhere] * (len(operands) - 1),
         out_specs=pl.BlockSpec((tokens, channels), lambda i: (0, 0)),
-        scratch_shapes=[
+        scratch_shapes=[pltpu.VMEM(array.shape, array.dtype) for array in operands[1:]]
+        + [
             pltpu.VMEM((channels, length), jnp.bfloat16),
             pltpu.VMEM((length, channels), jnp.bfloat16),
             pltpu.VMEM((tokens, channels), jnp.bfloat16),
             pltpu.VMEM((tokens, channels), jnp.bfloat16),
+            pltpu.SemaphoreType.DMA((len(operands) - 1,)),
         ],
     )(*operands)
 

time: 69.1 us -> 70 us (1.013)
  Pallas kernels: 48.8 us -> 49.5 us
    pallas_call x1, Pallas kernels: 16 us -> 16.7 us  [attention(): pl.pallas_call(functools.partial(attention_kernel, heads, len(sources)),...]
  transfers between devices with their start and end apart: 5 -> 5, of which waited for: 1 -> 1; matrix products, arithmetic and copies ran while one was open for 1% -> 1% of each run, Pallas kernels for 48% -> 47%
where the time goes in v20:
time: 70 us; the launch traced here: 69.8 us
  Pallas kernels  49.5 us (71%)
  starting transfers between devices  7.35 us (10%)
  matrix products  5.27 us (8%)
  waiting for transfers between devices  3.39 us (5%)
  local copies, waits for them, and re-layouts  1.71 us (2%)
  other arithmetic  1.54 us (2%)
  between operations  1.04 us (1%)
    pallas_call x1, Pallas kernels, staged_gather(): pl.pallas_call(functools.partial(staged_kernel, sizes), out_shape=jax.Sha...  32.8 us
    pallas_call x1, Pallas kernels, attention(): pl.pallas_call(functools.partial(attention_kernel, heads, len(sources)),...  16.7 us
    dot_general x9, matrix products, shards(): jnp.dot(window, conv_weight[row_tap, col_tap], preferred_element_type=jnp...  5.27 us
    ppermute x1, starting transfers between devices, extended(): before = lax.ppermute(last, axis, up)  4.86 us
    ppermute x1, waiting for transfers between devices, extended(): after = lax.ppermute(initial, axis, down)  3.38 us
    ppermute x1, starting transfers between devices, extended(): after = lax.ppermute(initial, axis, down)  1.92 us
  transfers between devices with their start and end apart: 5, of which 1 were waited for; matrix products, arithmetic and copies ran while one was open for 1% of the time, Pallas kernels for 47%

profile of v20, /device:TPU:1, one launch (start us, length us, event | category | flops | bytes accessed | tf_op | source)
XLA Modules:
  0.0 69.8 jit_solution(11268418025714047643)
XLA Ops:
  0.6 0.0 copy-start
  0.6 1.3 %multiply_convert_fusion = bf16[1,8,32,640]{3,2,1,0:T(8,128)(2,1)S(1)} fusion(bf16[1,8,32,640]{3,2,1,0:T(8,128)(2,1)} %param.9), kind=kLoop, calls=%fused_computation.34 | loop fusion | flops 983040 | bytes 655360 | tf_op jit(solution)/shard_map/convert_element_type | solution.py:249
  2.0 4.9 %collective-permute-start = (bf16[1,1,32,640]{3,2,1,0:T(8,128)(2,1)S(1)}, bf16[1,1,32,640]{3,2,1,0:T(8,128)(2,1)S(1)}, u32[]{:S(2)}, u32[]{:S(2)}) collective-permute-start(bf16[1,1,32,640]{3,2,1,0:T(8,128)(2,1)S(1)} %get-tuple-element.10), channel_id=1, source_target_pairs={{0,1},{1,2},{2,3},{4,5},{5,6},{6,7},{8,9},{9,10},{10,11},{12,13},{... | collective-permute-start | bytes 122888 | tf_op jit(solution)/shard_map/ppermute | solution.py:133
  6.8 1.9 %collective-permute-start.1 = (bf16[1,1,32,640]{3,2,1,0:T(8,128)(2,1)S(1)}, bf16[1,1,32,640]{3,2,1,0:T(8,128)(2,1)S(1)}, u32[]{:S(2)}, u32[]{:S(2)}) collective-permute-start(bf16[1,1,32,640]{3,2,1,0:T(8,128)(2,1)S(1)} %get-tuple-element.11), channel_id=1, source_target_pairs={{1,0},{2,1},{3,2},{5,4},{6,5},{7,6},{9,8},{10,9},{11,10},{13,12},{... | collective-permute-start | bytes 122888 | tf_op jit(solution)/shard_map/ppermute | solution.py:134
  8.8 0.0 collective-permute-done
  8.8 3.4 %collective-permute-done.1 = bf16[1,1,32,640]{3,2,1,0:T(8,128)(2,1)S(1)} collective-permute-done((bf16[1,1,32,640]{3,2,1,0:T(8,128)(2,1)S(1)}, bf16[1,1,32,640]{3,2,1,0:T(8,128)(2,1)S(1)}, u32[]{:S(2)}, u32[]{:S(2)}) %collective-permute-start.1) | collective-permute-done | bytes 40992 | tf_op jit(solution)/shard_map/ppermute | solution.py:134
  12.2 0.2 fusion.29
  12.3 0.2 fusion.30
  12.5 1.6 %fusion.14 = f32[256,640]{1,0:T(8,128)S(1)} fusion(bf16[256,640]{1,0:T(8,128)(2,1)S(1)} %bitcast.62, bf16[3,3,640,640]{3,2,1,0:T(8,128)(2,1)} %param.10), kind=kOutput, calls=%fused_computation.23 | convolution fusion | flops 209715200 | bytes 1802240 | tf_op jit(solution)/shard_map/dot_general | solution.py:258
  14.2 0.0 copy-done
  14.2 0.5 fusion.5
  14.6 0.1 pad_maximum_fusion
  14.7 0.0 copy-start.2
  14.7 0.0 copy-start.6
  14.7 0.5 convolution_add_fusion.6
  15.2 0.0 copy-start.7
  15.2 0.5 convolution_add_fusion.5
  15.7 0.5 convolution_add_fusion.4
  16.1 0.5 convolution_add_fusion.3
  16.6 0.5 convolution_add_fusion.2
  17.0 0.5 convolution_add_fusion.1
  17.5 0.0 copy-done.2
  17.5 0.0 copy-done.6
  17.5 0.5 fusion.3.after_ref.refs_5_
  18.0 0.0 copy-start.1
  18.0 0.1 collective-permute-start.2
  18.1 0.1 collective-permute-start.3
  18.2 0.4 collective-permute-start.4
  18.6 0.0 copy-done.7
  18.6 0.6 reshape.57.refs_0_
  19.2 0.0 copy-done.1
  19.2 32.8 %shard_map.104 = bf16[64,16,640]{2,1,0:T(8,128)(2,1)} custom-call(bf16[1,16,640]{2,1,0:T(8,128)(2,1)} %bitcast.64, bf16[256,640]{1,0:T(8,128)(2,1)} %copy-done.1), custom_call_target="tpu_custom_call" | custom-call | tf_op jit(solution)/shard_map/pallas_call | solution.py:115
  52.0 0.0 collective-permute-done.2.refs_6_
  52.0 0.0 copy-start.3
  52.0 0.0 collective-permute-done.3.refs_7_
  52.0 0.0 copy-start.4
  52.1 0.0 collective-permute-done.4.refs_8_
  52.1 0.0 copy-start.5
  52.1 0.7 copy-done.3
  52.8 0.1 copy-done.4
  52.9 0.1 copy-done.5
  53.0 16.7 %shard_map.105 = bf16[256,640]{1,0:T(8,128)(2,1)} custom-call(f32[1,640]{1,0:T(1,128)} %reshape.57.refs_0_, bf16[640,640]{1,0:T(8,128)(2,1)} %refs_1_.1, bf16[640,640]{1,0:T(8,128)(2,1)} %refs_2_.1, bf16[640,640]{1,0:T(8,128)(2,1)} %refs_3_.1, bf16[640,640]{1,0:T(8,128)(2,1)} %refs_4_.1, bf16[256,640]{1,0:T(8,128)(2,1)} %copy-done.1, ...), custom_call_target="tpu_custom_call" | custom-call | tf_op jit(solution)/shard_map/pallas_call | solution.py:218
  (1 shorter events, 0.0 us)
Async XLA Ops:
  0.6 13.5 %copy-start = (bf16[3,3,640,640]{3,2,1,0:T(8,128)(2,1)S(1)}, bf16[3,3,640,640]{3,2,1,0:T(8,128)(2,1)}, u32[]{:S(2)}) copy-start(bf16[3,3,640,640]{3,2,1,0:T(8,128)(2,1)} %param.10) | copy-start | bytes 22118404
  2.0 6.8 %collective-permute-start = (bf16[1,1,32,640]{3,2,1,0:T(8,128)(2,1)S(1)}, bf16[1,1,32,640]{3,2,1,0:T(8,128)(2,1)S(1)}, u32[]{:S(2)}, u32[]{:S(2)}) collective-permute-start(bf16[1,1,32,640]{3,2,1,0:T(8,128)(2,1)S(1)} %get-tuple-element.10), channel_id=1, source_target_pairs={{0,1},{1,2},{2,3},{4,5},{5,6},{6,7},{8,9},{9,10},{10,11},{12,13},{... | collective-permute-start | bytes 122888 | tf_op jit(solution)/shard_map/ppermute | solution.py:133
  6.8 5.3 %collective-permute-start.1 = (bf16[1,1,32,640]{3,2,1,0:T(8,128)(2,1)S(1)}, bf16[1,1,32,640]{3,2,1,0:T(8,128)(2,1)S(1)}, u32[]{:S(2)}, u32[]{:S(2)}) collective-permute-start(bf16[1,1,32,640]{3,2,1,0:T(8,128)(2,1)S(1)} %get-tuple-element.11), channel_id=1, source_target_pairs={{1,0},{2,1},{3,2},{5,4},{6,5},{7,6},{9,8},{10,9},{11,10},{13,12},{... | collective-permute-start | bytes 122888 | tf_op jit(solution)/shard_map/ppermute | solution.py:134
  14.7 2.8 %copy-start.2 = (bf16[1,8,32,640]{3,2,1,0:T(8,128)(2,1)S(1)}, bf16[1,8,32,640]{3,2,1,0:T(8,128)(2,1)}, u32[]{:S(2)}) copy-start(bf16[1,8,32,640]{3,2,1,0:T(8,128)(2,1)} %param.9) | copy-start | bytes 983044
  14.7 2.8 %copy-start.6 = (f32[640]{0:T(1024)S(1)}, f32[640]{0:T(1024)}, u32[]{:S(2)}) copy-start(f32[640]{0:T(1024)} %param.11) | copy-start | bytes 7684
  15.2 3.4 %copy-start.7 = (f32[640]{0:T(1024)S(1)}, f32[640]{0:T(1024)}, u32[]{:S(2)}) copy-start(f32[640]{0:T(1024)} %param.17) | copy-start | bytes 7684
  18.0 1.2 %copy-start.1 = (bf16[256,640]{1,0:T(8,128)(2,1)}, bf16[256,640]{1,0:T(8,128)(2,1)S(1)}, u32[]{:S(2)}) copy-start(bf16[256,640]{1,0:T(8,128)(2,1)S(1)} %fusion.3.after_ref.refs_5_) | copy-start | bytes 983044
  18.0 34.0 %collective-permute-start.2 = (bf16[256,640]{1,0:T(8,128)(2,1)S(1)}, bf16[256,640]{1,0:T(8,128)(2,1)S(1)}, u32[]{:S(2)}, u32[]{:S(2)}) collective-permute-start(bf16[256,640]{1,0:T(8,128)(2,1)S(1)} %fusion.3.after_ref.refs_5_), channel_id=1, source_target_pairs={{0,1},{1,2},{2,3},{3,0},{4,5},{5,6},{6,7},{7,4},{8,9},{9,10},{10,1... | collective-permute-start | bytes 983048 | tf_op jit(solution)/shard_map/ppermute | solution.py:266
  18.1 33.9 %collective-permute-start.3 = (bf16[256,640]{1,0:T(8,128)(2,1)S(1)}, bf16[256,640]{1,0:T(8,128)(2,1)S(1)}, u32[]{:S(2)}, u32[]{:S(2)}) collective-permute-start(bf16[256,640]{1,0:T(8,128)(2,1)S(1)} %fusion.3.after_ref.refs_5_), channel_id=1, source_target_pairs={{0,2},{1,3},{2,0},{3,1},{4,6},{5,7},{6,4},{7,5},{8,10},{9,11},{10,... | collective-permute-start | bytes 983048 | tf_op jit(solution)/shard_map/ppermute | solution.py:266
  18.2 33.8 %collective-permute-start.4 = (bf16[256,640]{1,0:T(8,128)(2,1)S(1)}, bf16[256,640]{1,0:T(8,128)(2,1)S(1)}, u32[]{:S(2)}, u32[]{:S(2)}) collective-permute-start(bf16[256,640]{1,0:T(8,128)(2,1)S(1)} %fusion.3.after_ref.refs_5_), channel_id=1, source_target_pairs={{0,3},{1,0},{2,1},{3,2},{4,7},{5,4},{6,5},{7,6},{8,11},{9,8},{10,9... | collective-permute-start | bytes 983048 | tf_op jit(solution)/shard_map/ppermute | solution.py:266
  52.0 0.7 %copy-start.3 = (bf16[256,640]{1,0:T(8,128)(2,1)}, bf16[256,640]{1,0:T(8,128)(2,1)S(1)}, u32[]{:S(2)}) copy-start(bf16[256,640]{1,0:T(8,128)(2,1)S(1)} %collective-permute-done.2.refs_6_) | copy-start | bytes 983044
  52.0 0.8 %copy-start.4 = (bf16[256,640]{1,0:T(8,128)(2,1)}, bf16[256,640]{1,0:T(8,128)(2,1)S(1)}, u32[]{:S(2)}) copy-start(bf16[256,640]{1,0:T(8,128)(2,1)S(1)} %collective-permute-done.3.refs_7_) | copy-start | bytes 983044
  52.1 0.9 %copy-start.5 = (bf16[256,640]{1,0:T(8,128)(2,1)}, bf16[256,640]{1,0:T(8,128)(2,1)S(1)}, u32[]{:S(2)}) copy-start(bf16[256,640]{1,0:T(8,128)(2,1)S(1)} %collective-permute-done.4.refs_8_) | copy-start | bytes 983044

commit v21 on v16

--- a/solution.py
+++ b/solution.py
@@ -168,10 +168,11 @@
         sources[0][...], wq_ref[...], preferred_element_type=jnp.float32
     ).astype(q_ref.dtype)
     offset = 0
+    key_weight = jnp.transpose(wk_ref[...])
     for source in sources:
         rows = source.shape[0]
         k_ref[:, offset : offset + rows] = lax.dot_general(
-            wk_ref[...], source[...], (((0,), (1,)), ((), ())), preferred_element_type=jnp.float32
+            key_weight, source[...], (((1,), (1,)), ((), ())), preferred_element_type=jnp.float32
         ).astype(k_ref.dtype)
         v_ref[offset : offset + rows, :] = jnp.dot(
             source[...], wv_ref[...], preferred_element_type=jnp.float32

time: 69.1 us -> 69.1 us (level)
  no operation moved by 1% of the time
where the time goes in v21:
time: 69.1 us; the launch traced here: 68.9 us
  Pallas kernels  48.8 us (71%)
  starting transfers between devices  7.35 us (11%)
  matrix products  5.27 us (8%)
  waiting for transfers between devices  3.39 us (5%)
  local copies, waits for them, and re-layouts  1.71 us (2%)
  other arithmetic  1.54 us (2%)
  between operations  0.88 us (1%)
    pallas_call x1, Pallas kernels, staged_gather(): pl.pallas_call(functools.partial(staged_kernel, sizes), out_shape=jax.Sha...  32.8 us
    pallas_call x1, Pallas kernels, attention(): pl.pallas_call(functools.partial(attention_kernel, heads, len(sources)),...  16 us
    dot_general x9, matrix products, shards(): jnp.dot(window, conv_weight[row_tap, col_tap], preferred_element_type=jnp...  5.27 us
    ppermute x1, starting transfers between devices, extended(): before = lax.ppermute(last, axis, up)  4.86 us
    ppermute x1, waiting for transfers between devices, extended(): after = lax.ppermute(initial, axis, down)  3.38 us
    ppermute x1, starting transfers between devices, extended(): after = lax.ppermute(initial, axis, down)  1.92 us
  transfers between devices with their start and end apart: 5, of which 1 were waited for; matrix products, arithmetic and copies ran while one was open for 1% of the time, Pallas kernels for 48%

profile of v21, /device:TPU:1, one launch (start us, length us, event | category | flops | bytes accessed | tf_op | source)
XLA Modules:
  0.0 68.9 jit_solution(7444581230596067309)
XLA Ops:
  0.6 0.0 copy-start
  0.6 1.3 %multiply_convert_fusion = bf16[1,8,32,640]{3,2,1,0:T(8,128)(2,1)S(1)} fusion(bf16[1,8,32,640]{3,2,1,0:T(8,128)(2,1)} %param.9), kind=kLoop, calls=%fused_computation.34 | loop fusion | flops 983040 | bytes 655360 | tf_op jit(solution)/shard_map/convert_element_type | solution.py:230
  2.0 4.9 %collective-permute-start = (bf16[1,1,32,640]{3,2,1,0:T(8,128)(2,1)S(1)}, bf16[1,1,32,640]{3,2,1,0:T(8,128)(2,1)S(1)}, u32[]{:S(2)}, u32[]{:S(2)}) collective-permute-start(bf16[1,1,32,640]{3,2,1,0:T(8,128)(2,1)S(1)} %get-tuple-element.10), channel_id=1, source_target_pairs={{0,1},{1,2},{2,3},{4,5},{5,6},{6,7},{8,9},{9,10},{10,11},{12,13},{... | collective-permute-start | bytes 122888 | tf_op jit(solution)/shard_map/ppermute | solution.py:133
  6.8 1.9 %collective-permute-start.1 = (bf16[1,1,32,640]{3,2,1,0:T(8,128)(2,1)S(1)}, bf16[1,1,32,640]{3,2,1,0:T(8,128)(2,1)S(1)}, u32[]{:S(2)}, u32[]{:S(2)}) collective-permute-start(bf16[1,1,32,640]{3,2,1,0:T(8,128)(2,1)S(1)} %get-tuple-element.11), channel_id=1, source_target_pairs={{1,0},{2,1},{3,2},{5,4},{6,5},{7,6},{9,8},{10,9},{11,10},{13,12},{... | collective-permute-start | bytes 122888 | tf_op jit(solution)/shard_map/ppermute | solution.py:134
  8.8 0.0 collective-permute-done
  8.8 3.4 %collective-permute-done.1 = bf16[1,1,32,640]{3,2,1,0:T(8,128)(2,1)S(1)} collective-permute-done((bf16[1,1,32,640]{3,2,1,0:T(8,128)(2,1)S(1)}, bf16[1,1,32,640]{3,2,1,0:T(8,128)(2,1)S(1)}, u32[]{:S(2)}, u32[]{:S(2)}) %collective-permute-start.1) | collective-permute-done | bytes 40992 | tf_op jit(solution)/shard_map/ppermute | solution.py:134
  12.2 0.2 fusion.29
  12.3 0.2 fusion.30
  12.5 1.6 %fusion.14 = f32[256,640]{1,0:T(8,128)S(1)} fusion(bf16[256,640]{1,0:T(8,128)(2,1)S(1)} %bitcast.62, bf16[3,3,640,640]{3,2,1,0:T(8,128)(2,1)} %param.10), kind=kOutput, calls=%fused_computation.23 | convolution fusion | flops 209715200 | bytes 1802240 | tf_op jit(solution)/shard_map/dot_general | solution.py:239
  14.2 0.0 copy-done
  14.2 0.5 fusion.5
  14.6 0.1 pad_maximum_fusion
  14.7 0.0 copy-start.2
  14.7 0.0 copy-start.6
  14.7 0.5 convolution_add_fusion.6
  15.2 0.0 copy-start.7
  15.2 0.5 convolution_add_fusion.5
  15.7 0.5 convolution_add_fusion.4
  16.1 0.5 convolution_add_fusion.3
  16.6 0.5 convolution_add_fusion.2
  17.0 0.5 convolution_add_fusion.1
  17.5 0.0 copy-done.2
  17.5 0.0 copy-done.6
  17.5 0.5 fusion.3.after_ref.refs_5_
  18.0 0.0 copy-start.1
  18.0 0.1 collective-permute-start.2
  18.1 0.1 collective-permute-start.3
  18.2 0.4 collective-permute-start.4
  18.6 0.0 copy-done.7
  18.6 0.6 reshape.57.refs_4_
  19.2 0.0 copy-done.1
  19.2 32.8 %shard_map.104 = bf16[64,16,640]{2,1,0:T(8,128)(2,1)} custom-call(bf16[1,16,640]{2,1,0:T(8,128)(2,1)} %bitcast.64, bf16[256,640]{1,0:T(8,128)(2,1)} %copy-done.1), custom_call_target="tpu_custom_call" | custom-call | tf_op jit(solution)/shard_map/pallas_call | solution.py:115
  52.0 0.0 collective-permute-done.2.refs_6_
  52.0 0.0 copy-start.3
  52.0 0.0 collective-permute-done.3.refs_7_
  52.0 0.0 copy-start.4
  52.1 0.0 collective-permute-done.4.refs_8_
  52.1 0.0 copy-start.5
  52.1 0.7 copy-done.3
  52.8 0.1 copy-done.4
  52.9 0.1 copy-done.5
  53.0 16.0 %shard_map.105 = bf16[256,640]{1,0:T(8,128)(2,1)} custom-call(bf16[640,640]{1,0:T(8,128)(2,1)} %refs_0_.1, bf16[640,640]{1,0:T(8,128)(2,1)} %refs_1_.1, bf16[640,640]{1,0:T(8,128)(2,1)} %refs_2_.1, bf16[640,640]{1,0:T(8,128)(2,1)} %refs_3_.1, f32[1,640]{1,0:T(1,128)} %reshape.57.refs_4_, bf16[256,640]{1,0:T(8,128)(2,1)} %copy-done.1, ...), custom_call_target="tpu_custom_call" | custom-call | tf_op jit(solution)/shard_map/pallas_call | solution.py:201
  (1 shorter events, 0.0 us)
Async XLA Ops:
  0.6 13.5 %copy-start = (bf16[3,3,640,640]{3,2,1,0:T(8,128)(2,1)S(1)}, bf16[3,3,640,640]{3,2,1,0:T(8,128)(2,1)}, u32[]{:S(2)}) copy-start(bf16[3,3,640,640]{3,2,1,0:T(8,128)(2,1)} %param.10) | copy-start | bytes 22118404
  2.0 6.8 %collective-permute-start = (bf16[1,1,32,640]{3,2,1,0:T(8,128)(2,1)S(1)}, bf16[1,1,32,640]{3,2,1,0:T(8,128)(2,1)S(1)}, u32[]{:S(2)}, u32[]{:S(2)}) collective-permute-start(bf16[1,1,32,640]{3,2,1,0:T(8,128)(2,1)S(1)} %get-tuple-element.10), channel_id=1, source_target_pairs={{0,1},{1,2},{2,3},{4,5},{5,6},{6,7},{8,9},{9,10},{10,11},{12,13},{... | collective-permute-start | bytes 122888 | tf_op jit(solution)/shard_map/ppermute | solution.py:133
  6.8 5.3 %collective-permute-start.1 = (bf16[1,1,32,640]{3,2,1,0:T(8,128)(2,1)S(1)}, bf16[1,1,32,640]{3,2,1,0:T(8,128)(2,1)S(1)}, u32[]{:S(2)}, u32[]{:S(2)}) collective-permute-start(bf16[1,1,32,640]{3,2,1,0:T(8,128)(2,1)S(1)} %get-tuple-element.11), channel_id=1, source_target_pairs={{1,0},{2,1},{3,2},{5,4},{6,5},{7,6},{9,8},{10,9},{11,10},{13,12},{... | collective-permute-start | bytes 122888 | tf_op jit(solution)/shard_map/ppermute | solution.py:134
  14.7 2.8 %copy-start.2 = (bf16[1,8,32,640]{3,2,1,0:T(8,128)(2,1)S(1)}, bf16[1,8,32,640]{3,2,1,0:T(8,128)(2,1)}, u32[]{:S(2)}) copy-start(bf16[1,8,32,640]{3,2,1,0:T(8,128)(2,1)} %param.9) | copy-start | bytes 983044
  14.7 2.8 %copy-start.6 = (f32[640]{0:T(1024)S(1)}, f32[640]{0:T(1024)}, u32[]{:S(2)}) copy-start(f32[640]{0:T(1024)} %param.11) | copy-start | bytes 7684
  15.2 3.4 %copy-start.7 = (f32[640]{0:T(1024)S(1)}, f32[640]{0:T(1024)}, u32[]{:S(2)}) copy-start(f32[640]{0:T(1024)} %param.17) | copy-start | bytes 7684
  18.0 1.2 %copy-start.1 = (bf16[256,640]{1,0:T(8,128)(2,1)}, bf16[256,640]{1,0:T(8,128)(2,1)S(1)}, u32[]{:S(2)}) copy-start(bf16[256,640]{1,0:T(8,128)(2,1)S(1)} %fusion.3.after_ref.refs_5_) | copy-start | bytes 983044
  18.0 34.0 %collective-permute-start.2 = (bf16[256,640]{1,0:T(8,128)(2,1)S(1)}, bf16[256,640]{1,0:T(8,128)(2,1)S(1)}, u32[]{:S(2)}, u32[]{:S(2)}) collective-permute-start(bf16[256,640]{1,0:T(8,128)(2,1)S(1)} %fusion.3.after_ref.refs_5_), channel_id=1, source_target_pairs={{0,1},{1,2},{2,3},{3,0},{4,5},{5,6},{6,7},{7,4},{8,9},{9,10},{10,1... | collective-permute-start | bytes 983048 | tf_op jit(solution)/shard_map/ppermute | solution.py:247
  18.1 33.9 %collective-permute-start.3 = (bf16[256,640]{1,0:T(8,128)(2,1)S(1)}, bf16[256,640]{1,0:T(8,128)(2,1)S(1)}, u32[]{:S(2)}, u32[]{:S(2)}) collective-permute-start(bf16[256,640]{1,0:T(8,128)(2,1)S(1)} %fusion.3.after_ref.refs_5_), channel_id=1, source_target_pairs={{0,2},{1,3},{2,0},{3,1},{4,6},{5,7},{6,4},{7,5},{8,10},{9,11},{10,... | collective-permute-start | bytes 983048 | tf_op jit(solution)/shard_map/ppermute | solution.py:247
  18.2 33.8 %collective-permute-start.4 = (bf16[256,640]{1,0:T(8,128)(2,1)S(1)}, bf16[256,640]{1,0:T(8,128)(2,1)S(1)}, u32[]{:S(2)}, u32[]{:S(2)}) collective-permute-start(bf16[256,640]{1,0:T(8,128)(2,1)S(1)} %fusion.3.after_ref.refs_5_), channel_id=1, source_target_pairs={{0,3},{1,0},{2,1},{3,2},{4,7},{5,4},{6,5},{7,6},{8,11},{9,8},{10,9... | collective-permute-start | bytes 983048 | tf_op jit(solution)/shard_map/ppermute | solution.py:247
  52.0 0.7 %copy-start.3 = (bf16[256,640]{1,0:T(8,128)(2,1)}, bf16[256,640]{1,0:T(8,128)(2,1)S(1)}, u32[]{:S(2)}) copy-start(bf16[256,640]{1,0:T(8,128)(2,1)S(1)} %collective-permute-done.2.refs_6_) | copy-start | bytes 983044
  52.0 0.8 %copy-start.4 = (bf16[256,640]{1,0:T(8,128)(2,1)}, bf16[256,640]{1,0:T(8,128)(2,1)S(1)}, u32[]{:S(2)}) copy-start(bf16[256,640]{1,0:T(8,128)(2,1)S(1)} %collective-permute-done.3.refs_7_) | copy-start | bytes 983044
  52.1 0.9 %copy-start.5 = (bf16[256,640]{1,0:T(8,128)(2,1)}, bf16[256,640]{1,0:T(8,128)(2,1)S(1)}, u32[]{:S(2)}) copy-start(bf16[256,640]{1,0:T(8,128)(2,1)S(1)} %collective-permute-done.4.refs_8_) | copy-start | bytes 983044

commit v22 on v16

--- a/solution.py
+++ b/solution.py
@@ -120,7 +120,7 @@
         scratch_shapes=[pltpu.SemaphoreType.DMA] + sems,
         compiler_params=pltpu.CompilerParams(collective_id=0, has_side_effects=True),
     )(value[None], after)
-    return gathered.reshape((total * value.shape[0],) + value.shape[1:])
+    return gathered
 
 
 def extended(value, axis, dim, width):
@@ -168,13 +168,15 @@
         sources[0][...], wq_ref[...], preferred_element_type=jnp.float32
     ).astype(q_ref.dtype)
     offset = 0
-    for source in sources:
+    for source_ref in sources:
+        source = source_ref[...]
+        source = source.reshape(-1, source.shape[-1])
         rows = source.shape[0]
         k_ref[:, offset : offset + rows] = lax.dot_general(
-            wk_ref[...], source[...], (((0,), (1,)), ((), ())), preferred_element_type=jnp.float32
+            wk_ref[...], source, (((0,), (1,)), ((), ())), preferred_element_type=jnp.float32
         ).astype(k_ref.dtype)
         v_ref[offset : offset + rows, :] = jnp.dot(
-            source[...], wv_ref[...], preferred_element_type=jnp.float32
+            source, wv_ref[...], preferred_element_type=jnp.float32
         ).astype(v_ref.dtype)
         offset += rows
     for head in range(heads):
@@ -194,8 +196,8 @@
 
 def attention(w_query, w_key, w_value, w_out, out_bias, sources, heads):
     tokens, channels = sources[0].shape
-    length = sum(source.shape[0] for source in sources)
-    whole = lambda array: pl.BlockSpec(array.shape, lambda i: (0, 0))
+    length = sum(source.size // channels for source in sources)
+    whole = lambda array: pl.BlockSpec(array.shape, lambda i: (0,) * array.ndim)
     operands = (w_query, w_key, w_value, w_out, out_bias.reshape(1, -1)) + tuple(sources)
     return pl.pallas_call(
         functools.partial(attention_kernel, heads, len(sources)),

time: 69.1 us -> 69.7 us (level)
  transfers between devices with their start and end apart: 5 -> 5, of which waited for: 1 -> 1; matrix products, arithmetic and copies ran while one was open for 1% -> 1% of each run, Pallas kernels for 48% -> 47%
where the time goes in v22:
time: 69.7 us; the launch traced here: 69.6 us
  Pallas kernels  48.8 us (70%)
  starting transfers between devices  7.35 us (11%)
  matrix products  5.27 us (8%)
  waiting for transfers between devices  3.39 us (5%)
  local copies, waits for them, and re-layouts  2.35 us (3%)
  other arithmetic  1.54 us (2%)
  between operations  0.88 us (1%)
    pallas_call x1, Pallas kernels, staged_gather(): pl.pallas_call(functools.partial(staged_kernel, sizes), out_shape=jax.Sha...  32.8 us
    pallas_call x1, Pallas kernels, attention(): pl.pallas_call(functools.partial(attention_kernel, heads, len(sources)),...  16 us
    dot_general x9, matrix products, shards(): jnp.dot(window, conv_weight[row_tap, col_tap], preferred_element_type=jnp...  5.27 us
    ppermute x1, starting transfers between devices, extended(): before = lax.ppermute(last, axis, up)  4.86 us
    ppermute x1, waiting for transfers between devices, extended(): after = lax.ppermute(initial, axis, down)  3.38 us
    ppermute x1, starting transfers between devices, extended(): after = lax.ppermute(initial, axis, down)  1.92 us
    unnamed x16, local copies, waits for them, and re-layouts  1.56 us
  transfers between devices with their start and end apart: 5, of which 1 were waited for; matrix products, arithmetic and copies ran while one was open for 1% of the time, Pallas kernels for 47%

profile of v22, /device:TPU:1, one launch (start us, length us, event | category | flops | bytes accessed | tf_op | source)
XLA Modules:
  0.0 69.6 jit_solution(13985193576697197611)
XLA Ops:
  0.6 0.0 copy-start
  0.6 1.3 %multiply_convert_fusion = bf16[1,8,32,640]{3,2,1,0:T(8,128)(2,1)S(1)} fusion(bf16[1,8,32,640]{3,2,1,0:T(8,128)(2,1)} %param.9), kind=kLoop, calls=%fused_computation.34 | loop fusion | flops 983040 | bytes 655360 | tf_op jit(solution)/shard_map/convert_element_type | solution.py:231
  2.0 4.9 %collective-permute-start = (bf16[1,1,32,640]{3,2,1,0:T(8,128)(2,1)S(1)}, bf16[1,1,32,640]{3,2,1,0:T(8,128)(2,1)S(1)}, u32[]{:S(2)}, u32[]{:S(2)}) collective-permute-start(bf16[1,1,32,640]{3,2,1,0:T(8,128)(2,1)S(1)} %get-tuple-element.10), channel_id=1, source_target_pairs={{0,1},{1,2},{2,3},{4,5},{5,6},{6,7},{8,9},{9,10},{10,11},{12,13},{... | collective-permute-start | bytes 122888 | tf_op jit(solution)/shard_map/ppermute | solution.py:133
  6.8 1.9 %collective-permute-start.1 = (bf16[1,1,32,640]{3,2,1,0:T(8,128)(2,1)S(1)}, bf16[1,1,32,640]{3,2,1,0:T(8,128)(2,1)S(1)}, u32[]{:S(2)}, u32[]{:S(2)}) collective-permute-start(bf16[1,1,32,640]{3,2,1,0:T(8,128)(2,1)S(1)} %get-tuple-element.11), channel_id=1, source_target_pairs={{1,0},{2,1},{3,2},{5,4},{6,5},{7,6},{9,8},{10,9},{11,10},{13,12},{... | collective-permute-start | bytes 122888 | tf_op jit(solution)/shard_map/ppermute | solution.py:134
  8.8 0.0 collective-permute-done
  8.8 3.4 %collective-permute-done.1 = bf16[1,1,32,640]{3,2,1,0:T(8,128)(2,1)S(1)} collective-permute-done((bf16[1,1,32,640]{3,2,1,0:T(8,128)(2,1)S(1)}, bf16[1,1,32,640]{3,2,1,0:T(8,128)(2,1)S(1)}, u32[]{:S(2)}, u32[]{:S(2)}) %collective-permute-start.1) | collective-permute-done | bytes 40992 | tf_op jit(solution)/shard_map/ppermute | solution.py:134
  12.2 0.2 fusion.29
  12.3 0.2 fusion.30
  12.5 1.6 %fusion.14 = f32[256,640]{1,0:T(8,128)S(1)} fusion(bf16[256,640]{1,0:T(8,128)(2,1)S(1)} %bitcast.60, bf16[3,3,640,640]{3,2,1,0:T(8,128)(2,1)} %param.10), kind=kOutput, calls=%fused_computation.23 | convolution fusion | flops 209715200 | bytes 1802240 | tf_op jit(solution)/shard_map/dot_general | solution.py:240
  14.2 0.0 copy-done
  14.2 0.5 fusion.5
  14.6 0.1 pad_maximum_fusion
  14.7 0.0 copy-start.2
  14.7 0.0 copy-start.6
  14.7 0.5 convolution_add_fusion.6
  15.2 0.0 copy-start.7
  15.2 0.5 convolution_add_fusion.5
  15.7 0.5 convolution_add_fusion.4
  16.1 0.5 convolution_add_fusion.3
  16.6 0.5 convolution_add_fusion.2
  17.0 0.5 convolution_add_fusion.1
  17.5 0.0 copy-done.2
  17.5 0.0 copy-done.6
  17.5 0.5 fusion.3.after_ref.refs_5_
  18.0 0.0 copy-start.1
  18.0 0.1 collective-permute-start.2
  18.1 0.1 collective-permute-start.3
  18.2 0.4 collective-permute-start.4
  18.6 0.0 copy-done.7
  18.6 0.6 reshape.54.refs_4_
  19.2 0.0 copy-done.1
  19.2 32.8 %shard_map.104.refs_9_ = bf16[64,16,640]{2,1,0:T(8,128)(2,1)} custom-call(bf16[1,16,640]{2,1,0:T(8,128)(2,1)} %bitcast.62, bf16[256,640]{1,0:T(8,128)(2,1)} %copy-done.1), custom_call_target="tpu_custom_call" | custom-call | tf_op jit(solution)/shard_map/pallas_call | solution.py:115
  52.0 0.0 collective-permute-done.2.refs_6_
  52.0 0.0 copy-start.3
  52.0 0.0 collective-permute-done.3.refs_7_
  52.0 0.0 copy-start.4
  52.1 0.0 collective-permute-done.4.refs_8_
  52.1 0.7 copy-done.3
  52.8 0.1 copy-done.4
  52.9 0.0 copy-start.5
  52.9 0.7 %copy-done.5 = bf16[256,640]{1,0:T(8,128)(2,1)} copy-done((bf16[256,640]{1,0:T(8,128)(2,1)}, bf16[256,640]{1,0:T(8,128)(2,1)S(1)}, u32[]{:S(2)}) %copy-start.5) | copy-done | bytes 327704
  53.6 16.0 %shard_map.105 = bf16[256,640]{1,0:T(8,128)(2,1)} custom-call(bf16[640,640]{1,0:T(8,128)(2,1)} %refs_0_.1, bf16[640,640]{1,0:T(8,128)(2,1)} %refs_1_.1, bf16[640,640]{1,0:T(8,128)(2,1)} %refs_2_.1, bf16[640,640]{1,0:T(8,128)(2,1)} %refs_3_.1, f32[1,640]{1,0:T(1,128)} %reshape.54.refs_4_, bf16[256,640]{1,0:T(8,128)(2,1)} %copy-done.1, ...), custom_call_target="tpu_custom_call" | custom-call | tf_op jit(solution)/shard_map/pallas_call | solution.py:202
  (1 shorter events, 0.0 us)
Async XLA Ops:
  0.6 13.5 %copy-start = (bf16[3,3,640,640]{3,2,1,0:T(8,128)(2,1)S(1)}, bf16[3,3,640,640]{3,2,1,0:T(8,128)(2,1)}, u32[]{:S(2)}) copy-start(bf16[3,3,640,640]{3,2,1,0:T(8,128)(2,1)} %param.10) | copy-start | bytes 22118404
  2.0 6.8 %collective-permute-start = (bf16[1,1,32,640]{3,2,1,0:T(8,128)(2,1)S(1)}, bf16[1,1,32,640]{3,2,1,0:T(8,128)(2,1)S(1)}, u32[]{:S(2)}, u32[]{:S(2)}) collective-permute-start(bf16[1,1,32,640]{3,2,1,0:T(8,128)(2,1)S(1)} %get-tuple-element.10), channel_id=1, source_target_pairs={{0,1},{1,2},{2,3},{4,5},{5,6},{6,7},{8,9},{9,10},{10,11},{12,13},{... | collective-permute-start | bytes 122888 | tf_op jit(solution)/shard_map/ppermute | solution.py:133
  6.8 5.3 %collective-permute-start.1 = (bf16[1,1,32,640]{3,2,1,0:T(8,128)(2,1)S(1)}, bf16[1,1,32,640]{3,2,1,0:T(8,128)(2,1)S(1)}, u32[]{:S(2)}, u32[]{:S(2)}) collective-permute-start(bf16[1,1,32,640]{3,2,1,0:T(8,128)(2,1)S(1)} %get-tuple-element.11), channel_id=1, source_target_pairs={{1,0},{2,1},{3,2},{5,4},{6,5},{7,6},{9,8},{10,9},{11,10},{13,12},{... | collective-permute-start | bytes 122888 | tf_op jit(solution)/shard_map/ppermute | solution.py:134
  14.7 2.8 %copy-start.2 = (bf16[1,8,32,640]{3,2,1,0:T(8,128)(2,1)S(1)}, bf16[1,8,32,640]{3,2,1,0:T(8,128)(2,1)}, u32[]{:S(2)}) copy-start(bf16[1,8,32,640]{3,2,1,0:T(8,128)(2,1)} %param.9) | copy-start | bytes 983044
  14.7 2.8 %copy-start.6 = (f32[640]{0:T(1024)S(1)}, f32[640]{0:T(1024)}, u32[]{:S(2)}) copy-start(f32[640]{0:T(1024)} %param.11) | copy-start | bytes 7684
  15.2 3.4 %copy-start.7 = (f32[640]{0:T(1024)S(1)}, f32[640]{0:T(1024)}, u32[]{:S(2)}) copy-start(f32[640]{0:T(1024)} %param.17) | copy-start | bytes 7684
  18.0 1.2 %copy-start.1 = (bf16[256,640]{1,0:T(8,128)(2,1)}, bf16[256,640]{1,0:T(8,128)(2,1)S(1)}, u32[]{:S(2)}) copy-start(bf16[256,640]{1,0:T(8,128)(2,1)S(1)} %fusion.3.after_ref.refs_5_) | copy-start | bytes 983044
  18.0 34.0 %collective-permute-start.2 = (bf16[256,640]{1,0:T(8,128)(2,1)S(1)}, bf16[256,640]{1,0:T(8,128)(2,1)S(1)}, u32[]{:S(2)}, u32[]{:S(2)}) collective-permute-start(bf16[256,640]{1,0:T(8,128)(2,1)S(1)} %fusion.3.after_ref.refs_5_), channel_id=1, source_target_pairs={{0,1},{1,2},{2,3},{3,0},{4,5},{5,6},{6,7},{7,4},{8,9},{9,10},{10,1... | collective-permute-start | bytes 983048 | tf_op jit(solution)/shard_map/ppermute | solution.py:248
  18.1 33.9 %collective-permute-start.3 = (bf16[256,640]{1,0:T(8,128)(2,1)S(1)}, bf16[256,640]{1,0:T(8,128)(2,1)S(1)}, u32[]{:S(2)}, u32[]{:S(2)}) collective-permute-start(bf16[256,640]{1,0:T(8,128)(2,1)S(1)} %fusion.3.after_ref.refs_5_), channel_id=1, source_target_pairs={{0,2},{1,3},{2,0},{3,1},{4,6},{5,7},{6,4},{7,5},{8,10},{9,11},{10,... | collective-permute-start | bytes 983048 | tf_op jit(solution)/shard_map/ppermute | solution.py:248
  18.2 33.8 %collective-permute-start.4 = (bf16[256,640]{1,0:T(8,128)(2,1)S(1)}, bf16[256,640]{1,0:T(8,128)(2,1)S(1)}, u32[]{:S(2)}, u32[]{:S(2)}) collective-permute-start(bf16[256,640]{1,0:T(8,128)(2,1)S(1)} %fusion.3.after_ref.refs_5_), channel_id=1, source_target_pairs={{0,3},{1,0},{2,1},{3,2},{4,7},{5,4},{6,5},{7,6},{8,11},{9,8},{10,9... | collective-permute-start | bytes 983048 | tf_op jit(solution)/shard_map/ppermute | solution.py:248
  52.0 0.7 %copy-start.3 = (bf16[256,640]{1,0:T(8,128)(2,1)}, bf16[256,640]{1,0:T(8,128)(2,1)S(1)}, u32[]{:S(2)}) copy-start(bf16[256,640]{1,0:T(8,128)(2,1)S(1)} %collective-permute-done.2.refs_6_) | copy-start | bytes 983044
  52.0 0.8 %copy-start.4 = (bf16[256,640]{1,0:T(8,128)(2,1)}, bf16[256,640]{1,0:T(8,128)(2,1)S(1)}, u32[]{:S(2)}) copy-start(bf16[256,640]{1,0:T(8,128)(2,1)S(1)} %collective-permute-done.3.refs_7_) | copy-start | bytes 983044
  52.9 0.7 %copy-start.5 = (bf16[256,640]{1,0:T(8,128)(2,1)}, bf16[256,640]{1,0:T(8,128)(2,1)S(1)}, u32[]{:S(2)}) copy-start(bf16[256,640]{1,0:T(8,128)(2,1)S(1)} %collective-permute-done.4.refs_8_) | copy-start | bytes 983044

commit v23 on v16

--- a/solution.py
+++ b/solution.py
@@ -59,15 +59,11 @@
     own = out_ref.at[pl.ds(block_of(zz), 1)]
     mine = zz // half == core
 
-    @pl.when(mine)
-    def _():
-        local = pltpu.make_async_copy(x_ref, own, local_sem)
-        local.start()
-        local.wait()
-
-    def remote(ref, peer, send_sem, recv_sem):
+    local = pltpu.make_async_copy(x_ref, own, local_sem)
+
+    def remote(ref, peer, send_sem, recv_sem, source=None):
         return pltpu.make_async_remote_copy(
-            src_ref=ref,
+            src_ref=ref if source is None else source,
             dst_ref=ref,
             send_sem=send_sem,
             recv_sem=recv_sem,
@@ -75,12 +71,16 @@
             device_id_type=MESH,
         )
 
-    z_copies = [remote(own, z_peer(s), sems[0].at[s], sems[1].at[s]) for s in range(1, along)]
+    z_copies = [
+        remote(own, z_peer(s), sems[0].at[s], sems[1].at[s], x_ref) for s in range(1, along)
+    ]
 
     @pl.when(mine)
     def _():
         for copy in z_copies:
             copy.start()
+        local.start()
+        local.wait()
         for copy in z_copies:
             copy.wait_send()
 

time: 69.1 us -> 67.4 us (0.975)
  Pallas kernels: 48.8 us -> 47.1 us
    pallas_call x1, Pallas kernels: 32.8 us -> 31.1 us  [staged_gather(): pl.pallas_call(functools.partial(staged_kernel, sizes), out_shape=jax.Sha...]
  transfers between devices with their start and end apart: 5 -> 5, of which waited for: 1 -> 1; matrix products, arithmetic and copies ran while one was open for 1% -> 1% of each run, Pallas kernels for 48% -> 46%
where the time goes in v23:
time: 67.4 us; the launch traced here: 67.2 us
  Pallas kernels  47.1 us (70%)
  starting transfers between devices  7.35 us (11%)
  matrix products  5.27 us (8%)
  waiting for transfers between devices  3.39 us (5%)
  local copies, waits for them, and re-layouts  1.71 us (3%)
  other arithmetic  1.54 us (2%)
  between operations  0.88 us (1%)
    pallas_call x1, Pallas kernels, staged_gather(): pl.pallas_call(functools.partial(staged_kernel, sizes), out_shape=jax.Sha...  31.1 us
    pallas_call x1, Pallas kernels, attention(): pl.pallas_call(functools.partial(attention_kernel, heads, len(sources)),...  16 us
    dot_general x9, matrix products, shards(): jnp.dot(window, conv_weight[row_tap, col_tap], preferred_element_type=jnp...  5.27 us
    ppermute x1, starting transfers between devices, extended(): before = lax.ppermute(last, axis, up)  4.86 us
    ppermute x1, waiting for transfers between devices, extended(): after = lax.ppermute(initial, axis, down)  3.38 us
    ppermute x1, starting transfers between devices, extended(): after = lax.ppermute(initial, axis, down)  1.92 us
  transfers between devices with their start and end apart: 5, of which 1 were waited for; matrix products, arithmetic and copies ran while one was open for 1% of the time, Pallas kernels for 46%

profile of v23, /device:TPU:1, one launch (start us, length us, event | category | flops | bytes accessed | tf_op | source)
XLA Modules:
  0.0 67.2 jit_solution(7971745612891773865)
XLA Ops:
  0.6 0.0 copy-start
  0.6 1.3 %multiply_convert_fusion = bf16[1,8,32,640]{3,2,1,0:T(8,128)(2,1)S(1)} fusion(bf16[1,8,32,640]{3,2,1,0:T(8,128)(2,1)} %param.9), kind=kLoop, calls=%fused_computation.34 | loop fusion | flops 983040 | bytes 655360 | tf_op jit(solution)/shard_map/convert_element_type | solution.py:229
  2.0 4.9 %collective-permute-start = (bf16[1,1,32,640]{3,2,1,0:T(8,128)(2,1)S(1)}, bf16[1,1,32,640]{3,2,1,0:T(8,128)(2,1)S(1)}, u32[]{:S(2)}, u32[]{:S(2)}) collective-permute-start(bf16[1,1,32,640]{3,2,1,0:T(8,128)(2,1)S(1)} %get-tuple-element.10), channel_id=1, source_target_pairs={{0,1},{1,2},{2,3},{4,5},{5,6},{6,7},{8,9},{9,10},{10,11},{12,13},{... | collective-permute-start | bytes 122888 | tf_op jit(solution)/shard_map/ppermute | solution.py:133
  6.8 1.9 %collective-permute-start.1 = (bf16[1,1,32,640]{3,2,1,0:T(8,128)(2,1)S(1)}, bf16[1,1,32,640]{3,2,1,0:T(8,128)(2,1)S(1)}, u32[]{:S(2)}, u32[]{:S(2)}) collective-permute-start(bf16[1,1,32,640]{3,2,1,0:T(8,128)(2,1)S(1)} %get-tuple-element.11), channel_id=1, source_target_pairs={{1,0},{2,1},{3,2},{5,4},{6,5},{7,6},{9,8},{10,9},{11,10},{13,12},{... | collective-permute-start | bytes 122888 | tf_op jit(solution)/shard_map/ppermute | solution.py:134
  8.8 0.0 collective-permute-done
  8.8 3.4 %collective-permute-done.1 = bf16[1,1,32,640]{3,2,1,0:T(8,128)(2,1)S(1)} collective-permute-done((bf16[1,1,32,640]{3,2,1,0:T(8,128)(2,1)S(1)}, bf16[1,1,32,640]{3,2,1,0:T(8,128)(2,1)S(1)}, u32[]{:S(2)}, u32[]{:S(2)}) %collective-permute-start.1) | collective-permute-done | bytes 40992 | tf_op jit(solution)/shard_map/ppermute | solution.py:134
  12.2 0.2 fusion.29
  12.3 0.2 fusion.30
  12.5 1.6 %fusion.14 = f32[256,640]{1,0:T(8,128)S(1)} fusion(bf16[256,640]{1,0:T(8,128)(2,1)S(1)} %bitcast.62, bf16[3,3,640,640]{3,2,1,0:T(8,128)(2,1)} %param.10), kind=kOutput, calls=%fused_computation.23 | convolution fusion | flops 209715200 | bytes 1802240 | tf_op jit(solution)/shard_map/dot_general | solution.py:238
  14.2 0.0 copy-done
  14.2 0.5 fusion.5
  14.6 0.1 pad_maximum_fusion
  14.7 0.0 copy-start.2
  14.7 0.0 copy-start.6
  14.7 0.5 convolution_add_fusion.6
  15.2 0.0 copy-start.7
  15.2 0.5 convolution_add_fusion.5
  15.7 0.5 convolution_add_fusion.4
  16.1 0.5 convolution_add_fusion.3
  16.6 0.5 convolution_add_fusion.2
  17.0 0.5 convolution_add_fusion.1
  17.5 0.0 copy-done.2
  17.5 0.0 copy-done.6
  17.5 0.5 fusion.3.after_ref.refs_5_
  18.0 0.0 copy-start.1
  18.0 0.1 collective-permute-start.2
  18.1 0.1 collective-permute-start.3
  18.2 0.4 collective-permute-start.4
  18.6 0.0 copy-done.7
  18.6 0.6 reshape.57.refs_4_
  19.2 0.0 copy-done.1
  19.2 31.1 %shard_map.104 = bf16[64,16,640]{2,1,0:T(8,128)(2,1)} custom-call(bf16[1,16,640]{2,1,0:T(8,128)(2,1)} %bitcast.64, bf16[256,640]{1,0:T(8,128)(2,1)} %copy-done.1), custom_call_target="tpu_custom_call" | custom-call | tf_op jit(solution)/shard_map/pallas_call | solution.py:115
  50.3 0.0 collective-permute-done.2.refs_6_
  50.3 0.0 copy-start.3
  50.3 0.0 collective-permute-done.3.refs_7_
  50.3 0.0 copy-start.4
  50.3 0.0 collective-permute-done.4.refs_8_
  50.4 0.0 copy-start.5
  50.4 0.7 %copy-done.3 = bf16[256,640]{1,0:T(8,128)(2,1)} copy-done((bf16[256,640]{1,0:T(8,128)(2,1)}, bf16[256,640]{1,0:T(8,128)(2,1)S(1)}, u32[]{:S(2)}) %copy-start.3) | copy-done | bytes 327704
  51.0 0.1 copy-done.4
  51.2 0.1 copy-done.5
  51.2 16.0 %shard_map.105 = bf16[256,640]{1,0:T(8,128)(2,1)} custom-call(bf16[640,640]{1,0:T(8,128)(2,1)} %refs_0_.1, bf16[640,640]{1,0:T(8,128)(2,1)} %refs_1_.1, bf16[640,640]{1,0:T(8,128)(2,1)} %refs_2_.1, bf16[640,640]{1,0:T(8,128)(2,1)} %refs_3_.1, f32[1,640]{1,0:T(1,128)} %reshape.57.refs_4_, bf16[256,640]{1,0:T(8,128)(2,1)} %copy-done.1, ...), custom_call_target="tpu_custom_call" | custom-call | tf_op jit(solution)/shard_map/pallas_call | solution.py:200
  (1 shorter events, 0.0 us)
Async XLA Ops:
  0.6 13.5 %copy-start = (bf16[3,3,640,640]{3,2,1,0:T(8,128)(2,1)S(1)}, bf16[3,3,640,640]{3,2,1,0:T(8,128)(2,1)}, u32[]{:S(2)}) copy-start(bf16[3,3,640,640]{3,2,1,0:T(8,128)(2,1)} %param.10) | copy-start | bytes 22118404
  2.0 6.8 %collective-permute-start = (bf16[1,1,32,640]{3,2,1,0:T(8,128)(2,1)S(1)}, bf16[1,1,32,640]{3,2,1,0:T(8,128)(2,1)S(1)}, u32[]{:S(2)}, u32[]{:S(2)}) collective-permute-start(bf16[1,1,32,640]{3,2,1,0:T(8,128)(2,1)S(1)} %get-tuple-element.10), channel_id=1, source_target_pairs={{0,1},{1,2},{2,3},{4,5},{5,6},{6,7},{8,9},{9,10},{10,11},{12,13},{... | collective-permute-start | bytes 122888 | tf_op jit(solution)/shard_map/ppermute | solution.py:133
  6.8 5.3 %collective-permute-start.1 = (bf16[1,1,32,640]{3,2,1,0:T(8,128)(2,1)S(1)}, bf16[1,1,32,640]{3,2,1,0:T(8,128)(2,1)S(1)}, u32[]{:S(2)}, u32[]{:S(2)}) collective-permute-start(bf16[1,1,32,640]{3,2,1,0:T(8,128)(2,1)S(1)} %get-tuple-element.11), channel_id=1, source_target_pairs={{1,0},{2,1},{3,2},{5,4},{6,5},{7,6},{9,8},{10,9},{11,10},{13,12},{... | collective-permute-start | bytes 122888 | tf_op jit(solution)/shard_map/ppermute | solution.py:134
  14.7 2.8 %copy-start.2 = (bf16[1,8,32,640]{3,2,1,0:T(8,128)(2,1)S(1)}, bf16[1,8,32,640]{3,2,1,0:T(8,128)(2,1)}, u32[]{:S(2)}) copy-start(bf16[1,8,32,640]{3,2,1,0:T(8,128)(2,1)} %param.9) | copy-start | bytes 983044
  14.7 2.8 %copy-start.6 = (f32[640]{0:T(1024)S(1)}, f32[640]{0:T(1024)}, u32[]{:S(2)}) copy-start(f32[640]{0:T(1024)} %param.11) | copy-start | bytes 7684
  15.2 3.4 %copy-start.7 = (f32[640]{0:T(1024)S(1)}, f32[640]{0:T(1024)}, u32[]{:S(2)}) copy-start(f32[640]{0:T(1024)} %param.17) | copy-start | bytes 7684
  18.0 1.2 %copy-start.1 = (bf16[256,640]{1,0:T(8,128)(2,1)}, bf16[256,640]{1,0:T(8,128)(2,1)S(1)}, u32[]{:S(2)}) copy-start(bf16[256,640]{1,0:T(8,128)(2,1)S(1)} %fusion.3.after_ref.refs_5_) | copy-start | bytes 983044
  18.0 32.3 %collective-permute-start.2 = (bf16[256,640]{1,0:T(8,128)(2,1)S(1)}, bf16[256,640]{1,0:T(8,128)(2,1)S(1)}, u32[]{:S(2)}, u32[]{:S(2)}) collective-permute-start(bf16[256,640]{1,0:T(8,128)(2,1)S(1)} %fusion.3.after_ref.refs_5_), channel_id=1, source_target_pairs={{0,1},{1,2},{2,3},{3,0},{4,5},{5,6},{6,7},{7,4},{8,9},{9,10},{10,1... | collective-permute-start | bytes 983048 | tf_op jit(solution)/shard_map/ppermute | solution.py:246
  18.1 32.2 %collective-permute-start.3 = (bf16[256,640]{1,0:T(8,128)(2,1)S(1)}, bf16[256,640]{1,0:T(8,128)(2,1)S(1)}, u32[]{:S(2)}, u32[]{:S(2)}) collective-permute-start(bf16[256,640]{1,0:T(8,128)(2,1)S(1)} %fusion.3.after_ref.refs_5_), channel_id=1, source_target_pairs={{0,2},{1,3},{2,0},{3,1},{4,6},{5,7},{6,4},{7,5},{8,10},{9,11},{10,... | collective-permute-start | bytes 983048 | tf_op jit(solution)/shard_map/ppermute | solution.py:246
  18.2 32.1 %collective-permute-start.4 = (bf16[256,640]{1,0:T(8,128)(2,1)S(1)}, bf16[256,640]{1,0:T(8,128)(2,1)S(1)}, u32[]{:S(2)}, u32[]{:S(2)}) collective-permute-start(bf16[256,640]{1,0:T(8,128)(2,1)S(1)} %fusion.3.after_ref.refs_5_), channel_id=1, source_target_pairs={{0,3},{1,0},{2,1},{3,2},{4,7},{5,4},{6,5},{7,6},{8,11},{9,8},{10,9... | collective-permute-start | bytes 983048 | tf_op jit(solution)/shard_map/ppermute | solution.py:246
  50.3 0.7 %copy-start.3 = (bf16[256,640]{1,0:T(8,128)(2,1)}, bf16[256,640]{1,0:T(8,128)(2,1)S(1)}, u32[]{:S(2)}) copy-start(bf16[256,640]{1,0:T(8,128)(2,1)S(1)} %collective-permute-done.2.refs_6_) | copy-start | bytes 983044
  50.3 0.8 %copy-start.4 = (bf16[256,640]{1,0:T(8,128)(2,1)}, bf16[256,640]{1,0:T(8,128)(2,1)S(1)}, u32[]{:S(2)}) copy-start(bf16[256,640]{1,0:T(8,128)(2,1)S(1)} %collective-permute-done.3.refs_7_) | copy-start | bytes 983044
  50.4 0.9 %copy-start.5 = (bf16[256,640]{1,0:T(8,128)(2,1)}, bf16[256,640]{1,0:T(8,128)(2,1)S(1)}, u32[]{:S(2)}) copy-start(bf16[256,640]{1,0:T(8,128)(2,1)S(1)} %collective-permute-done.4.refs_8_) | copy-start | bytes 983044
